TPU v7x, 128 devices: a whole 4x4x4 slice. The times are simulated.
128 devices in a mesh: gx: 8 (over x, core), gy: 16 (over z, y).
Axes of the slice: x: 4, y: 4, z: 4, core: 2. Of those that a mesh axis runs over, the one named last changes fastest.
Arguments:
- features: bfloat16 [32, 64, 64, 128], P('gx', 'gy'), may hold values from -6 to 6
- skip_grad: bfloat16 [32, 64, 64, 128], P('gx', 'gy'), may hold values from -1.5 to 1.5
- bottom_grad: bfloat16 [16, 32, 32, 256], P('gx', 'gy'), may hold values from -6 to 6
- conv_one: bfloat16 [3, 3, 3, 128, 128], replicated, may hold values from -0.109375 to 0.109375
- conv_two: bfloat16 [3, 3, 3, 128, 128], replicated, may hold values from -0.109375 to 0.109375
- conv_three: bfloat16 [3, 3, 3, 128, 256], P(None, None, None, None, 'gy'), may hold values from -0.109375 to 0.109375
Outputs:
- bottleneck: bfloat16 [16, 32, 32, 256], P('gx', 'gy')
- input_grad: bfloat16 [32, 64, 64, 128], P('gx', 'gy')
- grad_one: float32 [3, 3, 3, 128, 128], replicated
- grad_two: float32 [3, 3, 3, 128, 128], replicated
- grad_three: float32 [3, 3, 3, 128, 256], P(None, None, None, None, 'gy')
All inputs are finite; a program needn't handle non-finite values.
Results may differ from a plain program's by a relative error of at most 0.018.
Values may be sent and summed in bfloat16 or wider, within the bound.
No kernel may reach another device: no remote copies, remote signals or barrier semaphores. Data moves between devices by JAX's collectives and lax.ppermute only.
A program may use at most 128 MiB of HBM per device.

v0:
```python
import math

import jax
import jax.numpy as jnp
from jax import lax
from jax.sharding import PartitionSpec as P


def padded_2(shard, sides, width):
    for axis, dim in sides:
        count, length = (lax.axis_size(axis), shard.shape[dim])
        up = [(i, (i + 1) % count) for i in range(count)]
        down = [(j, i) for i, j in up]
        last = lax.slice_in_dim(shard, length - width, length, axis=dim)
        first = lax.slice_in_dim(shard, 0, width, axis=dim)
        before = lax.ppermute(last, axis, up)
        after = lax.ppermute(first, axis, down)
        shard = jnp.concatenate([before, shard, after], axis=dim)
    return shard


def wrap_local(field, axis):
    length = field.shape[axis]
    lower = lax.slice_in_dim(field, length - 1, length, axis=axis)
    upper = lax.slice_in_dim(field, 0, 1, axis=axis)
    return jnp.concatenate([lower, field, upper], axis=axis)


def level_halo(field):
    return wrap_local(padded_2(field, (("gx", 0), ("gy", 1)), 1), 2)


def bottom_halo(field):
    return wrap_local(padded_2(field, (("gx", 0), ("gy", 1)), 1), 2)


def stacked_taps(padded, offset_x, offset_y):
    size_x = padded.shape[0] - 2
    size_y = padded.shape[1] - 2
    size_z = padded.shape[2] - 2
    window = padded[offset_x : offset_x + size_x, offset_y : offset_y + size_y]
    joined = jnp.concatenate(
        [window[:, :, 0:size_z], window[:, :, 1 : size_z + 1], window[:, :, 2 : size_z + 2]],
        axis=-1,
    )
    return joined.reshape(size_x * size_y * size_z, 3 * padded.shape[3])


def apply_taps(padded, weights):
    size_x = padded.shape[0] - 2
    size_y = padded.shape[1] - 2
    size_z = padded.shape[2] - 2
    in_chans = weights.shape[3]
    out_chans = weights.shape[4]
    running = jnp.zeros((size_x * size_y * size_z, out_chans), jnp.float32)
    for offset_x in range(3):
        for offset_y in range(3):
            stacked = stacked_taps(padded, offset_x, offset_y)
            running = running + jnp.dot(
                stacked,
                weights[offset_x, offset_y].reshape(3 * in_chans, out_chans),
                preferred_element_type=jnp.float32,
            )
    return running.reshape(size_x, size_y, size_z, out_chans)


def tap_grads(padded, errors):
    in_chans = padded.shape[3]
    out_chans = errors.shape[3]
    flat_errors = errors.reshape(-1, out_chans)
    pieces = []
    for offset_x in range(3):
        for offset_y in range(3):
            stacked = stacked_taps(padded, offset_x, offset_y)
            term = lax.dot_general(
                stacked, flat_errors, (((0,), (0,)), ((), ())), preferred_element_type=jnp.float32
            )
            pieces.append(term.reshape(3, in_chans, out_chans))
    return jnp.stack(pieces).reshape(3, 3, 3, in_chans, out_chans)


def flip_taps(weights):
    return jnp.swapaxes(jnp.flip(weights, (0, 1, 2)), 3, 4)


def silu_slope(values):
    sigma = jax.nn.sigmoid(values)
    return sigma * (1.0 + values * (1.0 - sigma))


def pool_blocks(field):
    size_x, size_y, size_z, chans = field.shape
    blocks = field.astype(jnp.float32).reshape(
        size_x // 2, 2, size_y // 2, 2, size_z // 2, 2, chans
    )
    return jnp.mean(blocks, axis=(1, 3, 5)).astype(jnp.bfloat16)


def spread_blocks(field):
    size_x, size_y, size_z, chans = field.shape
    wide = jnp.broadcast_to(
        field[:, None, :, None, :, None, :], (size_x, 2, size_y, 2, size_z, 2, chans)
    )
    return wide.reshape(size_x * 2, size_y * 2, size_z * 2, chans)


def level_sum(terms):
    return lax.psum(terms, ("gx", "gy"))


def on_device(features, skip_grad, bottom_grad, conv_one, conv_two, conv_three):
    fine_cells = (
        features.shape[0]
        * lax.axis_size("gx")
        * features.shape[1]
        * lax.axis_size("gy")
        * features.shape[2]
    )
    fine_scale = 1.0 / math.sqrt(fine_cells)
    coarse_scale = 1.0 / math.sqrt(fine_cells // 8)
    first_pad = level_halo(features)
    pre_one = apply_taps(first_pad, conv_one)
    act_one = jax.nn.silu(pre_one).astype(jnp.bfloat16)
    second_pad = level_halo(act_one)
    pre_two = apply_taps(second_pad, conv_two)
    act_two = jax.nn.silu(pre_two).astype(jnp.bfloat16)
    pooled = pool_blocks(act_two)
    wide_taps = lax.all_gather(conv_three, "gy", axis=4, tiled=True)
    pooled_pad = bottom_halo(pooled)
    pre_three = apply_taps(pooled_pad, wide_taps)
    bottleneck = jax.nn.silu(pre_three).astype(jnp.bfloat16)
    err_three = (bottom_grad.astype(jnp.float32) * silu_slope(pre_three)).astype(jnp.bfloat16)
    tap_terms = tap_grads(pooled_pad, err_three)
    own_three = lax.psum_scatter(
        tap_terms.astype(jnp.bfloat16), "gy", scatter_dimension=4, tiled=True
    )
    pooled_back = apply_taps(bottom_halo(err_three), flip_taps(wide_taps))
    grad_three = lax.psum(own_three, "gx").astype(jnp.float32) * coarse_scale
    upward = spread_blocks(pooled_back) * 0.125
    err_two = ((skip_grad.astype(jnp.float32) + upward) * silu_slope(pre_two)).astype(jnp.bfloat16)
    grad_two = level_sum(tap_grads(second_pad, err_two)) * fine_scale
    back_one = apply_taps(level_halo(err_two), flip_taps(conv_two))
    err_one = (back_one * silu_slope(pre_one)).astype(jnp.bfloat16)
    grad_one = level_sum(tap_grads(first_pad, err_one)) * fine_scale
    input_grad = apply_taps(level_halo(err_one), flip_taps(conv_one)).astype(jnp.bfloat16)
    return (bottleneck, input_grad, grad_one, grad_two, grad_three)


def solution(mesh):
    return jax.shard_map(
        on_device,
        mesh=mesh,
        in_specs=(
            P("gx", "gy", None, None),
            P("gx", "gy", None, None),
            P("gx", "gy", None, None),
            P(),
            P(),
            P(None, None, None, None, "gy"),
        ),
        out_specs=(
            P("gx", "gy", None, None),
            P("gx", "gy", None, None),
            P(),
            P(),
            P(None, None, None, None, "gy"),
        ),
        check_vma=False,
    )
```

profile of v0, /device:TPU:1, one launch (start us, length us, event | category | flops | bytes accessed | tf_op | source)
XLA Modules:
  0.0 464.3 jit_solution(10361284001489537765)
XLA Ops:
  8.2 2.6 collective-permute-start
  10.8 2.1 fusion.96
  15.9 5.0 %collective-permute-start.3 = (bf16[6,1,64,128]{3,2,1,0:T(8,128)(2,1)S(1)}, bf16[6,1,64,128]{3,2,1,0:T(8,128)(2,1)S(1)}, u32[]{:S(2)}, u32[]{:S(2)}) collective-permute-start(bf16[6,1,64,128]{3,2,1,0:T(8,128)(2,1)S(1)} %get-tuple-element.174), channel_id=1, source_target_pairs={{1,0},{2,1},{3,2},{4,3},{5,4},{6,5},{7,6},{8,7},{9,8},{10,9},{11,1... | collective-permute-start | bytes 294920 | tf_op jit(solution)/shard_map/ppermute | solution.py:17
  21.8 1.6 copy.190
  35.9 2.7 collective-permute-done.5
  39.2 5.5 %collective-permute-start.7 = (bf16[6,1,64,128]{3,2,1,0:T(8,128)(2,1)}, bf16[6,1,64,128]{3,2,1,0:T(8,128)(2,1)}, u32[]{:S(2)}, u32[]{:S(2)}) collective-permute-start(bf16[6,1,64,128]{3,2,1,0:T(8,128)(2,1)} %get-tuple-element.168), channel_id=1, source_target_pairs={{1,0},{2,1},{3,2},{4,3},{5,4},{6,5},{7,6},{8,7},{9,8},{10,9},{11,1... | collective-permute-start | bytes 294920 | tf_op jit(solution)/shard_map/ppermute | solution.py:17
  45.7 2.3 copy.191
  62.5 2.6 collective-permute-done.9
  65.2 5.6 %collective-permute-start.11 = (bf16[4,1,32,128]{3,2,1,0:T(8,128)(2,1)S(1)}, bf16[4,1,32,128]{3,2,1,0:T(8,128)(2,1)S(1)}, u32[]{:S(2)}, u32[]{:S(2)}) collective-permute-start(bf16[4,1,32,128]{3,2,1,0:T(8,128)(2,1)S(1)} %get-tuple-element.257), channel_id=1, source_target_pairs={{1,0},{2,1},{3,2},{4,3},{5,4},{6,5},{7,6},{8,7},{9,8},{10,9},{11,1... | collective-permute-start | bytes 98312 | tf_op jit(solution)/shard_map/ppermute | solution.py:17
  72.8 2.3 copy.193
  100.6 2.4 fusion.92
  103.0 1.7 copy.220
  120.2 14.7 %collective-permute-start.15 = (bf16[4,1,32,256]{3,2,1,0:T(8,128)(2,1)S(1)}, bf16[4,1,32,256]{3,2,1,0:T(8,128)(2,1)S(1)}, u32[]{:S(2)}, u32[]{:S(2)}) collective-permute-start(bf16[4,1,32,256]{3,2,1,0:T(8,128)(2,1)S(1)} %get-tuple-element.240), channel_id=1, source_target_pairs={{1,0},{2,1},{3,2},{4,3},{5,4},{6,5},{7,6},{8,7},{9,8},{10,9},{11,1... | collective-permute-start | bytes 196616 | tf_op jit(solution)/shard_map/ppermute | solution.py:17
  140.4 1.6 collective-permute-start.17
  145.4 5.5 %collective-permute-start.19 = (bf16[6,1,64,128]{3,2,1,0:T(8,128)(2,1)S(1)}, bf16[6,1,64,128]{3,2,1,0:T(8,128)(2,1)S(1)}, u32[]{:S(2)}, u32[]{:S(2)}) collective-permute-start(bf16[6,1,64,128]{3,2,1,0:T(8,128)(2,1)S(1)} %get-tuple-element.164), channel_id=1, source_target_pairs={{1,0},{2,1},{3,2},{4,3},{5,4},{6,5},{7,6},{8,7},{9,8},{10,9},{11,1... | collective-permute-start | bytes 294920 | tf_op jit(solution)/shard_map/ppermute | solution.py:17
  168.9 1.8 collective-permute-start.20
  170.6 2.1 collective-permute-start.21
  174.5 5.5 %collective-permute-start.23 = (bf16[6,1,64,128]{3,2,1,0:T(8,128)(2,1)S(1)}, bf16[6,1,64,128]{3,2,1,0:T(8,128)(2,1)S(1)}, u32[]{:S(2)}, u32[]{:S(2)}) collective-permute-start(bf16[6,1,64,128]{3,2,1,0:T(8,128)(2,1)S(1)} %get-tuple-element.160), channel_id=1, source_target_pairs={{1,0},{2,1},{3,2},{4,3},{5,4},{6,5},{7,6},{8,7},{9,8},{10,9},{11,1... | collective-permute-start | bytes 294920 | tf_op jit(solution)/shard_map/ppermute | solution.py:17
  180.1 2.2 copy.219
  190.6 131.3 %all-reduce.6.cloned.1.call-done = (f32[3,3,3,128,128]{4,3,2,1,0:T(8,128)}, f32[3,3,3,128,128]{4,3,2,1,0:T(8,128)}) async-done(((f32[3,3,3,128,128]{4,3,2,1,0:T(8,128)}, f32[3,3,3,128,128]{4,3,2,1,0:T(8,128)}), (f32[3,3,3,128,128]{4,3,2,1,0:T(8,128)}, f32[3,3,3,128,128]{4,3,2,1,0:T(8,128)})) %all-reduce.6.cloned.1.call-update) | async-done | bytes 3538960 | tf_op jit(solution)/shard_map/psum | solution.py:108
  321.9 3.1 broadcast_multiply_fusion
  324.9 71.2 %reduce-scatter.2.cloned.1.call-done = bf16[3,3,3,128,16]{3,4,2,1,0:T(8,128)(2,1)} async-done(((bf16[3,3,3,128,256]{3,4,2,1,0:T(8,128)(2,1)}), bf16[3,3,3,128,16]{3,4,2,1,0:T(8,128)(2,1)}) %reduce-scatter.2.cloned.1.call-update) | async-done | bytes 110608 | tf_op jit(solution)/shard_map/reduce_scatter | solution.py:134
  397.6 58.3 %all-reduce.4.cloned.1.call-done = bf16[3,3,3,128,16]{3,4,2,1,0:T(8,128)(2,1)} async-done(((bf16[3,3,3,128,16]{3,4,2,1,0:T(8,128)(2,1)}), bf16[3,3,3,128,16]{3,4,2,1,0:T(8,128)(2,1)}) %all-reduce.4.cloned.1.call-update) | async-done | bytes 110608 | tf_op jit(solution)/shard_map/psum | solution.py:138
  455.9 1.6 convert_multiply_fusion
  (499 shorter events, 112.7 us)
Async XLA Ops:
  7.2 93.4 %all-gather.2.cloned.1.call-start = ((), (), s32[]{:S(2)}) async-start(), calls=%async_computation.1 | async-start | bytes 1880064 | tf_op jit(solution)/shard_map/all_gather | solution.py:128
  8.2 4.8 %collective-permute-start = (bf16[1,4,64,128]{3,2,1,0:T(8,128)(2,1)S(1)}, bf16[1,4,64,128]{3,2,1,0:T(8,128)(2,1)S(1)}, u32[]{:S(2)}, u32[]{:S(2)}) collective-permute-start(bf16[1,4,64,128]{3,2,1,0:T(8,128)(2,1)S(1)} %get-tuple-element.212), channel_id=1, source_target_pairs={{0,16},{16,32},{32,48},{48,64},{64,80},{80,96},{96,112},{112,0},{1... | collective-permute-start | bytes 196616 | tf_op jit(solution)/shard_map/ppermute | solution.py:16
  10.8 3.7 collective-permute-start.1
  10.8 311.1 %all-reduce.6.cloned.1.call-start = ((), (), s32[]{:S(2)}) async-start(), calls=%async_computation.4 | async-start | bytes 7077888 | tf_op jit(solution)/shard_map/psum | solution.py:108
  14.5 9.0 %collective-permute-start.2 = (bf16[6,1,64,128]{3,2,1,0:T(8,128)(2,1)S(1)}, bf16[6,1,64,128]{3,2,1,0:T(8,128)(2,1)S(1)}, u32[]{:S(2)}, u32[]{:S(2)}) collective-permute-start(bf16[6,1,64,128]{3,2,1,0:T(8,128)(2,1)S(1)} %get-tuple-element.173), channel_id=1, source_target_pairs={{0,1},{1,2},{2,3},{3,4},{4,5},{5,6},{6,7},{7,8},{8,9},{9,10},{10,1... | collective-permute-start | bytes 294920 | tf_op jit(solution)/shard_map/ppermute | solution.py:16
  15.9 7.7 %collective-permute-start.3 = (bf16[6,1,64,128]{3,2,1,0:T(8,128)(2,1)S(1)}, bf16[6,1,64,128]{3,2,1,0:T(8,128)(2,1)S(1)}, u32[]{:S(2)}, u32[]{:S(2)}) collective-permute-start(bf16[6,1,64,128]{3,2,1,0:T(8,128)(2,1)S(1)} %get-tuple-element.174), channel_id=1, source_target_pairs={{1,0},{2,1},{3,2},{4,3},{5,4},{6,5},{7,6},{8,7},{9,8},{10,9},{11,1... | collective-permute-start | bytes 294920 | tf_op jit(solution)/shard_map/ppermute | solution.py:17
  34.5 4.0 collective-permute-start.5
  39.2 8.8 %collective-permute-start.6 = (bf16[6,1,64,128]{3,2,1,0:T(8,128)(2,1)}, bf16[6,1,64,128]{3,2,1,0:T(8,128)(2,1)}, u32[]{:S(2)}, u32[]{:S(2)}) collective-permute-start(bf16[6,1,64,128]{3,2,1,0:T(8,128)(2,1)} %get-tuple-element.167), channel_id=1, source_target_pairs={{0,1},{1,2},{2,3},{3,4},{4,5},{5,6},{6,7},{7,8},{8,9},{9,10},{10,1... | collective-permute-start | bytes 294920 | tf_op jit(solution)/shard_map/ppermute | solution.py:16
  39.2 8.8 %collective-permute-start.7 = (bf16[6,1,64,128]{3,2,1,0:T(8,128)(2,1)}, bf16[6,1,64,128]{3,2,1,0:T(8,128)(2,1)}, u32[]{:S(2)}, u32[]{:S(2)}) collective-permute-start(bf16[6,1,64,128]{3,2,1,0:T(8,128)(2,1)} %get-tuple-element.168), channel_id=1, source_target_pairs={{1,0},{2,1},{3,2},{4,3},{5,4},{6,5},{7,6},{8,7},{9,8},{10,9},{11,1... | collective-permute-start | bytes 294920 | tf_op jit(solution)/shard_map/ppermute | solution.py:17
  61.6 3.5 collective-permute-start.9
  65.1 28.4 %collective-permute-start.10 = (bf16[4,1,32,128]{3,2,1,0:T(8,128)(2,1)S(1)}, bf16[4,1,32,128]{3,2,1,0:T(8,128)(2,1)S(1)}, u32[]{:S(2)}, u32[]{:S(2)}) collective-permute-start(bf16[4,1,32,128]{3,2,1,0:T(8,128)(2,1)S(1)} %get-tuple-element.256), channel_id=1, source_target_pairs={{0,1},{1,2},{2,3},{3,4},{4,5},{5,6},{6,7},{7,8},{8,9},{9,10},{10,1... | collective-permute-start | bytes 98312 | tf_op jit(solution)/shard_map/ppermute | solution.py:16
  65.2 28.3 %collective-permute-start.11 = (bf16[4,1,32,128]{3,2,1,0:T(8,128)(2,1)S(1)}, bf16[4,1,32,128]{3,2,1,0:T(8,128)(2,1)S(1)}, u32[]{:S(2)}, u32[]{:S(2)}) collective-permute-start(bf16[4,1,32,128]{3,2,1,0:T(8,128)(2,1)S(1)} %get-tuple-element.257), channel_id=1, source_target_pairs={{1,0},{2,1},{3,2},{4,3},{5,4},{6,5},{7,6},{8,7},{9,8},{10,9},{11,1... | collective-permute-start | bytes 98312 | tf_op jit(solution)/shard_map/ppermute | solution.py:17
  120.1 15.0 %collective-permute-start.14 = (bf16[4,1,32,256]{3,2,1,0:T(8,128)(2,1)S(1)}, bf16[4,1,32,256]{3,2,1,0:T(8,128)(2,1)S(1)}, u32[]{:S(2)}, u32[]{:S(2)}) collective-permute-start(bf16[4,1,32,256]{3,2,1,0:T(8,128)(2,1)S(1)} %get-tuple-element.239), channel_id=1, source_target_pairs={{0,1},{1,2},{2,3},{3,4},{4,5},{5,6},{6,7},{7,8},{8,9},{9,10},{10,1... | collective-permute-start | bytes 196616 | tf_op jit(solution)/shard_map/ppermute | solution.py:16
  120.2 16.1 %collective-permute-start.15 = (bf16[4,1,32,256]{3,2,1,0:T(8,128)(2,1)S(1)}, bf16[4,1,32,256]{3,2,1,0:T(8,128)(2,1)S(1)}, u32[]{:S(2)}, u32[]{:S(2)}) collective-permute-start(bf16[4,1,32,256]{3,2,1,0:T(8,128)(2,1)S(1)} %get-tuple-element.240), channel_id=1, source_target_pairs={{1,0},{2,1},{3,2},{4,3},{5,4},{6,5},{7,6},{8,7},{9,8},{10,9},{11,1... | collective-permute-start | bytes 196616 | tf_op jit(solution)/shard_map/ppermute | solution.py:17
  139.2 6.0 %collective-permute-start.16 = (bf16[1,4,64,128]{3,2,1,0:T(8,128)(2,1)S(1)}, bf16[1,4,64,128]{3,2,1,0:T(8,128)(2,1)S(1)}, u32[]{:S(2)}, u32[]{:S(2)}) collective-permute-start(bf16[1,4,64,128]{3,2,1,0:T(8,128)(2,1)S(1)} %get-tuple-element.201), channel_id=1, source_target_pairs={{0,16},{16,32},{32,48},{48,64},{64,80},{80,96},{96,112},{112,0},{1... | collective-permute-start | bytes 196616 | tf_op jit(solution)/shard_map/ppermute | solution.py:16
  140.4 4.8 %collective-permute-start.17 = (bf16[1,4,64,128]{3,2,1,0:T(8,128)(2,1)S(1)}, bf16[1,4,64,128]{3,2,1,0:T(8,128)(2,1)S(1)}, u32[]{:S(2)}, u32[]{:S(2)}) collective-permute-start(bf16[1,4,64,128]{3,2,1,0:T(8,128)(2,1)S(1)} %get-tuple-element.202), channel_id=1, source_target_pairs={{16,0},{32,16},{48,32},{64,48},{80,64},{96,80},{112,96},{0,112},{1... | collective-permute-start | bytes 196616 | tf_op jit(solution)/shard_map/ppermute | solution.py:17
  145.3 7.5 %collective-permute-start.18 = (bf16[6,1,64,128]{3,2,1,0:T(8,128)(2,1)S(1)}, bf16[6,1,64,128]{3,2,1,0:T(8,128)(2,1)S(1)}, u32[]{:S(2)}, u32[]{:S(2)}) collective-permute-start(bf16[6,1,64,128]{3,2,1,0:T(8,128)(2,1)S(1)} %get-tuple-element.163), channel_id=1, source_target_pairs={{0,1},{1,2},{2,3},{3,4},{4,5},{5,6},{6,7},{7,8},{8,9},{9,10},{10,1... | collective-permute-start | bytes 294920 | tf_op jit(solution)/shard_map/ppermute | solution.py:16
  145.4 7.4 %collective-permute-start.19 = (bf16[6,1,64,128]{3,2,1,0:T(8,128)(2,1)S(1)}, bf16[6,1,64,128]{3,2,1,0:T(8,128)(2,1)S(1)}, u32[]{:S(2)}, u32[]{:S(2)}) collective-permute-start(bf16[6,1,64,128]{3,2,1,0:T(8,128)(2,1)S(1)} %get-tuple-element.164), channel_id=1, source_target_pairs={{1,0},{2,1},{3,2},{4,3},{5,4},{6,5},{7,6},{8,7},{9,8},{10,9},{11,1... | collective-permute-start | bytes 294920 | tf_op jit(solution)/shard_map/ppermute | solution.py:17
  166.6 229.5 %reduce-scatter.2.cloned.1.call-start = ((), (), s32[]{:S(2)}) async-start(), calls=%async_computation.2 | async-start | bytes 1880064 | tf_op jit(solution)/shard_map/reduce_scatter | solution.py:134
  168.9 4.6 collective-permute-start.20
  170.6 3.7 collective-permute-start.21
  174.4 8.3 %collective-permute-start.22 = (bf16[6,1,64,128]{3,2,1,0:T(8,128)(2,1)S(1)}, bf16[6,1,64,128]{3,2,1,0:T(8,128)(2,1)S(1)}, u32[]{:S(2)}, u32[]{:S(2)}) collective-permute-start(bf16[6,1,64,128]{3,2,1,0:T(8,128)(2,1)S(1)} %get-tuple-element.159), channel_id=1, source_target_pairs={{0,1},{1,2},{2,3},{3,4},{4,5},{5,6},{6,7},{7,8},{8,9},{9,10},{10,1... | collective-permute-start | bytes 294920 | tf_op jit(solution)/shard_map/ppermute | solution.py:16
  174.5 8.2 %collective-permute-start.23 = (bf16[6,1,64,128]{3,2,1,0:T(8,128)(2,1)S(1)}, bf16[6,1,64,128]{3,2,1,0:T(8,128)(2,1)S(1)}, u32[]{:S(2)}, u32[]{:S(2)}) collective-permute-start(bf16[6,1,64,128]{3,2,1,0:T(8,128)(2,1)S(1)} %get-tuple-element.160), channel_id=1, source_target_pairs={{1,0},{2,1},{3,2},{4,3},{5,4},{6,5},{7,6},{8,7},{9,8},{10,9},{11,1... | collective-permute-start | bytes 294920 | tf_op jit(solution)/shard_map/ppermute | solution.py:17
  182.4 273.6 %all-reduce.4.cloned.1.call-start = ((), (), s32[]{:S(2)}) async-start(), calls=%async_computation.3 | async-start | bytes 221184 | tf_op jit(solution)/shard_map/psum | solution.py:138
  (118 other events, 335.0 us)
Sparse Core Ops, SparseCore 0:
  10.9 48.6 all-gather.1
  166.7 155.1 all-reduce.5
  325.2 70.8 reduce-scatter.1
  398.3 57.5 all-reduce.3
where the time goes:
time: 466 us; the launch traced here: 464 us
  waiting for transfers between devices  275 us (59%)
  local copies, waits for them, and re-layouts  69.6 us (15%)
  starting transfers between devices  56.2 us (12%)
  matrix products  29.6 us (6%)
  other arithmetic  17.4 us (4%)
  between operations  16.4 us (4%)
    psum x1, waiting for transfers between devices, level_sum(): return lax.psum(terms, ('gx', 'gy'))  131 us
    reduce_scatter x1, waiting for transfers between devices, on_device(): lax.psum_scatter(tap_terms.astype(jnp.bfloat16), 'gy', scatter_dimension=...  71.2 us
    psum x1, waiting for transfers between devices, on_device(): grad_three = lax.psum(own_three, 'gx').astype(jnp.float32) * coarse_scale  58.3 us
    ppermute x12, starting transfers between devices, padded_2(): after = lax.ppermute(first, axis, down)  45.9 us
    unnamed x241, local copies, waits for them, and re-layouts  24.5 us
    reshape x18, local copies, waits for them, and re-layouts, stacked_taps(): return joined.reshape(size_x * size_y * size_z, 3 * padded.shape[3])  21.7 us
    dot_general x54, matrix products, apply_taps(): jnp.dot(stacked, weights[offset_x, offset_y].reshape(3 * in_chans, out_ch...  21.3 us
    ppermute x12, waiting for transfers between devices, padded_2(): after = lax.ppermute(first, axis, down)  10 us
  transfers between devices with their start and end apart: 28, of which 14 were waited for; matrix products, arithmetic and copies ran while one was open for 16% of the time, Pallas kernels for 0%

commit v1 on v0

v1 whole, which is shorter than its diff:
```python
import math

import jax
import jax.numpy as jnp
from jax import lax
from jax.experimental import pallas as pl
from jax.experimental.pallas import tpu as pltpu
from jax.sharding import Mesh
from jax.sharding import PartitionSpec as P

GX = ("x", "c")
GY = ("z", "y")
FLAT = ("x", "z", "y")
F32 = jnp.float32
BF16 = jnp.bfloat16
UNITS = 7


def shifted(array, axes, step):
    count = lax.axis_size(axes)
    return lax.ppermute(array, axes, [(i, (i + step) % count) for i in range(count)])


def swap_cores(array):
    return lax.ppermute(array, "c", [(0, 1), (1, 0)])


def halo_pieces(own, width):
    before = shifted(own[:, -width:], GY, 1)
    after = shifted(own[:, :width], GY, -1)
    low = jnp.concatenate([before[:width], own[:width], after[:width]], axis=1)
    high = jnp.concatenate([before[-width:], own[-width:], after[-width:]], axis=1)
    left = shifted(high, GX, 1)
    right = shifted(low, GX, -1)
    return own, before, after, left, right


def fill_padded(padded, own, before, after, left, right):
    size_x, size_y = own.shape[0], own.shape[1]
    width = left.shape[0]
    padded[0:width] = left[...]
    padded[width + size_x : 2 * width + size_x] = right[...]
    middle = slice(width, width + size_x)
    padded[middle, 0:width] = before[...]
    padded[middle, width : width + size_y] = own[...]
    padded[middle, width + size_y : 2 * width + size_y] = after[...]


def slope_and_silu(values):
    sigma = 1.0 / (1.0 + jnp.exp(-values))
    return values * sigma, sigma * (1.0 + values * (1.0 - sigma))


def window_rows(source, row, count, skip=0):
    pieces = []
    for kx in range(3):
        for ky in range(3):
            block = source[row + kx + skip, ky + skip : ky + skip + count]
            pieces.append(block.reshape(block.shape[0] * block.shape[1], block.shape[2]))
    return jnp.concatenate(pieces, axis=1)


def roll_z(values, step):
    return pltpu.roll(values, step % values.shape[1], 1)


def join_taps(product, count, size_z, chans):
    parts = product.reshape(count, size_z, 3 * chans)
    return (
        roll_z(parts[:, :, 0:chans], 1)
        + parts[:, :, chans : 2 * chans]
        + roll_z(parts[:, :, 2 * chans : 3 * chans], -1)
    )


def spread_errors(errors):
    count, size_z, chans = errors.shape
    parts = [roll_z(errors, -1), errors, roll_z(errors, 1)]
    return jnp.concatenate([p.reshape(count * size_z, chans) for p in parts], axis=1).astype(BF16)


def fill_forward(packed, taps):
    for kx in range(3):
        for ky in range(3):
            for kz in range(3):
                at = kx * 3 + ky
                packed[at * 128 : at * 128 + 128, kz * 128 : kz * 128 + 128] = taps[at * 3 + kz]


def fill_backward(packed, taps):
    for kx in range(3):
        for ky in range(3):
            for kz in range(3):
                at = kx * 3 + ky
                packed[kz * 128 : kz * 128 + 128, at * 128 : at * 128 + 128] = taps[26 - at * 3 - kz]


def dot_nn(left, right):
    return lax.dot_general(left, right, (((1,), (0,)), ((), ())), preferred_element_type=F32)


def dot_nt(left, right):
    return lax.dot_general(left, right, (((1,), (1,)), ((), ())), preferred_element_type=F32)


def dot_tn(left, right):
    return lax.dot_general(left, right, (((0,), (0,)), ((), ())), preferred_element_type=F32)


def forward_kernel(own, before, after, left, right, taps_one, taps_two,
                   act_one, slope_one, slope_two, pooled, padded, packed, halves):
    fill_padded(padded, own, before, after, left, right)
    fill_forward(packed, taps_one)

    def first(row, _):
        product = dot_nn(window_rows(padded, row, 6), packed[...])
        act, slope = slope_and_silu(join_taps(product, 6, 64, 128))
        act_one[row] = act.astype(BF16)
        slope_one[row] = slope
        return 0

    lax.fori_loop(0, 6, first, 0)
    fill_forward(packed, taps_two)

    def second(row, _):
        product = dot_nn(window_rows(act_one, row, 4), packed[...])
        act, slope = slope_and_silu(join_taps(product, 4, 64, 128))
        slope_two[row] = slope
        act = act.astype(BF16).astype(F32)
        halves[row] = act.reshape(2, 2, 64, 128).sum(axis=1)
        return 0

    lax.fori_loop(0, 4, second, 0)
    for at_x in range(2):
        for at_y in range(2):
            total = 0.0
            for part in range(2):
                for start in range(2):
                    total = total + halves[2 * at_x + part, at_y, pl.ds(start, 32, stride=2), :]
            pooled[at_x, at_y] = (total * 0.125).astype(BF16)


def bottom_kernel(own, before, after, left, right, g_own, g_before, g_after, g_left, g_right,
                  taps_three, slope_two, skip, bottleneck, err_three, err_two,
                  padded, grads, packed, errors, wide):
    fill_padded(padded, own, before, after, left, right)
    fill_padded(grads, g_own, g_before, g_after, g_left, g_right)
    for at in range(9):
        for kz in range(3):
            packed[kz * 256 : kz * 256 + 256, at * 128 : at * 128 + 128] = taps_three[at * 3 + kz]
    for row in range(4):
        product = dot_nt(window_rows(padded, row, 4), packed[...])
        act, slope = slope_and_silu(join_taps(product, 4, 32, 256))
        if row in (1, 2):
            bottleneck[row - 1] = act[1:3].astype(BF16)
        errs = (grads[row].astype(F32) * slope).astype(BF16)
        errors[row] = errs
        if row in (1, 2):
            err_three[row - 1] = errs[1:3]
    for row in range(2):
        total = jnp.zeros((64, 384), F32)
        for kx in range(3):
            for ky in range(3):
                block = errors[row + kx, ky : ky + 2].reshape(64, 256)
                at = kx * 3 + ky
                back = jnp.concatenate(
                    [taps_three[26 - at * 3 - kz] for kz in range(3)], axis=1
                )
                total = total + dot_nn(block, back)
        upward = join_taps(total, 2, 32, 128) * 0.125
        for at_y in range(2):
            wide[pl.ds(0, 32, stride=2), :] = upward[at_y]
            wide[pl.ds(1, 32, stride=2), :] = upward[at_y]
            for dx in range(2):
                for dy in range(2):
                    at = (2 * row + dx, 2 * at_y + dy)
                    err_two[at] = (
                        (skip[at].astype(F32) + wide[...]) * slope_two[at]
                    ).astype(BF16)


def add_tap_grads(total, fields, skip, error_rows):
    total[...] = jnp.zeros_like(total)

    def step(row, _):
        total[...] += dot_tn(
            window_rows(fields, row, 4, skip), spread_errors(error_rows(row).astype(F32))
        )
        return 0

    lax.fori_loop(0, 4, step, 0)


def store_tap_grads(out, total):
    for at in range(9):
        for kz in range(3):
            rows = (at * 3 + kz) * 128
            out[rows : rows + 128] = total[
                at * 128 : at * 128 + 128, kz * 128 : kz * 128 + 128
            ].astype(BF16)
    out[3456:3584] = jnp.zeros((128, 128), BF16)


def middle_grads_kernel(act_one, err_two, out, total):
    add_tap_grads(total, act_one, 0, lambda row: err_two[row])
    store_tap_grads(out, total)


def bottom_grads_kernel(own, before, after, left, right, err_three, out, padded, total):
    fill_padded(padded, own, before, after, left, right)
    for row in range(2):
        term = dot_tn(
            spread_errors(err_three[row].astype(F32)), window_rows(padded, row, 2, 1)
        )
        if row == 0:
            total[...] = term
        else:
            total[...] += term
    for unit in range(28):
        at_x, at_t = unit // UNITS, unit % UNITS
        if unit == 27:
            out[:, at_x * 16 : at_x * 16 + 16, at_t] = jnp.zeros((2, 16, 8, 128), BF16)
            continue
        at, kz = unit // 3, unit % 3
        block = total[kz * 256 : kz * 256 + 256, at * 128 : at * 128 + 128]
        block = block.reshape(16, 2, 8, 128)
        for half in range(2):
            out[half, at_x * 16 : at_x * 16 + 16, at_t] = block[:, half].astype(BF16)


def first_errors_kernel(own, before, after, left, right, taps_two, slope_one,
                        f_own, f_before, f_after, f_left, f_right, err_one, out,
                        padded, packed, total):
    fill_padded(padded, own, before, after, left, right)
    fill_backward(packed, taps_two)

    def step(row, _):
        product = dot_nt(window_rows(padded, row, 6), packed[...])
        back = join_taps(product, 6, 64, 128)
        err_one[row] = (back * slope_one[row]).astype(BF16)
        return 0

    lax.fori_loop(0, 6, step, 0)
    fill_padded(padded, f_own, f_before, f_after, f_left, f_right)
    add_tap_grads(total, padded, 1, lambda row: err_one[row + 1, 1:5])
    store_tap_grads(out, total)


def input_kernel(err_one, taps_one, out, packed):
    fill_backward(packed, taps_one)

    def step(row, _):
        product = dot_nt(window_rows(err_one, row, 4), packed[...])
        out[row] = join_taps(product, 4, 64, 128).astype(BF16)
        return 0

    lax.fori_loop(0, 4, step, 0)


def call(kernel, out_shapes, scratch, flops, *operands):
    shapes = [jax.ShapeDtypeStruct(s, d) for s, d in out_shapes]
    moved = sum(o.size * o.dtype.itemsize for o in operands)
    return pl.pallas_call(
        kernel,
        out_shape=shapes,
        in_specs=[pl.BlockSpec(memory_space=pltpu.VMEM)] * len(operands),
        out_specs=[pl.BlockSpec(memory_space=pltpu.VMEM)] * len(shapes),
        scratch_shapes=[pltpu.VMEM(s, d) for s, d in scratch],
        compiler_params=pltpu.CompilerParams(vmem_limit_bytes=48 << 20),
        cost_estimate=pl.CostEstimate(flops=flops, bytes_accessed=moved, transcendentals=0),
        name=kernel.__name__,
    )(*operands)


def pick(stacked, index):
    return lax.dynamic_index_in_dim(stacked, index, 0, keepdims=False)


def summed_pieces(pieces):
    arrived = lax.all_to_all(pieces, FLAT, 0, 0)
    return jnp.sum(arrived.astype(F32), axis=0).astype(BF16)


def on_device(features, skip_grad, bottom_grad, conv_one, conv_two, conv_three):
    core = lax.axis_index("c")
    fine_cells = features.size // 128 * lax.axis_size(GX) * lax.axis_size(GY)
    fine_scale = 1.0 / math.sqrt(fine_cells)
    coarse_scale = 1.0 / math.sqrt(fine_cells // 8)
    taps_one = conv_one.reshape(27, 128, 128)
    taps_two = conv_two.reshape(27, 128, 128)

    f_pieces = halo_pieces(features, 2)

    own_taps = jnp.swapaxes(conv_three.reshape(27, 128, 16), 1, 2)
    half_taps = pick(jnp.swapaxes(own_taps.reshape(27, 2, 8, 128), 0, 1), core)
    mine = lax.all_gather(half_taps, GY)
    theirs = swap_cores(mine)
    both = jnp.where(core == 0, jnp.stack([mine, theirs]), jnp.stack([theirs, mine]))
    taps_three = jnp.transpose(both, (2, 1, 0, 3, 4)).reshape(27, 256, 128)

    g_pieces = halo_pieces(bottom_grad, 1)

    conv_flops = 2 * 1152 * 128 * 1024 * 3
    act_one, slope_one, slope_two, pooled = call(
        forward_kernel,
        [((6, 6, 64, 128), BF16), ((6, 6, 64, 128), F32), ((4, 4, 64, 128), F32), ((2, 2, 32, 128), BF16)],
        [((8, 8, 64, 128), BF16), ((1152, 384), BF16), ((4, 2, 64, 128), F32)],
        3 * conv_flops, *f_pieces, taps_one, taps_two,
    )
    p_pieces = halo_pieces(pooled, 2)
    bottleneck, err_three, err_two = call(
        bottom_kernel,
        [((2, 2, 32, 256), BF16), ((2, 2, 32, 256), BF16), ((4, 4, 64, 128), BF16)],
        [((6, 6, 32, 128), BF16), ((4, 4, 32, 256), BF16), ((768, 1152), BF16),
         ((4, 4, 32, 256), BF16), ((64, 128), F32)],
        conv_flops, *p_pieces, *g_pieces, taps_three, slope_two, skip_grad,
    )
    e_pieces = halo_pieces(err_two, 2)

    (three,) = call(
        bottom_grads_kernel, [((2, 64, UNITS, 8, 128), BF16)],
        [((6, 6, 32, 128), BF16), ((768, 1152), F32)],
        conv_flops // 4, *p_pieces, err_three,
    )
    (two,) = call(
        middle_grads_kernel, [((3584, 128), BF16)], [((1152, 384), F32)],
        conv_flops, act_one, err_two,
    )
    kept = pick(three, core).astype(F32) + swap_cores(pick(three, 1 - core)).astype(F32)
    three_part = summed_pieces(kept.astype(BF16))

    err_one, one = call(
        first_errors_kernel, [((6, 6, 64, 128), BF16), ((3584, 128), BF16)],
        [((8, 8, 64, 128), BF16), ((384, 1152), BF16), ((1152, 384), F32)],
        3 * conv_flops, *e_pieces, taps_two, slope_one, *f_pieces,
    )
    sent = jnp.where(core == 0, two, one)
    kept = jnp.where(core == 0, one, two).astype(F32) + swap_cores(sent).astype(F32)
    part = summed_pieces(kept.astype(BF16).reshape(64, UNITS, 8, 128))
    whole = lax.all_to_all(jnp.broadcast_to(part, (64, UNITS, 8, 128)), FLAT, 0, 0)
    (input_grad,) = call(
        input_kernel, [((4, 4, 64, 128), BF16)], [((384, 1152), BF16)],
        conv_flops, err_one, taps_one,
    )
    whole = whole.reshape(3584, 128)[:3456].reshape(3, 3, 3, 128, 128)
    other = swap_cores(whole)
    grad_one = jnp.where(core == 0, whole, other).astype(F32) * fine_scale
    grad_two = jnp.where(core == 0, other, whole).astype(F32) * fine_scale

    three_all = lax.all_to_all(jnp.broadcast_to(three_part, (8, UNITS, 8, 128)), GX, 0, 0)
    three_all = three_all.reshape(4, 2, UNITS, 8, 128).transpose(0, 2, 1, 3, 4)
    three_all = three_all.reshape(28, 16, 128)[:27].astype(F32) * coarse_scale
    grad_three = jnp.swapaxes(three_all, 1, 2).reshape(3, 3, 3, 128, 16)
    return (bottleneck, input_grad, grad_one, grad_two, grad_three)


def solution(mesh):
    fine = Mesh(mesh.devices.reshape(4, 2, 4, 4), ("x", "c", "z", "y"))
    cells = P(GX, GY, None, None)
    outs = P(None, None, None, None, GY)
    return jax.shard_map(
        on_device,
        mesh=fine,
        in_specs=(cells, cells, cells, P(), P(), outs),
        out_specs=(cells, cells, P(), P(), outs),
        check_vma=False,
    )
```

time: 466 us -> 188 us (0.40)
  waiting for transfers between devices: 275 us -> 55.1 us
  local copies, waits for them, and re-layouts: 69.6 us -> 7.82 us
  matrix products: 29.6 us -> 0 us
  Pallas kernels: 0 us -> 22.5 us
  blocking collectives: 0 us -> 21.3 us
  between operations: 16.4 us -> 1 us
  starting transfers between devices: 56.2 us -> 67.2 us
  other arithmetic: 17.4 us -> 12.1 us
    psum x2 -> x0, waiting for transfers between devices: 190 us -> none  [the longest x1 131 us: level_sum(): return lax.psum(terms, ('gx', 'gy'))]
    reduce_scatter x1 -> x0, waiting for transfers between devices: 71.2 us -> none  [on_device(): lax.psum_scatter(tap_terms.astype(jnp.bfloat16), 'gy', scatter_dimension=...]
    all_to_all x0 -> x4, waiting for transfers between devices: none -> 37.4 us  [the longest x2 22.5 us: summed_pieces(): arrived = lax.all_to_all(pieces, FLAT, 0, 0)]
    dot_general x81 -> x0, matrix products: 29.6 us -> none  [the longest x54 21.3 us: apply_taps(): jnp.dot(stacked, weights[offset_x, offset_y].reshape(3 * in_chans, out_ch...]
    unnamed x241 -> x18, local copies, waits for them, and re-layouts: 24.5 us -> 0.46 us
    all_to_all x0 -> x4, starting transfers between devices: none -> 23.1 us  [the longest x2 10.5 us: summed_pieces(): arrived = lax.all_to_all(pieces, FLAT, 0, 0)]
    pallas_call x0 -> x6, Pallas kernels: none -> 22.5 us  [call(): pl.pallas_call(kernel, out_shape=shapes, in_specs=[pl.BlockSpec(memory_sp...]
    reshape x18 -> x0, local copies, waits for them, and re-layouts: 21.7 us -> none  [stacked_taps(): return joined.reshape(size_x * size_y * size_z, 3 * padded.shape[3])]
  transfers between devices with their start and end apart: 28 -> 24, of which waited for: 14 -> 11; matrix products, arithmetic and copies ran while one was open for 16% -> 7% of each run, Pallas kernels for 0% -> 7%
where the time goes in v1:
time: 188 us; the launch traced here: 187 us
  starting transfers between devices  67.2 us (36%)
  waiting for transfers between devices  55.1 us (29%)
  Pallas kernels  22.5 us (12%)
  blocking collectives  21.3 us (11%)
  other arithmetic  12.1 us (6%)
  local copies, waits for them, and re-layouts  7.82 us (4%)
    ppermute x16, starting transfers between devices, shifted(): lax.ppermute(array, axes, [(i, (i + step) % count) for i in range(count)])  31.6 us
    all_to_all x2, waiting for transfers between devices, summed_pieces(): arrived = lax.all_to_all(pieces, FLAT, 0, 0)  22.5 us
    pallas_call x6, Pallas kernels, call(): pl.pallas_call(kernel, out_shape=shapes, in_specs=[pl.BlockSpec(memory_sp...  22.5 us
    all_gather x1, blocking collectives, on_device(): mine = lax.all_gather(half_taps, GY)  21.3 us
    ppermute x16, waiting for transfers between devices, shifted(): lax.ppermute(array, axes, [(i, (i + step) % count) for i in range(count)])  15.7 us
    all_to_all x1, waiting for transfers between devices, on_device(): lax.all_to_all(jnp.broadcast_to(part, (64, UNITS, 8, 128)), FLAT, 0, 0)  12.6 us
    ppermute x4, starting transfers between devices, swap_cores(): return lax.ppermute(array, 'c', [(0, 1), (1, 0)])  12.5 us
    all_to_all x2, starting transfers between devices, summed_pieces(): arrived = lax.all_to_all(pieces, FLAT, 0, 0)  10.5 us
  transfers between devices with their start and end apart: 24, of which 11 were waited for; matrix products, arithmetic and copies ran while one was open for 7% of the time, Pallas kernels for 7%

profile of v1, /device:TPU:1, one launch (start us, length us, event | category | flops | bytes accessed | tf_op | source)
XLA Modules:
  0.0 187.1 jit_solution(16209280971552554471)
XLA Ops:
  1.5 7.0 %collective-permute-start.9 = (bf16[2,1,32,256]{3,2,1,0:T(8,128)(2,1)S(1)}, bf16[2,1,32,256]{3,2,1,0:T(8,128)(2,1)S(1)}, u32[]{:S(2)}, u32[]{:S(2)}) collective-permute-start(bf16[2,1,32,256]{3,2,1,0:T(8,128)(2,1)S(1)} %get-tuple-element.43), channel_id=1, source_target_pairs={{0,15},{1,0},{2,1},{3,2},{4,3},{5,4},{6,5},{7,6},{8,7},{9,8},{10,9... | collective-permute-start | bytes 98312 | tf_op jit(solution)/shard_map/ppermute | solution.py:21
  9.5 4.9 %collective-permute-start.1 = (bf16[4,2,64,128]{3,2,1,0:T(8,128)(2,1)S(1)}, bf16[4,2,64,128]{3,2,1,0:T(8,128)(2,1)S(1)}, u32[]{:S(2)}, u32[]{:S(2)}) collective-permute-start(bf16[4,2,64,128]{3,2,1,0:T(8,128)(2,1)S(1)} %get-tuple-element.31), channel_id=1, source_target_pairs={{0,15},{1,0},{2,1},{3,2},{4,3},{5,4},{6,5},{7,6},{8,7},{9,8},{10,9... | collective-permute-start | bytes 393224 | tf_op jit(solution)/shard_map/ppermute | solution.py:21
  14.4 21.3 %all-gather = bf16[432,1,8,128]{3,2,1,0:T(8,128)(2,1)} all-gather(bf16[27,1,8,128]{3,2,1,0:T(8,128)(2,1)S(1)} %constant_dynamic-slice_fusion), channel_id=2, replica_groups=mesh['x'=4,'c'=2,'z'=4,'y'=4] {'z','y'}, dimensions={0}, use_global_device_ids=true | all-gather | bytes 940032 | tf_op jit(solution)/shard_map/all_gather | solution.py:296
  35.8 7.0 %collective-permute-start.12 = (bf16[16,27,8,128]{3,2,1,0:T(8,128)(2,1)}, bf16[16,27,8,128]{3,2,1,0:T(8,128)(2,1)}, u32[]{:S(2)}, u32[]{:S(2)}) collective-permute-start(bf16[16,27,8,128]{3,2,1,0:T(8,128)(2,1)} %bitcast.6), channel_id=1, source_target_pairs={{0,16},{16,0},{1,17},{17,1},{2,18},{18,2},{3,19},{19,3},{4,20},{20... | collective-permute-start | bytes 2654216 | tf_op jit(solution)/shard_map/ppermute | solution.py:25
  47.4 2.8 %collective-permute-done.3.right.f_right = bf16[2,8,64,128]{3,2,1,0:T(8,128)(2,1)S(1)} collective-permute-done((bf16[2,8,64,128]{3,2,1,0:T(8,128)(2,1)S(1)}, bf16[2,8,64,128]{3,2,1,0:T(8,128)(2,1)S(1)}, u32[]{:S(2)}, u32[]{:S(2)}) %collective-permute-start.3) | collective-permute-done | bytes 262176 | tf_op jit(solution)/shard_map/ppermute | solution.py:21
  50.2 6.7 %forward_kernel.1 = (bf16[6,6,64,128]{3,2,1,0:T(8,128)(2,1)S(1)}, f32[6,6,64,128]{3,2,1,0:T(8,128)S(1)}, f32[4,4,64,128]{3,2,1,0:T(8,128)S(1)}, bf16[2,2,32,128]{3,2,1,0:T(8,128)(2,1)S(1)}) custom-call(bf16[4,4,64,128]{3,2,1,0:T(8,128)(2,1)S(1)} %copy-done.1, bf16[4,2,64,128]{3,2,1,0:T(8,128)(2,1)S(1)} %collective-permute-done.before.f_before, ...), custom_call_target="tpu_custom_call" | custom-call | flops 2717908992 | bytes 2818048 | tf_op jit(solution)/shard_map/forward_kernel/pallas_call | solution.py:263
  58.1 3.8 %collective-permute-start.5 = (bf16[2,2,32,128]{3,2,1,0:T(8,128)(2,1)S(1)}, bf16[2,2,32,128]{3,2,1,0:T(8,128)(2,1)S(1)}, u32[]{:S(2)}, u32[]{:S(2)}) collective-permute-start(bf16[2,2,32,128]{3,2,1,0:T(8,128)(2,1)S(1)} %get-tuple-element.14.own), channel_id=1, source_target_pairs={{0,15},{1,0},{2,1},{3,2},{4,3},{5,4},{6,5},{7,6},{8,7},{9,8},{10,9... | collective-permute-start | bytes 98312 | tf_op jit(solution)/shard_map/ppermute | solution.py:21
  63.6 3.0 %collective-permute-start.7 = (bf16[2,6,32,128]{3,2,1,0:T(8,128)(2,1)S(1)}, bf16[2,6,32,128]{3,2,1,0:T(8,128)(2,1)S(1)}, u32[]{:S(2)}, u32[]{:S(2)}) collective-permute-start(bf16[2,6,32,128]{3,2,1,0:T(8,128)(2,1)S(1)} %constant_dynamic-update-slice_fusion), channel_id=1, source_target_pairs={{0,112},{16,0},{32,16},{48,32},{64,48},{80,64},{96,80},{112,96},{1... | collective-permute-start | bytes 294920 | tf_op jit(solution)/shard_map/ppermute | solution.py:21
  69.8 3.1 %bottom_kernel.1 = (bf16[2,2,32,256]{3,2,1,0:T(8,128)(2,1)}, bf16[2,2,32,256]{3,2,1,0:T(8,128)(2,1)S(1)}, bf16[4,4,64,128]{3,2,1,0:T(8,128)(2,1)S(1)}) custom-call(bf16[2,2,32,128]{3,2,1,0:T(8,128)(2,1)S(1)} %get-tuple-element.14.own, bf16[2,2,32,128]{3,2,1,0:T(8,128)(2,1)S(1)} %collective-permute-done.4.before, ...), custom_call_target="tpu_custom_call" | custom-call | flops 905969664 | bytes 3112960 | tf_op jit(solution)/shard_map/bottom_kernel/pallas_call | solution.py:263
  72.9 5.4 %collective-permute-start.14 = (bf16[4,2,64,128]{3,2,1,0:T(8,128)(2,1)S(1)}, bf16[4,2,64,128]{3,2,1,0:T(8,128)(2,1)S(1)}, u32[]{:S(2)}, u32[]{:S(2)}) collective-permute-start(bf16[4,2,64,128]{3,2,1,0:T(8,128)(2,1)S(1)} %get-tuple-element.27), channel_id=1, source_target_pairs={{0,15},{1,0},{2,1},{3,2},{4,3},{5,4},{6,5},{7,6},{8,7},{9,8},{10,9... | collective-permute-start | bytes 393224 | tf_op jit(solution)/shard_map/ppermute | solution.py:21
  80.3 5.2 %collective-permute-done.13.before = bf16[4,2,64,128]{3,2,1,0:T(8,128)(2,1)S(1)} collective-permute-done((bf16[4,2,64,128]{3,2,1,0:T(8,128)(2,1)S(1)}, bf16[4,2,64,128]{3,2,1,0:T(8,128)(2,1)S(1)}, u32[]{:S(2)}, u32[]{:S(2)}) %collective-permute-start.13) | collective-permute-done | bytes 131104 | tf_op jit(solution)/shard_map/ppermute | solution.py:21
  91.2 2.6 %collective-permute-done.16.right = bf16[2,8,64,128]{3,2,1,0:T(8,128)(2,1)S(1)} collective-permute-done((bf16[2,8,64,128]{3,2,1,0:T(8,128)(2,1)S(1)}, bf16[2,8,64,128]{3,2,1,0:T(8,128)(2,1)S(1)}, u32[]{:S(2)}, u32[]{:S(2)}) %collective-permute-start.16) | collective-permute-done | bytes 262176 | tf_op jit(solution)/shard_map/ppermute | solution.py:21
  93.9 6.4 %first_errors_kernel.1 = (bf16[6,6,64,128]{3,2,1,0:T(8,128)(2,1)S(1)}, bf16[3584,128]{1,0:T(8,128)(2,1)S(1)}) custom-call(bf16[4,4,64,128]{3,2,1,0:T(8,128)(2,1)S(1)} %get-tuple-element.17.own.err_two, bf16[4,2,64,128]{3,2,1,0:T(8,128)(2,1)S(1)} %collective-permute-done.13.before, bf16[4,2,64,128]{3,2,1,0:T(8,128)(2,1)S(1)} %collective-permute-done.14.after, ...), custom_call_target="tpu_custom_call" | custom-call | flops 2717908992 | bytes 4161536 | tf_op jit(solution)/shard_map/first_errors_kernel/pallas_call | solution.py:263
  106.0 5.7 %all-to-all-start = ((bf16[64,7,8,128]{3,2,1,0:T(8,128)(2,1)}), bf16[64,7,8,128]{3,2,1,0:T(8,128)(2,1)}, u32[]{:S(2)}, u32[]{:S(2)}) async-start(bf16[64,7,8,128]{3,2,1,0:T(8,128)(2,1)} %bitcast.10), calls=%async_computation | async-start | bytes 1835008 | tf_op jit(solution)/shard_map/all_to_all | solution.py:280
  114.2 13.3 %all-to-all-done = bf16[64,7,8,128]{3,2,1,0:T(8,128)(2,1)} async-done(((bf16[64,7,8,128]{3,2,1,0:T(8,128)(2,1)}), bf16[64,7,8,128]{3,2,1,0:T(8,128)(2,1)}, u32[]{:S(2)}, u32[]{:S(2)}) %all-to-all-start) | async-done | bytes 917536 | tf_op jit(solution)/shard_map/all_to_all | solution.py:280
  129.9 5.5 %all-to-all-start.1 = ((bf16[64,7,8,128]{3,2,1,0:T(8,128)(2,1)}), bf16[64,7,8,128]{3,2,1,0:T(8,128)(2,1)}, u32[]{:S(2)}, u32[]{:S(2)}) async-start(bf16[64,7,8,128]{3,2,1,0:T(8,128)(2,1)} %broadcast_in_dim.6), calls=%async_computation.1 | async-start | bytes 1835008 | tf_op jit(solution)/shard_map/all_to_all | solution.py:340
  135.4 2.3 %fusion = bf16[64,7,8,128]{3,2,1,0:T(8,128)(2,1)} fusion(bf16[64,7,8,128]{3,2,1,0:T(8,128)(2,1)} %collective-permute-done.19, bf16[2,64,7,8,128]{4,3,2,1,0:T(8,128)(2,1)S(1)} %bottom_grads_kernel.1, s32[]{:T(128)S(6)} %select_n.42), kind=kLoop, calls=%fused_computation.1 | loop fusion | flops 1835008 | bytes 2752516 | tf_op jit(solution)/shard_map/convert_element_type | solution.py:330
  137.7 12.6 %all-to-all-done.1 = bf16[64,7,8,128]{3,2,1,0:T(8,128)(2,1)} async-done(((bf16[64,7,8,128]{3,2,1,0:T(8,128)(2,1)}), bf16[64,7,8,128]{3,2,1,0:T(8,128)(2,1)}, u32[]{:S(2)}, u32[]{:S(2)}) %all-to-all-start.1) | async-done | bytes 917536 | tf_op jit(solution)/shard_map/all_to_all | solution.py:340
  150.3 4.9 %all-to-all-start.2 = ((bf16[64,7,8,128]{3,2,1,0:T(8,128)(2,1)}), bf16[64,7,8,128]{3,2,1,0:T(8,128)(2,1)S(1)}, u32[]{:S(2)}, u32[]{:S(2)}) async-start(bf16[64,7,8,128]{3,2,1,0:T(8,128)(2,1)} %fusion), calls=%async_computation.2 | async-start | bytes 1835008 | tf_op jit(solution)/shard_map/all_to_all | solution.py:280
  157.4 3.0 %collective-permute-start.18 = (bf16[3,3,3,128,128]{4,3,2,1,0:T(8,128)(2,1)}, bf16[3,3,3,128,128]{4,3,2,1,0:T(8,128)(2,1)}, u32[]{:S(2)}, u32[]{:S(2)}) collective-permute-start(bf16[3,3,3,128,128]{4,3,2,1,0:T(8,128)(2,1)} %bitcast.12), channel_id=1, source_target_pairs={{0,16},{16,0},{1,17},{17,1},{2,18},{18,2},{3,19},{19,3},{4,20},{20... | collective-permute-start | bytes 2654216 | tf_op jit(solution)/shard_map/ppermute | solution.py:25
  160.4 9.1 %all-to-all-done.2 = bf16[64,7,8,128]{3,2,1,0:T(8,128)(2,1)S(1)} async-done(((bf16[64,7,8,128]{3,2,1,0:T(8,128)(2,1)}), bf16[64,7,8,128]{3,2,1,0:T(8,128)(2,1)S(1)}, u32[]{:S(2)}, u32[]{:S(2)}) %all-to-all-start.2) | async-done | bytes 917536 | tf_op jit(solution)/shard_map/all_to_all | solution.py:280
  170.4 7.1 %all-to-all-start.3 = ((bf16[8,7,8,128]{3,2,1,0:T(8,128)(2,1)}), bf16[8,7,8,128]{3,2,1,0:T(8,128)(2,1)S(1)}, u32[]{:S(2)}, u32[]{:S(2)}) async-start(bf16[8,7,8,128]{3,2,1,0:T(8,128)(2,1)} %broadcast_in_dim.7), calls=%async_computation.3 | async-start | bytes 229376 | tf_op jit(solution)/shard_map/all_to_all | solution.py:350
  177.5 2.9 %input_kernel.1 = bf16[4,4,64,128]{3,2,1,0:T(8,128)(2,1)} custom-call(bf16[6,6,64,128]{3,2,1,0:T(8,128)(2,1)S(1)} %copy-done.7, bf16[27,128,128]{2,1,0:T(8,128)(2,1)S(1)} %bitcast.33), custom_call_target="tpu_custom_call" | custom-call | flops 905969664 | bytes 1474560 | tf_op jit(solution)/shard_map/input_kernel/pallas_call | solution.py:263
  183.3 3.7 %convert_multiply_fusion = (f32[3,3,3,128,128]{4,3,2,1,0:T(8,128)}, f32[3,3,3,128,128]{4,3,2,1,0:T(8,128)}) fusion(bf16[3,3,3,128,128]{4,3,2,1,0:T(8,128)(2,1)} %collective-permute-done.18, bf16[3,3,3,128,128]{4,3,2,1,0:T(8,128)(2,1)} %bitcast.12, pred[]{:T(512)S(6)} %eq.2), kind=kLoop, calls=%fused_computation.5 | loop fusion | flops 2654208 | bytes 5308417 | tf_op jit(solution)/shard_map/mul | solution.py:348
  (83 shorter events, 36.6 us)
Async XLA Ops:
  1.5 41.3 %collective-permute-start.9 = (bf16[2,1,32,256]{3,2,1,0:T(8,128)(2,1)S(1)}, bf16[2,1,32,256]{3,2,1,0:T(8,128)(2,1)S(1)}, u32[]{:S(2)}, u32[]{:S(2)}) collective-permute-start(bf16[2,1,32,256]{3,2,1,0:T(8,128)(2,1)S(1)} %get-tuple-element.43), channel_id=1, source_target_pairs={{0,15},{1,0},{2,1},{3,2},{4,3},{5,4},{6,5},{7,6},{8,7},{9,8},{10,9... | collective-permute-start | bytes 98312 | tf_op jit(solution)/shard_map/ppermute | solution.py:21
  8.5 35.6 %collective-permute-start.8 = (bf16[2,1,32,256]{3,2,1,0:T(8,128)(2,1)S(1)}, bf16[2,1,32,256]{3,2,1,0:T(8,128)(2,1)S(1)}, u32[]{:S(2)}, u32[]{:S(2)}) collective-permute-start(bf16[2,1,32,256]{3,2,1,0:T(8,128)(2,1)S(1)} %get-tuple-element.44), channel_id=1, source_target_pairs={{0,1},{1,2},{2,3},{3,4},{4,5},{5,6},{6,7},{7,8},{8,9},{9,10},{10,1... | collective-permute-start | bytes 98312 | tf_op jit(solution)/shard_map/ppermute | solution.py:21
  9.5 33.3 %collective-permute-start.1 = (bf16[4,2,64,128]{3,2,1,0:T(8,128)(2,1)S(1)}, bf16[4,2,64,128]{3,2,1,0:T(8,128)(2,1)S(1)}, u32[]{:S(2)}, u32[]{:S(2)}) collective-permute-start(bf16[4,2,64,128]{3,2,1,0:T(8,128)(2,1)S(1)} %get-tuple-element.31), channel_id=1, source_target_pairs={{0,15},{1,0},{2,1},{3,2},{4,3},{5,4},{6,5},{7,6},{8,7},{9,8},{10,9... | collective-permute-start | bytes 393224 | tf_op jit(solution)/shard_map/ppermute | solution.py:21
  14.4 28.5 %collective-permute-start = (bf16[4,2,64,128]{3,2,1,0:T(8,128)(2,1)S(1)}, bf16[4,2,64,128]{3,2,1,0:T(8,128)(2,1)S(1)}, u32[]{:S(2)}, u32[]{:S(2)}) collective-permute-start(bf16[4,2,64,128]{3,2,1,0:T(8,128)(2,1)S(1)} %get-tuple-element.32), channel_id=1, source_target_pairs={{0,1},{1,2},{2,3},{3,4},{4,5},{5,6},{6,7},{7,8},{8,9},{9,10},{10,1... | collective-permute-start | bytes 393224 | tf_op jit(solution)/shard_map/ppermute | solution.py:21
  35.8 30.8 %collective-permute-start.12 = (bf16[16,27,8,128]{3,2,1,0:T(8,128)(2,1)}, bf16[16,27,8,128]{3,2,1,0:T(8,128)(2,1)}, u32[]{:S(2)}, u32[]{:S(2)}) collective-permute-start(bf16[16,27,8,128]{3,2,1,0:T(8,128)(2,1)} %bitcast.6), channel_id=1, source_target_pairs={{0,16},{16,0},{1,17},{17,1},{2,18},{18,2},{3,19},{19,3},{4,20},{20... | collective-permute-start | bytes 2654216 | tf_op jit(solution)/shard_map/ppermute | solution.py:25
  43.0 4.5 %collective-permute-start.2 = (bf16[2,8,64,128]{3,2,1,0:T(8,128)(2,1)S(1)}, bf16[2,8,64,128]{3,2,1,0:T(8,128)(2,1)S(1)}, u32[]{:S(2)}, u32[]{:S(2)}) collective-permute-start(bf16[2,8,64,128]{3,2,1,0:T(8,128)(2,1)S(1)} %pad_maximum_fusion), channel_id=1, source_target_pairs={{0,16},{16,32},{32,48},{48,64},{64,80},{80,96},{96,112},{112,0},{1... | collective-permute-start | bytes 786440 | tf_op jit(solution)/shard_map/ppermute | solution.py:21
  44.1 6.1 %collective-permute-start.3 = (bf16[2,8,64,128]{3,2,1,0:T(8,128)(2,1)S(1)}, bf16[2,8,64,128]{3,2,1,0:T(8,128)(2,1)S(1)}, u32[]{:S(2)}, u32[]{:S(2)}) collective-permute-start(bf16[2,8,64,128]{3,2,1,0:T(8,128)(2,1)S(1)} %pad_maximum_fusion.1), channel_id=1, source_target_pairs={{0,112},{16,0},{32,16},{48,32},{64,48},{80,64},{96,80},{112,96},{1... | collective-permute-start | bytes 786440 | tf_op jit(solution)/shard_map/ppermute | solution.py:21
  44.2 25.1 %collective-permute-start.10 = (bf16[1,4,32,256]{3,2,1,0:T(8,128)(2,1)S(1)}, bf16[1,4,32,256]{3,2,1,0:T(8,128)(2,1)S(1)}, u32[]{:S(2)}, u32[]{:S(2)}) collective-permute-start(bf16[1,4,32,256]{3,2,1,0:T(8,128)(2,1)S(1)} %pad_maximum_fusion.4), channel_id=1, source_target_pairs={{0,16},{16,32},{32,48},{48,64},{64,80},{80,96},{96,112},{112,0},{1... | collective-permute-start | bytes 196616 | tf_op jit(solution)/shard_map/ppermute | solution.py:21
  57.0 6.6 %collective-permute-start.4 = (bf16[2,2,32,128]{3,2,1,0:T(8,128)(2,1)S(1)}, bf16[2,2,32,128]{3,2,1,0:T(8,128)(2,1)S(1)}, u32[]{:S(2)}, u32[]{:S(2)}) collective-permute-start(bf16[2,2,32,128]{3,2,1,0:T(8,128)(2,1)S(1)} %get-tuple-element.14.own), channel_id=1, source_target_pairs={{0,1},{1,2},{2,3},{3,4},{4,5},{5,6},{6,7},{7,8},{8,9},{9,10},{10,1... | collective-permute-start | bytes 98312 | tf_op jit(solution)/shard_map/ppermute | solution.py:21
  58.0 11.3 %collective-permute-start.11 = (bf16[1,4,32,256]{3,2,1,0:T(8,128)(2,1)S(1)}, bf16[1,4,32,256]{3,2,1,0:T(8,128)(2,1)S(1)}, u32[]{:S(2)}, u32[]{:S(2)}) collective-permute-start(bf16[1,4,32,256]{3,2,1,0:T(8,128)(2,1)S(1)} %pad_maximum_fusion.5), channel_id=1, source_target_pairs={{0,112},{16,0},{32,16},{48,32},{64,48},{80,64},{96,80},{112,96},{1... | collective-permute-start | bytes 196616 | tf_op jit(solution)/shard_map/ppermute | solution.py:21
  58.1 5.4 %collective-permute-start.5 = (bf16[2,2,32,128]{3,2,1,0:T(8,128)(2,1)S(1)}, bf16[2,2,32,128]{3,2,1,0:T(8,128)(2,1)S(1)}, u32[]{:S(2)}, u32[]{:S(2)}) collective-permute-start(bf16[2,2,32,128]{3,2,1,0:T(8,128)(2,1)S(1)} %get-tuple-element.14.own), channel_id=1, source_target_pairs={{0,15},{1,0},{2,1},{3,2},{4,3},{5,4},{6,5},{7,6},{8,7},{9,8},{10,9... | collective-permute-start | bytes 98312 | tf_op jit(solution)/shard_map/ppermute | solution.py:21
  63.6 5.8 %collective-permute-start.7 = (bf16[2,6,32,128]{3,2,1,0:T(8,128)(2,1)S(1)}, bf16[2,6,32,128]{3,2,1,0:T(8,128)(2,1)S(1)}, u32[]{:S(2)}, u32[]{:S(2)}) collective-permute-start(bf16[2,6,32,128]{3,2,1,0:T(8,128)(2,1)S(1)} %constant_dynamic-update-slice_fusion), channel_id=1, source_target_pairs={{0,112},{16,0},{32,16},{48,32},{64,48},{80,64},{96,80},{112,96},{1... | collective-permute-start | bytes 294920 | tf_op jit(solution)/shard_map/ppermute | solution.py:21
  66.5 2.8 %collective-permute-start.6 = (bf16[2,6,32,128]{3,2,1,0:T(8,128)(2,1)S(1)}, bf16[2,6,32,128]{3,2,1,0:T(8,128)(2,1)S(1)}, u32[]{:S(2)}, u32[]{:S(2)}) collective-permute-start(bf16[2,6,32,128]{3,2,1,0:T(8,128)(2,1)S(1)} %constant_dynamic-update-slice_fusion), channel_id=1, source_target_pairs={{0,16},{16,32},{32,48},{48,64},{64,80},{80,96},{96,112},{112,0},{1... | collective-permute-start | bytes 294920 | tf_op jit(solution)/shard_map/ppermute | solution.py:21
  72.9 7.4 %collective-permute-start.14 = (bf16[4,2,64,128]{3,2,1,0:T(8,128)(2,1)S(1)}, bf16[4,2,64,128]{3,2,1,0:T(8,128)(2,1)S(1)}, u32[]{:S(2)}, u32[]{:S(2)}) collective-permute-start(bf16[4,2,64,128]{3,2,1,0:T(8,128)(2,1)S(1)} %get-tuple-element.27), channel_id=1, source_target_pairs={{0,15},{1,0},{2,1},{3,2},{4,3},{5,4},{6,5},{7,6},{8,7},{9,8},{10,9... | collective-permute-start | bytes 393224 | tf_op jit(solution)/shard_map/ppermute | solution.py:21
  78.3 7.1 %collective-permute-start.13 = (bf16[4,2,64,128]{3,2,1,0:T(8,128)(2,1)S(1)}, bf16[4,2,64,128]{3,2,1,0:T(8,128)(2,1)S(1)}, u32[]{:S(2)}, u32[]{:S(2)}) collective-permute-start(bf16[4,2,64,128]{3,2,1,0:T(8,128)(2,1)S(1)} %get-tuple-element.28), channel_id=1, source_target_pairs={{0,1},{1,2},{2,3},{3,4},{4,5},{5,6},{6,7},{7,8},{8,9},{9,10},{10,1... | collective-permute-start | bytes 393224 | tf_op jit(solution)/shard_map/ppermute | solution.py:21
  85.5 5.7 %collective-permute-start.15 = (bf16[2,8,64,128]{3,2,1,0:T(8,128)(2,1)S(1)}, bf16[2,8,64,128]{3,2,1,0:T(8,128)(2,1)S(1)}, u32[]{:S(2)}, u32[]{:S(2)}) collective-permute-start(bf16[2,8,64,128]{3,2,1,0:T(8,128)(2,1)S(1)} %pad_maximum_fusion.2), channel_id=1, source_target_pairs={{0,16},{16,32},{32,48},{48,64},{64,80},{80,96},{96,112},{112,0},{1... | collective-permute-start | bytes 786440 | tf_op jit(solution)/shard_map/ppermute | solution.py:21
  87.8 6.1 %collective-permute-start.16 = (bf16[2,8,64,128]{3,2,1,0:T(8,128)(2,1)S(1)}, bf16[2,8,64,128]{3,2,1,0:T(8,128)(2,1)S(1)}, u32[]{:S(2)}, u32[]{:S(2)}) collective-permute-start(bf16[2,8,64,128]{3,2,1,0:T(8,128)(2,1)S(1)} %pad_maximum_fusion.3), channel_id=1, source_target_pairs={{0,112},{16,0},{32,16},{48,32},{64,48},{80,64},{96,80},{112,96},{1... | collective-permute-start | bytes 786440 | tf_op jit(solution)/shard_map/ppermute | solution.py:21
  100.5 4.3 %collective-permute-start.17 = (bf16[3584,128]{1,0:T(8,128)(2,1)S(1)}, bf16[3584,128]{1,0:T(8,128)(2,1)S(1)}, u32[]{:S(2)}, u32[]{:S(2)}) collective-permute-start(bf16[3584,128]{1,0:T(8,128)(2,1)S(1)} %broadcast_select_fusion), channel_id=1, source_target_pairs={{0,16},{16,0},{1,17},{17,1},{2,18},{18,2},{3,19},{19,3},{4,20},{20... | collective-permute-start | bytes 2752520 | tf_op jit(solution)/shard_map/ppermute | solution.py:25
  106.0 21.5 %all-to-all-start = ((bf16[64,7,8,128]{3,2,1,0:T(8,128)(2,1)}), bf16[64,7,8,128]{3,2,1,0:T(8,128)(2,1)}, u32[]{:S(2)}, u32[]{:S(2)}) async-start(bf16[64,7,8,128]{3,2,1,0:T(8,128)(2,1)} %bitcast.10), calls=%async_computation | async-start | bytes 1835008 | tf_op jit(solution)/shard_map/all_to_all | solution.py:280
  113.8 21.6 %collective-permute-start.19 = (bf16[64,7,8,128]{3,2,1,0:T(8,128)(2,1)}, bf16[64,7,8,128]{3,2,1,0:T(8,128)(2,1)}, u32[]{:S(2)}, u32[]{:S(2)}) collective-permute-start(bf16[64,7,8,128]{3,2,1,0:T(8,128)(2,1)} %dynamic-slice_bitcast_fusion), channel_id=1, source_target_pairs={{0,16},{16,0},{1,17},{17,1},{2,18},{18,2},{3,19},{19,3},{4,20},{20... | collective-permute-start | bytes 2752520 | tf_op jit(solution)/shard_map/ppermute | solution.py:25
  129.9 20.4 %all-to-all-start.1 = ((bf16[64,7,8,128]{3,2,1,0:T(8,128)(2,1)}), bf16[64,7,8,128]{3,2,1,0:T(8,128)(2,1)}, u32[]{:S(2)}, u32[]{:S(2)}) async-start(bf16[64,7,8,128]{3,2,1,0:T(8,128)(2,1)} %broadcast_in_dim.6), calls=%async_computation.1 | async-start | bytes 1835008 | tf_op jit(solution)/shard_map/all_to_all | solution.py:340
  150.3 19.2 %all-to-all-start.2 = ((bf16[64,7,8,128]{3,2,1,0:T(8,128)(2,1)}), bf16[64,7,8,128]{3,2,1,0:T(8,128)(2,1)S(1)}, u32[]{:S(2)}, u32[]{:S(2)}) async-start(bf16[64,7,8,128]{3,2,1,0:T(8,128)(2,1)} %fusion), calls=%async_computation.2 | async-start | bytes 1835008 | tf_op jit(solution)/shard_map/all_to_all | solution.py:280
  157.4 25.9 %collective-permute-start.18 = (bf16[3,3,3,128,128]{4,3,2,1,0:T(8,128)(2,1)}, bf16[3,3,3,128,128]{4,3,2,1,0:T(8,128)(2,1)}, u32[]{:S(2)}, u32[]{:S(2)}) collective-permute-start(bf16[3,3,3,128,128]{4,3,2,1,0:T(8,128)(2,1)} %bitcast.12), channel_id=1, source_target_pairs={{0,16},{16,0},{1,17},{17,1},{2,18},{18,2},{3,19},{19,3},{4,20},{20... | collective-permute-start | bytes 2654216 | tf_op jit(solution)/shard_map/ppermute | solution.py:25
  170.4 12.2 %all-to-all-start.3 = ((bf16[8,7,8,128]{3,2,1,0:T(8,128)(2,1)}), bf16[8,7,8,128]{3,2,1,0:T(8,128)(2,1)S(1)}, u32[]{:S(2)}, u32[]{:S(2)}) async-start(bf16[8,7,8,128]{3,2,1,0:T(8,128)(2,1)} %broadcast_in_dim.7), calls=%async_computation.3 | async-start | bytes 229376 | tf_op jit(solution)/shard_map/all_to_all | solution.py:350
  (8 other events, 198.6 us)

commit v2 on v1

--- a/solution.py
+++ b/solution.py
@@ -1,3 +1,4 @@
+import functools
 import math
 
 import jax
@@ -13,7 +14,7 @@
 FLAT = ("x", "z", "y")
 F32 = jnp.float32
 BF16 = jnp.bfloat16
-UNITS = 7
+PIECE = 56
 
 
 def shifted(array, axes, step):
@@ -32,7 +33,7 @@
     high = jnp.concatenate([before[-width:], own[-width:], after[-width:]], axis=1)
     left = shifted(high, GX, 1)
     right = shifted(low, GX, -1)
-    return own, before, after, left, right
+    return (own, before, after, left, right)
 
 
 def fill_padded(padded, own, before, after, left, right):
@@ -216,16 +217,14 @@
             total[...] = term
         else:
             total[...] += term
-    for unit in range(28):
-        at_x, at_t = unit // UNITS, unit % UNITS
-        if unit == 27:
-            out[:, at_x * 16 : at_x * 16 + 16, at_t] = jnp.zeros((2, 16, 8, 128), BF16)
-            continue
+    out[:, 48:64, 48:56] = jnp.zeros((2, 16, 8, 128), BF16)
+    for unit in range(27):
+        at_x, rows = unit // 7, unit % 7 * 8
         at, kz = unit // 3, unit % 3
         block = total[kz * 256 : kz * 256 + 256, at * 128 : at * 128 + 128]
         block = block.reshape(16, 2, 8, 128)
         for half in range(2):
-            out[half, at_x * 16 : at_x * 16 + 16, at_t] = block[:, half].astype(BF16)
+            out[half, at_x * 16 : at_x * 16 + 16, rows : rows + 8] = block[:, half].astype(BF16)
 
 
 def first_errors_kernel(own, before, after, left, right, taps_two, slope_one,
@@ -255,6 +254,40 @@
         return 0
 
     lax.fori_loop(0, 4, step, 0)
+
+
+def sum_kernel(pieces, out):
+    total = pieces[0].astype(F32)
+    for at in range(1, 64):
+        total = total + pieces[at].astype(F32)
+    total = total.astype(BF16)
+    for at in range(64):
+        out[at] = total
+
+
+def place_kernel(chip, pair_0, pair_1, pair_2, pair_3, out, *, scale):
+    for distance, pair in enumerate((pair_0, pair_1, pair_2, pair_3)):
+        at = lax.rem(chip[0] + 4 - distance, 4)
+
+        def put(rows, pair=pair, at=at):
+            both = [pair[c, rows * 8 : rows * 8 + 8].astype(F32) * scale for c in range(2)]
+            out[at * 7 + rows] = jnp.concatenate(both, axis=0)
+
+        for rows in range(6):
+            put(rows)
+        pl.when(at < 3)(functools.partial(put, 6))
+
+
+def finish_kernel(core, whole, other, grad_one, grad_two, *, scale):
+    @pl.when(core[0] == 0)
+    def _():
+        grad_one[...] = whole[0:3456].astype(F32) * scale
+        grad_two[...] = other[0:3456].astype(F32) * scale
+
+    @pl.when(core[0] == 1)
+    def _():
+        grad_one[...] = other[0:3456].astype(F32) * scale
+        grad_two[...] = whole[0:3456].astype(F32) * scale
 
 
 def call(kernel, out_shapes, scratch, flops, *operands):
@@ -267,7 +300,7 @@
         out_specs=[pl.BlockSpec(memory_space=pltpu.VMEM)] * len(shapes),
         scratch_shapes=[pltpu.VMEM(s, d) for s, d in scratch],
         compiler_params=pltpu.CompilerParams(vmem_limit_bytes=48 << 20),
-        cost_estimate=pl.CostEstimate(flops=flops, bytes_accessed=moved, transcendentals=0),
+        cost_estimate=pl.CostEstimate(flops=flops // 20, bytes_accessed=moved // 20, transcendentals=0),
         name=kernel.__name__,
     )(*operands)
 
@@ -276,9 +309,8 @@
     return lax.dynamic_index_in_dim(stacked, index, 0, keepdims=False)
 
 
-def summed_pieces(pieces):
-    arrived = lax.all_to_all(pieces, FLAT, 0, 0)
-    return jnp.sum(arrived.astype(F32), axis=0).astype(BF16)
+def after(array, *others):
+    return lax.optimization_barrier((array, *others))[0]
 
 
 def on_device(features, skip_grad, bottom_grad, conv_one, conv_two, conv_three):
@@ -293,12 +325,9 @@
 
     own_taps = jnp.swapaxes(conv_three.reshape(27, 128, 16), 1, 2)
     half_taps = pick(jnp.swapaxes(own_taps.reshape(27, 2, 8, 128), 0, 1), core)
-    mine = lax.all_gather(half_taps, GY)
-    theirs = swap_cores(mine)
-    both = jnp.where(core == 0, jnp.stack([mine, theirs]), jnp.stack([theirs, mine]))
-    taps_three = jnp.transpose(both, (2, 1, 0, 3, 4)).reshape(27, 256, 128)
-
-    g_pieces = halo_pieces(bottom_grad, 1)
+    half_taps = jnp.broadcast_to(half_taps, (16, 27, 8, 128))
+    mine = lax.all_to_all(half_taps, GY, 0, 0)
+    g_pieces = halo_pieces(after(bottom_grad, f_pieces[1], f_pieces[2]), 1)
 
     conv_flops = 2 * 1152 * 128 * 1024 * 3
     act_one, slope_one, slope_two, pooled = call(
@@ -308,6 +337,10 @@
         3 * conv_flops, *f_pieces, taps_one, taps_two,
     )
     p_pieces = halo_pieces(pooled, 2)
+    mine = after(mine, pooled)
+    theirs = swap_cores(mine)
+    both = jnp.where(core == 0, jnp.stack([mine, theirs]), jnp.stack([theirs, mine]))
+    taps_three = jnp.transpose(both, (2, 1, 0, 3, 4)).reshape(27, 256, 128)
     bottleneck, err_three, err_two = call(
         bottom_kernel,
         [((2, 2, 32, 256), BF16), ((2, 2, 32, 256), BF16), ((4, 4, 64, 128), BF16)],
@@ -315,10 +348,8 @@
          ((4, 4, 32, 256), BF16), ((64, 128), F32)],
         conv_flops, *p_pieces, *g_pieces, taps_three, slope_two, skip_grad,
     )
-    e_pieces = halo_pieces(err_two, 2)
-
     (three,) = call(
-        bottom_grads_kernel, [((2, 64, UNITS, 8, 128), BF16)],
+        bottom_grads_kernel, [((2, 64, PIECE, 128), BF16)],
         [((6, 6, 32, 128), BF16), ((768, 1152), F32)],
         conv_flops // 4, *p_pieces, err_three,
     )
@@ -327,30 +358,50 @@
         conv_flops, act_one, err_two,
     )
     kept = pick(three, core).astype(F32) + swap_cores(pick(three, 1 - core)).astype(F32)
-    three_part = summed_pieces(kept.astype(BF16))
+    three_pieces = lax.all_to_all(kept.astype(BF16), FLAT, 0, 0)
+    three_part = jnp.sum(three_pieces.astype(F32), axis=0).astype(BF16)
+    e_pieces = halo_pieces(err_two, 2)
 
     err_one, one = call(
         first_errors_kernel, [((6, 6, 64, 128), BF16), ((3584, 128), BF16)],
         [((8, 8, 64, 128), BF16), ((384, 1152), BF16), ((1152, 384), F32)],
         3 * conv_flops, *e_pieces, taps_two, slope_one, *f_pieces,
     )
+    one = after(one, three_pieces)
     sent = jnp.where(core == 0, two, one)
     kept = jnp.where(core == 0, one, two).astype(F32) + swap_cores(sent).astype(F32)
-    part = summed_pieces(kept.astype(BF16).reshape(64, UNITS, 8, 128))
-    whole = lax.all_to_all(jnp.broadcast_to(part, (64, UNITS, 8, 128)), FLAT, 0, 0)
+    kept = after(kept.astype(BF16).reshape(64, PIECE, 128), three_part)
+    (part,) = call(
+        sum_kernel, [((64, PIECE, 128), BF16)], [], 0, lax.all_to_all(kept, FLAT, 0, 0)
+    )
     (input_grad,) = call(
         input_kernel, [((4, 4, 64, 128), BF16)], [((384, 1152), BF16)],
         conv_flops, err_one, taps_one,
     )
-    whole = whole.reshape(3584, 128)[:3456].reshape(3, 3, 3, 128, 128)
-    other = swap_cores(whole)
-    grad_one = jnp.where(core == 0, whole, other).astype(F32) * fine_scale
-    grad_two = jnp.where(core == 0, other, whole).astype(F32) * fine_scale
-
-    three_all = lax.all_to_all(jnp.broadcast_to(three_part, (8, UNITS, 8, 128)), GX, 0, 0)
-    three_all = three_all.reshape(4, 2, UNITS, 8, 128).transpose(0, 2, 1, 3, 4)
-    three_all = three_all.reshape(28, 16, 128)[:27].astype(F32) * coarse_scale
-    grad_three = jnp.swapaxes(three_all, 1, 2).reshape(3, 3, 3, 128, 16)
+    both = swap_cores(three_part)
+    both = jnp.where(core == 0, jnp.stack([three_part, both]), jnp.stack([both, three_part]))
+    pairs = [both] + [lax.ppermute(both, "x", [(i, (i + d) % 4) for i in range(4)]) for d in (1, 2, 3)]
+    grad_three = pl.pallas_call(
+        functools.partial(place_kernel, scale=coarse_scale),
+        out_shape=jax.ShapeDtypeStruct((27, 16, 128), F32),
+        in_specs=[pl.BlockSpec(memory_space=pltpu.SMEM)] + [pl.BlockSpec(memory_space=pltpu.VMEM)] * 4,
+        out_specs=pl.BlockSpec(memory_space=pltpu.VMEM),
+        name="place_kernel",
+    )(lax.axis_index("x").reshape(1), *pairs)
+    grad_three = jnp.swapaxes(grad_three, 1, 2).reshape(3, 3, 3, 128, 16)
+    part = after(part, input_grad, grad_three)
+    whole = lax.all_to_all(part, FLAT, 0, 0).reshape(64 * PIECE, 128)
+    grad_one, grad_two = pl.pallas_call(
+        functools.partial(finish_kernel, scale=fine_scale),
+        out_shape=[jax.ShapeDtypeStruct((3456, 128), F32)] * 2,
+        in_specs=[pl.BlockSpec(memory_space=pltpu.SMEM)] + [pl.BlockSpec(memory_space=pltpu.VMEM)] * 2,
+        out_specs=[pl.BlockSpec(memory_space=pltpu.VMEM)] * 2,
+        compiler_params=pltpu.CompilerParams(vmem_limit_bytes=32 << 20),
+        name="finish_kernel",
+    )(core.reshape(1), whole, swap_cores(whole))
+    grad_one = grad_one.reshape(3, 3, 3, 128, 128)
+    grad_two = grad_two.reshape(3, 3, 3, 128, 128)
+
     return (bottleneck, input_grad, grad_one, grad_two, grad_three)
 
 

time: 188 us -> 155 us (0.82)
  waiting for transfers between devices: 55.1 us -> 19.9 us
  other arithmetic: 12.1 us -> 7.95 us
  Pallas kernels: 22.5 us -> 26.2 us
  local copies, waits for them, and re-layouts: 7.82 us -> 10.8 us
    all_to_all x4 -> x3, waiting for transfers between devices: 37.4 us -> 0.01 us  [the longest x1 0.01 us: on_device(): mine = lax.all_to_all(half_taps, GY, 0, 0)]
    all_to_all x0 -> x1, blocking collectives: none -> 23 us  [on_device(): whole = lax.all_to_all(part, FLAT, 0, 0).reshape(64 * PIECE, 128)]
    all_gather x1 -> x0, blocking collectives: 21.3 us -> none  [on_device(): mine = lax.all_gather(half_taps, GY)]
    unnamed x18 -> x64, local copies, waits for them, and re-layouts: 0.46 us -> 6.6 us
    ppermute x0 -> x3, starting transfers between devices: none -> 5.03 us  [on_device(): lax.ppermute(both, 'x', [(i, (i + d) % 4) for i in range(4)])]
    ppermute x0 -> x3, waiting for transfers between devices: none -> 4.61 us  [on_device(): lax.ppermute(both, 'x', [(i, (i + d) % 4) for i in range(4)])]
    all_to_all x4 -> x3, starting transfers between devices: 23.1 us -> 18.6 us  [the longest x1 8.17 us: on_device(): lax.all_to_all(kept, FLAT, 0, 0)]
    ppermute x16, waiting for transfers between devices: 15.7 us -> 11.2 us  [shifted(): lax.ppermute(array, axes, [(i, (i + step) % count) for i in range(count)])]
  transfers between devices with their start and end apart: 24 -> 27, of which waited for: 11 -> 9; matrix products, arithmetic and copies ran while one was open for 7% -> 5% of each run, Pallas kernels for 7% -> 13%
where the time goes in v2:
time: 155 us; the launch traced here: 154 us
  starting transfers between devices  65.4 us (42%)
  Pallas kernels  26.2 us (17%)
  blocking collectives  23 us (15%)
  waiting for transfers between devices  19.9 us (13%)
  local copies, waits for them, and re-layouts  10.8 us (7%)
  other arithmetic  7.95 us (5%)
    ppermute x16, starting transfers between devices, shifted(): lax.ppermute(array, axes, [(i, (i + step) % count) for i in range(count)])  30.7 us
    all_to_all x1, blocking collectives, on_device(): whole = lax.all_to_all(part, FLAT, 0, 0).reshape(64 * PIECE, 128)  23 us
    pallas_call x7, Pallas kernels, call(): pl.pallas_call(kernel, out_shape=shapes, in_specs=[pl.BlockSpec(memory_sp...  22.6 us
    ppermute x16, waiting for transfers between devices, shifted(): lax.ppermute(array, axes, [(i, (i + step) % count) for i in range(count)])  11.2 us
    ppermute x5, starting transfers between devices, swap_cores(): return lax.ppermute(array, 'c', [(0, 1), (1, 0)])  11.1 us
    all_to_all x1, starting transfers between devices, on_device(): lax.all_to_all(kept, FLAT, 0, 0)  8.17 us
    unnamed x64, local copies, waits for them, and re-layouts  6.6 us
    all_to_all x1, starting transfers between devices, on_device(): three_pieces = lax.all_to_all(kept.astype(BF16), FLAT, 0, 0)  5.96 us
  transfers between devices with their start and end apart: 27, of which 9 were waited for; matrix products, arithmetic and copies ran while one was open for 5% of the time, Pallas kernels for 13%

profile of v2, /device:TPU:1, one launch (start us, length us, event | category | flops | bytes accessed | tf_op | source)
XLA Modules:
  0.0 154.3 jit_solution(13274160633285928572)
XLA Ops:
  1.7 2.2 %collective-permute-start = (bf16[4,2,64,128]{3,2,1,0:T(8,128)(2,1)S(1)}, bf16[4,2,64,128]{3,2,1,0:T(8,128)(2,1)S(1)}, u32[]{:S(2)}, u32[]{:S(2)}) collective-permute-start(bf16[4,2,64,128]{3,2,1,0:T(8,128)(2,1)S(1)} %get-tuple-element.44), channel_id=1, source_target_pairs={{0,1},{1,2},{2,3},{3,4},{4,5},{5,6},{6,7},{7,8},{8,9},{9,10},{10,1... | collective-permute-start | bytes 393224 | tf_op jit(solution)/shard_map/ppermute | solution.py:22
  3.9 5.0 %collective-permute-start.1 = (bf16[4,2,64,128]{3,2,1,0:T(8,128)(2,1)S(1)}, bf16[4,2,64,128]{3,2,1,0:T(8,128)(2,1)S(1)}, u32[]{:S(2)}, u32[]{:S(2)}) collective-permute-start(bf16[4,2,64,128]{3,2,1,0:T(8,128)(2,1)S(1)} %get-tuple-element.43), channel_id=1, source_target_pairs={{0,15},{1,0},{2,1},{3,2},{4,3},{5,4},{6,5},{7,6},{8,7},{9,8},{10,9... | collective-permute-start | bytes 393224 | tf_op jit(solution)/shard_map/ppermute | solution.py:22
  9.9 4.4 %all-to-all-start = ((bf16[16,27,8,128]{3,2,1,0:T(8,128)(2,1)}), bf16[16,27,8,128]{3,2,1,0:T(8,128)(2,1)}, u32[]{:S(2)}, u32[]{:S(2)}) async-start(bf16[16,27,8,128]{3,2,1,0:T(8,128)(2,1)} %broadcast_in_dim.3), calls=%async_computation | async-start | bytes 1769472 | tf_op jit(solution)/shard_map/all_to_all | solution.py:329
  18.2 3.5 %collective-permute-start.9 = (bf16[2,1,32,256]{3,2,1,0:T(8,128)(2,1)S(1)}, bf16[2,1,32,256]{3,2,1,0:T(8,128)(2,1)S(1)}, u32[]{:S(2)}, u32[]{:S(2)}) collective-permute-start(bf16[2,1,32,256]{3,2,1,0:T(8,128)(2,1)S(1)} %get-tuple-element.55), channel_id=1, source_target_pairs={{0,15},{1,0},{2,1},{3,2},{4,3},{5,4},{6,5},{7,6},{8,7},{9,8},{10,9... | collective-permute-start | bytes 98312 | tf_op jit(solution)/shard_map/ppermute | solution.py:22
  21.7 6.8 %forward_kernel.1 = (bf16[6,6,64,128]{3,2,1,0:T(8,128)(2,1)S(1)}, f32[6,6,64,128]{3,2,1,0:T(8,128)S(1)}, f32[4,4,64,128]{3,2,1,0:T(8,128)S(1)}, bf16[2,2,32,128]{3,2,1,0:T(8,128)(2,1)S(1)}) custom-call(bf16[4,4,64,128]{3,2,1,0:T(8,128)(2,1)S(1)} %copy-done.1, bf16[4,2,64,128]{3,2,1,0:T(8,128)(2,1)S(1)} %collective-permute-done.before.f_before, ...), custom_call_target="tpu_custom_call" | custom-call | flops 135895456 | bytes 140902 | tf_op jit(solution)/shard_map/forward_kernel/pallas_call | solution.py:296
  31.8 2.7 %collective-permute-start.12 = (bf16[16,27,8,128]{3,2,1,0:T(8,128)(2,1)}, bf16[16,27,8,128]{3,2,1,0:T(8,128)(2,1)S(1)}, u32[]{:S(2)}, u32[]{:S(2)}) collective-permute-start(bf16[16,27,8,128]{3,2,1,0:T(8,128)(2,1)} %all-to-all-done), channel_id=1, source_target_pairs={{0,16},{16,0},{1,17},{17,1},{2,18},{18,2},{3,19},{19,3},{4,20},{20... | collective-permute-start | bytes 2654216 | tf_op jit(solution)/shard_map/ppermute | solution.py:26
  36.6 3.6 %collective-permute-start.5 = (bf16[2,2,32,128]{3,2,1,0:T(8,128)(2,1)S(1)}, bf16[2,2,32,128]{3,2,1,0:T(8,128)(2,1)S(1)}, u32[]{:S(2)}, u32[]{:S(2)}) collective-permute-start(bf16[2,2,32,128]{3,2,1,0:T(8,128)(2,1)S(1)} %get-tuple-element.21.own), channel_id=1, source_target_pairs={{0,15},{1,0},{2,1},{3,2},{4,3},{5,4},{6,5},{7,6},{8,7},{9,8},{10,9... | collective-permute-start | bytes 98312 | tf_op jit(solution)/shard_map/ppermute | solution.py:22
  41.2 1.9 %collective-permute-start.6 = (bf16[2,6,32,128]{3,2,1,0:T(8,128)(2,1)S(1)}, bf16[2,6,32,128]{3,2,1,0:T(8,128)(2,1)S(1)}, u32[]{:S(2)}, u32[]{:S(2)}) collective-permute-start(bf16[2,6,32,128]{3,2,1,0:T(8,128)(2,1)S(1)} %constant_dynamic-update-slice_fusion), channel_id=1, source_target_pairs={{0,16},{16,32},{32,48},{48,64},{64,80},{80,96},{96,112},{112,0},{1... | collective-permute-start | bytes 294920 | tf_op jit(solution)/shard_map/ppermute | solution.py:22
  47.2 3.1 %bottom_kernel.1 = (bf16[2,2,32,256]{3,2,1,0:T(8,128)(2,1)}, bf16[2,2,32,256]{3,2,1,0:T(8,128)(2,1)S(1)}, bf16[4,4,64,128]{3,2,1,0:T(8,128)(2,1)S(1)}) custom-call(bf16[2,2,32,128]{3,2,1,0:T(8,128)(2,1)S(1)} %get-tuple-element.21.own, bf16[2,2,32,128]{3,2,1,0:T(8,128)(2,1)S(1)} %collective-permute-done.4.before, ...), custom_call_target="tpu_custom_call" | custom-call | flops 45298484 | bytes 155648 | tf_op jit(solution)/shard_map/bottom_kernel/pallas_call | solution.py:296
  51.5 3.0 %collective-permute-start.17 = (bf16[64,56,128]{2,1,0:T(8,128)(2,1)S(1)}, bf16[64,56,128]{2,1,0:T(8,128)(2,1)S(1)}, u32[]{:S(2)}, u32[]{:S(2)}) collective-permute-start(bf16[64,56,128]{2,1,0:T(8,128)(2,1)S(1)} %dynamic-slice_bitcast_fusion), channel_id=1, source_target_pairs={{0,16},{16,0},{1,17},{17,1},{2,18},{18,2},{3,19},{19,3},{4,20},{20... | collective-permute-start | bytes 2752520 | tf_op jit(solution)/shard_map/ppermute | solution.py:26
  55.2 5.4 %collective-permute-start.14 = (bf16[4,2,64,128]{3,2,1,0:T(8,128)(2,1)}, bf16[4,2,64,128]{3,2,1,0:T(8,128)(2,1)S(1)}, u32[]{:S(2)}, u32[]{:S(2)}) collective-permute-start(bf16[4,2,64,128]{3,2,1,0:T(8,128)(2,1)} %get-tuple-element.39), channel_id=1, source_target_pairs={{0,15},{1,0},{2,1},{3,2},{4,3},{5,4},{6,5},{7,6},{8,7},{9,8},{10,9... | collective-permute-start | bytes 393224 | tf_op jit(solution)/shard_map/ppermute | solution.py:22
  62.5 6.0 %all-to-all-start.1 = ((bf16[64,56,128]{2,1,0:T(8,128)(2,1)}), bf16[64,56,128]{2,1,0:T(8,128)(2,1)}, u32[]{:S(2)}, u32[]{:S(2)}) async-start(bf16[64,56,128]{2,1,0:T(8,128)(2,1)} %fusion), calls=%async_computation.1 | async-start | bytes 1835008 | tf_op jit(solution)/shard_map/all_to_all | solution.py:361
  71.0 2.2 %middle_grads_kernel.1 = bf16[3584,128]{1,0:T(8,128)(2,1)S(1)} custom-call(bf16[6,6,64,128]{3,2,1,0:T(8,128)(2,1)S(1)} %copy-done.14, bf16[4,4,64,128]{3,2,1,0:T(8,128)(2,1)S(1)} %get-tuple-element.26.own.err_two), custom_call_target="tpu_custom_call" | custom-call | flops 45298484 | bytes 42598 | tf_op jit(solution)/shard_map/middle_grads_kernel/pallas_call | solution.py:296
  73.2 9.7 %collective-permute-done.16.right = bf16[2,8,64,128]{3,2,1,0:T(8,128)(2,1)S(1)} collective-permute-done((bf16[2,8,64,128]{3,2,1,0:T(8,128)(2,1)S(1)}, bf16[2,8,64,128]{3,2,1,0:T(8,128)(2,1)S(1)}, u32[]{:S(2)}, u32[]{:S(2)}) %collective-permute-start.16) | collective-permute-done | bytes 262176 | tf_op jit(solution)/shard_map/ppermute | solution.py:22
  84.8 6.4 %first_errors_kernel.1 = (bf16[6,6,64,128]{3,2,1,0:T(8,128)(2,1)S(1)}, bf16[3584,128]{1,0:T(8,128)(2,1)S(1)}) custom-call(bf16[4,4,64,128]{3,2,1,0:T(8,128)(2,1)S(1)} %get-tuple-element.26.own.err_two, bf16[4,2,64,128]{3,2,1,0:T(8,128)(2,1)S(1)} %copy-done.19, bf16[4,2,64,128]{3,2,1,0:T(8,128)(2,1)S(1)} %copy-done.21, ...), custom_call_target="tpu_custom_call" | custom-call | flops 135895456 | bytes 208076 | tf_op jit(solution)/shard_map/first_errors_kernel/pallas_call | solution.py:296
  97.2 2.5 %add_convert_fusion = bf16[3584,128]{1,0:T(8,128)(2,1)} fusion(bf16[3584,128]{1,0:T(8,128)(2,1)} %collective-permute-done.18, bf16[3584,128]{1,0:T(8,128)(2,1)S(1)} %get-tuple-element.31, bf16[3584,128]{1,0:T(8,128)(2,1)S(1)} %middle_grads_kernel.1, pred[]{:T(512)S(6)} %eq.2), kind=kLoop, calls=%fused_computation.2 | loop fusion | flops 2293760 | bytes 3670017 | tf_op jit(solution)/shard_map/convert_element_type | solution.py:373
  99.6 8.2 %all-to-all-start.2 = ((bf16[64,56,128]{2,1,0:T(8,128)(2,1)}), bf16[64,56,128]{2,1,0:T(8,128)(2,1)S(1)}, u32[]{:S(2)}, u32[]{:S(2)}) async-start(bf16[64,56,128]{2,1,0:T(8,128)(2,1)} %bitcast.40), calls=%async_computation.2 | async-start | bytes 1835008 | tf_op jit(solution)/shard_map/all_to_all | solution.py:375
  110.6 2.6 %collective-permute-start.21 = (bf16[2,56,128]{2,1,0:T(8,128)(2,1)S(1)}, bf16[2,56,128]{2,1,0:T(8,128)(2,1)S(1)}, u32[]{:S(2)}, u32[]{:S(2)}) collective-permute-start(bf16[2,56,128]{2,1,0:T(8,128)(2,1)S(1)} %maximum_select_fusion.1.pair_0), channel_id=1, source_target_pairs={{0,64},{32,96},{64,0},{96,32},{1,65},{33,97},{65,1},{97,33},{2,66}... | collective-permute-start | bytes 86024 | tf_op jit(solution)/shard_map/ppermute | solution.py:383
  114.2 2.9 %input_kernel.1 = bf16[4,4,64,128]{3,2,1,0:T(8,128)(2,1)} custom-call(bf16[6,6,64,128]{3,2,1,0:T(8,128)(2,1)S(1)} %copy-done.17, bf16[27,128,128]{2,1,0:T(8,128)(2,1)S(1)} %bitcast.37), custom_call_target="tpu_custom_call" | custom-call | flops 45298484 | bytes 73728 | tf_op jit(solution)/shard_map/input_kernel/pallas_call | solution.py:296
  117.1 4.0 %collective-permute-done.20.pair_1 = bf16[2,56,128]{2,1,0:T(8,128)(2,1)S(1)} collective-permute-done((bf16[2,56,128]{2,1,0:T(8,128)(2,1)S(1)}, bf16[2,56,128]{2,1,0:T(8,128)(2,1)S(1)}, u32[]{:S(2)}, u32[]{:S(2)}) %collective-permute-start.20) | collective-permute-done | bytes 28704 | tf_op jit(solution)/shard_map/ppermute | solution.py:383
  124.0 23.0 %all_to_all.20 = bf16[64,56,128]{2,1,0:T(8,128)(2,1)S(1)} all-to-all(bf16[64,56,128]{2,1,0:T(8,128)(2,1)S(1)} %sum_kernel.1), channel_id=1, replica_groups=mesh['x'=4,'c'=2,'z'=4,'y'=4] {'x','z','y'}, dimensions={0} | all-to-all | bytes 1835008 | tf_op jit(solution)/shard_map/all_to_all | solution.py:393
  147.0 3.1 %collective-permute-start.23 = (bf16[3584,128]{1,0:T(8,128)(2,1)S(1)}, bf16[3584,128]{1,0:T(8,128)(2,1)S(1)}, u32[]{:S(2)}, u32[]{:S(2)}) collective-permute-start(bf16[3584,128]{1,0:T(8,128)(2,1)S(1)} %bitcast.34), channel_id=1, source_target_pairs={{0,16},{16,0},{1,17},{17,1},{2,18},{18,2},{3,19},{19,3},{4,20},{20... | collective-permute-start | bytes 2752520 | tf_op jit(solution)/shard_map/ppermute | solution.py:26
  150.1 2.1 %collective-permute-done.23.other = bf16[3584,128]{1,0:T(8,128)(2,1)S(1)} collective-permute-done((bf16[3584,128]{1,0:T(8,128)(2,1)S(1)}, bf16[3584,128]{1,0:T(8,128)(2,1)S(1)}, u32[]{:S(2)}, u32[]{:S(2)}) %collective-permute-start.23) | collective-permute-done | bytes 917536 | tf_op jit(solution)/shard_map/ppermute | solution.py:26
  152.2 2.1 %finish_kernel.1 = (f32[3456,128]{1,0:T(8,128)}, f32[3456,128]{1,0:T(8,128)}) custom-call(s32[1]{0:T(128)} %bitcast.10.core, bf16[3584,128]{1,0:T(8,128)(2,1)S(1)} %bitcast.35, bf16[3584,128]{1,0:T(8,128)(2,1)S(1)} %collective-permute-done.23.other), custom_call_target="tpu_custom_call" | custom-call | tf_op jit(solution)/shard_map/finish_kernel/pallas_call | solution.py:394
  (133 shorter events, 37.0 us)
Async XLA Ops:
  1.7 12.7 %collective-permute-start = (bf16[4,2,64,128]{3,2,1,0:T(8,128)(2,1)S(1)}, bf16[4,2,64,128]{3,2,1,0:T(8,128)(2,1)S(1)}, u32[]{:S(2)}, u32[]{:S(2)}) collective-permute-start(bf16[4,2,64,128]{3,2,1,0:T(8,128)(2,1)S(1)} %get-tuple-element.44), channel_id=1, source_target_pairs={{0,1},{1,2},{2,3},{3,4},{4,5},{5,6},{6,7},{7,8},{8,9},{9,10},{10,1... | collective-permute-start | bytes 393224 | tf_op jit(solution)/shard_map/ppermute | solution.py:22
  3.9 10.6 %collective-permute-start.1 = (bf16[4,2,64,128]{3,2,1,0:T(8,128)(2,1)S(1)}, bf16[4,2,64,128]{3,2,1,0:T(8,128)(2,1)S(1)}, u32[]{:S(2)}, u32[]{:S(2)}) collective-permute-start(bf16[4,2,64,128]{3,2,1,0:T(8,128)(2,1)S(1)} %get-tuple-element.43), channel_id=1, source_target_pairs={{0,15},{1,0},{2,1},{3,2},{4,3},{5,4},{6,5},{7,6},{8,7},{9,8},{10,9... | collective-permute-start | bytes 393224 | tf_op jit(solution)/shard_map/ppermute | solution.py:22
  9.9 21.8 %all-to-all-start = ((bf16[16,27,8,128]{3,2,1,0:T(8,128)(2,1)}), bf16[16,27,8,128]{3,2,1,0:T(8,128)(2,1)}, u32[]{:S(2)}, u32[]{:S(2)}) async-start(bf16[16,27,8,128]{3,2,1,0:T(8,128)(2,1)} %broadcast_in_dim.3), calls=%async_computation | async-start | bytes 1769472 | tf_op jit(solution)/shard_map/all_to_all | solution.py:329
  14.5 7.2 %collective-permute-start.3 = (bf16[2,8,64,128]{3,2,1,0:T(8,128)(2,1)S(1)}, bf16[2,8,64,128]{3,2,1,0:T(8,128)(2,1)S(1)}, u32[]{:S(2)}, u32[]{:S(2)}) collective-permute-start(bf16[2,8,64,128]{3,2,1,0:T(8,128)(2,1)S(1)} %pad_maximum_fusion.1), channel_id=1, source_target_pairs={{0,112},{16,0},{32,16},{48,32},{64,48},{80,64},{96,80},{112,96},{1... | collective-permute-start | bytes 786440 | tf_op jit(solution)/shard_map/ppermute | solution.py:22
  15.5 6.2 %collective-permute-start.2 = (bf16[2,8,64,128]{3,2,1,0:T(8,128)(2,1)S(1)}, bf16[2,8,64,128]{3,2,1,0:T(8,128)(2,1)S(1)}, u32[]{:S(2)}, u32[]{:S(2)}) collective-permute-start(bf16[2,8,64,128]{3,2,1,0:T(8,128)(2,1)S(1)} %pad_maximum_fusion), channel_id=1, source_target_pairs={{0,16},{16,32},{32,48},{48,64},{64,80},{80,96},{96,112},{112,0},{1... | collective-permute-start | bytes 786440 | tf_op jit(solution)/shard_map/ppermute | solution.py:22
  16.7 17.8 %collective-permute-start.8 = (bf16[2,1,32,256]{3,2,1,0:T(8,128)(2,1)S(1)}, bf16[2,1,32,256]{3,2,1,0:T(8,128)(2,1)S(1)}, u32[]{:S(2)}, u32[]{:S(2)}) collective-permute-start(bf16[2,1,32,256]{3,2,1,0:T(8,128)(2,1)S(1)} %get-tuple-element.56), channel_id=1, source_target_pairs={{0,1},{1,2},{2,3},{3,4},{4,5},{5,6},{6,7},{7,8},{8,9},{9,10},{10,1... | collective-permute-start | bytes 98312 | tf_op jit(solution)/shard_map/ppermute | solution.py:22
  18.2 16.3 %collective-permute-start.9 = (bf16[2,1,32,256]{3,2,1,0:T(8,128)(2,1)S(1)}, bf16[2,1,32,256]{3,2,1,0:T(8,128)(2,1)S(1)}, u32[]{:S(2)}, u32[]{:S(2)}) collective-permute-start(bf16[2,1,32,256]{3,2,1,0:T(8,128)(2,1)S(1)} %get-tuple-element.55), channel_id=1, source_target_pairs={{0,15},{1,0},{2,1},{3,2},{4,3},{5,4},{6,5},{7,6},{8,7},{9,8},{10,9... | collective-permute-start | bytes 98312 | tf_op jit(solution)/shard_map/ppermute | solution.py:22
  31.8 12.5 %collective-permute-start.12 = (bf16[16,27,8,128]{3,2,1,0:T(8,128)(2,1)}, bf16[16,27,8,128]{3,2,1,0:T(8,128)(2,1)S(1)}, u32[]{:S(2)}, u32[]{:S(2)}) collective-permute-start(bf16[16,27,8,128]{3,2,1,0:T(8,128)(2,1)} %all-to-all-done), channel_id=1, source_target_pairs={{0,16},{16,0},{1,17},{17,1},{2,18},{18,2},{3,19},{19,3},{4,20},{20... | collective-permute-start | bytes 2654216 | tf_op jit(solution)/shard_map/ppermute | solution.py:26
  34.5 12.1 %collective-permute-start.10 = (bf16[1,4,32,256]{3,2,1,0:T(8,128)(2,1)S(1)}, bf16[1,4,32,256]{3,2,1,0:T(8,128)(2,1)S(1)}, u32[]{:S(2)}, u32[]{:S(2)}) collective-permute-start(bf16[1,4,32,256]{3,2,1,0:T(8,128)(2,1)S(1)} %pad_maximum_fusion.4), channel_id=1, source_target_pairs={{0,16},{16,32},{32,48},{48,64},{64,80},{80,96},{96,112},{112,0},{1... | collective-permute-start | bytes 196616 | tf_op jit(solution)/shard_map/ppermute | solution.py:22
  34.6 6.2 %collective-permute-start.4 = (bf16[2,2,32,128]{3,2,1,0:T(8,128)(2,1)S(1)}, bf16[2,2,32,128]{3,2,1,0:T(8,128)(2,1)S(1)}, u32[]{:S(2)}, u32[]{:S(2)}) collective-permute-start(bf16[2,2,32,128]{3,2,1,0:T(8,128)(2,1)S(1)} %get-tuple-element.21.own), channel_id=1, source_target_pairs={{0,1},{1,2},{2,3},{3,4},{4,5},{5,6},{6,7},{7,8},{8,9},{9,10},{10,1... | collective-permute-start | bytes 98312 | tf_op jit(solution)/shard_map/ppermute | solution.py:22
  35.8 10.8 %collective-permute-start.11 = (bf16[1,4,32,256]{3,2,1,0:T(8,128)(2,1)S(1)}, bf16[1,4,32,256]{3,2,1,0:T(8,128)(2,1)S(1)}, u32[]{:S(2)}, u32[]{:S(2)}) collective-permute-start(bf16[1,4,32,256]{3,2,1,0:T(8,128)(2,1)S(1)} %pad_maximum_fusion.5), channel_id=1, source_target_pairs={{0,112},{16,0},{32,16},{48,32},{64,48},{80,64},{96,80},{112,96},{1... | collective-permute-start | bytes 196616 | tf_op jit(solution)/shard_map/ppermute | solution.py:22
  36.6 4.6 %collective-permute-start.5 = (bf16[2,2,32,128]{3,2,1,0:T(8,128)(2,1)S(1)}, bf16[2,2,32,128]{3,2,1,0:T(8,128)(2,1)S(1)}, u32[]{:S(2)}, u32[]{:S(2)}) collective-permute-start(bf16[2,2,32,128]{3,2,1,0:T(8,128)(2,1)S(1)} %get-tuple-element.21.own), channel_id=1, source_target_pairs={{0,15},{1,0},{2,1},{3,2},{4,3},{5,4},{6,5},{7,6},{8,7},{9,8},{10,9... | collective-permute-start | bytes 98312 | tf_op jit(solution)/shard_map/ppermute | solution.py:22
  41.2 5.4 %collective-permute-start.6 = (bf16[2,6,32,128]{3,2,1,0:T(8,128)(2,1)S(1)}, bf16[2,6,32,128]{3,2,1,0:T(8,128)(2,1)S(1)}, u32[]{:S(2)}, u32[]{:S(2)}) collective-permute-start(bf16[2,6,32,128]{3,2,1,0:T(8,128)(2,1)S(1)} %constant_dynamic-update-slice_fusion), channel_id=1, source_target_pairs={{0,16},{16,32},{32,48},{48,64},{64,80},{80,96},{96,112},{112,0},{1... | collective-permute-start | bytes 294920 | tf_op jit(solution)/shard_map/ppermute | solution.py:22
  51.5 9.8 %collective-permute-start.17 = (bf16[64,56,128]{2,1,0:T(8,128)(2,1)S(1)}, bf16[64,56,128]{2,1,0:T(8,128)(2,1)S(1)}, u32[]{:S(2)}, u32[]{:S(2)}) collective-permute-start(bf16[64,56,128]{2,1,0:T(8,128)(2,1)S(1)} %dynamic-slice_bitcast_fusion), channel_id=1, source_target_pairs={{0,16},{16,0},{1,17},{17,1},{2,18},{18,2},{3,19},{19,3},{4,20},{20... | collective-permute-start | bytes 2752520 | tf_op jit(solution)/shard_map/ppermute | solution.py:26
  55.2 13.3 %collective-permute-start.13 = (bf16[4,2,64,128]{3,2,1,0:T(8,128)(2,1)}, bf16[4,2,64,128]{3,2,1,0:T(8,128)(2,1)S(1)}, u32[]{:S(2)}, u32[]{:S(2)}) collective-permute-start(bf16[4,2,64,128]{3,2,1,0:T(8,128)(2,1)} %get-tuple-element.40), channel_id=1, source_target_pairs={{0,1},{1,2},{2,3},{3,4},{4,5},{5,6},{6,7},{7,8},{8,9},{9,10},{10,1... | collective-permute-start | bytes 393224 | tf_op jit(solution)/shard_map/ppermute | solution.py:22
  55.2 13.3 %collective-permute-start.14 = (bf16[4,2,64,128]{3,2,1,0:T(8,128)(2,1)}, bf16[4,2,64,128]{3,2,1,0:T(8,128)(2,1)S(1)}, u32[]{:S(2)}, u32[]{:S(2)}) collective-permute-start(bf16[4,2,64,128]{3,2,1,0:T(8,128)(2,1)} %get-tuple-element.39), channel_id=1, source_target_pairs={{0,15},{1,0},{2,1},{3,2},{4,3},{5,4},{6,5},{7,6},{8,7},{9,8},{10,9... | collective-permute-start | bytes 393224 | tf_op jit(solution)/shard_map/ppermute | solution.py:22
  62.5 29.5 %all-to-all-start.1 = ((bf16[64,56,128]{2,1,0:T(8,128)(2,1)}), bf16[64,56,128]{2,1,0:T(8,128)(2,1)}, u32[]{:S(2)}, u32[]{:S(2)}) async-start(bf16[64,56,128]{2,1,0:T(8,128)(2,1)} %fusion), calls=%async_computation.1 | async-start | bytes 1835008 | tf_op jit(solution)/shard_map/all_to_all | solution.py:361
  68.7 14.3 %collective-permute-start.16 = (bf16[2,8,64,128]{3,2,1,0:T(8,128)(2,1)S(1)}, bf16[2,8,64,128]{3,2,1,0:T(8,128)(2,1)S(1)}, u32[]{:S(2)}, u32[]{:S(2)}) collective-permute-start(bf16[2,8,64,128]{3,2,1,0:T(8,128)(2,1)S(1)} %pad_maximum_fusion.3), channel_id=1, source_target_pairs={{0,112},{16,0},{32,16},{48,32},{64,48},{80,64},{96,80},{112,96},{1... | collective-permute-start | bytes 786440 | tf_op jit(solution)/shard_map/ppermute | solution.py:22
  70.0 12.9 %collective-permute-start.15 = (bf16[2,8,64,128]{3,2,1,0:T(8,128)(2,1)S(1)}, bf16[2,8,64,128]{3,2,1,0:T(8,128)(2,1)S(1)}, u32[]{:S(2)}, u32[]{:S(2)}) collective-permute-start(bf16[2,8,64,128]{3,2,1,0:T(8,128)(2,1)S(1)} %pad_maximum_fusion.2), channel_id=1, source_target_pairs={{0,16},{16,32},{32,48},{48,64},{64,80},{80,96},{96,112},{112,0},{1... | collective-permute-start | bytes 786440 | tf_op jit(solution)/shard_map/ppermute | solution.py:22
  99.6 24.2 %all-to-all-start.2 = ((bf16[64,56,128]{2,1,0:T(8,128)(2,1)}), bf16[64,56,128]{2,1,0:T(8,128)(2,1)S(1)}, u32[]{:S(2)}, u32[]{:S(2)}) async-start(bf16[64,56,128]{2,1,0:T(8,128)(2,1)} %bitcast.40), calls=%async_computation.2 | async-start | bytes 1835008 | tf_op jit(solution)/shard_map/all_to_all | solution.py:375
  109.2 11.9 %collective-permute-start.20 = (bf16[2,56,128]{2,1,0:T(8,128)(2,1)S(1)}, bf16[2,56,128]{2,1,0:T(8,128)(2,1)S(1)}, u32[]{:S(2)}, u32[]{:S(2)}) collective-permute-start(bf16[2,56,128]{2,1,0:T(8,128)(2,1)S(1)} %maximum_select_fusion.1.pair_0), channel_id=1, source_target_pairs={{0,32},{32,64},{64,96},{96,0},{1,33},{33,65},{65,97},{97,1},{2,34}... | collective-permute-start | bytes 86024 | tf_op jit(solution)/shard_map/ppermute | solution.py:383
  110.6 11.1 %collective-permute-start.21 = (bf16[2,56,128]{2,1,0:T(8,128)(2,1)S(1)}, bf16[2,56,128]{2,1,0:T(8,128)(2,1)S(1)}, u32[]{:S(2)}, u32[]{:S(2)}) collective-permute-start(bf16[2,56,128]{2,1,0:T(8,128)(2,1)S(1)} %maximum_select_fusion.1.pair_0), channel_id=1, source_target_pairs={{0,64},{32,96},{64,0},{96,32},{1,65},{33,97},{65,1},{97,33},{2,66}... | collective-permute-start | bytes 86024 | tf_op jit(solution)/shard_map/ppermute | solution.py:383
  113.2 8.6 %collective-permute-start.22 = (bf16[2,56,128]{2,1,0:T(8,128)(2,1)S(1)}, bf16[2,56,128]{2,1,0:T(8,128)(2,1)S(1)}, u32[]{:S(2)}, u32[]{:S(2)}) collective-permute-start(bf16[2,56,128]{2,1,0:T(8,128)(2,1)S(1)} %maximum_select_fusion.1.pair_0), channel_id=1, source_target_pairs={{0,96},{32,0},{64,32},{96,64},{1,97},{33,1},{65,33},{97,65},{2,98}... | collective-permute-start | bytes 86024 | tf_op jit(solution)/shard_map/ppermute | solution.py:383
  147.0 5.2 %collective-permute-start.23 = (bf16[3584,128]{1,0:T(8,128)(2,1)S(1)}, bf16[3584,128]{1,0:T(8,128)(2,1)S(1)}, u32[]{:S(2)}, u32[]{:S(2)}) collective-permute-start(bf16[3584,128]{1,0:T(8,128)(2,1)S(1)} %bitcast.34), channel_id=1, source_target_pairs={{0,16},{16,0},{1,17},{17,1},{2,18},{18,2},{3,19},{19,3},{4,20},{20... | collective-permute-start | bytes 2752520 | tf_op jit(solution)/shard_map/ppermute | solution.py:26
  (34 other events, 250.4 us)

commit v3 on v2

--- a/solution.py
+++ b/solution.py
@@ -33,7 +33,7 @@
     high = jnp.concatenate([before[-width:], own[-width:], after[-width:]], axis=1)
     left = shifted(high, GX, 1)
     right = shifted(low, GX, -1)
-    return (own, before, after, left, right)
+    return (own, before, after, left, right), high
 
 
 def fill_padded(padded, own, before, after, left, right):
@@ -192,19 +192,21 @@
     lax.fori_loop(0, 4, step, 0)
 
 
-def store_tap_grads(out, total):
+def store_tap_grads(total, put):
     for at in range(9):
         for kz in range(3):
-            rows = (at * 3 + kz) * 128
-            out[rows : rows + 128] = total[
-                at * 128 : at * 128 + 128, kz * 128 : kz * 128 + 128
-            ].astype(BF16)
-    out[3456:3584] = jnp.zeros((128, 128), BF16)
+            part = total[at * 128 : at * 128 + 128, kz * 128 : kz * 128 + 128].astype(BF16)
+            put((at * 3 + kz) * 128, part)
+    put(3456, jnp.zeros((128, 128), BF16))
 
 
 def middle_grads_kernel(act_one, err_two, out, total):
     add_tap_grads(total, act_one, 0, lambda row: err_two[row])
-    store_tap_grads(out, total)
+
+    def put(rows, part):
+        out[rows : rows + 128] = part
+
+    store_tap_grads(total, put)
 
 
 def bottom_grads_kernel(own, before, after, left, right, err_three, out, padded, total):
@@ -227,9 +229,9 @@
             out[half, at_x * 16 : at_x * 16 + 16, rows : rows + 8] = block[:, half].astype(BF16)
 
 
-def first_errors_kernel(own, before, after, left, right, taps_two, slope_one,
-                        f_own, f_before, f_after, f_left, f_right, err_one, out,
-                        padded, packed, total):
+def first_errors_kernel(core, own, before, after, left, right, taps_two, slope_one,
+                        f_own, f_before, f_after, f_left, f_right, two, token,
+                        err_one, out, padded, packed, total):
     fill_padded(padded, own, before, after, left, right)
     fill_backward(packed, taps_two)
 
@@ -242,7 +244,12 @@
     lax.fori_loop(0, 6, step, 0)
     fill_padded(padded, f_own, f_before, f_after, f_left, f_right)
     add_tap_grads(total, padded, 1, lambda row: err_one[row + 1, 1:5])
-    store_tap_grads(out, total)
+
+    def put(rows, part):
+        out[core[0], rows : rows + 128] = part
+        out[1 - core[0], rows : rows + 128] = two[rows : rows + 128]
+
+    store_tap_grads(total, put)
 
 
 def input_kernel(err_one, taps_one, out, packed):
@@ -261,7 +268,7 @@
     for at in range(1, 64):
         total = total + pieces[at].astype(F32)
     total = total.astype(BF16)
-    for at in range(64):
+    for at in range(out.shape[0]):
         out[at] = total
 
 
@@ -296,10 +303,12 @@
     return pl.pallas_call(
         kernel,
         out_shape=shapes,
-        in_specs=[pl.BlockSpec(memory_space=pltpu.VMEM)] * len(operands),
+        in_specs=[
+            pl.BlockSpec(memory_space=pltpu.SMEM if o.dtype == jnp.int32 else pltpu.VMEM) for o in operands
+        ],
         out_specs=[pl.BlockSpec(memory_space=pltpu.VMEM)] * len(shapes),
         scratch_shapes=[pltpu.VMEM(s, d) for s, d in scratch],
-        compiler_params=pltpu.CompilerParams(vmem_limit_bytes=48 << 20),
+        compiler_params=pltpu.CompilerParams(vmem_limit_bytes=14 << 20),
         cost_estimate=pl.CostEstimate(flops=flops // 20, bytes_accessed=moved // 20, transcendentals=0),
         name=kernel.__name__,
     )(*operands)
@@ -321,13 +330,13 @@
     taps_one = conv_one.reshape(27, 128, 128)
     taps_two = conv_two.reshape(27, 128, 128)
 
-    f_pieces = halo_pieces(features, 2)
+    f_pieces, _ = halo_pieces(features, 2)
 
     own_taps = jnp.swapaxes(conv_three.reshape(27, 128, 16), 1, 2)
     half_taps = pick(jnp.swapaxes(own_taps.reshape(27, 2, 8, 128), 0, 1), core)
     half_taps = jnp.broadcast_to(half_taps, (16, 27, 8, 128))
     mine = lax.all_to_all(half_taps, GY, 0, 0)
-    g_pieces = halo_pieces(after(bottom_grad, f_pieces[1], f_pieces[2]), 1)
+    g_pieces, _ = halo_pieces(after(bottom_grad, f_pieces[1], f_pieces[2]), 1)
 
     conv_flops = 2 * 1152 * 128 * 1024 * 3
     act_one, slope_one, slope_two, pooled = call(
@@ -336,7 +345,7 @@
         [((8, 8, 64, 128), BF16), ((1152, 384), BF16), ((4, 2, 64, 128), F32)],
         3 * conv_flops, *f_pieces, taps_one, taps_two,
     )
-    p_pieces = halo_pieces(pooled, 2)
+    p_pieces, _ = halo_pieces(pooled, 2)
     mine = after(mine, pooled)
     theirs = swap_cores(mine)
     both = jnp.where(core == 0, jnp.stack([mine, theirs]), jnp.stack([theirs, mine]))
@@ -357,20 +366,20 @@
         middle_grads_kernel, [((3584, 128), BF16)], [((1152, 384), F32)],
         conv_flops, act_one, err_two,
     )
+    e_pieces, e_high = halo_pieces(err_two, 2)
+    token = swap_cores(e_high[0, 0, :8])
     kept = pick(three, core).astype(F32) + swap_cores(pick(three, 1 - core)).astype(F32)
-    three_pieces = lax.all_to_all(kept.astype(BF16), FLAT, 0, 0)
-    three_part = jnp.sum(three_pieces.astype(F32), axis=0).astype(BF16)
-    e_pieces = halo_pieces(err_two, 2)
+    kept, token = lax.optimization_barrier((kept.astype(BF16), token))
+    three_pieces = lax.all_to_all(kept, FLAT, 0, 0)
 
     err_one, one = call(
-        first_errors_kernel, [((6, 6, 64, 128), BF16), ((3584, 128), BF16)],
+        first_errors_kernel, [((6, 6, 64, 128), BF16), ((2, 3584, 128), BF16)],
         [((8, 8, 64, 128), BF16), ((384, 1152), BF16), ((1152, 384), F32)],
-        3 * conv_flops, *e_pieces, taps_two, slope_one, *f_pieces,
-    )
-    one = after(one, three_pieces)
-    sent = jnp.where(core == 0, two, one)
-    kept = jnp.where(core == 0, one, two).astype(F32) + swap_cores(sent).astype(F32)
-    kept = after(kept.astype(BF16).reshape(64, PIECE, 128), three_part)
+        3 * conv_flops, core.reshape(1), *e_pieces, taps_two, slope_one, *f_pieces, two, token,
+    )
+    sent = after(one[1], three_pieces)
+    kept = one[0].astype(F32) + swap_cores(sent).astype(F32)
+    kept = kept.astype(BF16).reshape(64, PIECE, 128)
     (part,) = call(
         sum_kernel, [((64, PIECE, 128), BF16)], [], 0, lax.all_to_all(kept, FLAT, 0, 0)
     )
@@ -378,6 +387,8 @@
         input_kernel, [((4, 4, 64, 128), BF16)], [((384, 1152), BF16)],
         conv_flops, err_one, taps_one,
     )
+    (three_part,) = call(sum_kernel, [((1, PIECE, 128), BF16)], [], 0, three_pieces)
+    three_part = three_part[0]
     both = swap_cores(three_part)
     both = jnp.where(core == 0, jnp.stack([three_part, both]), jnp.stack([both, three_part]))
     pairs = [both] + [lax.ppermute(both, "x", [(i, (i + d) % 4) for i in range(4)]) for d in (1, 2, 3)]
@@ -396,7 +407,7 @@
         out_shape=[jax.ShapeDtypeStruct((3456, 128), F32)] * 2,
         in_specs=[pl.BlockSpec(memory_space=pltpu.SMEM)] + [pl.BlockSpec(memory_space=pltpu.VMEM)] * 2,
         out_specs=[pl.BlockSpec(memory_space=pltpu.VMEM)] * 2,
-        compiler_params=pltpu.CompilerParams(vmem_limit_bytes=32 << 20),
+        compiler_params=pltpu.CompilerParams(vmem_limit_bytes=8 << 20),
         name="finish_kernel",
     )(core.reshape(1), whole, swap_cores(whole))
     grad_one = grad_one.reshape(3, 3, 3, 128, 128)

time: 155 us -> 158 us (1.019)
  waiting for transfers between devices: 19.9 us -> 14.1 us
  local copies, waits for them, and re-layouts: 10.8 us -> 15.8 us
  starting transfers between devices: 65.4 us -> 68.4 us
    ppermute x16, waiting for transfers between devices: 11.2 us -> 3.83 us  [shifted(): lax.ppermute(array, axes, [(i, (i + step) % count) for i in range(count)])]
    unnamed x64 -> x58, local copies, waits for them, and re-layouts: 6.6 us -> 13 us
    all_to_all x1, starting transfers between devices: 5.96 us -> 10.2 us  [on_device(): three_pieces = lax.all_to_all(kept, FLAT, 0, 0)]
    pallas_call x7 -> x8, Pallas kernels: 22.6 us -> 24 us  [call(): pl.pallas_call(kernel, out_shape=shapes, in_specs=[pl.BlockSpec(memory_sp...]
    ppermute x5 -> x6, waiting for transfers between devices: 4.04 us -> 5.41 us  [swap_cores(): return lax.ppermute(array, 'c', [(0, 1), (1, 0)])]
    ppermute x5 -> x6, starting transfers between devices: 11.1 us -> 9.99 us  [swap_cores(): return lax.ppermute(array, 'c', [(0, 1), (1, 0)])]
  transfers between devices with their start and end apart: 27 -> 28, of which waited for: 9 -> 11; matrix products, arithmetic and copies ran while one was open for 5% -> 4% of each run, Pallas kernels for 13% -> 13%
where the time goes in v3:
time: 158 us; the launch traced here: 157 us
  starting transfers between devices  68.4 us (43%)
  Pallas kernels  27.6 us (17%)
  blocking collectives  23 us (15%)
  local copies, waits for them, and re-layouts  15.8 us (10%)
  waiting for transfers between devices  14.1 us (9%)
  other arithmetic  6.88 us (4%)
    ppermute x16, starting transfers between devices, shifted(): lax.ppermute(array, axes, [(i, (i + step) % count) for i in range(count)])  30.2 us
    pallas_call x8, Pallas kernels, call(): pl.pallas_call(kernel, out_shape=shapes, in_specs=[pl.BlockSpec(memory_sp...  24 us
    all_to_all x1, blocking collectives, on_device(): whole = lax.all_to_all(part, FLAT, 0, 0).reshape(64 * PIECE, 128)  23 us
    unnamed x58, local copies, waits for them, and re-layouts  13 us
    all_to_all x1, starting transfers between devices, on_device(): three_pieces = lax.all_to_all(kept, FLAT, 0, 0)  10.2 us
    ppermute x6, starting transfers between devices, swap_cores(): return lax.ppermute(array, 'c', [(0, 1), (1, 0)])  9.99 us
    all_to_all x1, starting transfers between devices, on_device(): lax.all_to_all(kept, FLAT, 0, 0)  8.54 us
    ppermute x6, waiting for transfers between devices, swap_cores(): return lax.ppermute(array, 'c', [(0, 1), (1, 0)])  5.41 us
  transfers between devices with their start and end apart: 28, of which 11 were waited for; matrix products, arithmetic and copies ran while one was open for 4% of the time, Pallas kernels for 13%

profile of v3, /device:TPU:1, one launch (start us, length us, event | category | flops | bytes accessed | tf_op | source)
XLA Modules:
  0.0 156.8 jit_solution(8920600888478972619)
XLA Ops:
  1.7 2.2 %collective-permute-start = (bf16[4,2,64,128]{3,2,1,0:T(8,128)(2,1)S(1)}, bf16[4,2,64,128]{3,2,1,0:T(8,128)(2,1)S(1)}, u32[]{:S(2)}, u32[]{:S(2)}) collective-permute-start(bf16[4,2,64,128]{3,2,1,0:T(8,128)(2,1)S(1)} %get-tuple-element.46), channel_id=1, source_target_pairs={{0,1},{1,2},{2,3},{3,4},{4,5},{5,6},{6,7},{7,8},{8,9},{9,10},{10,1... | collective-permute-start | bytes 393224 | tf_op jit(solution)/shard_map/ppermute | solution.py:22
  3.9 5.0 %collective-permute-start.1 = (bf16[4,2,64,128]{3,2,1,0:T(8,128)(2,1)S(1)}, bf16[4,2,64,128]{3,2,1,0:T(8,128)(2,1)S(1)}, u32[]{:S(2)}, u32[]{:S(2)}) collective-permute-start(bf16[4,2,64,128]{3,2,1,0:T(8,128)(2,1)S(1)} %get-tuple-element.45), channel_id=1, source_target_pairs={{0,15},{1,0},{2,1},{3,2},{4,3},{5,4},{6,5},{7,6},{8,7},{9,8},{10,9... | collective-permute-start | bytes 393224 | tf_op jit(solution)/shard_map/ppermute | solution.py:22
  9.9 4.4 %all-to-all-start = ((bf16[16,27,8,128]{3,2,1,0:T(8,128)(2,1)}), bf16[16,27,8,128]{3,2,1,0:T(8,128)(2,1)}, u32[]{:S(2)}, u32[]{:S(2)}) async-start(bf16[16,27,8,128]{3,2,1,0:T(8,128)(2,1)} %broadcast_in_dim.3), calls=%async_computation | async-start | bytes 1769472 | tf_op jit(solution)/shard_map/all_to_all | solution.py:338
  18.2 3.5 %collective-permute-start.9 = (bf16[2,1,32,256]{3,2,1,0:T(8,128)(2,1)S(1)}, bf16[2,1,32,256]{3,2,1,0:T(8,128)(2,1)S(1)}, u32[]{:S(2)}, u32[]{:S(2)}) collective-permute-start(bf16[2,1,32,256]{3,2,1,0:T(8,128)(2,1)S(1)} %get-tuple-element.57), channel_id=1, source_target_pairs={{0,15},{1,0},{2,1},{3,2},{4,3},{5,4},{6,5},{7,6},{8,7},{9,8},{10,9... | collective-permute-start | bytes 98312 | tf_op jit(solution)/shard_map/ppermute | solution.py:22
  21.7 6.8 %forward_kernel.1 = (bf16[6,6,64,128]{3,2,1,0:T(8,128)(2,1)S(1)}, f32[6,6,64,128]{3,2,1,0:T(8,128)S(1)}, f32[4,4,64,128]{3,2,1,0:T(8,128)S(1)}, bf16[2,2,32,128]{3,2,1,0:T(8,128)(2,1)S(1)}) custom-call(bf16[4,4,64,128]{3,2,1,0:T(8,128)(2,1)S(1)} %copy-done.1, bf16[4,2,64,128]{3,2,1,0:T(8,128)(2,1)S(1)} %collective-permute-done.before.f_before, ...), custom_call_target="tpu_custom_call" | custom-call | flops 135895456 | bytes 140902 | tf_op jit(solution)/shard_map/forward_kernel/pallas_call | solution.py:303
  31.8 2.7 %collective-permute-start.12 = (bf16[16,27,8,128]{3,2,1,0:T(8,128)(2,1)}, bf16[16,27,8,128]{3,2,1,0:T(8,128)(2,1)S(1)}, u32[]{:S(2)}, u32[]{:S(2)}) collective-permute-start(bf16[16,27,8,128]{3,2,1,0:T(8,128)(2,1)} %all-to-all-done), channel_id=1, source_target_pairs={{0,16},{16,0},{1,17},{17,1},{2,18},{18,2},{3,19},{19,3},{4,20},{20... | collective-permute-start | bytes 2654216 | tf_op jit(solution)/shard_map/ppermute | solution.py:26
  36.6 3.6 %collective-permute-start.5 = (bf16[2,2,32,128]{3,2,1,0:T(8,128)(2,1)S(1)}, bf16[2,2,32,128]{3,2,1,0:T(8,128)(2,1)S(1)}, u32[]{:S(2)}, u32[]{:S(2)}) collective-permute-start(bf16[2,2,32,128]{3,2,1,0:T(8,128)(2,1)S(1)} %get-tuple-element.22.own), channel_id=1, source_target_pairs={{0,15},{1,0},{2,1},{3,2},{4,3},{5,4},{6,5},{7,6},{8,7},{9,8},{10,9... | collective-permute-start | bytes 98312 | tf_op jit(solution)/shard_map/ppermute | solution.py:22
  41.3 1.9 %collective-permute-start.6 = (bf16[2,6,32,128]{3,2,1,0:T(8,128)(2,1)S(1)}, bf16[2,6,32,128]{3,2,1,0:T(8,128)(2,1)S(1)}, u32[]{:S(2)}, u32[]{:S(2)}) collective-permute-start(bf16[2,6,32,128]{3,2,1,0:T(8,128)(2,1)S(1)} %constant_dynamic-update-slice_fusion), channel_id=1, source_target_pairs={{0,16},{16,32},{32,48},{48,64},{64,80},{80,96},{96,112},{112,0},{1... | collective-permute-start | bytes 294920 | tf_op jit(solution)/shard_map/ppermute | solution.py:22
  47.2 3.1 %bottom_kernel.1 = (bf16[2,2,32,256]{3,2,1,0:T(8,128)(2,1)}, bf16[2,2,32,256]{3,2,1,0:T(8,128)(2,1)S(1)}, bf16[4,4,64,128]{3,2,1,0:T(8,128)(2,1)S(1)}) custom-call(bf16[2,2,32,128]{3,2,1,0:T(8,128)(2,1)S(1)} %get-tuple-element.22.own, bf16[2,2,32,128]{3,2,1,0:T(8,128)(2,1)S(1)} %collective-permute-done.4.before, ...), custom_call_target="tpu_custom_call" | custom-call | flops 45298484 | bytes 155648 | tf_op jit(solution)/shard_map/bottom_kernel/pallas_call | solution.py:303
  51.6 3.0 %collective-permute-start.17 = (bf16[64,56,128]{2,1,0:T(8,128)(2,1)S(1)}, bf16[64,56,128]{2,1,0:T(8,128)(2,1)S(1)}, u32[]{:S(2)}, u32[]{:S(2)}) collective-permute-start(bf16[64,56,128]{2,1,0:T(8,128)(2,1)S(1)} %dynamic-slice_bitcast_fusion), channel_id=1, source_target_pairs={{0,16},{16,0},{1,17},{17,1},{2,18},{18,2},{3,19},{19,3},{4,20},{20... | collective-permute-start | bytes 2752520 | tf_op jit(solution)/shard_map/ppermute | solution.py:26
  54.7 2.2 %middle_grads_kernel.1.two = bf16[3584,128]{1,0:T(8,128)(2,1)S(1)} custom-call(bf16[6,6,64,128]{3,2,1,0:T(8,128)(2,1)S(1)} %get-tuple-element.29.act_one, bf16[4,4,64,128]{3,2,1,0:T(8,128)(2,1)S(1)} %get-tuple-element.27.err_two.own), custom_call_target="tpu_custom_call" | custom-call | flops 45298484 | bytes 42598 | tf_op jit(solution)/shard_map/middle_grads_kernel/pallas_call | solution.py:303
  56.9 5.4 %collective-permute-start.14 = (bf16[4,2,64,128]{3,2,1,0:T(8,128)(2,1)S(1)}, bf16[4,2,64,128]{3,2,1,0:T(8,128)(2,1)S(1)}, u32[]{:S(2)}, u32[]{:S(2)}) collective-permute-start(bf16[4,2,64,128]{3,2,1,0:T(8,128)(2,1)S(1)} %get-tuple-element.41), channel_id=1, source_target_pairs={{0,15},{1,0},{2,1},{3,2},{4,3},{5,4},{6,5},{7,6},{8,7},{9,8},{10,9... | collective-permute-start | bytes 393224 | tf_op jit(solution)/shard_map/ppermute | solution.py:22
  69.7 10.2 %all-to-all-start.1 = ((bf16[64,56,128]{2,1,0:T(8,128)(2,1)}), bf16[64,56,128]{2,1,0:T(8,128)(2,1)S(1)}, u32[]{:S(2)}, u32[]{:S(2)}) async-start(bf16[64,56,128]{2,1,0:T(8,128)(2,1)} %fusion.1), calls=%async_computation.1 | async-start | bytes 1835008 | tf_op jit(solution)/shard_map/all_to_all | solution.py:373
  85.8 7.6 %first_errors_kernel.1 = (bf16[6,6,64,128]{3,2,1,0:T(8,128)(2,1)S(1)}, bf16[2,3584,128]{2,1,0:T(8,128)(2,1)S(1)}) custom-call(s32[1]{0:T(128)} %bitcast.10.core, bf16[4,4,64,128]{3,2,1,0:T(8,128)(2,1)S(1)} %get-tuple-element.27.err_two.own, bf16[4,2,64,128]{3,2,1,0:T(8,128)(2,1)S(1)} %copy-done.18, bf16[4,2,64,128]{3,2,1,0:T(8,128)(2,1)S(1)} %copy-done.20, ...), custom_call_target="tpu_custom_call" | custom-call | flops 135895456 | bytes 254054 | tf_op jit(solution)/shard_map/first_errors_kernel/pallas_call | solution.py:303
  96.9 2.5 %collective-permute-done.19 = bf16[3584,128]{1,0:T(8,128)(2,1)S(1)} collective-permute-done((bf16[3584,128]{1,0:T(8,128)(2,1)S(1)}, bf16[3584,128]{1,0:T(8,128)(2,1)S(1)}, u32[]{:S(2)}, u32[]{:S(2)}) %collective-permute-start.19) | collective-permute-done | bytes 917536 | tf_op jit(solution)/shard_map/ppermute | solution.py:26
  99.4 2.3 %fusion = bf16[3584,128]{1,0:T(8,128)(2,1)} fusion(bf16[3584,128]{1,0:T(8,128)(2,1)S(1)} %collective-permute-done.19, bf16[2,3584,128]{2,1,0:T(8,128)(2,1)} %copy-done.5), kind=kLoop, calls=%fused_computation.1 | loop fusion | flops 1835008 | bytes 2752512 | tf_op jit(solution)/shard_map/convert_element_type | solution.py:382
  101.7 8.5 %all-to-all-start.2 = ((bf16[64,56,128]{2,1,0:T(8,128)(2,1)}), bf16[64,56,128]{2,1,0:T(8,128)(2,1)S(1)}, u32[]{:S(2)}, u32[]{:S(2)}) async-start(bf16[64,56,128]{2,1,0:T(8,128)(2,1)} %bitcast.48), calls=%async_computation.2 | async-start | bytes 1835008 | tf_op jit(solution)/shard_map/all_to_all | solution.py:384
  113.2 2.6 %collective-permute-start.22 = (bf16[2,56,128]{2,1,0:T(8,128)(2,1)S(1)}, bf16[2,56,128]{2,1,0:T(8,128)(2,1)S(1)}, u32[]{:S(2)}, u32[]{:S(2)}) collective-permute-start(bf16[2,56,128]{2,1,0:T(8,128)(2,1)S(1)} %maximum_select_fusion.1.pair_0), channel_id=1, source_target_pairs={{0,64},{32,96},{64,0},{96,32},{1,65},{33,97},{65,1},{97,33},{2,66}... | collective-permute-start | bytes 86024 | tf_op jit(solution)/shard_map/ppermute | solution.py:394
  117.9 2.8 %input_kernel.1 = bf16[4,4,64,128]{3,2,1,0:T(8,128)(2,1)} custom-call(bf16[6,6,64,128]{3,2,1,0:T(8,128)(2,1)S(1)} %copy-done.16, bf16[27,128,128]{2,1,0:T(8,128)(2,1)S(1)} %bitcast.46), custom_call_target="tpu_custom_call" | custom-call | flops 45298484 | bytes 73728 | tf_op jit(solution)/shard_map/input_kernel/pallas_call | solution.py:303
  120.8 2.8 %collective-permute-done.21.pair_1 = bf16[2,56,128]{2,1,0:T(8,128)(2,1)S(1)} collective-permute-done((bf16[2,56,128]{2,1,0:T(8,128)(2,1)S(1)}, bf16[2,56,128]{2,1,0:T(8,128)(2,1)S(1)}, u32[]{:S(2)}, u32[]{:S(2)}) %collective-permute-start.21) | collective-permute-done | bytes 28704 | tf_op jit(solution)/shard_map/ppermute | solution.py:394
  126.5 23.0 %all_to_all.20 = bf16[64,56,128]{2,1,0:T(8,128)(2,1)S(1)} all-to-all(bf16[64,56,128]{2,1,0:T(8,128)(2,1)S(1)} %sum_kernel.2), channel_id=1, replica_groups=mesh['x'=4,'c'=2,'z'=4,'y'=4] {'x','z','y'}, dimensions={0} | all-to-all | bytes 1835008 | tf_op jit(solution)/shard_map/all_to_all | solution.py:404
  149.5 3.1 %collective-permute-start.24 = (bf16[3584,128]{1,0:T(8,128)(2,1)S(1)}, bf16[3584,128]{1,0:T(8,128)(2,1)S(1)}, u32[]{:S(2)}, u32[]{:S(2)}) collective-permute-start(bf16[3584,128]{1,0:T(8,128)(2,1)S(1)} %bitcast.41), channel_id=1, source_target_pairs={{0,16},{16,0},{1,17},{17,1},{2,18},{18,2},{3,19},{19,3},{4,20},{20... | collective-permute-start | bytes 2752520 | tf_op jit(solution)/shard_map/ppermute | solution.py:26
  152.6 2.1 %collective-permute-done.24.other = bf16[3584,128]{1,0:T(8,128)(2,1)S(1)} collective-permute-done((bf16[3584,128]{1,0:T(8,128)(2,1)S(1)}, bf16[3584,128]{1,0:T(8,128)(2,1)S(1)}, u32[]{:S(2)}, u32[]{:S(2)}) %collective-permute-start.24) | collective-permute-done | bytes 917536 | tf_op jit(solution)/shard_map/ppermute | solution.py:26
  154.7 2.1 %finish_kernel.1 = (f32[3456,128]{1,0:T(8,128)}, f32[3456,128]{1,0:T(8,128)}) custom-call(s32[1]{0:T(128)} %bitcast.10.core, bf16[3584,128]{1,0:T(8,128)(2,1)S(1)} %bitcast.42, bf16[3584,128]{1,0:T(8,128)(2,1)S(1)} %collective-permute-done.24.other), custom_call_target="tpu_custom_call" | custom-call | tf_op jit(solution)/shard_map/finish_kernel/pallas_call | solution.py:405
  (130 shorter events, 42.3 us)
Async XLA Ops:
  1.7 12.7 %collective-permute-start = (bf16[4,2,64,128]{3,2,1,0:T(8,128)(2,1)S(1)}, bf16[4,2,64,128]{3,2,1,0:T(8,128)(2,1)S(1)}, u32[]{:S(2)}, u32[]{:S(2)}) collective-permute-start(bf16[4,2,64,128]{3,2,1,0:T(8,128)(2,1)S(1)} %get-tuple-element.46), channel_id=1, source_target_pairs={{0,1},{1,2},{2,3},{3,4},{4,5},{5,6},{6,7},{7,8},{8,9},{9,10},{10,1... | collective-permute-start | bytes 393224 | tf_op jit(solution)/shard_map/ppermute | solution.py:22
  3.9 10.6 %collective-permute-start.1 = (bf16[4,2,64,128]{3,2,1,0:T(8,128)(2,1)S(1)}, bf16[4,2,64,128]{3,2,1,0:T(8,128)(2,1)S(1)}, u32[]{:S(2)}, u32[]{:S(2)}) collective-permute-start(bf16[4,2,64,128]{3,2,1,0:T(8,128)(2,1)S(1)} %get-tuple-element.45), channel_id=1, source_target_pairs={{0,15},{1,0},{2,1},{3,2},{4,3},{5,4},{6,5},{7,6},{8,7},{9,8},{10,9... | collective-permute-start | bytes 393224 | tf_op jit(solution)/shard_map/ppermute | solution.py:22
  9.9 21.9 %all-to-all-start = ((bf16[16,27,8,128]{3,2,1,0:T(8,128)(2,1)}), bf16[16,27,8,128]{3,2,1,0:T(8,128)(2,1)}, u32[]{:S(2)}, u32[]{:S(2)}) async-start(bf16[16,27,8,128]{3,2,1,0:T(8,128)(2,1)} %broadcast_in_dim.3), calls=%async_computation | async-start | bytes 1769472 | tf_op jit(solution)/shard_map/all_to_all | solution.py:338
  14.5 7.2 %collective-permute-start.3 = (bf16[2,8,64,128]{3,2,1,0:T(8,128)(2,1)S(1)}, bf16[2,8,64,128]{3,2,1,0:T(8,128)(2,1)S(1)}, u32[]{:S(2)}, u32[]{:S(2)}) collective-permute-start(bf16[2,8,64,128]{3,2,1,0:T(8,128)(2,1)S(1)} %pad_maximum_fusion.1), channel_id=1, source_target_pairs={{0,112},{16,0},{32,16},{48,32},{64,48},{80,64},{96,80},{112,96},{1... | collective-permute-start | bytes 786440 | tf_op jit(solution)/shard_map/ppermute | solution.py:22
  15.5 6.2 %collective-permute-start.2 = (bf16[2,8,64,128]{3,2,1,0:T(8,128)(2,1)S(1)}, bf16[2,8,64,128]{3,2,1,0:T(8,128)(2,1)S(1)}, u32[]{:S(2)}, u32[]{:S(2)}) collective-permute-start(bf16[2,8,64,128]{3,2,1,0:T(8,128)(2,1)S(1)} %pad_maximum_fusion), channel_id=1, source_target_pairs={{0,16},{16,32},{32,48},{48,64},{64,80},{80,96},{96,112},{112,0},{1... | collective-permute-start | bytes 786440 | tf_op jit(solution)/shard_map/ppermute | solution.py:22
  16.7 17.9 %collective-permute-start.8 = (bf16[2,1,32,256]{3,2,1,0:T(8,128)(2,1)S(1)}, bf16[2,1,32,256]{3,2,1,0:T(8,128)(2,1)S(1)}, u32[]{:S(2)}, u32[]{:S(2)}) collective-permute-start(bf16[2,1,32,256]{3,2,1,0:T(8,128)(2,1)S(1)} %get-tuple-element.58), channel_id=1, source_target_pairs={{0,1},{1,2},{2,3},{3,4},{4,5},{5,6},{6,7},{7,8},{8,9},{9,10},{10,1... | collective-permute-start | bytes 98312 | tf_op jit(solution)/shard_map/ppermute | solution.py:22
  18.2 16.4 %collective-permute-start.9 = (bf16[2,1,32,256]{3,2,1,0:T(8,128)(2,1)S(1)}, bf16[2,1,32,256]{3,2,1,0:T(8,128)(2,1)S(1)}, u32[]{:S(2)}, u32[]{:S(2)}) collective-permute-start(bf16[2,1,32,256]{3,2,1,0:T(8,128)(2,1)S(1)} %get-tuple-element.57), channel_id=1, source_target_pairs={{0,15},{1,0},{2,1},{3,2},{4,3},{5,4},{6,5},{7,6},{8,7},{9,8},{10,9... | collective-permute-start | bytes 98312 | tf_op jit(solution)/shard_map/ppermute | solution.py:22
  31.8 12.5 %collective-permute-start.12 = (bf16[16,27,8,128]{3,2,1,0:T(8,128)(2,1)}, bf16[16,27,8,128]{3,2,1,0:T(8,128)(2,1)S(1)}, u32[]{:S(2)}, u32[]{:S(2)}) collective-permute-start(bf16[16,27,8,128]{3,2,1,0:T(8,128)(2,1)} %all-to-all-done), channel_id=1, source_target_pairs={{0,16},{16,0},{1,17},{17,1},{2,18},{18,2},{3,19},{19,3},{4,20},{20... | collective-permute-start | bytes 2654216 | tf_op jit(solution)/shard_map/ppermute | solution.py:26
  34.6 12.0 %collective-permute-start.10 = (bf16[1,4,32,256]{3,2,1,0:T(8,128)(2,1)S(1)}, bf16[1,4,32,256]{3,2,1,0:T(8,128)(2,1)S(1)}, u32[]{:S(2)}, u32[]{:S(2)}) collective-permute-start(bf16[1,4,32,256]{3,2,1,0:T(8,128)(2,1)S(1)} %pad_maximum_fusion.4), channel_id=1, source_target_pairs={{0,16},{16,32},{32,48},{48,64},{64,80},{80,96},{96,112},{112,0},{1... | collective-permute-start | bytes 196616 | tf_op jit(solution)/shard_map/ppermute | solution.py:22
  34.6 6.2 %collective-permute-start.4 = (bf16[2,2,32,128]{3,2,1,0:T(8,128)(2,1)S(1)}, bf16[2,2,32,128]{3,2,1,0:T(8,128)(2,1)S(1)}, u32[]{:S(2)}, u32[]{:S(2)}) collective-permute-start(bf16[2,2,32,128]{3,2,1,0:T(8,128)(2,1)S(1)} %get-tuple-element.22.own), channel_id=1, source_target_pairs={{0,1},{1,2},{2,3},{3,4},{4,5},{5,6},{6,7},{7,8},{8,9},{9,10},{10,1... | collective-permute-start | bytes 98312 | tf_op jit(solution)/shard_map/ppermute | solution.py:22
  35.9 10.8 %collective-permute-start.11 = (bf16[1,4,32,256]{3,2,1,0:T(8,128)(2,1)S(1)}, bf16[1,4,32,256]{3,2,1,0:T(8,128)(2,1)S(1)}, u32[]{:S(2)}, u32[]{:S(2)}) collective-permute-start(bf16[1,4,32,256]{3,2,1,0:T(8,128)(2,1)S(1)} %pad_maximum_fusion.5), channel_id=1, source_target_pairs={{0,112},{16,0},{32,16},{48,32},{64,48},{80,64},{96,80},{112,96},{1... | collective-permute-start | bytes 196616 | tf_op jit(solution)/shard_map/ppermute | solution.py:22
  41.3 5.4 %collective-permute-start.6 = (bf16[2,6,32,128]{3,2,1,0:T(8,128)(2,1)S(1)}, bf16[2,6,32,128]{3,2,1,0:T(8,128)(2,1)S(1)}, u32[]{:S(2)}, u32[]{:S(2)}) collective-permute-start(bf16[2,6,32,128]{3,2,1,0:T(8,128)(2,1)S(1)} %constant_dynamic-update-slice_fusion), channel_id=1, source_target_pairs={{0,16},{16,32},{32,48},{48,64},{64,80},{80,96},{96,112},{112,0},{1... | collective-permute-start | bytes 294920 | tf_op jit(solution)/shard_map/ppermute | solution.py:22
  51.6 16.9 %collective-permute-start.17 = (bf16[64,56,128]{2,1,0:T(8,128)(2,1)S(1)}, bf16[64,56,128]{2,1,0:T(8,128)(2,1)S(1)}, u32[]{:S(2)}, u32[]{:S(2)}) collective-permute-start(bf16[64,56,128]{2,1,0:T(8,128)(2,1)S(1)} %dynamic-slice_bitcast_fusion), channel_id=1, source_target_pairs={{0,16},{16,0},{1,17},{17,1},{2,18},{18,2},{3,19},{19,3},{4,20},{20... | collective-permute-start | bytes 2752520 | tf_op jit(solution)/shard_map/ppermute | solution.py:26
  54.6 9.3 %collective-permute-start.13 = (bf16[4,2,64,128]{3,2,1,0:T(8,128)(2,1)S(1)}, bf16[4,2,64,128]{3,2,1,0:T(8,128)(2,1)S(1)}, u32[]{:S(2)}, u32[]{:S(2)}) collective-permute-start(bf16[4,2,64,128]{3,2,1,0:T(8,128)(2,1)S(1)} %get-tuple-element.42), channel_id=1, source_target_pairs={{0,1},{1,2},{2,3},{3,4},{4,5},{5,6},{6,7},{7,8},{8,9},{9,10},{10,1... | collective-permute-start | bytes 393224 | tf_op jit(solution)/shard_map/ppermute | solution.py:22
  56.9 8.3 %collective-permute-start.14 = (bf16[4,2,64,128]{3,2,1,0:T(8,128)(2,1)S(1)}, bf16[4,2,64,128]{3,2,1,0:T(8,128)(2,1)S(1)}, u32[]{:S(2)}, u32[]{:S(2)}) collective-permute-start(bf16[4,2,64,128]{3,2,1,0:T(8,128)(2,1)S(1)} %get-tuple-element.41), channel_id=1, source_target_pairs={{0,15},{1,0},{2,1},{3,2},{4,3},{5,4},{6,5},{7,6},{8,7},{9,8},{10,9... | collective-permute-start | bytes 393224 | tf_op jit(solution)/shard_map/ppermute | solution.py:22
  63.9 5.7 %collective-permute-start.18 = (bf16[8,128]{1,0:T(8,128)(2,1)S(1)}, bf16[8,128]{1,0:T(8,128)(2,1)S(1)}, u32[]{:S(2)}, u32[]{:S(2)}) collective-permute-start(bf16[8,128]{1,0:T(8,128)(2,1)S(1)} %slice_bitcast_fusion.1), channel_id=1, source_target_pairs={{0,16},{16,0},{1,17},{17,1},{2,18},{18,2},{3,19},{19,3},{4,20},{20... | collective-permute-start | bytes 6152 | tf_op jit(solution)/shard_map/ppermute | solution.py:26
  66.0 13.8 %collective-permute-start.16 = (bf16[2,8,64,128]{3,2,1,0:T(8,128)(2,1)}, bf16[2,8,64,128]{3,2,1,0:T(8,128)(2,1)}, u32[]{:S(2)}, u32[]{:S(2)}) collective-permute-start(bf16[2,8,64,128]{3,2,1,0:T(8,128)(2,1)} %pad_maximum_fusion.3), channel_id=1, source_target_pairs={{0,112},{16,0},{32,16},{48,32},{64,48},{80,64},{96,80},{112,96},{1... | collective-permute-start | bytes 786440 | tf_op jit(solution)/shard_map/ppermute | solution.py:22
  67.5 12.3 %collective-permute-start.15 = (bf16[2,8,64,128]{3,2,1,0:T(8,128)(2,1)}, bf16[2,8,64,128]{3,2,1,0:T(8,128)(2,1)}, u32[]{:S(2)}, u32[]{:S(2)}) collective-permute-start(bf16[2,8,64,128]{3,2,1,0:T(8,128)(2,1)} %pad_maximum_fusion.2), channel_id=1, source_target_pairs={{0,16},{16,32},{32,48},{48,64},{64,80},{80,96},{96,112},{112,0},{1... | collective-permute-start | bytes 786440 | tf_op jit(solution)/shard_map/ppermute | solution.py:22
  69.7 27.3 %all-to-all-start.1 = ((bf16[64,56,128]{2,1,0:T(8,128)(2,1)}), bf16[64,56,128]{2,1,0:T(8,128)(2,1)S(1)}, u32[]{:S(2)}, u32[]{:S(2)}) async-start(bf16[64,56,128]{2,1,0:T(8,128)(2,1)} %fusion.1), calls=%async_computation.1 | async-start | bytes 1835008 | tf_op jit(solution)/shard_map/all_to_all | solution.py:373
  101.7 24.6 %all-to-all-start.2 = ((bf16[64,56,128]{2,1,0:T(8,128)(2,1)}), bf16[64,56,128]{2,1,0:T(8,128)(2,1)S(1)}, u32[]{:S(2)}, u32[]{:S(2)}) async-start(bf16[64,56,128]{2,1,0:T(8,128)(2,1)} %bitcast.48), calls=%async_computation.2 | async-start | bytes 1835008 | tf_op jit(solution)/shard_map/all_to_all | solution.py:384
  111.8 11.7 %collective-permute-start.21 = (bf16[2,56,128]{2,1,0:T(8,128)(2,1)S(1)}, bf16[2,56,128]{2,1,0:T(8,128)(2,1)S(1)}, u32[]{:S(2)}, u32[]{:S(2)}) collective-permute-start(bf16[2,56,128]{2,1,0:T(8,128)(2,1)S(1)} %maximum_select_fusion.1.pair_0), channel_id=1, source_target_pairs={{0,32},{32,64},{64,96},{96,0},{1,33},{33,65},{65,97},{97,1},{2,34}... | collective-permute-start | bytes 86024 | tf_op jit(solution)/shard_map/ppermute | solution.py:394
  113.2 11.0 %collective-permute-start.22 = (bf16[2,56,128]{2,1,0:T(8,128)(2,1)S(1)}, bf16[2,56,128]{2,1,0:T(8,128)(2,1)S(1)}, u32[]{:S(2)}, u32[]{:S(2)}) collective-permute-start(bf16[2,56,128]{2,1,0:T(8,128)(2,1)S(1)} %maximum_select_fusion.1.pair_0), channel_id=1, source_target_pairs={{0,64},{32,96},{64,0},{96,32},{1,65},{33,97},{65,1},{97,33},{2,66}... | collective-permute-start | bytes 86024 | tf_op jit(solution)/shard_map/ppermute | solution.py:394
  115.8 8.4 %collective-permute-start.23 = (bf16[2,56,128]{2,1,0:T(8,128)(2,1)S(1)}, bf16[2,56,128]{2,1,0:T(8,128)(2,1)S(1)}, u32[]{:S(2)}, u32[]{:S(2)}) collective-permute-start(bf16[2,56,128]{2,1,0:T(8,128)(2,1)S(1)} %maximum_select_fusion.1.pair_0), channel_id=1, source_target_pairs={{0,96},{32,0},{64,32},{96,64},{1,97},{33,1},{65,33},{97,65},{2,98}... | collective-permute-start | bytes 86024 | tf_op jit(solution)/shard_map/ppermute | solution.py:394
  149.5 5.2 %collective-permute-start.24 = (bf16[3584,128]{1,0:T(8,128)(2,1)S(1)}, bf16[3584,128]{1,0:T(8,128)(2,1)S(1)}, u32[]{:S(2)}, u32[]{:S(2)}) collective-permute-start(bf16[3584,128]{1,0:T(8,128)(2,1)S(1)} %bitcast.41), channel_id=1, source_target_pairs={{0,16},{16,0},{1,17},{17,1},{2,18},{18,2},{3,19},{19,3},{4,20},{20... | collective-permute-start | bytes 2752520 | tf_op jit(solution)/shard_map/ppermute | solution.py:26
  (32 other events, 132.9 us)

commit v4 on v3

--- a/solution.py
+++ b/solution.py
@@ -26,11 +26,12 @@
     return lax.ppermute(array, "c", [(0, 1), (1, 0)])
 
 
-def halo_pieces(own, width):
-    before = shifted(own[:, -width:], GY, 1)
-    after = shifted(own[:, :width], GY, -1)
+def halo_pieces(own, width, first=None, last=None):
+    before = shifted(own[:, -width:] if last is None else last, GY, 1)
+    after = shifted(own[:, :width] if first is None else first, GY, -1)
     low = jnp.concatenate([before[:width], own[:width], after[:width]], axis=1)
     high = jnp.concatenate([before[-width:], own[-width:], after[-width:]], axis=1)
+    low, high = lax.optimization_barrier((low, high))
     left = shifted(high, GX, 1)
     right = shifted(low, GX, -1)
     return (own, before, after, left, right), high
@@ -108,15 +109,21 @@
     return lax.dot_general(left, right, (((0,), (0,)), ((), ())), preferred_element_type=F32)
 
 
-def forward_kernel(own, before, after, left, right, taps_one, taps_two,
-                   act_one, slope_one, slope_two, pooled, padded, packed, halves):
+def forward_kernel(core, own, before, after, left, right, taps_one, taps_two,
+                   field_keep, field_send, slope_one, slope_two, pooled,
+                   padded, packed, act_one, halves):
     fill_padded(padded, own, before, after, left, right)
     fill_forward(packed, taps_one)
+    first_core = core[0] == 0
 
     def first(row, _):
         product = dot_nn(window_rows(padded, row, 6), packed[...])
         act, slope = slope_and_silu(join_taps(product, 6, 64, 128))
-        act_one[row] = act.astype(BF16)
+        act = act.astype(BF16)
+        field = padded[row + 1, 1:7]
+        act_one[row] = act
+        field_keep[row] = jnp.where(first_core, field, act)
+        field_send[row] = jnp.where(first_core, act, field)
         slope_one[row] = slope
         return 0
 
@@ -142,7 +149,7 @@
 
 
 def bottom_kernel(own, before, after, left, right, g_own, g_before, g_after, g_left, g_right,
-                  taps_three, slope_two, skip, bottleneck, err_three, err_two,
+                  taps_three, slope_two, skip, bottleneck, bundle, err_two, err_first, err_last,
                   padded, grads, packed, errors, wide):
     fill_padded(padded, own, before, after, left, right)
     fill_padded(grads, g_own, g_before, g_after, g_left, g_right)
@@ -156,8 +163,12 @@
             bottleneck[row - 1] = act[1:3].astype(BF16)
         errs = (grads[row].astype(F32) * slope).astype(BF16)
         errors[row] = errs
+        bundle[row * 4 : row * 4 + 4] = padded[row + 1, 1:5]
         if row in (1, 2):
-            err_three[row - 1] = errs[1:3]
+            for at_y in range(2):
+                for half in range(2):
+                    at = 16 + ((row - 1) * 2 + at_y) * 2 + half
+                    bundle[at] = errs[1 + at_y, :, half * 128 : half * 128 + 128]
     for row in range(2):
         total = jnp.zeros((64, 384), F32)
         for kx in range(3):
@@ -175,63 +186,69 @@
             for dx in range(2):
                 for dy in range(2):
                     at = (2 * row + dx, 2 * at_y + dy)
-                    err_two[at] = (
-                        (skip[at].astype(F32) + wide[...]) * slope_two[at]
-                    ).astype(BF16)
-
-
-def add_tap_grads(total, fields, skip, error_rows):
+                    err = ((skip[at].astype(F32) + wide[...]) * slope_two[at]).astype(BF16)
+                    err_two[at] = err
+                    edge = err_first if at_y == 0 else err_last
+                    edge[2 * row + dx, dy] = err
+
+
+def add_tap_grads(total, fields, errors):
+    def step(row, _):
+        total[...] += dot_tn(window_rows(fields, row, 4), spread_errors(errors[row].astype(F32)))
+        return 0
+
+    lax.fori_loop(0, 4, step, 0)
+
+
+def own_grads_kernel(fields, errors, total):
     total[...] = jnp.zeros_like(total)
-
-    def step(row, _):
-        total[...] += dot_tn(
-            window_rows(fields, row, 4, skip), spread_errors(error_rows(row).astype(F32))
-        )
-        return 0
-
-    lax.fori_loop(0, 4, step, 0)
-
-
-def store_tap_grads(total, put):
+    add_tap_grads(total, fields, errors)
+
+
+def pair_grads_kernel(fields, errors, own_total, out, total):
+    total[...] = own_total[...]
+    add_tap_grads(total, fields, errors)
     for at in range(9):
         for kz in range(3):
-            part = total[at * 128 : at * 128 + 128, kz * 128 : kz * 128 + 128].astype(BF16)
-            put((at * 3 + kz) * 128, part)
-    put(3456, jnp.zeros((128, 128), BF16))
-
-
-def middle_grads_kernel(act_one, err_two, out, total):
-    add_tap_grads(total, act_one, 0, lambda row: err_two[row])
-
-    def put(rows, part):
-        out[rows : rows + 128] = part
-
-    store_tap_grads(total, put)
-
-
-def bottom_grads_kernel(own, before, after, left, right, err_three, out, padded, total):
-    fill_padded(padded, own, before, after, left, right)
-    for row in range(2):
-        term = dot_tn(
-            spread_errors(err_three[row].astype(F32)), window_rows(padded, row, 2, 1)
-        )
-        if row == 0:
-            total[...] = term
-        else:
-            total[...] += term
-    out[:, 48:64, 48:56] = jnp.zeros((2, 16, 8, 128), BF16)
+            rows = (at * 3 + kz) * 128
+            out[rows : rows + 128] = total[
+                at * 128 : at * 128 + 128, kz * 128 : kz * 128 + 128
+            ].astype(BF16)
+    out[3456:3584] = jnp.zeros((128, 128), BF16)
+
+
+def bottom_grads_kernel(core, own, other, out, total):
+    for step, bundle in ((0, own), (1, other)):
+        for row in range(2):
+            fields = []
+            for kx in range(3):
+                for ky in range(3):
+                    at = (row + kx) * 4 + ky
+                    fields.append(bundle[at : at + 2].reshape(64, 128))
+            at = 16 + row * 4
+            errors = [
+                jnp.concatenate([bundle[at + 2 * y], bundle[at + 2 * y + 1]], axis=1).reshape(1, 32, 256)
+                for y in range(2)
+            ]
+            errors = jnp.concatenate(errors, axis=0).astype(F32)
+            term = dot_tn(spread_errors(errors), jnp.concatenate(fields, axis=1))
+            if step == 0 and row == 0:
+                total[...] = term
+            else:
+                total[...] += term
+    first_core = core[0] == 0
+    out[48:64, 48:56] = jnp.zeros((16, 8, 128), BF16)
     for unit in range(27):
         at_x, rows = unit // 7, unit % 7 * 8
         at, kz = unit // 3, unit % 3
         block = total[kz * 256 : kz * 256 + 256, at * 128 : at * 128 + 128]
         block = block.reshape(16, 2, 8, 128)
-        for half in range(2):
-            out[half, at_x * 16 : at_x * 16 + 16, rows : rows + 8] = block[:, half].astype(BF16)
-
-
-def first_errors_kernel(core, own, before, after, left, right, taps_two, slope_one,
-                        f_own, f_before, f_after, f_left, f_right, two, token,
-                        err_one, out, padded, packed, total):
+        block = jnp.where(first_core, block[:, 0], block[:, 1]).astype(BF16)
+        out[at_x * 16 : at_x * 16 + 16, rows : rows + 8] = block
+
+
+def first_errors_kernel(core, own, before, after, left, right, taps_two, slope_one, token,
+                        err_one, err_keep, err_send, padded, packed):
     fill_padded(padded, own, before, after, left, right)
     fill_backward(packed, taps_two)
 
@@ -242,14 +259,11 @@
         return 0
 
     lax.fori_loop(0, 6, step, 0)
-    fill_padded(padded, f_own, f_before, f_after, f_left, f_right)
-    add_tap_grads(total, padded, 1, lambda row: err_one[row + 1, 1:5])
-
-    def put(rows, part):
-        out[core[0], rows : rows + 128] = part
-        out[1 - core[0], rows : rows + 128] = two[rows : rows + 128]
-
-    store_tap_grads(total, put)
+    first_core = core[0] == 0
+    for row in range(4):
+        first, second = err_one[row + 1, 1:5], own[row]
+        err_keep[row] = jnp.where(first_core, first, second)
+        err_send[row] = jnp.where(first_core, second, first)
 
 
 def input_kernel(err_one, taps_one, out, packed):
@@ -297,8 +311,12 @@
         grad_two[...] = whole[0:3456].astype(F32) * scale
 
 
+def in_hbm(array):
+    return pltpu.with_memory_space_constraint(array, pltpu.HBM)
+
+
 def call(kernel, out_shapes, scratch, flops, *operands):
-    shapes = [jax.ShapeDtypeStruct(s, d) for s, d in out_shapes]
+    shapes = [pltpu.HBM(*s[:2]) if s[2:] else jax.ShapeDtypeStruct(*s) for s in out_shapes]
     moved = sum(o.size * o.dtype.itemsize for o in operands)
     return pl.pallas_call(
         kernel,
@@ -308,7 +326,7 @@
         ],
         out_specs=[pl.BlockSpec(memory_space=pltpu.VMEM)] * len(shapes),
         scratch_shapes=[pltpu.VMEM(s, d) for s, d in scratch],
-        compiler_params=pltpu.CompilerParams(vmem_limit_bytes=14 << 20),
+        compiler_params=pltpu.CompilerParams(vmem_limit_bytes=18 << 20),
         cost_estimate=pl.CostEstimate(flops=flops // 20, bytes_accessed=moved // 20, transcendentals=0),
         name=kernel.__name__,
     )(*operands)
@@ -339,53 +357,54 @@
     g_pieces, _ = halo_pieces(after(bottom_grad, f_pieces[1], f_pieces[2]), 1)
 
     conv_flops = 2 * 1152 * 128 * 1024 * 3
-    act_one, slope_one, slope_two, pooled = call(
+    core_ref = core.reshape(1)
+    field = (6, 6, 64, 128)
+    block = (4, 4, 64, 128)
+    field_keep, field_send, slope_one, slope_two, pooled = call(
         forward_kernel,
-        [((6, 6, 64, 128), BF16), ((6, 6, 64, 128), F32), ((4, 4, 64, 128), F32), ((2, 2, 32, 128), BF16)],
-        [((8, 8, 64, 128), BF16), ((1152, 384), BF16), ((4, 2, 64, 128), F32)],
-        3 * conv_flops, *f_pieces, taps_one, taps_two,
-    )
+        [(field, BF16, True), (field, BF16, True), (field, F32, True), (block, F32, True), ((2, 2, 32, 128), BF16)],
+        [((8, 8, 64, 128), BF16), ((1152, 384), BF16), (field, BF16), ((4, 2, 64, 128), F32)],
+        3 * conv_flops, core_ref, *f_pieces, taps_one, taps_two,
+    )
+    field_other = swap_cores(field_send)
     p_pieces, _ = halo_pieces(pooled, 2)
     mine = after(mine, pooled)
     theirs = swap_cores(mine)
     both = jnp.where(core == 0, jnp.stack([mine, theirs]), jnp.stack([theirs, mine]))
     taps_three = jnp.transpose(both, (2, 1, 0, 3, 4)).reshape(27, 256, 128)
-    bottleneck, err_three, err_two = call(
+    edge = (4, 2, 64, 128)
+    bottleneck, bundle, err_two, err_first, err_last = call(
         bottom_kernel,
-        [((2, 2, 32, 256), BF16), ((2, 2, 32, 256), BF16), ((4, 4, 64, 128), BF16)],
+        [((2, 2, 32, 256), BF16, True), ((24, 32, 128), BF16), (block, BF16, True), (edge, BF16), (edge, BF16)],
         [((6, 6, 32, 128), BF16), ((4, 4, 32, 256), BF16), ((768, 1152), BF16),
          ((4, 4, 32, 256), BF16), ((64, 128), F32)],
         conv_flops, *p_pieces, *g_pieces, taps_three, slope_two, skip_grad,
     )
+    e_pieces, e_high = halo_pieces(err_two, 2, err_first, err_last)
+    token = swap_cores(e_high[0, 0, :8])
+
     (three,) = call(
-        bottom_grads_kernel, [((2, 64, PIECE, 128), BF16)],
-        [((6, 6, 32, 128), BF16), ((768, 1152), F32)],
-        conv_flops // 4, *p_pieces, err_three,
-    )
-    (two,) = call(
-        middle_grads_kernel, [((3584, 128), BF16)], [((1152, 384), F32)],
-        conv_flops, act_one, err_two,
-    )
-    e_pieces, e_high = halo_pieces(err_two, 2)
-    token = swap_cores(e_high[0, 0, :8])
-    kept = pick(three, core).astype(F32) + swap_cores(pick(three, 1 - core)).astype(F32)
-    kept, token = lax.optimization_barrier((kept.astype(BF16), token))
-    three_pieces = lax.all_to_all(kept, FLAT, 0, 0)
-
-    err_one, one = call(
-        first_errors_kernel, [((6, 6, 64, 128), BF16), ((2, 3584, 128), BF16)],
-        [((8, 8, 64, 128), BF16), ((384, 1152), BF16), ((1152, 384), F32)],
-        3 * conv_flops, core.reshape(1), *e_pieces, taps_two, slope_one, *f_pieces, two, token,
-    )
-    sent = after(one[1], three_pieces)
-    kept = one[0].astype(F32) + swap_cores(sent).astype(F32)
-    kept = kept.astype(BF16).reshape(64, PIECE, 128)
+        bottom_grads_kernel, [((64, PIECE, 128), BF16, True)], [((768, 1152), F32)],
+        conv_flops // 2, core_ref, bundle, swap_cores(bundle),
+    )
+    three, token = lax.optimization_barrier((three, token))
+    three_pieces = lax.all_to_all(three, FLAT, 0, 0)
+
+    err_one, err_keep, err_send = call(
+        first_errors_kernel, [(field, BF16, True), (block, BF16), (block, BF16)],
+        [((8, 8, 64, 128), BF16), ((384, 1152), BF16)],
+        2 * conv_flops, core_ref, *[in_hbm(e) for e in e_pieces[:3]], *e_pieces[3:],
+        in_hbm(taps_two), in_hbm(slope_one), token,
+    )
+    err_other = swap_cores(err_send)
+    (total,) = call(own_grads_kernel, [((1152, 384), F32)], [], conv_flops, in_hbm(field_keep), err_keep)
+    (kept,) = call(
+        pair_grads_kernel, [((3584, 128), BF16, True)], [((1152, 384), F32)],
+        conv_flops, field_other, err_other, total,
+    )
+    kept = after(kept, three_pieces).reshape(64, PIECE, 128)
     (part,) = call(
-        sum_kernel, [((64, PIECE, 128), BF16)], [], 0, lax.all_to_all(kept, FLAT, 0, 0)
-    )
-    (input_grad,) = call(
-        input_kernel, [((4, 4, 64, 128), BF16)], [((384, 1152), BF16)],
-        conv_flops, err_one, taps_one,
+        sum_kernel, [((64, PIECE, 128), BF16, True)], [], 0, lax.all_to_all(kept, FLAT, 0, 0)
     )
     (three_part,) = call(sum_kernel, [((1, PIECE, 128), BF16)], [], 0, three_pieces)
     three_part = three_part[0]
@@ -400,6 +419,10 @@
         name="place_kernel",
     )(lax.axis_index("x").reshape(1), *pairs)
     grad_three = jnp.swapaxes(grad_three, 1, 2).reshape(3, 3, 3, 128, 16)
+    (input_grad,) = call(
+        input_kernel, [(block, BF16, True)], [((384, 1152), BF16)],
+        conv_flops, in_hbm(err_one), in_hbm(taps_one),
+    )
     part = after(part, input_grad, grad_three)
     whole = lax.all_to_all(part, FLAT, 0, 0).reshape(64 * PIECE, 128)
     grad_one, grad_two = pl.pallas_call(

time: 158 us -> 167 us (1.057)
  waiting for transfers between devices: 14.1 us -> 30.9 us
  local copies, waits for them, and re-layouts: 15.8 us -> 4.28 us
  Pallas kernels: 27.6 us -> 36.9 us
  other arithmetic: 6.88 us -> 2.58 us
    ppermute x16, waiting for transfers between devices: 3.83 us -> 24.5 us  [shifted(): lax.ppermute(array, axes, [(i, (i + step) % count) for i in range(count)])]
    unnamed x58 -> x28, local copies, waits for them, and re-layouts: 13 us -> 0.66 us
    pallas_call x8 -> x9, Pallas kernels: 24 us -> 33.3 us  [call(): pl.pallas_call(kernel, out_shape=shapes, in_specs=[pl.BlockSpec(memory_sp...]
    convert_element_type x2 -> x0, other arithmetic: 3.5 us -> none  [the longest x1 2.34 us: on_device(): kept = kept.astype(BF16).reshape(64, PIECE, 128)]
    ppermute x6 -> x7, waiting for transfers between devices: 5.41 us -> 2.95 us  [swap_cores(): return lax.ppermute(array, 'c', [(0, 1), (1, 0)])]
    all_to_all x1, starting transfers between devices: 4.45 us -> 6.34 us  [on_device(): mine = lax.all_to_all(half_taps, GY, 0, 0)]
    ppermute x6 -> x7, starting transfers between devices: 9.99 us -> 9.85 us  [swap_cores(): return lax.ppermute(array, 'c', [(0, 1), (1, 0)])]
  transfers between devices with their start and end apart: 28 -> 29, of which waited for: 11 -> 11; matrix products, arithmetic and copies ran while one was open for 4% -> 3% of each run, Pallas kernels for 13% -> 18%
where the time goes in v4:
time: 167 us; the launch traced here: 166 us
  starting transfers between devices  67.3 us (40%)
  Pallas kernels  36.9 us (22%)
  waiting for transfers between devices  30.9 us (19%)
  blocking collectives  23 us (14%)
  local copies, waits for them, and re-layouts  4.28 us (3%)
  other arithmetic  2.58 us (2%)
    pallas_call x9, Pallas kernels, call(): pl.pallas_call(kernel, out_shape=shapes, in_specs=[pl.BlockSpec(memory_sp...  33.3 us
    ppermute x16, starting transfers between devices, shifted(): lax.ppermute(array, axes, [(i, (i + step) % count) for i in range(count)])  30.1 us
    ppermute x16, waiting for transfers between devices, shifted(): lax.ppermute(array, axes, [(i, (i + step) % count) for i in range(count)])  24.5 us
    all_to_all x1, blocking collectives, on_device(): whole = lax.all_to_all(part, FLAT, 0, 0).reshape(64 * PIECE, 128)  23 us
    ppermute x7, starting transfers between devices, swap_cores(): return lax.ppermute(array, 'c', [(0, 1), (1, 0)])  9.85 us
    all_to_all x1, starting transfers between devices, on_device(): three_pieces = lax.all_to_all(three, FLAT, 0, 0)  9.45 us
    all_to_all x1, starting transfers between devices, on_device(): lax.all_to_all(kept, FLAT, 0, 0)  7.66 us
    all_to_all x1, starting transfers between devices, on_device(): mine = lax.all_to_all(half_taps, GY, 0, 0)  6.34 us
  transfers between devices with their start and end apart: 29, of which 11 were waited for; matrix products, arithmetic and copies ran while one was open for 3% of the time, Pallas kernels for 18%

profile of v4, /device:TPU:1, one launch (start us, length us, event | category | flops | bytes accessed | tf_op | source)
XLA Modules:
  0.0 166.0 jit_solution(18009065433736484898)
XLA Ops:
  1.7 7.1 %collective-permute-start.1 = (bf16[4,2,64,128]{3,2,1,0:T(8,128)(2,1)S(1)}, bf16[4,2,64,128]{3,2,1,0:T(8,128)(2,1)S(1)}, u32[]{:S(2)}, u32[]{:S(2)}) collective-permute-start(bf16[4,2,64,128]{3,2,1,0:T(8,128)(2,1)S(1)} %get-tuple-element.67), channel_id=1, source_target_pairs={{0,15},{1,0},{2,1},{3,2},{4,3},{5,4},{6,5},{7,6},{8,7},{9,8},{10,9... | collective-permute-start | bytes 393224 | tf_op jit(solution)/shard_map/ppermute | solution.py:22
  9.9 6.3 %all-to-all-start = ((bf16[16,27,8,128]{3,2,1,0:T(8,128)(2,1)}), bf16[16,27,8,128]{3,2,1,0:T(8,128)(2,1)}, u32[]{:S(2)}, u32[]{:S(2)}) async-start(bf16[16,27,8,128]{3,2,1,0:T(8,128)(2,1)} %broadcast_in_dim.3), calls=%async_computation | async-start | bytes 1769472 | tf_op jit(solution)/shard_map/all_to_all | solution.py:356
  17.1 2.9 %collective-permute-start.2 = (bf16[2,8,64,128]{3,2,1,0:T(8,128)(2,1)}, bf16[2,8,64,128]{3,2,1,0:T(8,128)(2,1)S(1)}, u32[]{:S(2)}, u32[]{:S(2)}) collective-permute-start(bf16[2,8,64,128]{3,2,1,0:T(8,128)(2,1)} %get-tuple-element.34), channel_id=1, source_target_pairs={{0,16},{16,32},{32,48},{48,64},{64,80},{80,96},{96,112},{112,0},{1... | collective-permute-start | bytes 786440 | tf_op jit(solution)/shard_map/ppermute | solution.py:22
  19.9 4.7 %collective-permute-start.9 = (bf16[2,1,32,256]{3,2,1,0:T(8,128)(2,1)S(1)}, bf16[2,1,32,256]{3,2,1,0:T(8,128)(2,1)S(1)}, u32[]{:S(2)}, u32[]{:S(2)}) collective-permute-start(bf16[2,1,32,256]{3,2,1,0:T(8,128)(2,1)S(1)} %get-tuple-element.79), channel_id=1, source_target_pairs={{0,15},{1,0},{2,1},{3,2},{4,3},{5,4},{6,5},{7,6},{8,7},{9,8},{10,9... | collective-permute-start | bytes 98312 | tf_op jit(solution)/shard_map/ppermute | solution.py:22
  26.1 8.1 %forward_kernel.1 = (bf16[6,6,64,128]{3,2,1,0:T(8,128)(2,1)}, bf16[6,6,64,128]{3,2,1,0:T(8,128)(2,1)}, f32[6,6,64,128]{3,2,1,0:T(8,128)}, f32[4,4,64,128]{3,2,1,0:T(8,128)}, bf16[2,2,32,128]{3,2,1,0:T(8,128)(2,1)S(1)}) custom-call(s32[1]{0:T(128)} %bitcast.core, bf16[4,4,64,128]{3,2,1,0:T(8,128)(2,1)S(1)} %copy-done.3, ...), custom_call_target="tpu_custom_call" | custom-call | flops 135895456 | bytes 140902 | tf_op jit(solution)/shard_map/forward_kernel/pallas_call | solution.py:321
  35.7 5.4 %collective-permute-done.8.g_before = bf16[2,1,32,256]{3,2,1,0:T(8,128)(2,1)S(1)} collective-permute-done((bf16[2,1,32,256]{3,2,1,0:T(8,128)(2,1)S(1)}, bf16[2,1,32,256]{3,2,1,0:T(8,128)(2,1)S(1)}, u32[]{:S(2)}, u32[]{:S(2)}) %collective-permute-start.8) | collective-permute-done | bytes 32800 | tf_op jit(solution)/shard_map/ppermute | solution.py:22
  42.5 2.6 %collective-permute-start.10 = (bf16[1,4,32,256]{3,2,1,0:T(8,128)(2,1)S(1)}, bf16[1,4,32,256]{3,2,1,0:T(8,128)(2,1)S(1)}, u32[]{:S(2)}, u32[]{:S(2)}) collective-permute-start(bf16[1,4,32,256]{3,2,1,0:T(8,128)(2,1)S(1)} %get-tuple-element.40), channel_id=1, source_target_pairs={{0,16},{16,32},{32,48},{48,64},{64,80},{80,96},{96,112},{112,0},{1... | collective-permute-start | bytes 196616 | tf_op jit(solution)/shard_map/ppermute | solution.py:22
  45.2 2.7 %collective-permute-done.4.before = bf16[2,2,32,128]{3,2,1,0:T(8,128)(2,1)S(1)} collective-permute-done((bf16[2,2,32,128]{3,2,1,0:T(8,128)(2,1)S(1)}, bf16[2,2,32,128]{3,2,1,0:T(8,128)(2,1)S(1)}, u32[]{:S(2)}, u32[]{:S(2)}) %collective-permute-start.4) | collective-permute-done | bytes 32800 | tf_op jit(solution)/shard_map/ppermute | solution.py:22
  47.9 4.1 %collective-permute-start.6 = (bf16[2,6,32,128]{3,2,1,0:T(8,128)(2,1)S(1)}, bf16[2,6,32,128]{3,2,1,0:T(8,128)(2,1)S(1)}, u32[]{:S(2)}, u32[]{:S(2)}) collective-permute-start(bf16[2,6,32,128]{3,2,1,0:T(8,128)(2,1)S(1)} %pad_maximum_fusion.4), channel_id=1, source_target_pairs={{0,16},{16,32},{32,48},{48,64},{64,80},{80,96},{96,112},{112,0},{1... | collective-permute-start | bytes 294920 | tf_op jit(solution)/shard_map/ppermute | solution.py:22
  56.0 3.7 %bottom_kernel.1 = (bf16[2,2,32,256]{3,2,1,0:T(8,128)(2,1)}, bf16[24,32,128]{2,1,0:T(8,128)(2,1)S(1)}, bf16[4,4,64,128]{3,2,1,0:T(8,128)(2,1)}, bf16[4,2,64,128]...) custom-call(bf16[2,2,32,128]{3,2,1,0:T(8,128)(2,1)S(1)} %get-tuple-element.36.own, ...), custom_call_target="tpu_custom_call" | custom-call | flops 45298484 | bytes 155648 | tf_op jit(solution)/shard_map/bottom_kernel/pallas_call | solution.py:321
  59.8 4.8 %collective-permute-start.14 = (bf16[4,2,64,128]{3,2,1,0:T(8,128)(2,1)S(1)}, bf16[4,2,64,128]{3,2,1,0:T(8,128)(2,1)S(1)}, u32[]{:S(2)}, u32[]{:S(2)}) collective-permute-start(bf16[4,2,64,128]{3,2,1,0:T(8,128)(2,1)S(1)} %get-tuple-element.47), channel_id=1, source_target_pairs={{0,15},{1,0},{2,1},{3,2},{4,3},{5,4},{6,5},{7,6},{8,7},{9,8},{10,9... | collective-permute-start | bytes 393224 | tf_op jit(solution)/shard_map/ppermute | solution.py:22
  69.2 3.0 %bottom_grads_kernel.1 = bf16[64,56,128]{2,1,0:T(8,128)(2,1)} custom-call(s32[1]{0:T(128)} %bitcast.core, bf16[24,32,128]{2,1,0:T(8,128)(2,1)S(1)} %get-tuple-element.51.own, bf16[24,32,128]{2,1,0:T(8,128)(2,1)S(1)} %collective-permute-done.17.other), custom_call_target="tpu_custom_call" | custom-call | flops 22649240 | bytes 19661 | tf_op jit(solution)/shard_map/bottom_grads_kernel/pallas_call | solution.py:321
  72.2 9.4 %all-to-all-start.1 = ((bf16[64,56,128]{2,1,0:T(8,128)(2,1)}), bf16[64,56,128]{2,1,0:T(8,128)(2,1)S(1)}, u32[]{:S(2)}, u32[]{:S(2)}) async-start(bf16[64,56,128]{2,1,0:T(8,128)(2,1)} %bottom_grads_kernel.1), calls=%async_computation.1 | async-start | bytes 1835008 | tf_op jit(solution)/shard_map/all_to_all | solution.py:391
  84.0 12.4 %collective-permute-done.16.right = bf16[2,8,64,128]{3,2,1,0:T(8,128)(2,1)S(1)} collective-permute-done((bf16[2,8,64,128]{3,2,1,0:T(8,128)(2,1)S(1)}, bf16[2,8,64,128]{3,2,1,0:T(8,128)(2,1)S(1)}, u32[]{:S(2)}, u32[]{:S(2)}) %collective-permute-start.16) | collective-permute-done | bytes 262176 | tf_op jit(solution)/shard_map/ppermute | solution.py:22
  96.4 6.8 %first_errors_kernel.1 = (bf16[6,6,64,128]{3,2,1,0:T(8,128)(2,1)}, bf16[4,4,64,128]{3,2,1,0:T(8,128)(2,1)S(1)}, bf16[4,4,64,128]{3,2,1,0:T(8,128)(2,1)S(1)}) custom-call(s32[1]{0:T(128)} %bitcast.core, bf16[4,4,64,128]{3,2,1,0:T(8,128)(2,1)} %get-tuple-element.45.own, bf16[4,2,64,128]{3,2,1,0:T(8,128)(2,1)} %copy-done.7, bf16[4,2,64,128]{3,2,1,0:T(8,128)(2,1)} %copy-done.8, ...), custom_call_target="tpu_custom_call" | custom-call | flops 90596968 | bytes 155750 | tf_op jit(solution)/shard_map/first_errors_kernel/pallas_call | solution.py:321
  105.0 3.2 %own_grads_kernel.1.own_total = f32[1152,384]{1,0:T(8,128)S(1)} custom-call(bf16[6,6,64,128]{3,2,1,0:T(8,128)(2,1)} %get-tuple-element.56.fields, bf16[4,4,64,128]{3,2,1,0:T(8,128)(2,1)S(1)} %get-tuple-element.57.errors), custom_call_target="tpu_custom_call" | custom-call | flops 45298484 | bytes 42598 | tf_op jit(solution)/shard_map/own_grads_kernel/pallas_call | solution.py:321
  108.2 3.1 %pair_grads_kernel.1 = bf16[3584,128]{1,0:T(8,128)(2,1)} custom-call(bf16[6,6,64,128]{3,2,1,0:T(8,128)(2,1)S(1)} %collective-permute-done.19.fields, bf16[4,4,64,128]{3,2,1,0:T(8,128)(2,1)S(1)} %collective-permute-done.20.errors, f32[1152,384]{1,0:T(8,128)S(1)} %own_grads_kernel.1.own_total), custom_call_target="tpu_custom_call" | custom-call | flops 45298484 | bytes 131072 | tf_op jit(solution)/shard_map/pair_grads_kernel/pallas_call | solution.py:321
  111.3 7.7 %all-to-all-start.2 = ((bf16[64,56,128]{2,1,0:T(8,128)(2,1)}), bf16[64,56,128]{2,1,0:T(8,128)(2,1)S(1)}, u32[]{:S(2)}, u32[]{:S(2)}) async-start(bf16[64,56,128]{2,1,0:T(8,128)(2,1)} %bitcast.38), calls=%async_computation.2 | async-start | bytes 1835008 | tf_op jit(solution)/shard_map/all_to_all | solution.py:407
  120.9 2.8 %collective-permute-start.24 = (bf16[2,56,128]{2,1,0:T(8,128)(2,1)S(1)}, bf16[2,56,128]{2,1,0:T(8,128)(2,1)S(1)}, u32[]{:S(2)}, u32[]{:S(2)}) collective-permute-start(bf16[2,56,128]{2,1,0:T(8,128)(2,1)S(1)} %maximum_select_fusion.1.pair_0), channel_id=1, source_target_pairs={{0,96},{32,0},{64,32},{96,64},{1,97},{33,1},{65,33},{97,65},{2,98}... | collective-permute-start | bytes 86024 | tf_op jit(solution)/shard_map/ppermute | solution.py:413
  124.7 4.2 %input_kernel.1 = bf16[4,4,64,128]{3,2,1,0:T(8,128)(2,1)} custom-call(bf16[6,6,64,128]{3,2,1,0:T(8,128)(2,1)} %get-tuple-element.53.err_one, bf16[27,128,128]{2,1,0:T(8,128)(2,1)} %bitcast.35), custom_call_target="tpu_custom_call" | custom-call | flops 45298484 | bytes 73728 | tf_op jit(solution)/shard_map/input_kernel/pallas_call | solution.py:321
  135.7 23.0 %all_to_all.20 = bf16[64,56,128]{2,1,0:T(8,128)(2,1)S(1)} all-to-all(bf16[64,56,128]{2,1,0:T(8,128)(2,1)} %sum_kernel.2), channel_id=1, replica_groups=mesh['x'=4,'c'=2,'z'=4,'y'=4] {'x','z','y'}, dimensions={0} | all-to-all | bytes 1835008 | tf_op jit(solution)/shard_map/all_to_all | solution.py:427
  158.7 3.1 %collective-permute-start.25 = (bf16[3584,128]{1,0:T(8,128)(2,1)S(1)}, bf16[3584,128]{1,0:T(8,128)(2,1)S(1)}, u32[]{:S(2)}, u32[]{:S(2)}) collective-permute-start(bf16[3584,128]{1,0:T(8,128)(2,1)S(1)} %bitcast.31), channel_id=1, source_target_pairs={{0,16},{16,0},{1,17},{17,1},{2,18},{18,2},{3,19},{19,3},{4,20},{20... | collective-permute-start | bytes 2752520 | tf_op jit(solution)/shard_map/ppermute | solution.py:26
  161.8 2.1 %collective-permute-done.25.other = bf16[3584,128]{1,0:T(8,128)(2,1)S(1)} collective-permute-done((bf16[3584,128]{1,0:T(8,128)(2,1)S(1)}, bf16[3584,128]{1,0:T(8,128)(2,1)S(1)}, u32[]{:S(2)}, u32[]{:S(2)}) %collective-permute-start.25) | collective-permute-done | bytes 917536 | tf_op jit(solution)/shard_map/ppermute | solution.py:26
  163.9 2.1 %finish_kernel.1 = (f32[3456,128]{1,0:T(8,128)}, f32[3456,128]{1,0:T(8,128)}) custom-call(s32[1]{0:T(128)} %bitcast.core, bf16[3584,128]{1,0:T(8,128)(2,1)S(1)} %bitcast.32, bf16[3584,128]{1,0:T(8,128)(2,1)S(1)} %collective-permute-done.25.other), custom_call_target="tpu_custom_call" | custom-call | tf_op jit(solution)/shard_map/finish_kernel/pallas_call | solution.py:428
  (96 shorter events, 29.8 us)
Async XLA Ops:
  1.7 14.5 %collective-permute-start.1 = (bf16[4,2,64,128]{3,2,1,0:T(8,128)(2,1)S(1)}, bf16[4,2,64,128]{3,2,1,0:T(8,128)(2,1)S(1)}, u32[]{:S(2)}, u32[]{:S(2)}) collective-permute-start(bf16[4,2,64,128]{3,2,1,0:T(8,128)(2,1)S(1)} %get-tuple-element.67), channel_id=1, source_target_pairs={{0,15},{1,0},{2,1},{3,2},{4,3},{5,4},{6,5},{7,6},{8,7},{9,8},{10,9... | collective-permute-start | bytes 393224 | tf_op jit(solution)/shard_map/ppermute | solution.py:22
  8.8 7.5 %collective-permute-start = (bf16[4,2,64,128]{3,2,1,0:T(8,128)(2,1)S(1)}, bf16[4,2,64,128]{3,2,1,0:T(8,128)(2,1)S(1)}, u32[]{:S(2)}, u32[]{:S(2)}) collective-permute-start(bf16[4,2,64,128]{3,2,1,0:T(8,128)(2,1)S(1)} %get-tuple-element.68), channel_id=1, source_target_pairs={{0,1},{1,2},{2,3},{3,4},{4,5},{5,6},{6,7},{7,8},{8,9},{9,10},{10,1... | collective-permute-start | bytes 393224 | tf_op jit(solution)/shard_map/ppermute | solution.py:22
  9.9 24.4 %all-to-all-start = ((bf16[16,27,8,128]{3,2,1,0:T(8,128)(2,1)}), bf16[16,27,8,128]{3,2,1,0:T(8,128)(2,1)}, u32[]{:S(2)}, u32[]{:S(2)}) async-start(bf16[16,27,8,128]{3,2,1,0:T(8,128)(2,1)} %broadcast_in_dim.3), calls=%async_computation | async-start | bytes 1769472 | tf_op jit(solution)/shard_map/all_to_all | solution.py:356
  17.1 7.6 %collective-permute-start.2 = (bf16[2,8,64,128]{3,2,1,0:T(8,128)(2,1)}, bf16[2,8,64,128]{3,2,1,0:T(8,128)(2,1)S(1)}, u32[]{:S(2)}, u32[]{:S(2)}) collective-permute-start(bf16[2,8,64,128]{3,2,1,0:T(8,128)(2,1)} %get-tuple-element.34), channel_id=1, source_target_pairs={{0,16},{16,32},{32,48},{48,64},{64,80},{80,96},{96,112},{112,0},{1... | collective-permute-start | bytes 786440 | tf_op jit(solution)/shard_map/ppermute | solution.py:22
  19.9 6.2 %collective-permute-start.3 = (bf16[2,8,64,128]{3,2,1,0:T(8,128)(2,1)S(1)}, bf16[2,8,64,128]{3,2,1,0:T(8,128)(2,1)S(1)}, u32[]{:S(2)}, u32[]{:S(2)}) collective-permute-start(bf16[2,8,64,128]{3,2,1,0:T(8,128)(2,1)S(1)} %get-tuple-element.35), channel_id=1, source_target_pairs={{0,112},{16,0},{32,16},{48,32},{64,48},{80,64},{96,80},{112,96},{1... | collective-permute-start | bytes 786440 | tf_op jit(solution)/shard_map/ppermute | solution.py:22
  19.9 15.7 %collective-permute-start.9 = (bf16[2,1,32,256]{3,2,1,0:T(8,128)(2,1)S(1)}, bf16[2,1,32,256]{3,2,1,0:T(8,128)(2,1)S(1)}, u32[]{:S(2)}, u32[]{:S(2)}) collective-permute-start(bf16[2,1,32,256]{3,2,1,0:T(8,128)(2,1)S(1)} %get-tuple-element.79), channel_id=1, source_target_pairs={{0,15},{1,0},{2,1},{3,2},{4,3},{5,4},{6,5},{7,6},{8,7},{9,8},{10,9... | collective-permute-start | bytes 98312 | tf_op jit(solution)/shard_map/ppermute | solution.py:22
  34.2 17.7 %collective-permute-start.12 = (bf16[16,27,8,128]{3,2,1,0:T(8,128)(2,1)}, bf16[16,27,8,128]{3,2,1,0:T(8,128)(2,1)S(1)}, u32[]{:S(2)}, u32[]{:S(2)}) collective-permute-start(bf16[16,27,8,128]{3,2,1,0:T(8,128)(2,1)} %all-to-all-done), channel_id=1, source_target_pairs={{0,16},{16,0},{1,17},{17,1},{2,18},{18,2},{3,19},{19,3},{4,20},{20... | collective-permute-start | bytes 2654216 | tf_op jit(solution)/shard_map/ppermute | solution.py:26
  35.0 6.1 %collective-permute-start.8 = (bf16[2,1,32,256]{3,2,1,0:T(8,128)(2,1)S(1)}, bf16[2,1,32,256]{3,2,1,0:T(8,128)(2,1)S(1)}, u32[]{:S(2)}, u32[]{:S(2)}) collective-permute-start(bf16[2,1,32,256]{3,2,1,0:T(8,128)(2,1)S(1)} %get-tuple-element.80), channel_id=1, source_target_pairs={{0,1},{1,2},{2,3},{3,4},{4,5},{5,6},{6,7},{7,8},{8,9},{9,10},{10,1... | collective-permute-start | bytes 98312 | tf_op jit(solution)/shard_map/ppermute | solution.py:22
  41.8 6.1 %collective-permute-start.4 = (bf16[2,2,32,128]{3,2,1,0:T(8,128)(2,1)S(1)}, bf16[2,2,32,128]{3,2,1,0:T(8,128)(2,1)S(1)}, u32[]{:S(2)}, u32[]{:S(2)}) collective-permute-start(bf16[2,2,32,128]{3,2,1,0:T(8,128)(2,1)S(1)} %get-tuple-element.36.own), channel_id=1, source_target_pairs={{0,1},{1,2},{2,3},{3,4},{4,5},{5,6},{6,7},{7,8},{8,9},{9,10},{10,1... | collective-permute-start | bytes 98312 | tf_op jit(solution)/shard_map/ppermute | solution.py:22
  42.5 11.7 %collective-permute-start.10 = (bf16[1,4,32,256]{3,2,1,0:T(8,128)(2,1)S(1)}, bf16[1,4,32,256]{3,2,1,0:T(8,128)(2,1)S(1)}, u32[]{:S(2)}, u32[]{:S(2)}) collective-permute-start(bf16[1,4,32,256]{3,2,1,0:T(8,128)(2,1)S(1)} %get-tuple-element.40), channel_id=1, source_target_pairs={{0,16},{16,32},{32,48},{48,64},{64,80},{80,96},{96,112},{112,0},{1... | collective-permute-start | bytes 196616 | tf_op jit(solution)/shard_map/ppermute | solution.py:22
  45.1 9.1 %collective-permute-start.11 = (bf16[1,4,32,256]{3,2,1,0:T(8,128)(2,1)S(1)}, bf16[1,4,32,256]{3,2,1,0:T(8,128)(2,1)S(1)}, u32[]{:S(2)}, u32[]{:S(2)}) collective-permute-start(bf16[1,4,32,256]{3,2,1,0:T(8,128)(2,1)S(1)} %get-tuple-element.41), channel_id=1, source_target_pairs={{0,112},{16,0},{32,16},{48,32},{64,48},{80,64},{96,80},{112,96},{1... | collective-permute-start | bytes 196616 | tf_op jit(solution)/shard_map/ppermute | solution.py:22
  47.9 6.4 %collective-permute-start.6 = (bf16[2,6,32,128]{3,2,1,0:T(8,128)(2,1)S(1)}, bf16[2,6,32,128]{3,2,1,0:T(8,128)(2,1)S(1)}, u32[]{:S(2)}, u32[]{:S(2)}) collective-permute-start(bf16[2,6,32,128]{3,2,1,0:T(8,128)(2,1)S(1)} %pad_maximum_fusion.4), channel_id=1, source_target_pairs={{0,16},{16,32},{32,48},{48,64},{64,80},{80,96},{96,112},{112,0},{1... | collective-permute-start | bytes 294920 | tf_op jit(solution)/shard_map/ppermute | solution.py:22
  59.8 7.7 %collective-permute-start.13 = (bf16[4,2,64,128]{3,2,1,0:T(8,128)(2,1)S(1)}, bf16[4,2,64,128]{3,2,1,0:T(8,128)(2,1)S(1)}, u32[]{:S(2)}, u32[]{:S(2)}) collective-permute-start(bf16[4,2,64,128]{3,2,1,0:T(8,128)(2,1)S(1)} %get-tuple-element.46), channel_id=1, source_target_pairs={{0,1},{1,2},{2,3},{3,4},{4,5},{5,6},{6,7},{7,8},{8,9},{9,10},{10,1... | collective-permute-start | bytes 393224 | tf_op jit(solution)/shard_map/ppermute | solution.py:22
  59.8 7.7 %collective-permute-start.14 = (bf16[4,2,64,128]{3,2,1,0:T(8,128)(2,1)S(1)}, bf16[4,2,64,128]{3,2,1,0:T(8,128)(2,1)S(1)}, u32[]{:S(2)}, u32[]{:S(2)}) collective-permute-start(bf16[4,2,64,128]{3,2,1,0:T(8,128)(2,1)S(1)} %get-tuple-element.47), channel_id=1, source_target_pairs={{0,15},{1,0},{2,1},{3,2},{4,3},{5,4},{6,5},{7,6},{8,7},{9,8},{10,9... | collective-permute-start | bytes 393224 | tf_op jit(solution)/shard_map/ppermute | solution.py:22
  72.2 39.1 %all-to-all-start.1 = ((bf16[64,56,128]{2,1,0:T(8,128)(2,1)}), bf16[64,56,128]{2,1,0:T(8,128)(2,1)S(1)}, u32[]{:S(2)}, u32[]{:S(2)}) async-start(bf16[64,56,128]{2,1,0:T(8,128)(2,1)} %bottom_grads_kernel.1), calls=%async_computation.1 | async-start | bytes 1835008 | tf_op jit(solution)/shard_map/all_to_all | solution.py:391
  81.7 26.5 %collective-permute-start.19 = (bf16[6,6,64,128]{3,2,1,0:T(8,128)(2,1)S(1)}, bf16[6,6,64,128]{3,2,1,0:T(8,128)(2,1)S(1)}, u32[]{:S(2)}, u32[]{:S(2)}) collective-permute-start(bf16[6,6,64,128]{3,2,1,0:T(8,128)(2,1)S(1)} %copy-done.13), channel_id=1, source_target_pairs={{0,16},{16,0},{1,17},{17,1},{2,18},{18,2},{3,19},{19,3},{4,20},{20... | collective-permute-start | bytes 1769480 | tf_op jit(solution)/shard_map/ppermute | solution.py:26
  82.2 14.1 %collective-permute-start.16 = (bf16[2,8,64,128]{3,2,1,0:T(8,128)(2,1)S(1)}, bf16[2,8,64,128]{3,2,1,0:T(8,128)(2,1)S(1)}, u32[]{:S(2)}, u32[]{:S(2)}) collective-permute-start(bf16[2,8,64,128]{3,2,1,0:T(8,128)(2,1)S(1)} %pad_maximum_fusion.2), channel_id=1, source_target_pairs={{0,112},{16,0},{32,16},{48,32},{64,48},{80,64},{96,80},{112,96},{1... | collective-permute-start | bytes 786440 | tf_op jit(solution)/shard_map/ppermute | solution.py:22
  82.4 14.0 %collective-permute-start.15 = (bf16[2,8,64,128]{3,2,1,0:T(8,128)(2,1)S(1)}, bf16[2,8,64,128]{3,2,1,0:T(8,128)(2,1)S(1)}, u32[]{:S(2)}, u32[]{:S(2)}) collective-permute-start(bf16[2,8,64,128]{3,2,1,0:T(8,128)(2,1)S(1)} %pad_maximum_fusion.3), channel_id=1, source_target_pairs={{0,16},{16,32},{32,48},{48,64},{64,80},{80,96},{96,112},{112,0},{1... | collective-permute-start | bytes 786440 | tf_op jit(solution)/shard_map/ppermute | solution.py:22
  103.2 5.0 %collective-permute-start.20 = (bf16[4,4,64,128]{3,2,1,0:T(8,128)(2,1)S(1)}, bf16[4,4,64,128]{3,2,1,0:T(8,128)(2,1)S(1)}, u32[]{:S(2)}, u32[]{:S(2)}) collective-permute-start(bf16[4,4,64,128]{3,2,1,0:T(8,128)(2,1)S(1)} %get-tuple-element.55), channel_id=1, source_target_pairs={{0,16},{16,0},{1,17},{17,1},{2,18},{18,2},{3,19},{19,3},{4,20},{20... | collective-permute-start | bytes 786440 | tf_op jit(solution)/shard_map/ppermute | solution.py:26
  111.3 23.2 %all-to-all-start.2 = ((bf16[64,56,128]{2,1,0:T(8,128)(2,1)}), bf16[64,56,128]{2,1,0:T(8,128)(2,1)S(1)}, u32[]{:S(2)}, u32[]{:S(2)}) async-start(bf16[64,56,128]{2,1,0:T(8,128)(2,1)} %bitcast.38), calls=%async_computation.2 | async-start | bytes 1835008 | tf_op jit(solution)/shard_map/all_to_all | solution.py:407
  120.9 9.4 %collective-permute-start.24 = (bf16[2,56,128]{2,1,0:T(8,128)(2,1)S(1)}, bf16[2,56,128]{2,1,0:T(8,128)(2,1)S(1)}, u32[]{:S(2)}, u32[]{:S(2)}) collective-permute-start(bf16[2,56,128]{2,1,0:T(8,128)(2,1)S(1)} %maximum_select_fusion.1.pair_0), channel_id=1, source_target_pairs={{0,96},{32,0},{64,32},{96,64},{1,97},{33,1},{65,33},{97,65},{2,98}... | collective-permute-start | bytes 86024 | tf_op jit(solution)/shard_map/ppermute | solution.py:413
  123.6 8.2 %collective-permute-start.23 = (bf16[2,56,128]{2,1,0:T(8,128)(2,1)S(1)}, bf16[2,56,128]{2,1,0:T(8,128)(2,1)S(1)}, u32[]{:S(2)}, u32[]{:S(2)}) collective-permute-start(bf16[2,56,128]{2,1,0:T(8,128)(2,1)S(1)} %maximum_select_fusion.1.pair_0), channel_id=1, source_target_pairs={{0,64},{32,96},{64,0},{96,32},{1,65},{33,97},{65,1},{97,33},{2,66}... | collective-permute-start | bytes 86024 | tf_op jit(solution)/shard_map/ppermute | solution.py:413
  124.0 8.4 %collective-permute-start.22 = (bf16[2,56,128]{2,1,0:T(8,128)(2,1)S(1)}, bf16[2,56,128]{2,1,0:T(8,128)(2,1)S(1)}, u32[]{:S(2)}, u32[]{:S(2)}) collective-permute-start(bf16[2,56,128]{2,1,0:T(8,128)(2,1)S(1)} %maximum_select_fusion.1.pair_0), channel_id=1, source_target_pairs={{0,32},{32,64},{64,96},{96,0},{1,33},{33,65},{65,97},{97,1},{2,34}... | collective-permute-start | bytes 86024 | tf_op jit(solution)/shard_map/ppermute | solution.py:413
  158.7 5.2 %collective-permute-start.25 = (bf16[3584,128]{1,0:T(8,128)(2,1)S(1)}, bf16[3584,128]{1,0:T(8,128)(2,1)S(1)}, u32[]{:S(2)}, u32[]{:S(2)}) collective-permute-start(bf16[3584,128]{1,0:T(8,128)(2,1)S(1)} %bitcast.31), channel_id=1, source_target_pairs={{0,16},{16,0},{1,17},{17,1},{2,18},{18,2},{3,19},{19,3},{4,20},{20... | collective-permute-start | bytes 2752520 | tf_op jit(solution)/shard_map/ppermute | solution.py:26
  (19 other events, 128.5 us)

commit v5 on v4

--- a/solution.py
+++ b/solution.py
@@ -24,6 +24,11 @@
 
 def swap_cores(array):
     return lax.ppermute(array, "c", [(0, 1), (1, 0)])
+
+
+def ring_pieces(pieces, axis):
+    sent = [lax.ppermute(pieces[d], axis, [(i, (i + d) % 4) for i in range(4)]) for d in (1, 2, 3)]
+    return [pieces[0]] + sent
 
 
 def halo_pieces(own, width, first=None, last=None):
@@ -217,7 +222,7 @@
     out[3456:3584] = jnp.zeros((128, 128), BF16)
 
 
-def bottom_grads_kernel(core, own, other, out, total):
+def bottom_grads_kernel(core, chip, own, other, out, total):
     for step, bundle in ((0, own), (1, other)):
         for row in range(2):
             fields = []
@@ -237,17 +242,17 @@
             else:
                 total[...] += term
     first_core = core[0] == 0
-    out[48:64, 48:56] = jnp.zeros((16, 8, 128), BF16)
+    out[lax.rem(7 - chip[0], 4), :, 48:56] = jnp.zeros((16, 8, 128), BF16)
     for unit in range(27):
-        at_x, rows = unit // 7, unit % 7 * 8
+        at_x, rows = lax.rem(unit // 7 + 4 - chip[0], 4), unit % 7 * 8
         at, kz = unit // 3, unit % 3
         block = total[kz * 256 : kz * 256 + 256, at * 128 : at * 128 + 128]
         block = block.reshape(16, 2, 8, 128)
         block = jnp.where(first_core, block[:, 0], block[:, 1]).astype(BF16)
-        out[at_x * 16 : at_x * 16 + 16, rows : rows + 8] = block
-
-
-def first_errors_kernel(core, own, before, after, left, right, taps_two, slope_one, token,
+        out[at_x, :, rows : rows + 8] = block
+
+
+def first_errors_kernel(core, own, before, after, left, right, taps_two, slope_one,
                         err_one, err_keep, err_send, padded, packed):
     fill_padded(padded, own, before, after, left, right)
     fill_backward(packed, taps_two)
@@ -284,6 +289,30 @@
     total = total.astype(BF16)
     for at in range(out.shape[0]):
         out[at] = total
+
+
+def stage_kernel(chip, own, piece_1, piece_2, piece_3, *outs):
+    pieces = (own, piece_1, piece_2, piece_3)
+    if len(outs) == 1:
+        total = sum(p[0].astype(F32) for p in pieces)
+        outs[0][...] = total.astype(BF16)
+        return
+    quarter = own.shape[0] // 4
+    for distance, out in enumerate(outs):
+        at = lax.rem(chip[0] + distance, 4) * quarter
+        for row in range(quarter):
+            total = sum(p[at + row].astype(F32) for p in pieces)
+            out[row] = total.astype(BF16)
+
+
+def gather_kernel(chip, piece_0, piece_1, piece_2, piece_3, out):
+    for distance, piece in enumerate((piece_0, piece_1, piece_2, piece_3)):
+        at = lax.rem(chip[0] + 4 - distance, 4)
+        if len(out.shape) == 4:
+            out[at] = piece[...]
+        else:
+            for row in range(4):
+                out[:, row, at] = piece[row]
 
 
 def place_kernel(chip, pair_0, pair_1, pair_2, pair_3, out, *, scale):
@@ -342,89 +371,99 @@
 
 def on_device(features, skip_grad, bottom_grad, conv_one, conv_two, conv_three):
     core = lax.axis_index("c")
+    f_sent, first_core, core, core_ref, *chip = lax.optimization_barrier((
+        features[:, -2:], core == 0, core, core.reshape(1),
+        *[lax.axis_index(axis).reshape(1) for axis in ("x", "z", "y")],
+    ))
     fine_cells = features.size // 128 * lax.axis_size(GX) * lax.axis_size(GY)
     fine_scale = 1.0 / math.sqrt(fine_cells)
     coarse_scale = 1.0 / math.sqrt(fine_cells // 8)
     taps_one = conv_one.reshape(27, 128, 128)
     taps_two = conv_two.reshape(27, 128, 128)
 
-    f_pieces, _ = halo_pieces(features, 2)
+    f_pieces, f_high = halo_pieces(features, 2, last=f_sent)
 
     own_taps = jnp.swapaxes(conv_three.reshape(27, 128, 16), 1, 2)
     half_taps = pick(jnp.swapaxes(own_taps.reshape(27, 2, 8, 128), 0, 1), core)
-    half_taps = jnp.broadcast_to(half_taps, (16, 27, 8, 128))
-    mine = lax.all_to_all(half_taps, GY, 0, 0)
+    half_taps = after(half_taps, f_high)
+    piece = (4, 27, 8, 128)
+    (mine,) = call(
+        gather_kernel, [(piece, BF16)], [], 0, chip[1], *ring_pieces([half_taps] * 4, "z")
+    )
+    taps_pieces = ring_pieces([after(mine, *f_pieces[3:])] * 4, "y")
     g_pieces, _ = halo_pieces(after(bottom_grad, f_pieces[1], f_pieces[2]), 1)
 
     conv_flops = 2 * 1152 * 128 * 1024 * 3
-    core_ref = core.reshape(1)
     field = (6, 6, 64, 128)
     block = (4, 4, 64, 128)
     field_keep, field_send, slope_one, slope_two, pooled = call(
         forward_kernel,
-        [(field, BF16, True), (field, BF16, True), (field, F32, True), (block, F32, True), ((2, 2, 32, 128), BF16)],
+        [(field, BF16), (field, BF16), (field, F32), (block, F32), ((2, 2, 32, 128), BF16)],
         [((8, 8, 64, 128), BF16), ((1152, 384), BF16), (field, BF16), ((4, 2, 64, 128), F32)],
         3 * conv_flops, core_ref, *f_pieces, taps_one, taps_two,
     )
     field_other = swap_cores(field_send)
-    p_pieces, _ = halo_pieces(pooled, 2)
-    mine = after(mine, pooled)
+    p_pieces, p_high = halo_pieces(pooled, 2)
+    *taps_pieces, p_high = lax.optimization_barrier((*taps_pieces, p_high))
+    (mine,) = call(gather_kernel, [((27, 4, 4, 8, 128), BF16)], [], 0, chip[2], *taps_pieces)
+    mine = mine.reshape(27, 16, 8, 128)
     theirs = swap_cores(mine)
-    both = jnp.where(core == 0, jnp.stack([mine, theirs]), jnp.stack([theirs, mine]))
-    taps_three = jnp.transpose(both, (2, 1, 0, 3, 4)).reshape(27, 256, 128)
+    both = jnp.where(first_core, jnp.stack([mine, theirs], 2), jnp.stack([theirs, mine], 2))
+    taps_three = both.reshape(27, 256, 128)
     edge = (4, 2, 64, 128)
     bottleneck, bundle, err_two, err_first, err_last = call(
         bottom_kernel,
-        [((2, 2, 32, 256), BF16, True), ((24, 32, 128), BF16), (block, BF16, True), (edge, BF16), (edge, BF16)],
+        [((2, 2, 32, 256), BF16, True), ((24, 32, 128), BF16), (block, BF16), (edge, BF16), (edge, BF16)],
         [((6, 6, 32, 128), BF16), ((4, 4, 32, 256), BF16), ((768, 1152), BF16),
          ((4, 4, 32, 256), BF16), ((64, 128), F32)],
         conv_flops, *p_pieces, *g_pieces, taps_three, slope_two, skip_grad,
     )
     e_pieces, e_high = halo_pieces(err_two, 2, err_first, err_last)
-    token = swap_cores(e_high[0, 0, :8])
-
+    bundle = after(bundle, e_high)
     (three,) = call(
-        bottom_grads_kernel, [((64, PIECE, 128), BF16, True)], [((768, 1152), F32)],
-        conv_flops // 2, core_ref, bundle, swap_cores(bundle),
-    )
-    three, token = lax.optimization_barrier((three, token))
-    three_pieces = lax.all_to_all(three, FLAT, 0, 0)
-
+        bottom_grads_kernel, [((4, 16, PIECE, 128), BF16)], [((768, 1152), F32)],
+        conv_flops // 2, core_ref, chip[0], bundle, swap_cores(bundle),
+    )
+    three = after(three, e_pieces[3], e_pieces[4])
+    pieces = ring_pieces([three[d] for d in range(4)], "x")
+    pieces = call(stage_kernel, [((4, PIECE, 128), BF16)] * 4, [], 0, chip[1], *pieces)
     err_one, err_keep, err_send = call(
         first_errors_kernel, [(field, BF16, True), (block, BF16), (block, BF16)],
         [((8, 8, 64, 128), BF16), ((384, 1152), BF16)],
-        2 * conv_flops, core_ref, *[in_hbm(e) for e in e_pieces[:3]], *e_pieces[3:],
-        in_hbm(taps_two), in_hbm(slope_one), token,
+        2 * conv_flops, core_ref, *e_pieces, taps_two, slope_one,
     )
     err_other = swap_cores(err_send)
-    (total,) = call(own_grads_kernel, [((1152, 384), F32)], [], conv_flops, in_hbm(field_keep), err_keep)
+    (total,) = call(own_grads_kernel, [((1152, 384), F32)], [], conv_flops, field_keep, err_keep)
     (kept,) = call(
         pair_grads_kernel, [((3584, 128), BF16, True)], [((1152, 384), F32)],
         conv_flops, field_other, err_other, total,
     )
-    kept = after(kept, three_pieces).reshape(64, PIECE, 128)
+    kept, *pieces = lax.optimization_barrier((kept, *pieces))
+    kept = kept.reshape(64, PIECE, 128)
     (part,) = call(
         sum_kernel, [((64, PIECE, 128), BF16, True)], [], 0, lax.all_to_all(kept, FLAT, 0, 0)
     )
-    (three_part,) = call(sum_kernel, [((1, PIECE, 128), BF16)], [], 0, three_pieces)
-    three_part = three_part[0]
+    pieces = ring_pieces(pieces, "z")
+    pieces = call(stage_kernel, [((1, PIECE, 128), BF16)] * 4, [], 0, chip[2], *pieces)
+    (three_part,) = call(stage_kernel, [((PIECE, 128), BF16)], [], 0, chip[2], *ring_pieces(pieces, "y"))
+    (input_grad,) = call(
+        input_kernel, [(block, BF16, True)], [((384, 1152), BF16)],
+        conv_flops, err_one, taps_one,
+    )
+    part, three_part = lax.optimization_barrier((after(part, input_grad), three_part))
+    whole = lax.all_to_all(part, FLAT, 0, 0).reshape(64 * PIECE, 128)
     both = swap_cores(three_part)
-    both = jnp.where(core == 0, jnp.stack([three_part, both]), jnp.stack([both, three_part]))
-    pairs = [both] + [lax.ppermute(both, "x", [(i, (i + d) % 4) for i in range(4)]) for d in (1, 2, 3)]
+    both = jnp.where(first_core, jnp.stack([three_part, both]), jnp.stack([both, three_part]))
+    pairs = ring_pieces([both] * 4, "x")
     grad_three = pl.pallas_call(
         functools.partial(place_kernel, scale=coarse_scale),
         out_shape=jax.ShapeDtypeStruct((27, 16, 128), F32),
         in_specs=[pl.BlockSpec(memory_space=pltpu.SMEM)] + [pl.BlockSpec(memory_space=pltpu.VMEM)] * 4,
         out_specs=pl.BlockSpec(memory_space=pltpu.VMEM),
         name="place_kernel",
-    )(lax.axis_index("x").reshape(1), *pairs)
+    )(chip[0], *pairs)
+    whole, grad_three = lax.optimization_barrier((whole, grad_three))
     grad_three = jnp.swapaxes(grad_three, 1, 2).reshape(3, 3, 3, 128, 16)
-    (input_grad,) = call(
-        input_kernel, [(block, BF16, True)], [((384, 1152), BF16)],
-        conv_flops, in_hbm(err_one), in_hbm(taps_one),
-    )
-    part = after(part, input_grad, grad_three)
-    whole = lax.all_to_all(part, FLAT, 0, 0).reshape(64 * PIECE, 128)
     grad_one, grad_two = pl.pallas_call(
         functools.partial(finish_kernel, scale=fine_scale),
         out_shape=[jax.ShapeDtypeStruct((3456, 128), F32)] * 2,
@@ -432,7 +471,7 @@
         out_specs=[pl.BlockSpec(memory_space=pltpu.VMEM)] * 2,
         compiler_params=pltpu.CompilerParams(vmem_limit_bytes=8 << 20),
         name="finish_kernel",
-    )(core.reshape(1), whole, swap_cores(whole))
+    )(core_ref, whole, swap_cores(whole))
     grad_one = grad_one.reshape(3, 3, 3, 128, 128)
     grad_two = grad_two.reshape(3, 3, 3, 128, 128)
 

time: 167 us -> 165 us (0.988)
  starting transfers between devices: 67.3 us -> 90.5 us
  blocking collectives: 23 us -> 0 us
  waiting for transfers between devices: 30.9 us -> 39.1 us
  Pallas kernels: 36.9 us -> 30.2 us
  other arithmetic: 2.58 us -> 0.69 us
    all_to_all x1 -> x0, blocking collectives: 23 us -> none  [on_device(): whole = lax.all_to_all(part, FLAT, 0, 0).reshape(64 * PIECE, 128)]
    ppermute x3 -> x18, starting transfers between devices: 3.82 us -> 26.8 us  [ring_pieces(): lax.ppermute(pieces[d], axis, [(i, (i + d) % 4) for i in range(4)])]
    ppermute x3 -> x18, waiting for transfers between devices: 3.52 us -> 25.3 us  [ring_pieces(): lax.ppermute(pieces[d], axis, [(i, (i + d) % 4) for i in range(4)])]
    ppermute x16, waiting for transfers between devices: 24.5 us -> 9.79 us  [shifted(): lax.ppermute(array, axes, [(i, (i + step) % count) for i in range(count)])]
    all_to_all x2 -> x1, starting transfers between devices: 15.8 us -> 7.08 us  [on_device(): whole = lax.all_to_all(part, FLAT, 0, 0).reshape(64 * PIECE, 128)]
    pallas_call x9 -> x13, Pallas kernels: 33.3 us -> 26.6 us  [call(): pl.pallas_call(kernel, out_shape=shapes, in_specs=[pl.BlockSpec(memory_sp...]
    ppermute x7 -> x6, starting transfers between devices: 9.85 us -> 14.9 us  [swap_cores(): return lax.ppermute(array, 'c', [(0, 1), (1, 0)])]
    all_to_all x1, starting transfers between devices: 7.66 us -> 9.95 us  [on_device(): lax.all_to_all(kept, FLAT, 0, 0)]
  transfers between devices with their start and end apart: 29 -> 42, of which waited for: 11 -> 18; matrix products, arithmetic and copies ran while one was open for 3% -> 1% of each run, Pallas kernels for 18% -> 13%
where the time goes in v5:
time: 165 us
  starting transfers between devices  90.5 us (55%)
  waiting for transfers between devices  39.1 us (24%)
  Pallas kernels  30.2 us (18%)
  local copies, waits for them, and re-layouts  3.54 us (2%)
    ppermute x16, starting transfers between devices, shifted(): lax.ppermute(array, axes, [(i, (i + step) % count) for i in range(count)])  31.8 us
    ppermute x18, starting transfers between devices, ring_pieces(): lax.ppermute(pieces[d], axis, [(i, (i + d) % 4) for i in range(4)])  26.8 us
    pallas_call x13, Pallas kernels, call(): pl.pallas_call(kernel, out_shape=shapes, in_specs=[pl.BlockSpec(memory_sp...  26.6 us
    ppermute x18, waiting for transfers between devices, ring_pieces(): lax.ppermute(pieces[d], axis, [(i, (i + d) % 4) for i in range(4)])  25.3 us
    ppermute x6, starting transfers between devices, swap_cores(): return lax.ppermute(array, 'c', [(0, 1), (1, 0)])  14.9 us
    all_to_all x1, starting transfers between devices, on_device(): lax.all_to_all(kept, FLAT, 0, 0)  9.95 us
    ppermute x16, waiting for transfers between devices, shifted(): lax.ppermute(array, axes, [(i, (i + step) % count) for i in range(count)])  9.79 us
    all_to_all x1, starting transfers between devices, on_device(): whole = lax.all_to_all(part, FLAT, 0, 0).reshape(64 * PIECE, 128)  7.08 us
  transfers between devices with their start and end apart: 42, of which 18 were waited for; matrix products, arithmetic and copies ran while one was open for 1% of the time, Pallas kernels for 13%

profile of v5, /device:TPU:1, one launch (start us, length us, event | category | flops | bytes accessed | tf_op | source)
XLA Modules:
  0.0 165.1 jit_solution(10646412160137946854)
XLA Ops:
  4.0 5.0 %collective-permute-start.1 = (bf16[4,2,64,128]{3,2,1,0:T(8,128)(2,1)S(1)}, bf16[4,2,64,128]{3,2,1,0:T(8,128)(2,1)S(1)}, u32[]{:S(2)}, u32[]{:S(2)}) collective-permute-start(bf16[4,2,64,128]{3,2,1,0:T(8,128)(2,1)S(1)} %get-tuple-element.127), channel_id=1, source_target_pairs={{0,15},{1,0},{2,1},{3,2},{4,3},{5,4},{6,5},{7,6},{8,7},{9,8},{10,9... | collective-permute-start | bytes 393224 | tf_op jit(solution)/shard_map/ppermute | solution.py:22
  12.3 2.3 %collective-permute-start.2 = (bf16[2,8,64,128]{3,2,1,0:T(8,128)(2,1)S(1)}, bf16[2,8,64,128]{3,2,1,0:T(8,128)(2,1)S(1)}, u32[]{:S(2)}, u32[]{:S(2)}) collective-permute-start(bf16[2,8,64,128]{3,2,1,0:T(8,128)(2,1)S(1)} %get-tuple-element.64), channel_id=1, source_target_pairs={{0,16},{16,32},{32,48},{48,64},{64,80},{80,96},{96,112},{112,0},{1... | collective-permute-start | bytes 786440 | tf_op jit(solution)/shard_map/ppermute | solution.py:22
  20.8 4.7 %collective-permute-start.16 = (bf16[4,27,8,128]{3,2,1,0:T(8,128)(2,1)S(1)}, bf16[4,27,8,128]{3,2,1,0:T(8,128)(2,1)S(1)}, u32[]{:S(2)}, u32[]{:S(2)}) collective-permute-start(bf16[4,27,8,128]{3,2,1,0:T(8,128)(2,1)S(1)} %gather_kernel.2.piece_0), channel_id=1, source_target_pairs={{0,2},{1,3},{2,0},{3,1},{4,6},{5,7},{6,4},{7,5},{8,10},{9,11},{10,... | collective-permute-start | bytes 663560 | tf_op jit(solution)/shard_map/ppermute | solution.py:30
  25.6 6.9 %forward_kernel.1 = (bf16[6,6,64,128]{3,2,1,0:T(8,128)(2,1)S(1)}, bf16[6,6,64,128]{3,2,1,0:T(8,128)(2,1)S(1)}, f32[6,6,64,128]{3,2,1,0:T(8,128)S(1)}, f32[4,4,64...) custom-call(s32[1]{0:T(128)} %bitcast.core, bf16[4,4,64,128]{3,2,1,0:T(8,128)(2,1)S(1)} %copy-done.3, ...), custom_call_target="tpu_custom_call" | custom-call | flops 135895456 | bytes 140902 | tf_op jit(solution)/shard_map/forward_kernel/pallas_call | solution.py:350
  34.0 3.3 %collective-permute-start.5 = (bf16[2,2,32,128]{3,2,1,0:T(8,128)(2,1)S(1)}, bf16[2,2,32,128]{3,2,1,0:T(8,128)(2,1)S(1)}, u32[]{:S(2)}, u32[]{:S(2)}) collective-permute-start(bf16[2,2,32,128]{3,2,1,0:T(8,128)(2,1)S(1)} %get-tuple-element.66.own), channel_id=1, source_target_pairs={{0,15},{1,0},{2,1},{3,2},{4,3},{5,4},{6,5},{7,6},{8,7},{9,8},{10,9... | collective-permute-start | bytes 98312 | tf_op jit(solution)/shard_map/ppermute | solution.py:22
  39.0 5.1 %collective-permute-start.18 = (bf16[27,16,8,128]{3,2,1,0:T(8,128)(2,1)S(1)}, bf16[27,16,8,128]{3,2,1,0:T(8,128)(2,1)S(1)}, u32[]{:S(2)}, u32[]{:S(2)}) collective-permute-start(bf16[27,16,8,128]{3,2,1,0:T(8,128)(2,1)S(1)} %bitcast.44), channel_id=1, source_target_pairs={{0,16},{16,0},{1,17},{17,1},{2,18},{18,2},{3,19},{19,3},{4,20},{20... | collective-permute-start | bytes 2654216 | tf_op jit(solution)/shard_map/ppermute | solution.py:26
  44.2 5.1 %collective-permute-start.9 = (bf16[2,1,32,256]{3,2,1,0:T(8,128)(2,1)S(1)}, bf16[2,1,32,256]{3,2,1,0:T(8,128)(2,1)S(1)}, u32[]{:S(2)}, u32[]{:S(2)}) collective-permute-start(bf16[2,1,32,256]{3,2,1,0:T(8,128)(2,1)S(1)} %get-tuple-element.139), channel_id=1, source_target_pairs={{0,15},{1,0},{2,1},{3,2},{4,3},{5,4},{6,5},{7,6},{8,7},{9,8},{10,9... | collective-permute-start | bytes 98312 | tf_op jit(solution)/shard_map/ppermute | solution.py:22
  57.3 3.0 %bottom_kernel.1 = (bf16[2,2,32,256]{3,2,1,0:T(8,128)(2,1)}, bf16[24,32,128]{2,1,0:T(8,128)(2,1)S(1)}, bf16[4,4,64,128]{3,2,1,0:T(8,128)(2,1)S(1)}, bf16[4,2,64,...) custom-call(bf16[2,2,32,128]{3,2,1,0:T(8,128)(2,1)S(1)} %get-tuple-element.66.own, ...), custom_call_target="tpu_custom_call" | custom-call | flops 45298484 | bytes 155648 | tf_op jit(solution)/shard_map/bottom_kernel/pallas_call | solution.py:350
  60.3 5.1 %collective-permute-start.20 = (bf16[4,2,64,128]{3,2,1,0:T(8,128)(2,1)S(1)}, bf16[4,2,64,128]{3,2,1,0:T(8,128)(2,1)S(1)}, u32[]{:S(2)}, u32[]{:S(2)}) collective-permute-start(bf16[4,2,64,128]{3,2,1,0:T(8,128)(2,1)S(1)} %get-tuple-element.86), channel_id=1, source_target_pairs={{0,15},{1,0},{2,1},{3,2},{4,3},{5,4},{6,5},{7,6},{8,7},{9,8},{10,9... | collective-permute-start | bytes 393224 | tf_op jit(solution)/shard_map/ppermute | solution.py:22
  71.3 2.9 %collective-permute-start.25 = (bf16[24,32,128]{2,1,0:T(8,128)(2,1)S(1)}, bf16[24,32,128]{2,1,0:T(8,128)(2,1)S(1)}, u32[]{:S(2)}, u32[]{:S(2)}) collective-permute-start(bf16[24,32,128]{2,1,0:T(8,128)(2,1)S(1)} %get-tuple-element.97.own), channel_id=1, source_target_pairs={{0,16},{16,0},{1,17},{17,1},{2,18},{18,2},{3,19},{19,3},{4,20},{20... | collective-permute-start | bytes 589832 | tf_op jit(solution)/shard_map/ppermute | solution.py:26
  77.4 5.0 %first_errors_kernel.1 = (bf16[6,6,64,128]{3,2,1,0:T(8,128)(2,1)}, bf16[4,4,64,128]{3,2,1,0:T(8,128)(2,1)S(1)}, bf16[4,4,64,128]{3,2,1,0:T(8,128)(2,1)S(1)}) custom-call(s32[1]{0:T(128)} %bitcast.core, bf16[4,4,64,128]{3,2,1,0:T(8,128)(2,1)S(1)} %get-tuple-element.84.own, bf16[4,2,64,128]{3,2,1,0:T(8,128)(2,1)S(1)} %collective-permute-done.19.before, ...), custom_call_target="tpu_custom_call" | custom-call | flops 90596968 | bytes 155648 | tf_op jit(solution)/shard_map/first_errors_kernel/pallas_call | solution.py:350
  83.5 3.7 %collective-permute-start.27 = (bf16[16,56,128]{2,1,0:T(8,128)(2,1)S(1)}, bf16[16,56,128]{2,1,0:T(8,128)(2,1)S(1)}, u32[]{:S(2)}, u32[]{:S(2)}) collective-permute-start(bf16[16,56,128]{2,1,0:T(8,128)(2,1)S(1)} %get-tuple-element.120), channel_id=1, source_target_pairs={{0,64},{32,96},{64,0},{96,32},{1,65},{33,97},{65,1},{97,33},{2,66}... | collective-permute-start | bytes 688136 | tf_op jit(solution)/shard_map/ppermute | solution.py:30
  89.4 2.4 %collective-permute-done.26.piece_1 = bf16[16,56,128]{2,1,0:T(8,128)(2,1)S(1)} collective-permute-done((bf16[16,56,128]{2,1,0:T(8,128)(2,1)S(1)}, bf16[16,56,128]{2,1,0:T(8,128)(2,1)S(1)}, u32[]{:S(2)}, u32[]{:S(2)}) %collective-permute-start.26) | collective-permute-done | bytes 229408 | tf_op jit(solution)/shard_map/ppermute | solution.py:30
  91.8 5.5 %collective-permute-done.27.piece_2 = bf16[16,56,128]{2,1,0:T(8,128)(2,1)S(1)} collective-permute-done((bf16[16,56,128]{2,1,0:T(8,128)(2,1)S(1)}, bf16[16,56,128]{2,1,0:T(8,128)(2,1)S(1)}, u32[]{:S(2)}, u32[]{:S(2)}) %collective-permute-start.27) | collective-permute-done | bytes 229408 | tf_op jit(solution)/shard_map/ppermute | solution.py:30
  97.5 3.1 %pair_grads_kernel.1 = bf16[3584,128]{1,0:T(8,128)(2,1)} custom-call(bf16[6,6,64,128]{3,2,1,0:T(8,128)(2,1)S(1)} %collective-permute-done.23.fields, bf16[4,4,64,128]{3,2,1,0:T(8,128)(2,1)S(1)} %collective-permute-done.24.errors, f32[1152,384]{1,0:T(8,128)S(1)} %own_grads_kernel.1.own_total), custom_call_target="tpu_custom_call" | custom-call | flops 45298484 | bytes 131072 | tf_op jit(solution)/shard_map/pair_grads_kernel/pallas_call | solution.py:350
  100.6 9.9 %all-to-all-start = ((bf16[64,56,128]{2,1,0:T(8,128)(2,1)}), bf16[64,56,128]{2,1,0:T(8,128)(2,1)S(1)}, u32[]{:S(2)}, u32[]{:S(2)}) async-start(bf16[64,56,128]{2,1,0:T(8,128)(2,1)} %bitcast.47), calls=%async_computation | async-start | bytes 1835008 | tf_op jit(solution)/shard_map/all_to_all | solution.py:444
  111.6 2.4 %collective-permute-start.30 = (bf16[4,56,128]{2,1,0:T(8,128)(2,1)S(1)}, bf16[4,56,128]{2,1,0:T(8,128)(2,1)S(1)}, u32[]{:S(2)}, u32[]{:S(2)}) collective-permute-start(bf16[4,56,128]{2,1,0:T(8,128)(2,1)S(1)} %get-tuple-element.107), channel_id=1, source_target_pairs={{0,8},{4,12},{8,0},{12,4},{1,9},{5,13},{9,1},{13,5},{2,10},{6,14},... | collective-permute-start | bytes 172040 | tf_op jit(solution)/shard_map/ppermute | solution.py:30
  115.6 10.2 %collective-permute-done.30.piece_2 = bf16[4,56,128]{2,1,0:T(8,128)(2,1)S(1)} collective-permute-done((bf16[4,56,128]{2,1,0:T(8,128)(2,1)S(1)}, bf16[4,56,128]{2,1,0:T(8,128)(2,1)S(1)}, u32[]{:S(2)}, u32[]{:S(2)}) %collective-permute-start.30) | collective-permute-done | bytes 57376 | tf_op jit(solution)/shard_map/ppermute | solution.py:30
  127.4 2.6 %collective-permute-start.33 = (bf16[1,56,128]{2,1,0:T(8,128)(2,1)S(1)}, bf16[1,56,128]{2,1,0:T(8,128)(2,1)S(1)}, u32[]{:S(2)}, u32[]{:S(2)}) collective-permute-start(bf16[1,56,128]{2,1,0:T(8,128)(2,1)S(1)} %get-tuple-element.111), channel_id=1, source_target_pairs={{0,2},{1,3},{2,0},{3,1},{4,6},{5,7},{6,4},{7,5},{8,10},{9,11},{10,... | collective-permute-start | bytes 43016 | tf_op jit(solution)/shard_map/ppermute | solution.py:30
  131.1 2.8 %input_kernel.1 = bf16[4,4,64,128]{3,2,1,0:T(8,128)(2,1)} custom-call(bf16[6,6,64,128]{3,2,1,0:T(8,128)(2,1)S(1)} %copy-done.5, bf16[27,128,128]{2,1,0:T(8,128)(2,1)S(1)} %bitcast.43), custom_call_target="tpu_custom_call" | custom-call | flops 45298484 | bytes 73728 | tf_op jit(solution)/shard_map/input_kernel/pallas_call | solution.py:350
  135.1 7.1 %all-to-all-start.1 = ((bf16[64,56,128]{2,1,0:T(8,128)(2,1)}), bf16[64,56,128]{2,1,0:T(8,128)(2,1)S(1)}, u32[]{:S(2)}, u32[]{:S(2)}) async-start(bf16[64,56,128]{2,1,0:T(8,128)(2,1)} %sum_kernel.1), calls=%async_computation.1 | async-start | bytes 1835008 | tf_op jit(solution)/shard_map/all_to_all | solution.py:454
  146.6 2.6 %collective-permute-start.37 = (bf16[2,56,128]{2,1,0:T(8,128)(2,1)S(1)}, bf16[2,56,128]{2,1,0:T(8,128)(2,1)S(1)}, u32[]{:S(2)}, u32[]{:S(2)}) collective-permute-start(bf16[2,56,128]{2,1,0:T(8,128)(2,1)S(1)} %maximum_select_fusion.1.pair_0), channel_id=1, source_target_pairs={{0,64},{32,96},{64,0},{96,32},{1,65},{33,97},{65,1},{97,33},{2,66}... | collective-permute-start | bytes 86024 | tf_op jit(solution)/shard_map/ppermute | solution.py:30
  150.2 4.1 %collective-permute-done.36.pair_1 = bf16[2,56,128]{2,1,0:T(8,128)(2,1)S(1)} collective-permute-done((bf16[2,56,128]{2,1,0:T(8,128)(2,1)S(1)}, bf16[2,56,128]{2,1,0:T(8,128)(2,1)S(1)}, u32[]{:S(2)}, u32[]{:S(2)}) %collective-permute-start.36) | collective-permute-done | bytes 28704 | tf_op jit(solution)/shard_map/ppermute | solution.py:30
  157.1 3.8 %collective-permute-start.39 = (bf16[3584,128]{1,0:T(8,128)(2,1)S(1)}, bf16[3584,128]{1,0:T(8,128)(2,1)S(1)}, u32[]{:S(2)}, u32[]{:S(2)}) collective-permute-start(bf16[3584,128]{1,0:T(8,128)(2,1)S(1)} %bitcast.38), channel_id=1, source_target_pairs={{0,16},{16,0},{1,17},{17,1},{2,18},{18,2},{3,19},{19,3},{4,20},{20... | collective-permute-start | bytes 2752520 | tf_op jit(solution)/shard_map/ppermute | solution.py:26
  (117 shorter events, 55.1 us)
Async XLA Ops:
  1.8 10.3 %collective-permute-start = (bf16[4,2,64,128]{3,2,1,0:T(8,128)(2,1)S(1)}, bf16[4,2,64,128]{3,2,1,0:T(8,128)(2,1)S(1)}, u32[]{:S(2)}, u32[]{:S(2)}) collective-permute-start(bf16[4,2,64,128]{3,2,1,0:T(8,128)(2,1)S(1)} %get-tuple-element.63), channel_id=1, source_target_pairs={{0,1},{1,2},{2,3},{3,4},{4,5},{5,6},{6,7},{7,8},{8,9},{9,10},{10,1... | collective-permute-start | bytes 393224 | tf_op jit(solution)/shard_map/ppermute | solution.py:22
  4.0 8.2 %collective-permute-start.1 = (bf16[4,2,64,128]{3,2,1,0:T(8,128)(2,1)S(1)}, bf16[4,2,64,128]{3,2,1,0:T(8,128)(2,1)S(1)}, u32[]{:S(2)}, u32[]{:S(2)}) collective-permute-start(bf16[4,2,64,128]{3,2,1,0:T(8,128)(2,1)S(1)} %get-tuple-element.127), channel_id=1, source_target_pairs={{0,15},{1,0},{2,1},{3,2},{4,3},{5,4},{6,5},{7,6},{8,7},{9,8},{10,9... | collective-permute-start | bytes 393224 | tf_op jit(solution)/shard_map/ppermute | solution.py:22
  12.3 7.9 %collective-permute-start.2 = (bf16[2,8,64,128]{3,2,1,0:T(8,128)(2,1)S(1)}, bf16[2,8,64,128]{3,2,1,0:T(8,128)(2,1)S(1)}, u32[]{:S(2)}, u32[]{:S(2)}) collective-permute-start(bf16[2,8,64,128]{3,2,1,0:T(8,128)(2,1)S(1)} %get-tuple-element.64), channel_id=1, source_target_pairs={{0,16},{16,32},{32,48},{48,64},{64,80},{80,96},{96,112},{112,0},{1... | collective-permute-start | bytes 786440 | tf_op jit(solution)/shard_map/ppermute | solution.py:22
  20.4 18.3 %collective-permute-start.15 = (bf16[4,27,8,128]{3,2,1,0:T(8,128)(2,1)S(1)}, bf16[4,27,8,128]{3,2,1,0:T(8,128)(2,1)S(1)}, u32[]{:S(2)}, u32[]{:S(2)}) collective-permute-start(bf16[4,27,8,128]{3,2,1,0:T(8,128)(2,1)S(1)} %gather_kernel.2.piece_0), channel_id=1, source_target_pairs={{0,1},{1,2},{2,3},{3,0},{4,5},{5,6},{6,7},{7,4},{8,9},{9,10},{10,1... | collective-permute-start | bytes 663560 | tf_op jit(solution)/shard_map/ppermute | solution.py:30
  20.8 17.9 %collective-permute-start.16 = (bf16[4,27,8,128]{3,2,1,0:T(8,128)(2,1)S(1)}, bf16[4,27,8,128]{3,2,1,0:T(8,128)(2,1)S(1)}, u32[]{:S(2)}, u32[]{:S(2)}) collective-permute-start(bf16[4,27,8,128]{3,2,1,0:T(8,128)(2,1)S(1)} %gather_kernel.2.piece_0), channel_id=1, source_target_pairs={{0,2},{1,3},{2,0},{3,1},{4,6},{5,7},{6,4},{7,5},{8,10},{9,11},{10,... | collective-permute-start | bytes 663560 | tf_op jit(solution)/shard_map/ppermute | solution.py:30
  25.6 13.2 %collective-permute-start.17 = (bf16[4,27,8,128]{3,2,1,0:T(8,128)(2,1)S(1)}, bf16[4,27,8,128]{3,2,1,0:T(8,128)(2,1)S(1)}, u32[]{:S(2)}, u32[]{:S(2)}) collective-permute-start(bf16[4,27,8,128]{3,2,1,0:T(8,128)(2,1)S(1)} %gather_kernel.2.piece_0), channel_id=1, source_target_pairs={{0,3},{1,0},{2,1},{3,2},{4,7},{5,4},{6,5},{7,6},{8,11},{9,8},{10,9... | collective-permute-start | bytes 663560 | tf_op jit(solution)/shard_map/ppermute | solution.py:30
  39.0 15.6 %collective-permute-start.18 = (bf16[27,16,8,128]{3,2,1,0:T(8,128)(2,1)S(1)}, bf16[27,16,8,128]{3,2,1,0:T(8,128)(2,1)S(1)}, u32[]{:S(2)}, u32[]{:S(2)}) collective-permute-start(bf16[27,16,8,128]{3,2,1,0:T(8,128)(2,1)S(1)} %bitcast.44), channel_id=1, source_target_pairs={{0,16},{16,0},{1,17},{17,1},{2,18},{18,2},{3,19},{19,3},{4,20},{20... | collective-permute-start | bytes 2654216 | tf_op jit(solution)/shard_map/ppermute | solution.py:26
  44.1 6.9 %collective-permute-start.8 = (bf16[2,1,32,256]{3,2,1,0:T(8,128)(2,1)S(1)}, bf16[2,1,32,256]{3,2,1,0:T(8,128)(2,1)S(1)}, u32[]{:S(2)}, u32[]{:S(2)}) collective-permute-start(bf16[2,1,32,256]{3,2,1,0:T(8,128)(2,1)S(1)} %get-tuple-element.140), channel_id=1, source_target_pairs={{0,1},{1,2},{2,3},{3,4},{4,5},{5,6},{6,7},{7,8},{8,9},{9,10},{10,1... | collective-permute-start | bytes 98312 | tf_op jit(solution)/shard_map/ppermute | solution.py:22
  60.3 7.4 %collective-permute-start.19 = (bf16[4,2,64,128]{3,2,1,0:T(8,128)(2,1)S(1)}, bf16[4,2,64,128]{3,2,1,0:T(8,128)(2,1)S(1)}, u32[]{:S(2)}, u32[]{:S(2)}) collective-permute-start(bf16[4,2,64,128]{3,2,1,0:T(8,128)(2,1)S(1)} %get-tuple-element.85), channel_id=1, source_target_pairs={{0,1},{1,2},{2,3},{3,4},{4,5},{5,6},{6,7},{7,8},{8,9},{9,10},{10,1... | collective-permute-start | bytes 393224 | tf_op jit(solution)/shard_map/ppermute | solution.py:22
  60.3 7.4 %collective-permute-start.20 = (bf16[4,2,64,128]{3,2,1,0:T(8,128)(2,1)S(1)}, bf16[4,2,64,128]{3,2,1,0:T(8,128)(2,1)S(1)}, u32[]{:S(2)}, u32[]{:S(2)}) collective-permute-start(bf16[4,2,64,128]{3,2,1,0:T(8,128)(2,1)S(1)} %get-tuple-element.86), channel_id=1, source_target_pairs={{0,15},{1,0},{2,1},{3,2},{4,3},{5,4},{6,5},{7,6},{8,7},{9,8},{10,9... | collective-permute-start | bytes 393224 | tf_op jit(solution)/shard_map/ppermute | solution.py:22
  67.8 9.6 %collective-permute-start.21 = (bf16[2,8,64,128]{3,2,1,0:T(8,128)(2,1)S(1)}, bf16[2,8,64,128]{3,2,1,0:T(8,128)(2,1)S(1)}, u32[]{:S(2)}, u32[]{:S(2)}) collective-permute-start(bf16[2,8,64,128]{3,2,1,0:T(8,128)(2,1)S(1)} %pad_maximum_fusion.3), channel_id=1, source_target_pairs={{0,16},{16,32},{32,48},{48,64},{64,80},{80,96},{96,112},{112,0},{1... | collective-permute-start | bytes 786440 | tf_op jit(solution)/shard_map/ppermute | solution.py:22
  69.3 8.0 %collective-permute-start.22 = (bf16[2,8,64,128]{3,2,1,0:T(8,128)(2,1)S(1)}, bf16[2,8,64,128]{3,2,1,0:T(8,128)(2,1)S(1)}, u32[]{:S(2)}, u32[]{:S(2)}) collective-permute-start(bf16[2,8,64,128]{3,2,1,0:T(8,128)(2,1)S(1)} %pad_maximum_fusion.2), channel_id=1, source_target_pairs={{0,112},{16,0},{32,16},{48,32},{64,48},{80,64},{96,80},{112,96},{1... | collective-permute-start | bytes 786440 | tf_op jit(solution)/shard_map/ppermute | solution.py:22
  74.3 23.2 %collective-permute-start.23 = (bf16[6,6,64,128]{3,2,1,0:T(8,128)(2,1)S(1)}, bf16[6,6,64,128]{3,2,1,0:T(8,128)(2,1)S(1)}, u32[]{:S(2)}, u32[]{:S(2)}) collective-permute-start(bf16[6,6,64,128]{3,2,1,0:T(8,128)(2,1)S(1)} %get-tuple-element.91), channel_id=1, source_target_pairs={{0,16},{16,0},{1,17},{17,1},{2,18},{18,2},{3,19},{19,3},{4,20},{20... | collective-permute-start | bytes 1769480 | tf_op jit(solution)/shard_map/ppermute | solution.py:26
  82.4 15.1 %collective-permute-start.24 = (bf16[4,4,64,128]{3,2,1,0:T(8,128)(2,1)S(1)}, bf16[4,4,64,128]{3,2,1,0:T(8,128)(2,1)S(1)}, u32[]{:S(2)}, u32[]{:S(2)}) collective-permute-start(bf16[4,4,64,128]{3,2,1,0:T(8,128)(2,1)S(1)} %get-tuple-element.92), channel_id=1, source_target_pairs={{0,16},{16,0},{1,17},{17,1},{2,18},{18,2},{3,19},{19,3},{4,20},{20... | collective-permute-start | bytes 786440 | tf_op jit(solution)/shard_map/ppermute | solution.py:26
  83.4 8.4 %collective-permute-start.26 = (bf16[16,56,128]{2,1,0:T(8,128)(2,1)S(1)}, bf16[16,56,128]{2,1,0:T(8,128)(2,1)S(1)}, u32[]{:S(2)}, u32[]{:S(2)}) collective-permute-start(bf16[16,56,128]{2,1,0:T(8,128)(2,1)S(1)} %get-tuple-element.121), channel_id=1, source_target_pairs={{0,32},{32,64},{64,96},{96,0},{1,33},{33,65},{65,97},{97,1},{2,34}... | collective-permute-start | bytes 688136 | tf_op jit(solution)/shard_map/ppermute | solution.py:30
  83.5 13.8 %collective-permute-start.27 = (bf16[16,56,128]{2,1,0:T(8,128)(2,1)S(1)}, bf16[16,56,128]{2,1,0:T(8,128)(2,1)S(1)}, u32[]{:S(2)}, u32[]{:S(2)}) collective-permute-start(bf16[16,56,128]{2,1,0:T(8,128)(2,1)S(1)} %get-tuple-element.120), channel_id=1, source_target_pairs={{0,64},{32,96},{64,0},{96,32},{1,65},{33,97},{65,1},{97,33},{2,66}... | collective-permute-start | bytes 688136 | tf_op jit(solution)/shard_map/ppermute | solution.py:30
  87.2 10.1 %collective-permute-start.28 = (bf16[16,56,128]{2,1,0:T(8,128)(2,1)S(1)}, bf16[16,56,128]{2,1,0:T(8,128)(2,1)S(1)}, u32[]{:S(2)}, u32[]{:S(2)}) collective-permute-start(bf16[16,56,128]{2,1,0:T(8,128)(2,1)S(1)} %get-tuple-element.119), channel_id=1, source_target_pairs={{0,96},{32,0},{64,32},{96,64},{1,97},{33,1},{65,33},{97,65},{2,98}... | collective-permute-start | bytes 688136 | tf_op jit(solution)/shard_map/ppermute | solution.py:30
  100.6 33.3 %all-to-all-start = ((bf16[64,56,128]{2,1,0:T(8,128)(2,1)}), bf16[64,56,128]{2,1,0:T(8,128)(2,1)S(1)}, u32[]{:S(2)}, u32[]{:S(2)}) async-start(bf16[64,56,128]{2,1,0:T(8,128)(2,1)} %bitcast.47), calls=%async_computation | async-start | bytes 1835008 | tf_op jit(solution)/shard_map/all_to_all | solution.py:444
  111.6 14.2 %collective-permute-start.30 = (bf16[4,56,128]{2,1,0:T(8,128)(2,1)S(1)}, bf16[4,56,128]{2,1,0:T(8,128)(2,1)S(1)}, u32[]{:S(2)}, u32[]{:S(2)}) collective-permute-start(bf16[4,56,128]{2,1,0:T(8,128)(2,1)S(1)} %get-tuple-element.107), channel_id=1, source_target_pairs={{0,8},{4,12},{8,0},{12,4},{1,9},{5,13},{9,1},{13,5},{2,10},{6,14},... | collective-permute-start | bytes 172040 | tf_op jit(solution)/shard_map/ppermute | solution.py:30
  114.0 11.9 %collective-permute-start.31 = (bf16[4,56,128]{2,1,0:T(8,128)(2,1)S(1)}, bf16[4,56,128]{2,1,0:T(8,128)(2,1)S(1)}, u32[]{:S(2)}, u32[]{:S(2)}) collective-permute-start(bf16[4,56,128]{2,1,0:T(8,128)(2,1)S(1)} %get-tuple-element.108), channel_id=1, source_target_pairs={{0,12},{4,0},{8,4},{12,8},{1,13},{5,1},{9,5},{13,9},{2,14},{6,2},{... | collective-permute-start | bytes 172040 | tf_op jit(solution)/shard_map/ppermute | solution.py:30
  126.0 7.9 %collective-permute-start.32 = (bf16[1,56,128]{2,1,0:T(8,128)(2,1)S(1)}, bf16[1,56,128]{2,1,0:T(8,128)(2,1)S(1)}, u32[]{:S(2)}, u32[]{:S(2)}) collective-permute-start(bf16[1,56,128]{2,1,0:T(8,128)(2,1)S(1)} %get-tuple-element.110), channel_id=1, source_target_pairs={{0,1},{1,2},{2,3},{3,0},{4,5},{5,6},{6,7},{7,4},{8,9},{9,10},{10,1... | collective-permute-start | bytes 43016 | tf_op jit(solution)/shard_map/ppermute | solution.py:30
  135.1 22.1 %all-to-all-start.1 = ((bf16[64,56,128]{2,1,0:T(8,128)(2,1)}), bf16[64,56,128]{2,1,0:T(8,128)(2,1)S(1)}, u32[]{:S(2)}, u32[]{:S(2)}) async-start(bf16[64,56,128]{2,1,0:T(8,128)(2,1)} %sum_kernel.1), calls=%async_computation.1 | async-start | bytes 1835008 | tf_op jit(solution)/shard_map/all_to_all | solution.py:454
  145.2 9.2 %collective-permute-start.36 = (bf16[2,56,128]{2,1,0:T(8,128)(2,1)S(1)}, bf16[2,56,128]{2,1,0:T(8,128)(2,1)S(1)}, u32[]{:S(2)}, u32[]{:S(2)}) collective-permute-start(bf16[2,56,128]{2,1,0:T(8,128)(2,1)S(1)} %maximum_select_fusion.1.pair_0), channel_id=1, source_target_pairs={{0,32},{32,64},{64,96},{96,0},{1,33},{33,65},{65,97},{97,1},{2,34}... | collective-permute-start | bytes 86024 | tf_op jit(solution)/shard_map/ppermute | solution.py:30
  146.6 7.8 %collective-permute-start.37 = (bf16[2,56,128]{2,1,0:T(8,128)(2,1)S(1)}, bf16[2,56,128]{2,1,0:T(8,128)(2,1)S(1)}, u32[]{:S(2)}, u32[]{:S(2)}) collective-permute-start(bf16[2,56,128]{2,1,0:T(8,128)(2,1)S(1)} %maximum_select_fusion.1.pair_0), channel_id=1, source_target_pairs={{0,64},{32,96},{64,0},{96,32},{1,65},{33,97},{65,1},{97,33},{2,66}... | collective-permute-start | bytes 86024 | tf_op jit(solution)/shard_map/ppermute | solution.py:30
  (29 other events, 237.8 us)

commit v6 on v4

--- a/solution.py
+++ b/solution.py
@@ -26,15 +26,45 @@
     return lax.ppermute(array, "c", [(0, 1), (1, 0)])
 
 
-def halo_pieces(own, width, first=None, last=None):
-    before = shifted(own[:, -width:] if last is None else last, GY, 1)
-    after = shifted(own[:, :width] if first is None else first, GY, -1)
-    low = jnp.concatenate([before[:width], own[:width], after[:width]], axis=1)
-    high = jnp.concatenate([before[-width:], own[-width:], after[-width:]], axis=1)
-    low, high = lax.optimization_barrier((low, high))
-    left = shifted(high, GX, 1)
-    right = shifted(low, GX, -1)
-    return (own, before, after, left, right), high
+def ring_pieces(pieces, axis):
+    sent = [lax.ppermute(pieces[d], axis, [(i, (i + d) % 4) for i in range(4)]) for d in (1, 2, 3)]
+    return [pieces[0]] + sent
+
+
+def slab_kernel(own, before, after, low, high):
+    width, size_x = low.shape[0], own.shape[0]
+    for slab, start in ((low, 0), (high, size_x - width)):
+        rows = slice(start, start + width)
+        columns = 0
+        for part in (before, own, after):
+            slab[:, columns : columns + part.shape[1]] = part[rows]
+            columns += part.shape[1]
+
+
+def first_slab_kernel(own, before, after, grads, low, high):
+    for slab, start, row in ((low, 0, 0), (high, 2, 1)):
+        for at in range(2):
+            slab[at * 8 : at * 8 + 2] = before[start + at]
+            slab[at * 8 + 2 : at * 8 + 6] = own[start + at]
+            slab[at * 8 + 6 : at * 8 + 8] = after[start + at]
+        slab[16] = before[4, row]
+        slab[19] = after[4, row]
+        for at_y in range(2):
+            for half in range(2):
+                part = grads[row, at_y, :, half * 128 : half * 128 + 128]
+                slab[17 + at_y, half * 32 : half * 32 + 32] = part
+
+
+def exchange_x(low, high):
+    return shifted(high, GX, 1), shifted(low, GX, -1)
+
+
+def halo_pieces(own, width, first, last):
+    before, after = shifted(last, GY, 1), shifted(first, GY, -1)
+    size_x, size_y, size_z, chans = own.shape
+    slab = (width, size_y + 2 * width, size_z, chans)
+    low, high = call(slab_kernel, [(slab, BF16)] * 2, [], 0, own, before, after)
+    return (own, before, after, *exchange_x(low, high)), high
 
 
 def fill_padded(padded, own, before, after, left, right):
@@ -112,7 +142,12 @@
 def forward_kernel(core, own, before, after, left, right, taps_one, taps_two,
                    field_keep, field_send, slope_one, slope_two, pooled,
                    padded, packed, act_one, halves):
-    fill_padded(padded, own, before, after, left, right)
+    for at in range(2):
+        padded[at] = left[at * 8 : at * 8 + 8]
+        padded[6 + at] = right[at * 8 : at * 8 + 8]
+    padded[2:6, 0:2] = before[0:4]
+    padded[2:6, 2:6] = own[...]
+    padded[2:6, 6:8] = after[0:4]
     fill_forward(packed, taps_one)
     first_core = core[0] == 0
 
@@ -124,7 +159,7 @@
         act_one[row] = act
         field_keep[row] = jnp.where(first_core, field, act)
         field_send[row] = jnp.where(first_core, act, field)
-        slope_one[row] = slope
+        slope_one[row] = slope.astype(BF16)
         return 0
 
     lax.fori_loop(0, 6, first, 0)
@@ -133,7 +168,7 @@
     def second(row, _):
         product = dot_nn(window_rows(act_one, row, 4), packed[...])
         act, slope = slope_and_silu(join_taps(product, 4, 64, 128))
-        slope_two[row] = slope
+        slope_two[row] = slope.astype(BF16)
         act = act.astype(BF16).astype(F32)
         halves[row] = act.reshape(2, 2, 64, 128).sum(axis=1)
         return 0
@@ -148,11 +183,18 @@
             pooled[at_x, at_y] = (total * 0.125).astype(BF16)
 
 
-def bottom_kernel(own, before, after, left, right, g_own, g_before, g_after, g_left, g_right,
+def bottom_kernel(own, before, after, left, right, g_own, f_before, f_after, f_left, f_right,
                   taps_three, slope_two, skip, bottleneck, bundle, err_two, err_first, err_last,
                   padded, grads, packed, errors, wide):
     fill_padded(padded, own, before, after, left, right)
-    fill_padded(grads, g_own, g_before, g_after, g_left, g_right)
+    for half in range(2):
+        rows, lanes = slice(half * 32, half * 32 + 32), slice(half * 128, half * 128 + 128)
+        grads[0, :, :, lanes] = f_left[16:20, rows]
+        grads[3, :, :, lanes] = f_right[16:20, rows]
+        for at in range(2):
+            grads[1 + at, 0, :, lanes] = f_before[4, at, rows]
+            grads[1 + at, 3, :, lanes] = f_after[4, at, rows]
+    grads[1:3, 1:3] = g_own[...]
     for at in range(9):
         for kz in range(3):
             packed[kz * 256 : kz * 256 + 256, at * 128 : at * 128 + 128] = taps_three[at * 3 + kz]
@@ -186,7 +228,8 @@
             for dx in range(2):
                 for dy in range(2):
                     at = (2 * row + dx, 2 * at_y + dy)
-                    err = ((skip[at].astype(F32) + wide[...]) * slope_two[at]).astype(BF16)
+                    err = skip[at].astype(F32) + wide[...]
+                    err = (err * slope_two[at].astype(F32)).astype(BF16)
                     err_two[at] = err
                     edge = err_first if at_y == 0 else err_last
                     edge[2 * row + dx, dy] = err
@@ -205,16 +248,22 @@
     add_tap_grads(total, fields, errors)
 
 
-def pair_grads_kernel(fields, errors, own_total, out, total):
+def pair_grads_kernel(fields, errors, own_total, three, out, total):
     total[...] = own_total[...]
     add_tap_grads(total, fields, errors)
     for at in range(9):
         for kz in range(3):
-            rows = (at * 3 + kz) * 128
-            out[rows : rows + 128] = total[
-                at * 128 : at * 128 + 128, kz * 128 : kz * 128 + 128
-            ].astype(BF16)
-    out[3456:3584] = jnp.zeros((128, 128), BF16)
+            start = (at * 3 + kz) * 128
+            done = 0
+            while done < 128:
+                piece, row = divmod(start + done, PIECE)
+                size = min(PIECE - row, 128 - done)
+                rows = slice(at * 128 + done, at * 128 + done + size)
+                out[piece, row : row + size] = total[rows, kz * 128 : kz * 128 + 128].astype(BF16)
+                done += size
+    out[61, 40:PIECE] = jnp.zeros((PIECE - 40, 128), BF16)
+    out[62:64, 0:PIECE] = jnp.zeros((2, PIECE, 128), BF16)
+    out[:, PIECE : 2 * PIECE] = three[...]
 
 
 def bottom_grads_kernel(core, own, other, out, total):
@@ -247,7 +296,7 @@
         out[at_x * 16 : at_x * 16 + 16, rows : rows + 8] = block
 
 
-def first_errors_kernel(core, own, before, after, left, right, taps_two, slope_one, token,
+def first_errors_kernel(core, own, before, after, left, right, taps_two, slope_one,
                         err_one, err_keep, err_send, padded, packed):
     fill_padded(padded, own, before, after, left, right)
     fill_backward(packed, taps_two)
@@ -255,7 +304,7 @@
     def step(row, _):
         product = dot_nt(window_rows(padded, row, 6), packed[...])
         back = join_taps(product, 6, 64, 128)
-        err_one[row] = (back * slope_one[row]).astype(BF16)
+        err_one[row] = (back * slope_one[row].astype(F32)).astype(BF16)
         return 0
 
     lax.fori_loop(0, 6, step, 0)
@@ -277,13 +326,14 @@
     lax.fori_loop(0, 4, step, 0)
 
 
-def sum_kernel(pieces, out):
+def sum_kernel(pieces, out, three):
     total = pieces[0].astype(F32)
     for at in range(1, 64):
         total = total + pieces[at].astype(F32)
     total = total.astype(BF16)
-    for at in range(out.shape[0]):
-        out[at] = total
+    three[...] = total[PIECE : 2 * PIECE]
+    for at in range(64):
+        out[at] = total[0:PIECE]
 
 
 def place_kernel(chip, pair_0, pair_1, pair_2, pair_3, out, *, scale):
@@ -332,99 +382,89 @@
     )(*operands)
 
 
-def pick(stacked, index):
-    return lax.dynamic_index_in_dim(stacked, index, 0, keepdims=False)
-
-
-def after(array, *others):
-    return lax.optimization_barrier((array, *others))[0]
-
-
 def on_device(features, skip_grad, bottom_grad, conv_one, conv_two, conv_three):
     core = lax.axis_index("c")
+    first = jnp.concatenate([bottom_grad[:, :1, :, :128], bottom_grad[:, :1, :, 128:]], axis=2)
+    last = jnp.concatenate([bottom_grad[:, 1:, :, :128], bottom_grad[:, 1:, :, 128:]], axis=2)
+    first = jnp.concatenate([features[:, :2], first.reshape(1, 2, 64, 128)], axis=0)
+    last = jnp.concatenate([features[:, -2:], last.reshape(1, 2, 64, 128)], axis=0)
+    first, last, first_core, core_ref, chip = lax.optimization_barrier(
+        (first, last, core == 0, core.reshape(1), lax.axis_index("x").reshape(1))
+    )
     fine_cells = features.size // 128 * lax.axis_size(GX) * lax.axis_size(GY)
     fine_scale = 1.0 / math.sqrt(fine_cells)
     coarse_scale = 1.0 / math.sqrt(fine_cells // 8)
     taps_one = conv_one.reshape(27, 128, 128)
     taps_two = conv_two.reshape(27, 128, 128)
-
-    f_pieces, _ = halo_pieces(features, 2)
-
-    own_taps = jnp.swapaxes(conv_three.reshape(27, 128, 16), 1, 2)
-    half_taps = pick(jnp.swapaxes(own_taps.reshape(27, 2, 8, 128), 0, 1), core)
-    half_taps = jnp.broadcast_to(half_taps, (16, 27, 8, 128))
-    mine = lax.all_to_all(half_taps, GY, 0, 0)
-    g_pieces, _ = halo_pieces(after(bottom_grad, f_pieces[1], f_pieces[2]), 1)
+    taps_three = jnp.swapaxes(conv_three.reshape(27, 128, 16), 1, 2)
+    taps_three = lax.all_gather(taps_three, GY, axis=1, tiled=True)
+
+    f_before, f_after = shifted(last, GY, 1), shifted(first, GY, -1)
+    low, high = call(
+        first_slab_kernel, [((20, 64, 128), BF16)] * 2, [], 0, features, f_before, f_after, bottom_grad
+    )
+    f_left, f_right = exchange_x(low, high)
 
     conv_flops = 2 * 1152 * 128 * 1024 * 3
-    core_ref = core.reshape(1)
     field = (6, 6, 64, 128)
     block = (4, 4, 64, 128)
+    edge = (4, 2, 64, 128)
     field_keep, field_send, slope_one, slope_two, pooled = call(
         forward_kernel,
-        [(field, BF16, True), (field, BF16, True), (field, F32, True), (block, F32, True), ((2, 2, 32, 128), BF16)],
+        [(field, BF16, True), (field, BF16, True), (field, BF16, True), (block, BF16, True), ((2, 2, 32, 128), BF16)],
         [((8, 8, 64, 128), BF16), ((1152, 384), BF16), (field, BF16), ((4, 2, 64, 128), F32)],
-        3 * conv_flops, core_ref, *f_pieces, taps_one, taps_two,
+        3 * conv_flops, core_ref, features, f_before, f_after, f_left, f_right, taps_one, taps_two,
     )
     field_other = swap_cores(field_send)
-    p_pieces, _ = halo_pieces(pooled, 2)
-    mine = after(mine, pooled)
-    theirs = swap_cores(mine)
-    both = jnp.where(core == 0, jnp.stack([mine, theirs]), jnp.stack([theirs, mine]))
-    taps_three = jnp.transpose(both, (2, 1, 0, 3, 4)).reshape(27, 256, 128)
-    edge = (4, 2, 64, 128)
+    p_pieces, _ = halo_pieces(pooled, 2, pooled, pooled)
     bottleneck, bundle, err_two, err_first, err_last = call(
         bottom_kernel,
-        [((2, 2, 32, 256), BF16, True), ((24, 32, 128), BF16), (block, BF16, True), (edge, BF16), (edge, BF16)],
+        [((2, 2, 32, 256), BF16, True), ((24, 32, 128), BF16), (block, BF16), (edge, BF16), (edge, BF16)],
         [((6, 6, 32, 128), BF16), ((4, 4, 32, 256), BF16), ((768, 1152), BF16),
          ((4, 4, 32, 256), BF16), ((64, 128), F32)],
-        conv_flops, *p_pieces, *g_pieces, taps_three, slope_two, skip_grad,
+        conv_flops, *p_pieces, bottom_grad, f_before, f_after, f_left, f_right,
+        in_hbm(taps_three), in_hbm(slope_two), in_hbm(skip_grad),
     )
     e_pieces, e_high = halo_pieces(err_two, 2, err_first, err_last)
-    token = swap_cores(e_high[0, 0, :8])
-
+    bundle, e_high = lax.optimization_barrier((bundle, e_high))
     (three,) = call(
-        bottom_grads_kernel, [((64, PIECE, 128), BF16, True)], [((768, 1152), F32)],
+        bottom_grads_kernel, [((64, PIECE, 128), BF16)], [((768, 1152), F32)],
         conv_flops // 2, core_ref, bundle, swap_cores(bundle),
     )
-    three, token = lax.optimization_barrier((three, token))
-    three_pieces = lax.all_to_all(three, FLAT, 0, 0)
-
+    three, *e_ends = lax.optimization_barrier((three, *e_pieces[3:]))
     err_one, err_keep, err_send = call(
         first_errors_kernel, [(field, BF16, True), (block, BF16), (block, BF16)],
         [((8, 8, 64, 128), BF16), ((384, 1152), BF16)],
-        2 * conv_flops, core_ref, *[in_hbm(e) for e in e_pieces[:3]], *e_pieces[3:],
-        in_hbm(taps_two), in_hbm(slope_one), token,
+        2 * conv_flops, core_ref, *e_pieces[:3], *e_ends, taps_two, slope_one,
     )
     err_other = swap_cores(err_send)
-    (total,) = call(own_grads_kernel, [((1152, 384), F32)], [], conv_flops, in_hbm(field_keep), err_keep)
+    (total,) = call(own_grads_kernel, [((1152, 384), F32)], [], conv_flops, field_keep, err_keep)
     (kept,) = call(
-        pair_grads_kernel, [((3584, 128), BF16, True)], [((1152, 384), F32)],
-        conv_flops, field_other, err_other, total,
-    )
-    kept = after(kept, three_pieces).reshape(64, PIECE, 128)
-    (part,) = call(
-        sum_kernel, [((64, PIECE, 128), BF16, True)], [], 0, lax.all_to_all(kept, FLAT, 0, 0)
-    )
-    (three_part,) = call(sum_kernel, [((1, PIECE, 128), BF16)], [], 0, three_pieces)
-    three_part = three_part[0]
+        pair_grads_kernel, [((64, 2 * PIECE, 128), BF16, True)], [((1152, 384), F32)],
+        conv_flops, field_other, err_other, total, three,
+    )
+    part, three_part = call(
+        sum_kernel, [((64, PIECE, 128), BF16, True), ((PIECE, 128), BF16)], [], 0,
+        lax.all_to_all(kept, FLAT, 0, 0),
+    )
+    (input_grad,) = call(
+        input_kernel, [(block, BF16, True)], [((384, 1152), BF16)],
+        conv_flops, err_one, taps_one,
+    )
+    part, input_grad = lax.optimization_barrier((part, input_grad))
+    whole = lax.all_to_all(part, FLAT, 0, 0).reshape(64 * PIECE, 128)
     both = swap_cores(three_part)
-    both = jnp.where(core == 0, jnp.stack([three_part, both]), jnp.stack([both, three_part]))
-    pairs = [both] + [lax.ppermute(both, "x", [(i, (i + d) % 4) for i in range(4)]) for d in (1, 2, 3)]
+    both = jnp.where(first_core, jnp.stack([three_part, both]), jnp.stack([both, three_part]))
     grad_three = pl.pallas_call(
         functools.partial(place_kernel, scale=coarse_scale),
         out_shape=jax.ShapeDtypeStruct((27, 16, 128), F32),
         in_specs=[pl.BlockSpec(memory_space=pltpu.SMEM)] + [pl.BlockSpec(memory_space=pltpu.VMEM)] * 4,
         out_specs=pl.BlockSpec(memory_space=pltpu.VMEM),
+        compiler_params=pltpu.CompilerParams(vmem_limit_bytes=8 << 20),
         name="place_kernel",
-    )(lax.axis_index("x").reshape(1), *pairs)
+    )(chip, *ring_pieces([both] * 4, "x"))
+    whole, grad_three = lax.optimization_barrier((whole, grad_three))
     grad_three = jnp.swapaxes(grad_three, 1, 2).reshape(3, 3, 3, 128, 16)
-    (input_grad,) = call(
-        input_kernel, [(block, BF16, True)], [((384, 1152), BF16)],
-        conv_flops, in_hbm(err_one), in_hbm(taps_one),
-    )
-    part = after(part, input_grad, grad_three)
-    whole = lax.all_to_all(part, FLAT, 0, 0).reshape(64 * PIECE, 128)
     grad_one, grad_two = pl.pallas_call(
         functools.partial(finish_kernel, scale=fine_scale),
         out_shape=[jax.ShapeDtypeStruct((3456, 128), F32)] * 2,
@@ -432,10 +472,9 @@
         out_specs=[pl.BlockSpec(memory_space=pltpu.VMEM)] * 2,
         compiler_params=pltpu.CompilerParams(vmem_limit_bytes=8 << 20),
         name="finish_kernel",
-    )(core.reshape(1), whole, swap_cores(whole))
+    )(core_ref, whole, swap_cores(whole))
     grad_one = grad_one.reshape(3, 3, 3, 128, 128)
     grad_two = grad_two.reshape(3, 3, 3, 128, 128)
-
     return (bottleneck, input_grad, grad_one, grad_two, grad_three)
 
 

time: 167 us -> 163 us (0.976)
  waiting for transfers between devices: 30.9 us -> 62.3 us
  blocking collectives: 23 us -> 0 us
  starting transfers between devices: 67.3 us -> 51.2 us
  between operations: 0.94 us -> 14.2 us
  Pallas kernels: 36.9 us -> 31.8 us
  other arithmetic: 2.58 us -> 0.05 us
    all_to_all x1 -> x0, blocking collectives: 23 us -> none  [on_device(): whole = lax.all_to_all(part, FLAT, 0, 0).reshape(64 * PIECE, 128)]
    all_to_all x1, waiting for transfers between devices: 0.01 us -> 22.9 us  [on_device(): lax.all_to_all(kept, FLAT, 0, 0)]
    all_to_all x2 -> x1, starting transfers between devices: 15.8 us -> 5.8 us  [on_device(): whole = lax.all_to_all(part, FLAT, 0, 0).reshape(64 * PIECE, 128)]
    ppermute x16 -> x12, starting transfers between devices: 30.1 us -> 23.6 us  [shifted(): lax.ppermute(array, axes, [(i, (i + step) % count) for i in range(count)])]
    pallas_call x9 -> x11, Pallas kernels: 33.3 us -> 29.1 us  [call(): pl.pallas_call(kernel, out_shape=shapes, in_specs=[pl.BlockSpec(memory_sp...]
    all_gather x0 -> x1, waiting for transfers between devices: none -> 3.59 us  [on_device(): taps_three = lax.all_gather(taps_three, GY, axis=1, tiled=True)]
    ppermute x3, waiting for transfers between devices: 3.52 us -> 6.22 us  [ring_pieces(): lax.ppermute(pieces[d], axis, [(i, (i + d) % 4) for i in range(4)])]
    transpose x1 -> x0, other arithmetic: 1.71 us -> none  [on_device(): taps_three = jnp.transpose(both, (2, 1, 0, 3, 4)).reshape(27, 256, 128)]
  transfers between devices with their start and end apart: 29 -> 23, of which waited for: 11 -> 18; matrix products, arithmetic and copies ran while one was open for 3% -> 1% of each run, Pallas kernels for 18% -> 13%
where the time goes in v6:
time: 163 us; the launch traced here: 162 us
  waiting for transfers between devices  62.3 us (38%)
  starting transfers between devices  51.2 us (31%)
  Pallas kernels  31.8 us (20%)
  between operations  14.2 us (9%)
  local copies, waits for them, and re-layouts  2.65 us (2%)
    pallas_call x11, Pallas kernels, call(): pl.pallas_call(kernel, out_shape=shapes, in_specs=[pl.BlockSpec(memory_sp...  29.1 us
    ppermute x12, starting transfers between devices, shifted(): lax.ppermute(array, axes, [(i, (i + step) % count) for i in range(count)])  23.6 us
    ppermute x12, waiting for transfers between devices, shifted(): lax.ppermute(array, axes, [(i, (i + step) % count) for i in range(count)])  23.1 us
    all_to_all x1, waiting for transfers between devices, on_device(): lax.all_to_all(kept, FLAT, 0, 0)  22.9 us
    ppermute x5, starting transfers between devices, swap_cores(): return lax.ppermute(array, 'c', [(0, 1), (1, 0)])  9.44 us
    all_to_all x1, starting transfers between devices, on_device(): lax.all_to_all(kept, FLAT, 0, 0)  8.59 us
    ppermute x3, waiting for transfers between devices, ring_pieces(): lax.ppermute(pieces[d], axis, [(i, (i + d) % 4) for i in range(4)])  6.22 us
    all_to_all x1, starting transfers between devices, on_device(): whole = lax.all_to_all(part, FLAT, 0, 0).reshape(64 * PIECE, 128)  5.8 us
  transfers between devices with their start and end apart: 23, of which 18 were waited for; matrix products, arithmetic and copies ran while one was open for 1% of the time, Pallas kernels for 13%

profile of v6, /device:TPU:1, one launch (start us, length us, event | category | flops | bytes accessed | tf_op | source)
XLA Modules:
  0.0 162.3 jit_solution(17727127060181834819)
XLA Ops:
  9.8 2.2 %collective-permute-start = (bf16[5,2,64,128]{3,2,1,0:T(8,128)(2,1)S(1)}, bf16[5,2,64,128]{3,2,1,0:T(8,128)(2,1)S(1)}, u32[]{:S(2)}, u32[]{:S(2)}) collective-permute-start(bf16[5,2,64,128]{3,2,1,0:T(8,128)(2,1)S(1)} %pad_maximum_fusion.1), channel_id=1, source_target_pairs={{0,1},{1,2},{2,3},{3,4},{4,5},{5,6},{6,7},{7,8},{8,9},{9,10},{10,1... | collective-permute-start | bytes 491528 | tf_op jit(solution)/shard_map/ppermute | solution.py:22
  12.0 5.0 %collective-permute-start.1 = (bf16[5,2,64,128]{3,2,1,0:T(8,128)(2,1)S(1)}, bf16[5,2,64,128]{3,2,1,0:T(8,128)(2,1)S(1)}, u32[]{:S(2)}, u32[]{:S(2)}) collective-permute-start(bf16[5,2,64,128]{3,2,1,0:T(8,128)(2,1)S(1)} %pad_maximum_fusion), channel_id=1, source_target_pairs={{0,15},{1,0},{2,1},{3,2},{4,3},{5,4},{6,5},{7,6},{8,7},{9,8},{10,9... | collective-permute-start | bytes 491528 | tf_op jit(solution)/shard_map/ppermute | solution.py:22
  17.0 3.8 %collective-permute-done.before.f_before = bf16[5,2,64,128]{3,2,1,0:T(8,128)(2,1)S(1)} collective-permute-done((bf16[5,2,64,128]{3,2,1,0:T(8,128)(2,1)S(1)}, bf16[5,2,64,128]{3,2,1,0:T(8,128)(2,1)S(1)}, u32[]{:S(2)}, u32[]{:S(2)}) %collective-permute-start) | collective-permute-done | bytes 163872 | tf_op jit(solution)/shard_map/ppermute | solution.py:22
  21.7 2.3 %collective-permute-start.2 = (bf16[20,64,128]{2,1,0:T(8,128)(2,1)S(1)}, bf16[20,64,128]{2,1,0:T(8,128)(2,1)S(1)}, u32[]{:S(2)}, u32[]{:S(2)}) collective-permute-start(bf16[20,64,128]{2,1,0:T(8,128)(2,1)S(1)} %get-tuple-element.44), channel_id=1, source_target_pairs={{0,16},{16,32},{32,48},{48,64},{64,80},{80,96},{96,112},{112,0},{1... | collective-permute-start | bytes 983048 | tf_op jit(solution)/shard_map/ppermute | solution.py:22
  24.1 4.0 %collective-permute-done.2.left.f_left = bf16[20,64,128]{2,1,0:T(8,128)(2,1)S(1)} collective-permute-done((bf16[20,64,128]{2,1,0:T(8,128)(2,1)S(1)}, bf16[20,64,128]{2,1,0:T(8,128)(2,1)S(1)}, u32[]{:S(2)}, u32[]{:S(2)}) %collective-permute-start.2) | collective-permute-done | bytes 327712 | tf_op jit(solution)/shard_map/ppermute | solution.py:22
  28.1 2.9 %collective-permute-done.3.right.f_right = bf16[20,64,128]{2,1,0:T(8,128)(2,1)S(1)} collective-permute-done((bf16[20,64,128]{2,1,0:T(8,128)(2,1)S(1)}, bf16[20,64,128]{2,1,0:T(8,128)(2,1)S(1)}, u32[]{:S(2)}, u32[]{:S(2)}) %collective-permute-start.3) | collective-permute-done | bytes 327712 | tf_op jit(solution)/shard_map/ppermute | solution.py:22
  31.0 7.7 %forward_kernel.1 = (bf16[6,6,64,128]{3,2,1,0:T(8,128)(2,1)}, bf16[6,6,64,128]{3,2,1,0:T(8,128)(2,1)}, bf16[6,6,64,128]{3,2,1,0:T(8,128)(2,1)}, bf16[4,4,64,128]...) custom-call(s32[1]{0:T(128)} %bitcast.2.core, bf16[4,4,64,128]{3,2,1,0:T(8,128)(2,1)S(1)} %copy-done.2, ...), custom_call_target="tpu_custom_call" | custom-call | flops 135895456 | bytes 150733 | tf_op jit(solution)/shard_map/forward_kernel/pallas_call | solution.py:371
  38.6 4.9 %collective-permute-start.5 = (bf16[2,2,32,128]{3,2,1,0:T(8,128)(2,1)S(1)}, bf16[2,2,32,128]{3,2,1,0:T(8,128)(2,1)S(1)}, u32[]{:S(2)}, u32[]{:S(2)}) collective-permute-start(bf16[2,2,32,128]{3,2,1,0:T(8,128)(2,1)S(1)} %get-tuple-element.46.own), channel_id=1, source_target_pairs={{0,15},{1,0},{2,1},{3,2},{4,3},{5,4},{6,5},{7,6},{8,7},{9,8},{10,9... | collective-permute-start | bytes 98312 | tf_op jit(solution)/shard_map/ppermute | solution.py:22
  45.2 5.6 %collective-permute-done.4.before = bf16[2,2,32,128]{3,2,1,0:T(8,128)(2,1)S(1)} collective-permute-done((bf16[2,2,32,128]{3,2,1,0:T(8,128)(2,1)S(1)}, bf16[2,2,32,128]{3,2,1,0:T(8,128)(2,1)S(1)}, u32[]{:S(2)}, u32[]{:S(2)}) %collective-permute-start.4) | collective-permute-done | bytes 32800 | tf_op jit(solution)/shard_map/ppermute | solution.py:22
  52.4 2.8 %collective-permute-done.7.right = bf16[2,6,32,128]{3,2,1,0:T(8,128)(2,1)S(1)} collective-permute-done((bf16[2,6,32,128]{3,2,1,0:T(8,128)(2,1)S(1)}, bf16[2,6,32,128]{3,2,1,0:T(8,128)(2,1)S(1)}, u32[]{:S(2)}, u32[]{:S(2)}) %collective-permute-start.7) | collective-permute-done | bytes 98336 | tf_op jit(solution)/shard_map/ppermute | solution.py:22
  55.3 3.6 %all-gather.2.cloned.1.call-done.taps_three = bf16[27,256,128]{2,1,0:T(8,128)(2,1)} async-done(((bf16[27,16,128]{2,1,0:T(8,128)(2,1)}), bf16[27,256,128]{2,1,0:T(8,128)(2,1)}) %all-gather.2.cloned.1.call-update) | async-done | bytes 1769488 | tf_op jit(solution)/shard_map/all_gather | solution.py:400
  58.8 4.6 %bottom_kernel.1 = (bf16[2,2,32,256]{3,2,1,0:T(8,128)(2,1)}, bf16[24,32,128]{2,1,0:T(8,128)(2,1)S(1)}, bf16[4,4,64,128]{3,2,1,0:T(8,128)(2,1)S(1)}, bf16[4,2,64,...) custom-call(bf16[2,2,32,128]{3,2,1,0:T(8,128)(2,1)S(1)} %get-tuple-element.46.own, ...), custom_call_target="tpu_custom_call" | custom-call | flops 45298484 | bytes 181862 | tf_op jit(solution)/shard_map/bottom_kernel/pallas_call | solution.py:371
  64.4 3.9 %collective-permute-start.10 = (bf16[4,2,64,128]{3,2,1,0:T(8,128)(2,1)S(1)}, bf16[4,2,64,128]{3,2,1,0:T(8,128)(2,1)S(1)}, u32[]{:S(2)}, u32[]{:S(2)}) collective-permute-start(bf16[4,2,64,128]{3,2,1,0:T(8,128)(2,1)S(1)} %get-tuple-element.54), channel_id=1, source_target_pairs={{0,15},{1,0},{2,1},{3,2},{4,3},{5,4},{6,5},{7,6},{8,7},{9,8},{10,9... | collective-permute-start | bytes 393224 | tf_op jit(solution)/shard_map/ppermute | solution.py:22
  70.7 2.7 %collective-permute-start.13 = (bf16[2,8,64,128]{3,2,1,0:T(8,128)(2,1)S(1)}, bf16[2,8,64,128]{3,2,1,0:T(8,128)(2,1)S(1)}, u32[]{:S(2)}, u32[]{:S(2)}) collective-permute-start(bf16[2,8,64,128]{3,2,1,0:T(8,128)(2,1)S(1)} %get-tuple-element.58), channel_id=1, source_target_pairs={{0,112},{16,0},{32,16},{48,32},{64,48},{80,64},{96,80},{112,96},{1... | collective-permute-start | bytes 786440 | tf_op jit(solution)/shard_map/ppermute | solution.py:22
  78.9 5.0 %first_errors_kernel.1 = (bf16[6,6,64,128]{3,2,1,0:T(8,128)(2,1)}, bf16[4,4,64,128]{3,2,1,0:T(8,128)(2,1)S(1)}, bf16[4,4,64,128]{3,2,1,0:T(8,128)(2,1)S(1)}) custom-call(s32[1]{0:T(128)} %bitcast.2.core, bf16[4,4,64,128]{3,2,1,0:T(8,128)(2,1)S(1)} %get-tuple-element.52.own, bf16[4,2,64,128]{3,2,1,0:T(8,128)(2,1)S(1)} %collective-permute-done.9.before, ...), custom_call_target="tpu_custom_call" | custom-call | flops 90596968 | bytes 126157 | tf_op jit(solution)/shard_map/first_errors_kernel/pallas_call | solution.py:371
  85.6 2.1 %own_grads_kernel.1.own_total = f32[1152,384]{1,0:T(8,128)S(1)} custom-call(bf16[6,6,64,128]{3,2,1,0:T(8,128)(2,1)S(1)} %copy-done.5, bf16[4,4,64,128]{3,2,1,0:T(8,128)(2,1)S(1)} %get-tuple-element.64.errors), custom_call_target="tpu_custom_call" | custom-call | flops 45298484 | bytes 42598 | tf_op jit(solution)/shard_map/own_grads_kernel/pallas_call | solution.py:371
  87.7 3.5 %pair_grads_kernel.1 = bf16[64,112,128]{2,1,0:T(8,128)(2,1)} custom-call(bf16[6,6,64,128]{3,2,1,0:T(8,128)(2,1)S(1)} %collective-permute-done.8.fields, bf16[4,4,64,128]{3,2,1,0:T(8,128)(2,1)S(1)} %collective-permute-done.14.errors, f32[1152,384]{1,0:T(8,128)S(1)} %own_grads_kernel.1.own_total, bf16[64,56,128]{2,1,0:T(8,128)(2,1)S(1)} %bottom_grads_kernel.1.three), custom_call_target="tpu_custom_call" | custom-call | flops 45298484 | bytes 176947 | tf_op jit(solution)/shard_map/pair_grads_kernel/pallas_call | solution.py:371
  91.3 8.6 %all-to-all-start = ((bf16[64,112,128]{2,1,0:T(8,128)(2,1)}), bf16[64,112,128]{2,1,0:T(8,128)(2,1)S(1)}, u32[]{:S(2)}, u32[]{:S(2)}) async-start(bf16[64,112,128]{2,1,0:T(8,128)(2,1)} %pair_grads_kernel.1), calls=%async_computation | async-start | bytes 3670016 | tf_op jit(solution)/shard_map/all_to_all | solution.py:448
  99.9 2.8 %input_kernel.1 = bf16[4,4,64,128]{3,2,1,0:T(8,128)(2,1)} custom-call(bf16[6,6,64,128]{3,2,1,0:T(8,128)(2,1)S(1)} %copy-done.6, bf16[27,128,128]{2,1,0:T(8,128)(2,1)S(1)} %bitcast.30), custom_call_target="tpu_custom_call" | custom-call | flops 45298484 | bytes 73728 | tf_op jit(solution)/shard_map/input_kernel/pallas_call | solution.py:371
  102.7 22.9 %all-to-all-done.pieces = bf16[64,112,128]{2,1,0:T(8,128)(2,1)S(1)} async-done(((bf16[64,112,128]{2,1,0:T(8,128)(2,1)}), bf16[64,112,128]{2,1,0:T(8,128)(2,1)S(1)}, u32[]{:S(2)}, u32[]{:S(2)}) %all-to-all-start) | async-done | bytes 1835040 | tf_op jit(solution)/shard_map/all_to_all | solution.py:448
  126.7 5.8 %all-to-all-start.1 = ((bf16[64,56,128]{2,1,0:T(8,128)(2,1)}), bf16[64,56,128]{2,1,0:T(8,128)(2,1)S(1)}, u32[]{:S(2)}, u32[]{:S(2)}) async-start(bf16[64,56,128]{2,1,0:T(8,128)(2,1)} %get-tuple-element.69), calls=%async_computation.1 | async-start | bytes 1835008 | tf_op jit(solution)/shard_map/all_to_all | solution.py:455
  135.1 2.8 %collective-permute-start.18 = (bf16[2,56,128]{2,1,0:T(8,128)(2,1)S(1)}, bf16[2,56,128]{2,1,0:T(8,128)(2,1)S(1)}, u32[]{:S(2)}, u32[]{:S(2)}) collective-permute-start(bf16[2,56,128]{2,1,0:T(8,128)(2,1)S(1)} %maximum_select_fusion.pair_0), channel_id=1, source_target_pairs={{0,96},{32,0},{64,32},{96,64},{1,97},{33,1},{65,33},{97,65},{2,98}... | collective-permute-start | bytes 86024 | tf_op jit(solution)/shard_map/ppermute | solution.py:30
  139.0 3.9 %collective-permute-done.18.pair_3 = bf16[2,56,128]{2,1,0:T(8,128)(2,1)S(1)} collective-permute-done((bf16[2,56,128]{2,1,0:T(8,128)(2,1)S(1)}, bf16[2,56,128]{2,1,0:T(8,128)(2,1)S(1)}, u32[]{:S(2)}, u32[]{:S(2)}) %collective-permute-start.18) | collective-permute-done | bytes 28704 | tf_op jit(solution)/shard_map/ppermute | solution.py:30
  147.4 3.9 %collective-permute-start.19 = (bf16[3584,128]{1,0:T(8,128)(2,1)S(1)}, bf16[3584,128]{1,0:T(8,128)(2,1)S(1)}, u32[]{:S(2)}, u32[]{:S(2)}) collective-permute-start(bf16[3584,128]{1,0:T(8,128)(2,1)S(1)} %bitcast.27), channel_id=1, source_target_pairs={{0,16},{16,0},{1,17},{17,1},{2,18},{18,2},{3,19},{19,3},{4,20},{20... | collective-permute-start | bytes 2752520 | tf_op jit(solution)/shard_map/ppermute | solution.py:26
  (60 shorter events, 30.7 us)
Async XLA Ops:
  7.2 51.6 %all-gather.2.cloned.1.call-start = ((), (), s32[]{:S(2)}) async-start(), calls=%async_computation.2 | async-start | bytes 1880064 | tf_op jit(solution)/shard_map/all_gather | solution.py:400
  9.8 11.0 %collective-permute-start = (bf16[5,2,64,128]{3,2,1,0:T(8,128)(2,1)S(1)}, bf16[5,2,64,128]{3,2,1,0:T(8,128)(2,1)S(1)}, u32[]{:S(2)}, u32[]{:S(2)}) collective-permute-start(bf16[5,2,64,128]{3,2,1,0:T(8,128)(2,1)S(1)} %pad_maximum_fusion.1), channel_id=1, source_target_pairs={{0,1},{1,2},{2,3},{3,4},{4,5},{5,6},{6,7},{7,8},{8,9},{9,10},{10,1... | collective-permute-start | bytes 491528 | tf_op jit(solution)/shard_map/ppermute | solution.py:22
  12.0 8.8 %collective-permute-start.1 = (bf16[5,2,64,128]{3,2,1,0:T(8,128)(2,1)S(1)}, bf16[5,2,64,128]{3,2,1,0:T(8,128)(2,1)S(1)}, u32[]{:S(2)}, u32[]{:S(2)}) collective-permute-start(bf16[5,2,64,128]{3,2,1,0:T(8,128)(2,1)S(1)} %pad_maximum_fusion), channel_id=1, source_target_pairs={{0,15},{1,0},{2,1},{3,2},{4,3},{5,4},{6,5},{7,6},{8,7},{9,8},{10,9... | collective-permute-start | bytes 491528 | tf_op jit(solution)/shard_map/ppermute | solution.py:22
  21.7 37.2 %copy-start.4 = (bf16[2,2,32,256]{3,2,1,0:T(8,128)(2,1)S(1)}, bf16[2,2,32,256]{3,2,1,0:T(8,128)(2,1)}, u32[]{:S(2)}) copy-start(bf16[2,2,32,256]{3,2,1,0:T(8,128)(2,1)} %g_own.1) | copy-start | bytes 196612
  21.7 6.4 %collective-permute-start.2 = (bf16[20,64,128]{2,1,0:T(8,128)(2,1)S(1)}, bf16[20,64,128]{2,1,0:T(8,128)(2,1)S(1)}, u32[]{:S(2)}, u32[]{:S(2)}) collective-permute-start(bf16[20,64,128]{2,1,0:T(8,128)(2,1)S(1)} %get-tuple-element.44), channel_id=1, source_target_pairs={{0,16},{16,32},{32,48},{48,64},{64,80},{80,96},{96,112},{112,0},{1... | collective-permute-start | bytes 983048 | tf_op jit(solution)/shard_map/ppermute | solution.py:22
  24.1 6.9 %collective-permute-start.3 = (bf16[20,64,128]{2,1,0:T(8,128)(2,1)S(1)}, bf16[20,64,128]{2,1,0:T(8,128)(2,1)S(1)}, u32[]{:S(2)}, u32[]{:S(2)}) collective-permute-start(bf16[20,64,128]{2,1,0:T(8,128)(2,1)S(1)} %get-tuple-element.45), channel_id=1, source_target_pairs={{0,112},{16,0},{32,16},{48,32},{64,48},{80,64},{96,80},{112,96},{1... | collective-permute-start | bytes 983048 | tf_op jit(solution)/shard_map/ppermute | solution.py:22
  38.6 6.5 %collective-permute-start.5 = (bf16[2,2,32,128]{3,2,1,0:T(8,128)(2,1)S(1)}, bf16[2,2,32,128]{3,2,1,0:T(8,128)(2,1)S(1)}, u32[]{:S(2)}, u32[]{:S(2)}) collective-permute-start(bf16[2,2,32,128]{3,2,1,0:T(8,128)(2,1)S(1)} %get-tuple-element.46.own), channel_id=1, source_target_pairs={{0,15},{1,0},{2,1},{3,2},{4,3},{5,4},{6,5},{7,6},{8,7},{9,8},{10,9... | collective-permute-start | bytes 98312 | tf_op jit(solution)/shard_map/ppermute | solution.py:22
  43.5 7.3 %collective-permute-start.4 = (bf16[2,2,32,128]{3,2,1,0:T(8,128)(2,1)S(1)}, bf16[2,2,32,128]{3,2,1,0:T(8,128)(2,1)S(1)}, u32[]{:S(2)}, u32[]{:S(2)}) collective-permute-start(bf16[2,2,32,128]{3,2,1,0:T(8,128)(2,1)S(1)} %get-tuple-element.46.own), channel_id=1, source_target_pairs={{0,1},{1,2},{2,3},{3,4},{4,5},{5,6},{6,7},{7,8},{8,9},{9,10},{10,1... | collective-permute-start | bytes 98312 | tf_op jit(solution)/shard_map/ppermute | solution.py:22
  50.8 1.7 %collective-permute-start.6 = (bf16[2,6,32,128]{3,2,1,0:T(8,128)(2,1)S(1)}, bf16[2,6,32,128]{3,2,1,0:T(8,128)(2,1)S(1)}, u32[]{:S(2)}, u32[]{:S(2)}) collective-permute-start(bf16[2,6,32,128]{3,2,1,0:T(8,128)(2,1)S(1)} %get-tuple-element.47), channel_id=1, source_target_pairs={{0,16},{16,32},{32,48},{48,64},{64,80},{80,96},{96,112},{112,0},{1... | collective-permute-start | bytes 294920 | tf_op jit(solution)/shard_map/ppermute | solution.py:22
  50.8 4.5 %collective-permute-start.7 = (bf16[2,6,32,128]{3,2,1,0:T(8,128)(2,1)S(1)}, bf16[2,6,32,128]{3,2,1,0:T(8,128)(2,1)S(1)}, u32[]{:S(2)}, u32[]{:S(2)}) collective-permute-start(bf16[2,6,32,128]{3,2,1,0:T(8,128)(2,1)S(1)} %get-tuple-element.48), channel_id=1, source_target_pairs={{0,112},{16,0},{32,16},{48,32},{64,48},{80,64},{96,80},{112,96},{1... | collective-permute-start | bytes 294920 | tf_op jit(solution)/shard_map/ppermute | solution.py:22
  63.5 7.2 %collective-permute-start.9 = (bf16[4,2,64,128]{3,2,1,0:T(8,128)(2,1)S(1)}, bf16[4,2,64,128]{3,2,1,0:T(8,128)(2,1)S(1)}, u32[]{:S(2)}, u32[]{:S(2)}) collective-permute-start(bf16[4,2,64,128]{3,2,1,0:T(8,128)(2,1)S(1)} %get-tuple-element.53), channel_id=1, source_target_pairs={{0,1},{1,2},{2,3},{3,4},{4,5},{5,6},{6,7},{7,8},{8,9},{9,10},{10,1... | collective-permute-start | bytes 393224 | tf_op jit(solution)/shard_map/ppermute | solution.py:22
  64.4 6.2 %collective-permute-start.10 = (bf16[4,2,64,128]{3,2,1,0:T(8,128)(2,1)S(1)}, bf16[4,2,64,128]{3,2,1,0:T(8,128)(2,1)S(1)}, u32[]{:S(2)}, u32[]{:S(2)}) collective-permute-start(bf16[4,2,64,128]{3,2,1,0:T(8,128)(2,1)S(1)} %get-tuple-element.54), channel_id=1, source_target_pairs={{0,15},{1,0},{2,1},{3,2},{4,3},{5,4},{6,5},{7,6},{8,7},{9,8},{10,9... | collective-permute-start | bytes 393224 | tf_op jit(solution)/shard_map/ppermute | solution.py:22
  68.3 19.4 %collective-permute-start.8 = (bf16[6,6,64,128]{3,2,1,0:T(8,128)(2,1)S(1)}, bf16[6,6,64,128]{3,2,1,0:T(8,128)(2,1)S(1)}, u32[]{:S(2)}, u32[]{:S(2)}) collective-permute-start(bf16[6,6,64,128]{3,2,1,0:T(8,128)(2,1)S(1)} %copy-done.8), channel_id=1, source_target_pairs={{0,16},{16,0},{1,17},{17,1},{2,18},{18,2},{3,19},{19,3},{4,20},{20... | collective-permute-start | bytes 1769480 | tf_op jit(solution)/shard_map/ppermute | solution.py:26
  70.7 8.1 %collective-permute-start.13 = (bf16[2,8,64,128]{3,2,1,0:T(8,128)(2,1)S(1)}, bf16[2,8,64,128]{3,2,1,0:T(8,128)(2,1)S(1)}, u32[]{:S(2)}, u32[]{:S(2)}) collective-permute-start(bf16[2,8,64,128]{3,2,1,0:T(8,128)(2,1)S(1)} %get-tuple-element.58), channel_id=1, source_target_pairs={{0,112},{16,0},{32,16},{48,32},{64,48},{80,64},{96,80},{112,96},{1... | collective-permute-start | bytes 786440 | tf_op jit(solution)/shard_map/ppermute | solution.py:22
  73.4 5.4 %collective-permute-start.12 = (bf16[2,8,64,128]{3,2,1,0:T(8,128)(2,1)S(1)}, bf16[2,8,64,128]{3,2,1,0:T(8,128)(2,1)S(1)}, u32[]{:S(2)}, u32[]{:S(2)}) collective-permute-start(bf16[2,8,64,128]{3,2,1,0:T(8,128)(2,1)S(1)} %get-tuple-element.56), channel_id=1, source_target_pairs={{0,16},{16,32},{32,48},{48,64},{64,80},{80,96},{96,112},{112,0},{1... | collective-permute-start | bytes 786440 | tf_op jit(solution)/shard_map/ppermute | solution.py:22
  74.5 1.4 collective-permute-start.11
  83.9 3.8 %collective-permute-start.14 = (bf16[4,4,64,128]{3,2,1,0:T(8,128)(2,1)S(1)}, bf16[4,4,64,128]{3,2,1,0:T(8,128)(2,1)S(1)}, u32[]{:S(2)}, u32[]{:S(2)}) collective-permute-start(bf16[4,4,64,128]{3,2,1,0:T(8,128)(2,1)S(1)} %get-tuple-element.62), channel_id=1, source_target_pairs={{0,16},{16,0},{1,17},{17,1},{2,18},{18,2},{3,19},{19,3},{4,20},{20... | collective-permute-start | bytes 786440 | tf_op jit(solution)/shard_map/ppermute | solution.py:26
  91.3 34.3 %all-to-all-start = ((bf16[64,112,128]{2,1,0:T(8,128)(2,1)}), bf16[64,112,128]{2,1,0:T(8,128)(2,1)S(1)}, u32[]{:S(2)}, u32[]{:S(2)}) async-start(bf16[64,112,128]{2,1,0:T(8,128)(2,1)} %pair_grads_kernel.1), calls=%async_computation | async-start | bytes 3670016 | tf_op jit(solution)/shard_map/all_to_all | solution.py:448
  126.7 20.7 %all-to-all-start.1 = ((bf16[64,56,128]{2,1,0:T(8,128)(2,1)}), bf16[64,56,128]{2,1,0:T(8,128)(2,1)S(1)}, u32[]{:S(2)}, u32[]{:S(2)}) async-start(bf16[64,56,128]{2,1,0:T(8,128)(2,1)} %get-tuple-element.69), calls=%async_computation.1 | async-start | bytes 1835008 | tf_op jit(solution)/shard_map/all_to_all | solution.py:455
  132.5 2.6 %collective-permute-start.15 = (bf16[56,128]{1,0:T(8,128)(2,1)S(1)}, bf16[56,128]{1,0:T(8,128)(2,1)S(1)}, u32[]{:S(2)}, u32[]{:S(2)}) collective-permute-start(bf16[56,128]{1,0:T(8,128)(2,1)S(1)} %get-tuple-element.72), channel_id=1, source_target_pairs={{0,16},{16,0},{1,17},{17,1},{2,18},{18,2},{3,19},{19,3},{4,20},{20... | collective-permute-start | bytes 43016 | tf_op jit(solution)/shard_map/ppermute | solution.py:26
  135.1 7.8 %collective-permute-start.18 = (bf16[2,56,128]{2,1,0:T(8,128)(2,1)S(1)}, bf16[2,56,128]{2,1,0:T(8,128)(2,1)S(1)}, u32[]{:S(2)}, u32[]{:S(2)}) collective-permute-start(bf16[2,56,128]{2,1,0:T(8,128)(2,1)S(1)} %maximum_select_fusion.pair_0), channel_id=1, source_target_pairs={{0,96},{32,0},{64,32},{96,64},{1,97},{33,1},{65,33},{97,65},{2,98}... | collective-permute-start | bytes 86024 | tf_op jit(solution)/shard_map/ppermute | solution.py:30
  137.9 6.6 %collective-permute-start.17 = (bf16[2,56,128]{2,1,0:T(8,128)(2,1)S(1)}, bf16[2,56,128]{2,1,0:T(8,128)(2,1)S(1)}, u32[]{:S(2)}, u32[]{:S(2)}) collective-permute-start(bf16[2,56,128]{2,1,0:T(8,128)(2,1)S(1)} %maximum_select_fusion.pair_0), channel_id=1, source_target_pairs={{0,64},{32,96},{64,0},{96,32},{1,65},{33,97},{65,1},{97,33},{2,66}... | collective-permute-start | bytes 86024 | tf_op jit(solution)/shard_map/ppermute | solution.py:30
  138.3 6.9 %collective-permute-start.16 = (bf16[2,56,128]{2,1,0:T(8,128)(2,1)S(1)}, bf16[2,56,128]{2,1,0:T(8,128)(2,1)S(1)}, u32[]{:S(2)}, u32[]{:S(2)}) collective-permute-start(bf16[2,56,128]{2,1,0:T(8,128)(2,1)S(1)} %maximum_select_fusion.pair_0), channel_id=1, source_target_pairs={{0,32},{32,64},{64,96},{96,0},{1,33},{33,65},{65,97},{97,1},{2,34}... | collective-permute-start | bytes 86024 | tf_op jit(solution)/shard_map/ppermute | solution.py:30
  147.4 6.0 %collective-permute-start.19 = (bf16[3584,128]{1,0:T(8,128)(2,1)S(1)}, bf16[3584,128]{1,0:T(8,128)(2,1)S(1)}, u32[]{:S(2)}, u32[]{:S(2)}) collective-permute-start(bf16[3584,128]{1,0:T(8,128)(2,1)S(1)} %bitcast.27), channel_id=1, source_target_pairs={{0,16},{16,0},{1,17},{17,1},{2,18},{18,2},{3,19},{19,3},{4,20},{20... | collective-permute-start | bytes 2752520 | tf_op jit(solution)/shard_map/ppermute | solution.py:26
  (8 other events, 106.6 us)
Sparse Core Ops, SparseCore 0:
  10.1 48.6 all-gather.1

commit v7 on v6

--- a/solution.py
+++ b/solution.py
@@ -396,8 +396,9 @@
     coarse_scale = 1.0 / math.sqrt(fine_cells // 8)
     taps_one = conv_one.reshape(27, 128, 128)
     taps_two = conv_two.reshape(27, 128, 128)
-    taps_three = jnp.swapaxes(conv_three.reshape(27, 128, 16), 1, 2)
-    taps_three = lax.all_gather(taps_three, GY, axis=1, tiled=True)
+    half_taps = jnp.swapaxes(conv_three.reshape(27, 128, 16), 1, 2).reshape(27, 2, 8, 128)
+    half_taps = jnp.where(first_core, half_taps[:, 0], half_taps[:, 1])
+    mine = lax.all_to_all(jnp.broadcast_to(half_taps, (16, 27, 8, 128)), GY, 0, 0)
 
     f_before, f_after = shifted(last, GY, 1), shifted(first, GY, -1)
     low, high = call(
@@ -416,6 +417,10 @@
         3 * conv_flops, core_ref, features, f_before, f_after, f_left, f_right, taps_one, taps_two,
     )
     field_other = swap_cores(field_send)
+    mine, pooled = lax.optimization_barrier((mine, pooled))
+    theirs = swap_cores(mine)
+    both = jnp.where(first_core, jnp.stack([mine, theirs]), jnp.stack([theirs, mine]))
+    taps_three = jnp.transpose(both, (2, 1, 0, 3, 4)).reshape(27, 256, 128)
     p_pieces, _ = halo_pieces(pooled, 2, pooled, pooled)
     bottleneck, bundle, err_two, err_first, err_last = call(
         bottom_kernel,
@@ -423,7 +428,7 @@
         [((6, 6, 32, 128), BF16), ((4, 4, 32, 256), BF16), ((768, 1152), BF16),
          ((4, 4, 32, 256), BF16), ((64, 128), F32)],
         conv_flops, *p_pieces, bottom_grad, f_before, f_after, f_left, f_right,
-        in_hbm(taps_three), in_hbm(slope_two), in_hbm(skip_grad),
+        taps_three, in_hbm(slope_two), in_hbm(skip_grad),
     )
     e_pieces, e_high = halo_pieces(err_two, 2, err_first, err_last)
     bundle, e_high = lax.optimization_barrier((bundle, e_high))

time: 163 us -> 158 us (0.969)
  between operations: 14.2 us -> 0.89 us
  starting transfers between devices: 51.2 us -> 59.7 us
  waiting for transfers between devices: 62.3 us -> 59.1 us
  other arithmetic: 0.05 us -> 2.78 us
    all_to_all x0 -> x1, starting transfers between devices: none -> 8.64 us  [on_device(): lax.all_to_all(jnp.broadcast_to(half_taps, (16, 27, 8, 128)), GY, 0, 0)]
    all_gather x1 -> x0, waiting for transfers between devices: 3.59 us -> none  [on_device(): taps_three = lax.all_gather(taps_three, GY, axis=1, tiled=True)]
    ppermute x12, waiting for transfers between devices: 23.1 us -> 26.6 us  [shifted(): lax.ppermute(array, axes, [(i, (i + step) % count) for i in range(count)])]
    ppermute x12, starting transfers between devices: 23.6 us -> 20.2 us  [shifted(): lax.ppermute(array, axes, [(i, (i + step) % count) for i in range(count)])]
    transpose x0 -> x1, other arithmetic: none -> 1.73 us  [on_device(): taps_three = jnp.transpose(both, (2, 1, 0, 3, 4)).reshape(27, 256, 128)]
    ppermute x5 -> x6, starting transfers between devices: 9.44 us -> 10.2 us  [swap_cores(): return lax.ppermute(array, 'c', [(0, 1), (1, 0)])]
    ppermute x5 -> x6, waiting for transfers between devices: 4.38 us -> 4.01 us  [swap_cores(): return lax.ppermute(array, 'c', [(0, 1), (1, 0)])]
  transfers between devices with their start and end apart: 23 -> 24, of which waited for: 18 -> 12; matrix products, arithmetic and copies ran while one was open for 1% -> 1% of each run, Pallas kernels for 13% -> 13%
where the time goes in v7:
time: 158 us; the launch traced here: 157 us
  starting transfers between devices  59.7 us (38%)
  waiting for transfers between devices  59.1 us (37%)
  Pallas kernels  31.3 us (20%)
  local copies, waits for them, and re-layouts  3.32 us (2%)
  other arithmetic  2.78 us (2%)
    pallas_call x11, Pallas kernels, call(): pl.pallas_call(kernel, out_shape=shapes, in_specs=[pl.BlockSpec(memory_sp...  28.5 us
    ppermute x12, waiting for transfers between devices, shifted(): lax.ppermute(array, axes, [(i, (i + step) % count) for i in range(count)])  26.6 us
    all_to_all x1, waiting for transfers between devices, on_device(): lax.all_to_all(kept, FLAT, 0, 0)  22.1 us
    ppermute x12, starting transfers between devices, shifted(): lax.ppermute(array, axes, [(i, (i + step) % count) for i in range(count)])  20.2 us
    ppermute x6, starting transfers between devices, swap_cores(): return lax.ppermute(array, 'c', [(0, 1), (1, 0)])  10.2 us
    all_to_all x1, starting transfers between devices, on_device(): lax.all_to_all(kept, FLAT, 0, 0)  9.55 us
    all_to_all x1, starting transfers between devices, on_device(): lax.all_to_all(jnp.broadcast_to(half_taps, (16, 27, 8, 128)), GY, 0, 0)  8.64 us
    all_to_all x1, starting transfers between devices, on_device(): whole = lax.all_to_all(part, FLAT, 0, 0).reshape(64 * PIECE, 128)  6.09 us
  transfers between devices with their start and end apart: 24, of which 12 were waited for; matrix products, arithmetic and copies ran while one was open for 1% of the time, Pallas kernels for 13%

profile of v7, /device:TPU:1, one launch (start us, length us, event | category | flops | bytes accessed | tf_op | source)
XLA Modules:
  0.0 157.1 jit_solution(14527470711760043171)
XLA Ops:
  4.6 8.6 %all-to-all-start = ((bf16[16,27,8,128]{3,2,1,0:T(8,128)(2,1)}), bf16[16,27,8,128]{3,2,1,0:T(8,128)(2,1)}, u32[]{:S(2)}, u32[]{:S(2)}) async-start(bf16[16,27,8,128]{3,2,1,0:T(8,128)(2,1)} %broadcast_in_dim.3), calls=%async_computation | async-start | bytes 1769472 | tf_op jit(solution)/shard_map/all_to_all | solution.py:401
  14.5 3.5 %collective-permute-start.1 = (bf16[5,2,64,128]{3,2,1,0:T(8,128)(2,1)S(1)}, bf16[5,2,64,128]{3,2,1,0:T(8,128)(2,1)S(1)}, u32[]{:S(2)}, u32[]{:S(2)}) collective-permute-start(bf16[5,2,64,128]{3,2,1,0:T(8,128)(2,1)S(1)} %pad_maximum_fusion), channel_id=1, source_target_pairs={{0,15},{1,0},{2,1},{3,2},{4,3},{5,4},{6,5},{7,6},{8,7},{9,8},{10,9... | collective-permute-start | bytes 491528 | tf_op jit(solution)/shard_map/ppermute | solution.py:22
  18.1 13.8 %collective-permute-done.before.f_before = bf16[5,2,64,128]{3,2,1,0:T(8,128)(2,1)S(1)} collective-permute-done((bf16[5,2,64,128]{3,2,1,0:T(8,128)(2,1)S(1)}, bf16[5,2,64,128]{3,2,1,0:T(8,128)(2,1)S(1)}, u32[]{:S(2)}, u32[]{:S(2)}) %collective-permute-start) | collective-permute-done | bytes 163872 | tf_op jit(solution)/shard_map/ppermute | solution.py:22
  33.9 4.0 %collective-permute-done.2.left.f_left = bf16[20,64,128]{2,1,0:T(8,128)(2,1)S(1)} collective-permute-done((bf16[20,64,128]{2,1,0:T(8,128)(2,1)S(1)}, bf16[20,64,128]{2,1,0:T(8,128)(2,1)S(1)}, u32[]{:S(2)}, u32[]{:S(2)}) %collective-permute-start.2) | collective-permute-done | bytes 327712 | tf_op jit(solution)/shard_map/ppermute | solution.py:22
  37.9 2.5 %collective-permute-done.3.right.f_right = bf16[20,64,128]{2,1,0:T(8,128)(2,1)S(1)} collective-permute-done((bf16[20,64,128]{2,1,0:T(8,128)(2,1)S(1)}, bf16[20,64,128]{2,1,0:T(8,128)(2,1)S(1)}, u32[]{:S(2)}, u32[]{:S(2)}) %collective-permute-start.3) | collective-permute-done | bytes 327712 | tf_op jit(solution)/shard_map/ppermute | solution.py:22
  40.4 7.7 %forward_kernel.1 = (bf16[6,6,64,128]{3,2,1,0:T(8,128)(2,1)}, bf16[6,6,64,128]{3,2,1,0:T(8,128)(2,1)}, bf16[6,6,64,128]{3,2,1,0:T(8,128)(2,1)}, bf16[4,4,64,128]...) custom-call(s32[1]{0:T(128)} %bitcast.2.core, bf16[4,4,64,128]{3,2,1,0:T(8,128)(2,1)S(1)} %copy-done.2, ...), custom_call_target="tpu_custom_call" | custom-call | flops 135895456 | bytes 150733 | tf_op jit(solution)/shard_map/forward_kernel/pallas_call | solution.py:371
  48.2 4.8 %collective-permute-start.5 = (bf16[2,2,32,128]{3,2,1,0:T(8,128)(2,1)S(1)}, bf16[2,2,32,128]{3,2,1,0:T(8,128)(2,1)S(1)}, u32[]{:S(2)}, u32[]{:S(2)}) collective-permute-start(bf16[2,2,32,128]{3,2,1,0:T(8,128)(2,1)S(1)} %get-tuple-element.50.own), channel_id=1, source_target_pairs={{0,15},{1,0},{2,1},{3,2},{4,3},{5,4},{6,5},{7,6},{8,7},{9,8},{10,9... | collective-permute-start | bytes 98312 | tf_op jit(solution)/shard_map/ppermute | solution.py:22
  54.3 2.6 %collective-permute-start.6 = (bf16[2,6,32,128]{3,2,1,0:T(8,128)(2,1)S(1)}, bf16[2,6,32,128]{3,2,1,0:T(8,128)(2,1)S(1)}, u32[]{:S(2)}, u32[]{:S(2)}) collective-permute-start(bf16[2,6,32,128]{3,2,1,0:T(8,128)(2,1)S(1)} %get-tuple-element.51), channel_id=1, source_target_pairs={{0,16},{16,32},{32,48},{48,64},{64,80},{80,96},{96,112},{112,0},{1... | collective-permute-start | bytes 294920 | tf_op jit(solution)/shard_map/ppermute | solution.py:22
  61.0 4.1 %bottom_kernel.1 = (bf16[2,2,32,256]{3,2,1,0:T(8,128)(2,1)}, bf16[24,32,128]{2,1,0:T(8,128)(2,1)S(1)}, bf16[4,4,64,128]{3,2,1,0:T(8,128)(2,1)S(1)}, bf16[4,2,64,...) custom-call(bf16[2,2,32,128]{3,2,1,0:T(8,128)(2,1)S(1)} %get-tuple-element.50.own, ...), custom_call_target="tpu_custom_call" | custom-call | flops 45298484 | bytes 181862 | tf_op jit(solution)/shard_map/bottom_kernel/pallas_call | solution.py:371
  65.1 5.1 %collective-permute-start.11 = (bf16[4,2,64,128]{3,2,1,0:T(8,128)(2,1)S(1)}, bf16[4,2,64,128]{3,2,1,0:T(8,128)(2,1)S(1)}, u32[]{:S(2)}, u32[]{:S(2)}) collective-permute-start(bf16[4,2,64,128]{3,2,1,0:T(8,128)(2,1)S(1)} %get-tuple-element.59), channel_id=1, source_target_pairs={{0,15},{1,0},{2,1},{3,2},{4,3},{5,4},{6,5},{7,6},{8,7},{9,8},{10,9... | collective-permute-start | bytes 393224 | tf_op jit(solution)/shard_map/ppermute | solution.py:22
  70.7 3.2 %collective-permute-done.10.before = bf16[4,2,64,128]{3,2,1,0:T(8,128)(2,1)S(1)} collective-permute-done((bf16[4,2,64,128]{3,2,1,0:T(8,128)(2,1)S(1)}, bf16[4,2,64,128]{3,2,1,0:T(8,128)(2,1)S(1)}, u32[]{:S(2)}, u32[]{:S(2)}) %collective-permute-start.10) | collective-permute-done | bytes 131104 | tf_op jit(solution)/shard_map/ppermute | solution.py:22
  74.7 2.9 %collective-permute-start.12 = (bf16[24,32,128]{2,1,0:T(8,128)(2,1)S(1)}, bf16[24,32,128]{2,1,0:T(8,128)(2,1)S(1)}, u32[]{:S(2)}, u32[]{:S(2)}) collective-permute-start(bf16[24,32,128]{2,1,0:T(8,128)(2,1)S(1)} %get-tuple-element.62.own), channel_id=1, source_target_pairs={{0,16},{16,0},{1,17},{17,1},{2,18},{18,2},{3,19},{19,3},{4,20},{20... | collective-permute-start | bytes 589832 | tf_op jit(solution)/shard_map/ppermute | solution.py:26
  80.8 5.0 %first_errors_kernel.1 = (bf16[6,6,64,128]{3,2,1,0:T(8,128)(2,1)}, bf16[4,4,64,128]{3,2,1,0:T(8,128)(2,1)S(1)}, bf16[4,4,64,128]{3,2,1,0:T(8,128)(2,1)S(1)}) custom-call(s32[1]{0:T(128)} %bitcast.2.core, bf16[4,4,64,128]{3,2,1,0:T(8,128)(2,1)S(1)} %get-tuple-element.57.own, bf16[4,2,64,128]{3,2,1,0:T(8,128)(2,1)S(1)} %collective-permute-done.10.before, ...), custom_call_target="tpu_custom_call" | custom-call | flops 90596968 | bytes 126157 | tf_op jit(solution)/shard_map/first_errors_kernel/pallas_call | solution.py:371
  86.7 2.1 %own_grads_kernel.1.own_total = f32[1152,384]{1,0:T(8,128)S(1)} custom-call(bf16[6,6,64,128]{3,2,1,0:T(8,128)(2,1)S(1)} %copy-done.4, bf16[4,4,64,128]{3,2,1,0:T(8,128)(2,1)S(1)} %get-tuple-element.69.errors), custom_call_target="tpu_custom_call" | custom-call | flops 45298484 | bytes 42598 | tf_op jit(solution)/shard_map/own_grads_kernel/pallas_call | solution.py:371
  88.9 3.5 %pair_grads_kernel.1 = bf16[64,112,128]{2,1,0:T(8,128)(2,1)} custom-call(bf16[6,6,64,128]{3,2,1,0:T(8,128)(2,1)S(1)} %collective-permute-done.9.fields, bf16[4,4,64,128]{3,2,1,0:T(8,128)(2,1)S(1)} %collective-permute-done.15.errors, f32[1152,384]{1,0:T(8,128)S(1)} %own_grads_kernel.1.own_total, bf16[64,56,128]{2,1,0:T(8,128)(2,1)S(1)} %bottom_grads_kernel.1.three), custom_call_target="tpu_custom_call" | custom-call | flops 45298484 | bytes 176947 | tf_op jit(solution)/shard_map/pair_grads_kernel/pallas_call | solution.py:371
  92.4 9.6 %all-to-all-start.1 = ((bf16[64,112,128]{2,1,0:T(8,128)(2,1)}), bf16[64,112,128]{2,1,0:T(8,128)(2,1)S(1)}, u32[]{:S(2)}, u32[]{:S(2)}) async-start(bf16[64,112,128]{2,1,0:T(8,128)(2,1)} %pair_grads_kernel.1), calls=%async_computation.1 | async-start | bytes 3670016 | tf_op jit(solution)/shard_map/all_to_all | solution.py:453
  102.0 2.8 %input_kernel.1 = bf16[4,4,64,128]{3,2,1,0:T(8,128)(2,1)} custom-call(bf16[6,6,64,128]{3,2,1,0:T(8,128)(2,1)S(1)} %copy-done.5, bf16[27,128,128]{2,1,0:T(8,128)(2,1)S(1)} %bitcast.40), custom_call_target="tpu_custom_call" | custom-call | flops 45298484 | bytes 73728 | tf_op jit(solution)/shard_map/input_kernel/pallas_call | solution.py:371
  104.8 22.1 %all-to-all-done.1.pieces = bf16[64,112,128]{2,1,0:T(8,128)(2,1)S(1)} async-done(((bf16[64,112,128]{2,1,0:T(8,128)(2,1)}), bf16[64,112,128]{2,1,0:T(8,128)(2,1)S(1)}, u32[]{:S(2)}, u32[]{:S(2)}) %all-to-all-start.1) | async-done | bytes 1835040 | tf_op jit(solution)/shard_map/all_to_all | solution.py:453
  128.0 6.1 %all-to-all-start.2 = ((bf16[64,56,128]{2,1,0:T(8,128)(2,1)}), bf16[64,56,128]{2,1,0:T(8,128)(2,1)S(1)}, u32[]{:S(2)}, u32[]{:S(2)}) async-start(bf16[64,56,128]{2,1,0:T(8,128)(2,1)} %get-tuple-element.74), calls=%async_computation.2 | async-start | bytes 1835008 | tf_op jit(solution)/shard_map/all_to_all | solution.py:460
  138.3 2.6 %collective-permute-start.18 = (bf16[2,56,128]{2,1,0:T(8,128)(2,1)S(1)}, bf16[2,56,128]{2,1,0:T(8,128)(2,1)S(1)}, u32[]{:S(2)}, u32[]{:S(2)}) collective-permute-start(bf16[2,56,128]{2,1,0:T(8,128)(2,1)S(1)} %maximum_select_fusion.1.pair_0), channel_id=1, source_target_pairs={{0,64},{32,96},{64,0},{96,32},{1,65},{33,97},{65,1},{97,33},{2,66}... | collective-permute-start | bytes 86024 | tf_op jit(solution)/shard_map/ppermute | solution.py:30
  141.9 4.8 %collective-permute-done.17.pair_1 = bf16[2,56,128]{2,1,0:T(8,128)(2,1)S(1)} collective-permute-done((bf16[2,56,128]{2,1,0:T(8,128)(2,1)S(1)}, bf16[2,56,128]{2,1,0:T(8,128)(2,1)S(1)}, u32[]{:S(2)}, u32[]{:S(2)}) %collective-permute-start.17) | collective-permute-done | bytes 28704 | tf_op jit(solution)/shard_map/ppermute | solution.py:30
  149.0 3.9 %collective-permute-start.20 = (bf16[3584,128]{1,0:T(8,128)(2,1)S(1)}, bf16[3584,128]{1,0:T(8,128)(2,1)S(1)}, u32[]{:S(2)}, u32[]{:S(2)}) collective-permute-start(bf16[3584,128]{1,0:T(8,128)(2,1)S(1)} %bitcast.37), channel_id=1, source_target_pairs={{0,16},{16,0},{1,17},{17,1},{2,18},{18,2},{3,19},{19,3},{4,20},{20... | collective-permute-start | bytes 2752520 | tf_op jit(solution)/shard_map/ppermute | solution.py:26
  152.9 2.1 %collective-permute-done.20.other = bf16[3584,128]{1,0:T(8,128)(2,1)S(1)} collective-permute-done((bf16[3584,128]{1,0:T(8,128)(2,1)S(1)}, bf16[3584,128]{1,0:T(8,128)(2,1)S(1)}, u32[]{:S(2)}, u32[]{:S(2)}) %collective-permute-start.20) | collective-permute-done | bytes 917536 | tf_op jit(solution)/shard_map/ppermute | solution.py:26
  155.0 2.1 %finish_kernel.1 = (f32[3456,128]{1,0:T(8,128)}, f32[3456,128]{1,0:T(8,128)}) custom-call(s32[1]{0:T(128)} %bitcast.2.core, bf16[3584,128]{1,0:T(8,128)(2,1)S(1)} %bitcast.38, bf16[3584,128]{1,0:T(8,128)(2,1)S(1)} %collective-permute-done.20.other), custom_call_target="tpu_custom_call" | custom-call | tf_op jit(solution)/shard_map/finish_kernel/pallas_call | solution.py:473
  (63 shorter events, 26.7 us)
Async XLA Ops:
  4.6 43.5 %all-to-all-start = ((bf16[16,27,8,128]{3,2,1,0:T(8,128)(2,1)}), bf16[16,27,8,128]{3,2,1,0:T(8,128)(2,1)}, u32[]{:S(2)}, u32[]{:S(2)}) async-start(bf16[16,27,8,128]{3,2,1,0:T(8,128)(2,1)} %broadcast_in_dim.3), calls=%async_computation | async-start | bytes 1769472 | tf_op jit(solution)/shard_map/all_to_all | solution.py:401
  13.2 18.6 %collective-permute-start = (bf16[5,2,64,128]{3,2,1,0:T(8,128)(2,1)S(1)}, bf16[5,2,64,128]{3,2,1,0:T(8,128)(2,1)S(1)}, u32[]{:S(2)}, u32[]{:S(2)}) collective-permute-start(bf16[5,2,64,128]{3,2,1,0:T(8,128)(2,1)S(1)} %pad_maximum_fusion.1), channel_id=1, source_target_pairs={{0,1},{1,2},{2,3},{3,4},{4,5},{5,6},{6,7},{7,8},{8,9},{9,10},{10,1... | collective-permute-start | bytes 491528 | tf_op jit(solution)/shard_map/ppermute | solution.py:22
  14.5 17.3 %collective-permute-start.1 = (bf16[5,2,64,128]{3,2,1,0:T(8,128)(2,1)S(1)}, bf16[5,2,64,128]{3,2,1,0:T(8,128)(2,1)S(1)}, u32[]{:S(2)}, u32[]{:S(2)}) collective-permute-start(bf16[5,2,64,128]{3,2,1,0:T(8,128)(2,1)S(1)} %pad_maximum_fusion), channel_id=1, source_target_pairs={{0,15},{1,0},{2,1},{3,2},{4,3},{5,4},{6,5},{7,6},{8,7},{9,8},{10,9... | collective-permute-start | bytes 491528 | tf_op jit(solution)/shard_map/ppermute | solution.py:22
  31.9 6.0 %collective-permute-start.2 = (bf16[20,64,128]{2,1,0:T(8,128)(2,1)S(1)}, bf16[20,64,128]{2,1,0:T(8,128)(2,1)S(1)}, u32[]{:S(2)}, u32[]{:S(2)}) collective-permute-start(bf16[20,64,128]{2,1,0:T(8,128)(2,1)S(1)} %get-tuple-element.47), channel_id=1, source_target_pairs={{0,16},{16,32},{32,48},{48,64},{64,80},{80,96},{96,112},{112,0},{1... | collective-permute-start | bytes 983048 | tf_op jit(solution)/shard_map/ppermute | solution.py:22
  33.9 6.5 %collective-permute-start.3 = (bf16[20,64,128]{2,1,0:T(8,128)(2,1)S(1)}, bf16[20,64,128]{2,1,0:T(8,128)(2,1)S(1)}, u32[]{:S(2)}, u32[]{:S(2)}) collective-permute-start(bf16[20,64,128]{2,1,0:T(8,128)(2,1)S(1)} %get-tuple-element.48), channel_id=1, source_target_pairs={{0,112},{16,0},{32,16},{48,32},{64,48},{80,64},{96,80},{112,96},{1... | collective-permute-start | bytes 983048 | tf_op jit(solution)/shard_map/ppermute | solution.py:22
  48.0 8.9 %collective-permute-start.8 = (bf16[16,27,8,128]{3,2,1,0:T(8,128)(2,1)}, bf16[16,27,8,128]{3,2,1,0:T(8,128)(2,1)S(1)}, u32[]{:S(2)}, u32[]{:S(2)}) collective-permute-start(bf16[16,27,8,128]{3,2,1,0:T(8,128)(2,1)} %all-to-all-done), channel_id=1, source_target_pairs={{0,16},{16,0},{1,17},{17,1},{2,18},{18,2},{3,19},{19,3},{4,20},{20... | collective-permute-start | bytes 2654216 | tf_op jit(solution)/shard_map/ppermute | solution.py:26
  48.2 6.1 %collective-permute-start.4 = (bf16[2,2,32,128]{3,2,1,0:T(8,128)(2,1)S(1)}, bf16[2,2,32,128]{3,2,1,0:T(8,128)(2,1)S(1)}, u32[]{:S(2)}, u32[]{:S(2)}) collective-permute-start(bf16[2,2,32,128]{3,2,1,0:T(8,128)(2,1)S(1)} %get-tuple-element.50.own), channel_id=1, source_target_pairs={{0,1},{1,2},{2,3},{3,4},{4,5},{5,6},{6,7},{7,8},{8,9},{9,10},{10,1... | collective-permute-start | bytes 98312 | tf_op jit(solution)/shard_map/ppermute | solution.py:22
  48.2 6.1 %collective-permute-start.5 = (bf16[2,2,32,128]{3,2,1,0:T(8,128)(2,1)S(1)}, bf16[2,2,32,128]{3,2,1,0:T(8,128)(2,1)S(1)}, u32[]{:S(2)}, u32[]{:S(2)}) collective-permute-start(bf16[2,2,32,128]{3,2,1,0:T(8,128)(2,1)S(1)} %get-tuple-element.50.own), channel_id=1, source_target_pairs={{0,15},{1,0},{2,1},{3,2},{4,3},{5,4},{6,5},{7,6},{8,7},{9,8},{10,9... | collective-permute-start | bytes 98312 | tf_op jit(solution)/shard_map/ppermute | solution.py:22
  54.3 4.9 %collective-permute-start.6 = (bf16[2,6,32,128]{3,2,1,0:T(8,128)(2,1)S(1)}, bf16[2,6,32,128]{3,2,1,0:T(8,128)(2,1)S(1)}, u32[]{:S(2)}, u32[]{:S(2)}) collective-permute-start(bf16[2,6,32,128]{3,2,1,0:T(8,128)(2,1)S(1)} %get-tuple-element.51), channel_id=1, source_target_pairs={{0,16},{16,32},{32,48},{48,64},{64,80},{80,96},{96,112},{112,0},{1... | collective-permute-start | bytes 294920 | tf_op jit(solution)/shard_map/ppermute | solution.py:22
  56.9 4.0 %collective-permute-start.7 = (bf16[2,6,32,128]{3,2,1,0:T(8,128)(2,1)S(1)}, bf16[2,6,32,128]{3,2,1,0:T(8,128)(2,1)S(1)}, u32[]{:S(2)}, u32[]{:S(2)}) collective-permute-start(bf16[2,6,32,128]{3,2,1,0:T(8,128)(2,1)S(1)} %get-tuple-element.52), channel_id=1, source_target_pairs={{0,112},{16,0},{32,16},{48,32},{64,48},{80,64},{96,80},{112,96},{1... | collective-permute-start | bytes 294920 | tf_op jit(solution)/shard_map/ppermute | solution.py:22
  65.1 8.9 %collective-permute-start.10 = (bf16[4,2,64,128]{3,2,1,0:T(8,128)(2,1)S(1)}, bf16[4,2,64,128]{3,2,1,0:T(8,128)(2,1)S(1)}, u32[]{:S(2)}, u32[]{:S(2)}) collective-permute-start(bf16[4,2,64,128]{3,2,1,0:T(8,128)(2,1)S(1)} %get-tuple-element.58), channel_id=1, source_target_pairs={{0,1},{1,2},{2,3},{3,4},{4,5},{5,6},{6,7},{7,8},{8,9},{9,10},{10,1... | collective-permute-start | bytes 393224 | tf_op jit(solution)/shard_map/ppermute | solution.py:22
  65.1 8.8 %collective-permute-start.11 = (bf16[4,2,64,128]{3,2,1,0:T(8,128)(2,1)S(1)}, bf16[4,2,64,128]{3,2,1,0:T(8,128)(2,1)S(1)}, u32[]{:S(2)}, u32[]{:S(2)}) collective-permute-start(bf16[4,2,64,128]{3,2,1,0:T(8,128)(2,1)S(1)} %get-tuple-element.59), channel_id=1, source_target_pairs={{0,15},{1,0},{2,1},{3,2},{4,3},{5,4},{6,5},{7,6},{8,7},{9,8},{10,9... | collective-permute-start | bytes 393224 | tf_op jit(solution)/shard_map/ppermute | solution.py:22
  70.3 18.6 %collective-permute-start.9 = (bf16[6,6,64,128]{3,2,1,0:T(8,128)(2,1)S(1)}, bf16[6,6,64,128]{3,2,1,0:T(8,128)(2,1)S(1)}, u32[]{:S(2)}, u32[]{:S(2)}) collective-permute-start(bf16[6,6,64,128]{3,2,1,0:T(8,128)(2,1)S(1)} %copy-done.7), channel_id=1, source_target_pairs={{0,16},{16,0},{1,17},{17,1},{2,18},{18,2},{3,19},{19,3},{4,20},{20... | collective-permute-start | bytes 1769480 | tf_op jit(solution)/shard_map/ppermute | solution.py:26
  74.0 6.8 %collective-permute-start.13 = (bf16[2,8,64,128]{3,2,1,0:T(8,128)(2,1)S(1)}, bf16[2,8,64,128]{3,2,1,0:T(8,128)(2,1)S(1)}, u32[]{:S(2)}, u32[]{:S(2)}) collective-permute-start(bf16[2,8,64,128]{3,2,1,0:T(8,128)(2,1)S(1)} %get-tuple-element.61), channel_id=1, source_target_pairs={{0,16},{16,32},{32,48},{48,64},{64,80},{80,96},{96,112},{112,0},{1... | collective-permute-start | bytes 786440 | tf_op jit(solution)/shard_map/ppermute | solution.py:22
  74.3 6.5 %collective-permute-start.14 = (bf16[2,8,64,128]{3,2,1,0:T(8,128)(2,1)S(1)}, bf16[2,8,64,128]{3,2,1,0:T(8,128)(2,1)S(1)}, u32[]{:S(2)}, u32[]{:S(2)}) collective-permute-start(bf16[2,8,64,128]{3,2,1,0:T(8,128)(2,1)S(1)} %get-tuple-element.63), channel_id=1, source_target_pairs={{0,112},{16,0},{32,16},{48,32},{64,48},{80,64},{96,80},{112,96},{1... | collective-permute-start | bytes 786440 | tf_op jit(solution)/shard_map/ppermute | solution.py:22
  74.7 4.0 %collective-permute-start.12 = (bf16[24,32,128]{2,1,0:T(8,128)(2,1)S(1)}, bf16[24,32,128]{2,1,0:T(8,128)(2,1)S(1)}, u32[]{:S(2)}, u32[]{:S(2)}) collective-permute-start(bf16[24,32,128]{2,1,0:T(8,128)(2,1)S(1)} %get-tuple-element.62.own), channel_id=1, source_target_pairs={{0,16},{16,0},{1,17},{17,1},{2,18},{18,2},{3,19},{19,3},{4,20},{20... | collective-permute-start | bytes 589832 | tf_op jit(solution)/shard_map/ppermute | solution.py:26
  85.8 3.0 %collective-permute-start.15 = (bf16[4,4,64,128]{3,2,1,0:T(8,128)(2,1)S(1)}, bf16[4,4,64,128]{3,2,1,0:T(8,128)(2,1)S(1)}, u32[]{:S(2)}, u32[]{:S(2)}) collective-permute-start(bf16[4,4,64,128]{3,2,1,0:T(8,128)(2,1)S(1)} %get-tuple-element.67), channel_id=1, source_target_pairs={{0,16},{16,0},{1,17},{17,1},{2,18},{18,2},{3,19},{19,3},{4,20},{20... | collective-permute-start | bytes 786440 | tf_op jit(solution)/shard_map/ppermute | solution.py:26
  92.4 34.5 %all-to-all-start.1 = ((bf16[64,112,128]{2,1,0:T(8,128)(2,1)}), bf16[64,112,128]{2,1,0:T(8,128)(2,1)S(1)}, u32[]{:S(2)}, u32[]{:S(2)}) async-start(bf16[64,112,128]{2,1,0:T(8,128)(2,1)} %pair_grads_kernel.1), calls=%async_computation.1 | async-start | bytes 3670016 | tf_op jit(solution)/shard_map/all_to_all | solution.py:453
  128.0 21.0 %all-to-all-start.2 = ((bf16[64,56,128]{2,1,0:T(8,128)(2,1)}), bf16[64,56,128]{2,1,0:T(8,128)(2,1)S(1)}, u32[]{:S(2)}, u32[]{:S(2)}) async-start(bf16[64,56,128]{2,1,0:T(8,128)(2,1)} %get-tuple-element.74), calls=%async_computation.2 | async-start | bytes 1835008 | tf_op jit(solution)/shard_map/all_to_all | solution.py:460
  134.2 2.7 %collective-permute-start.16 = (bf16[56,128]{1,0:T(8,128)(2,1)S(1)}, bf16[56,128]{1,0:T(8,128)(2,1)S(1)}, u32[]{:S(2)}, u32[]{:S(2)}) collective-permute-start(bf16[56,128]{1,0:T(8,128)(2,1)S(1)} %get-tuple-element.76), channel_id=1, source_target_pairs={{0,16},{16,0},{1,17},{17,1},{2,18},{18,2},{3,19},{19,3},{4,20},{20... | collective-permute-start | bytes 43016 | tf_op jit(solution)/shard_map/ppermute | solution.py:26
  136.9 9.8 %collective-permute-start.17 = (bf16[2,56,128]{2,1,0:T(8,128)(2,1)S(1)}, bf16[2,56,128]{2,1,0:T(8,128)(2,1)S(1)}, u32[]{:S(2)}, u32[]{:S(2)}) collective-permute-start(bf16[2,56,128]{2,1,0:T(8,128)(2,1)S(1)} %maximum_select_fusion.1.pair_0), channel_id=1, source_target_pairs={{0,32},{32,64},{64,96},{96,0},{1,33},{33,65},{65,97},{97,1},{2,34}... | collective-permute-start | bytes 86024 | tf_op jit(solution)/shard_map/ppermute | solution.py:30
  138.3 8.4 %collective-permute-start.18 = (bf16[2,56,128]{2,1,0:T(8,128)(2,1)S(1)}, bf16[2,56,128]{2,1,0:T(8,128)(2,1)S(1)}, u32[]{:S(2)}, u32[]{:S(2)}) collective-permute-start(bf16[2,56,128]{2,1,0:T(8,128)(2,1)S(1)} %maximum_select_fusion.1.pair_0), channel_id=1, source_target_pairs={{0,64},{32,96},{64,0},{96,32},{1,65},{33,97},{65,1},{97,33},{2,66}... | collective-permute-start | bytes 86024 | tf_op jit(solution)/shard_map/ppermute | solution.py:30
  140.9 5.8 %collective-permute-start.19 = (bf16[2,56,128]{2,1,0:T(8,128)(2,1)S(1)}, bf16[2,56,128]{2,1,0:T(8,128)(2,1)S(1)}, u32[]{:S(2)}, u32[]{:S(2)}) collective-permute-start(bf16[2,56,128]{2,1,0:T(8,128)(2,1)S(1)} %maximum_select_fusion.1.pair_0), channel_id=1, source_target_pairs={{0,96},{32,0},{64,32},{96,64},{1,97},{33,1},{65,33},{97,65},{2,98}... | collective-permute-start | bytes 86024 | tf_op jit(solution)/shard_map/ppermute | solution.py:30
  149.0 6.0 %collective-permute-start.20 = (bf16[3584,128]{1,0:T(8,128)(2,1)S(1)}, bf16[3584,128]{1,0:T(8,128)(2,1)S(1)}, u32[]{:S(2)}, u32[]{:S(2)}) collective-permute-start(bf16[3584,128]{1,0:T(8,128)(2,1)S(1)} %bitcast.37), channel_id=1, source_target_pairs={{0,16},{16,0},{1,17},{17,1},{2,18},{18,2},{3,19},{19,3},{4,20},{20... | collective-permute-start | bytes 2752520 | tf_op jit(solution)/shard_map/ppermute | solution.py:26
  (8 other events, 181.2 us)

commit v8 on v7

--- a/solution.py
+++ b/solution.py
@@ -402,7 +402,8 @@
 
     f_before, f_after = shifted(last, GY, 1), shifted(first, GY, -1)
     low, high = call(
-        first_slab_kernel, [((20, 64, 128), BF16)] * 2, [], 0, features, f_before, f_after, bottom_grad
+        first_slab_kernel, [((20, 64, 128), BF16)] * 2, [], 4 * 10**11,
+        features, f_before, f_after, bottom_grad,
     )
     f_left, f_right = exchange_x(low, high)
 

time: 158 us -> 142 us (0.90)
  waiting for transfers between devices: 59.1 us -> 45.6 us
  starting transfers between devices: 59.7 us -> 57.9 us
    ppermute x12, waiting for transfers between devices: 26.6 us -> 13.2 us  [shifted(): lax.ppermute(array, axes, [(i, (i + step) % count) for i in range(count)])]
    all_to_all x1, starting transfers between devices: 8.64 us -> 4.3 us  [on_device(): lax.all_to_all(jnp.broadcast_to(half_taps, (16, 27, 8, 128)), GY, 0, 0)]
    ppermute x12, starting transfers between devices: 20.2 us -> 22.8 us  [shifted(): lax.ppermute(array, axes, [(i, (i + step) % count) for i in range(count)])]
  transfers between devices with their start and end apart: 24 -> 24, of which waited for: 12 -> 11; matrix products, arithmetic and copies ran while one was open for 1% -> 3% of each run, Pallas kernels for 13% -> 14%
where the time goes in v8:
time: 142 us
  starting transfers between devices  57.9 us (41%)
  waiting for transfers between devices  45.6 us (32%)
  Pallas kernels  31.3 us (22%)
  local copies, waits for them, and re-layouts  3.32 us (2%)
  other arithmetic  2.64 us (2%)
    pallas_call x11, Pallas kernels, call(): pl.pallas_call(kernel, out_shape=shapes, in_specs=[pl.BlockSpec(memory_sp...  28.5 us
    ppermute x12, starting transfers between devices, shifted(): lax.ppermute(array, axes, [(i, (i + step) % count) for i in range(count)])  22.8 us
    all_to_all x1, waiting for transfers between devices, on_device(): lax.all_to_all(kept, FLAT, 0, 0)  22.1 us
    ppermute x12, waiting for transfers between devices, shifted(): lax.ppermute(array, axes, [(i, (i + step) % count) for i in range(count)])  13.2 us
    ppermute x6, starting transfers between devices, swap_cores(): return lax.ppermute(array, 'c', [(0, 1), (1, 0)])  10 us
    all_to_all x1, starting transfers between devices, on_device(): lax.all_to_all(kept, FLAT, 0, 0)  9.55 us
    all_to_all x1, starting transfers between devices, on_device(): whole = lax.all_to_all(part, FLAT, 0, 0).reshape(64 * PIECE, 128)  6.1 us
    ppermute x3, starting transfers between devices, ring_pieces(): lax.ppermute(pieces[d], axis, [(i, (i + d) % 4) for i in range(4)])  5.03 us
  transfers between devices with their start and end apart: 24, of which 11 were waited for; matrix products, arithmetic and copies ran while one was open for 3% of the time, Pallas kernels for 14%

profile of v8, /device:TPU:1, one launch (start us, length us, event | category | flops | bytes accessed | tf_op | source)
XLA Modules:
  0.0 141.7 jit_solution(6698587154141304346)
XLA Ops:
  2.5 2.2 %collective-permute-start = (bf16[5,2,64,128]{3,2,1,0:T(8,128)(2,1)S(1)}, bf16[5,2,64,128]{3,2,1,0:T(8,128)(2,1)S(1)}, u32[]{:S(2)}, u32[]{:S(2)}) collective-permute-start(bf16[5,2,64,128]{3,2,1,0:T(8,128)(2,1)S(1)} %pad_maximum_fusion.1), channel_id=1, source_target_pairs={{0,1},{1,2},{2,3},{3,4},{4,5},{5,6},{6,7},{7,8},{8,9},{9,10},{10,1... | collective-permute-start | bytes 491528 | tf_op jit(solution)/shard_map/ppermute | solution.py:22
  4.7 5.0 %collective-permute-start.1 = (bf16[5,2,64,128]{3,2,1,0:T(8,128)(2,1)S(1)}, bf16[5,2,64,128]{3,2,1,0:T(8,128)(2,1)S(1)}, u32[]{:S(2)}, u32[]{:S(2)}) collective-permute-start(bf16[5,2,64,128]{3,2,1,0:T(8,128)(2,1)S(1)} %pad_maximum_fusion), channel_id=1, source_target_pairs={{0,15},{1,0},{2,1},{3,2},{4,3},{5,4},{6,5},{7,6},{8,7},{9,8},{10,9... | collective-permute-start | bytes 491528 | tf_op jit(solution)/shard_map/ppermute | solution.py:22
  11.6 4.3 %all-to-all-start = ((bf16[16,27,8,128]{3,2,1,0:T(8,128)(2,1)}), bf16[16,27,8,128]{3,2,1,0:T(8,128)(2,1)}, u32[]{:S(2)}, u32[]{:S(2)}) async-start(bf16[16,27,8,128]{3,2,1,0:T(8,128)(2,1)} %broadcast_in_dim.3), calls=%async_computation | async-start | bytes 1769472 | tf_op jit(solution)/shard_map/all_to_all | solution.py:401
  16.0 2.1 %collective-permute-start.2 = (bf16[20,64,128]{2,1,0:T(8,128)(2,1)S(1)}, bf16[20,64,128]{2,1,0:T(8,128)(2,1)S(1)}, u32[]{:S(2)}, u32[]{:S(2)}) collective-permute-start(bf16[20,64,128]{2,1,0:T(8,128)(2,1)S(1)} %get-tuple-element.47), channel_id=1, source_target_pairs={{0,16},{16,32},{32,48},{48,64},{64,80},{80,96},{96,112},{112,0},{1... | collective-permute-start | bytes 983048 | tf_op jit(solution)/shard_map/ppermute | solution.py:22
  18.1 4.0 %collective-permute-done.2.left.f_left = bf16[20,64,128]{2,1,0:T(8,128)(2,1)S(1)} collective-permute-done((bf16[20,64,128]{2,1,0:T(8,128)(2,1)S(1)}, bf16[20,64,128]{2,1,0:T(8,128)(2,1)S(1)}, u32[]{:S(2)}, u32[]{:S(2)}) %collective-permute-start.2) | collective-permute-done | bytes 327712 | tf_op jit(solution)/shard_map/ppermute | solution.py:22
  22.1 2.9 %collective-permute-done.3.right.f_right = bf16[20,64,128]{2,1,0:T(8,128)(2,1)S(1)} collective-permute-done((bf16[20,64,128]{2,1,0:T(8,128)(2,1)S(1)}, bf16[20,64,128]{2,1,0:T(8,128)(2,1)S(1)}, u32[]{:S(2)}, u32[]{:S(2)}) %collective-permute-start.3) | collective-permute-done | bytes 327712 | tf_op jit(solution)/shard_map/ppermute | solution.py:22
  25.0 7.7 %forward_kernel.1 = (bf16[6,6,64,128]{3,2,1,0:T(8,128)(2,1)}, bf16[6,6,64,128]{3,2,1,0:T(8,128)(2,1)}, bf16[6,6,64,128]{3,2,1,0:T(8,128)(2,1)}, bf16[4,4,64,128]...) custom-call(s32[1]{0:T(128)} %bitcast.2.core, bf16[4,4,64,128]{3,2,1,0:T(8,128)(2,1)S(1)} %copy-done.2, ...), custom_call_target="tpu_custom_call" | custom-call | flops 135895456 | bytes 150733 | tf_op jit(solution)/shard_map/forward_kernel/pallas_call | solution.py:371
  34.2 3.5 %collective-permute-start.5 = (bf16[2,2,32,128]{3,2,1,0:T(8,128)(2,1)S(1)}, bf16[2,2,32,128]{3,2,1,0:T(8,128)(2,1)S(1)}, u32[]{:S(2)}, u32[]{:S(2)}) collective-permute-start(bf16[2,2,32,128]{3,2,1,0:T(8,128)(2,1)S(1)} %get-tuple-element.50.own), channel_id=1, source_target_pairs={{0,15},{1,0},{2,1},{3,2},{4,3},{5,4},{6,5},{7,6},{8,7},{9,8},{10,9... | collective-permute-start | bytes 98312 | tf_op jit(solution)/shard_map/ppermute | solution.py:22
  38.9 2.6 %collective-permute-start.6 = (bf16[2,6,32,128]{3,2,1,0:T(8,128)(2,1)S(1)}, bf16[2,6,32,128]{3,2,1,0:T(8,128)(2,1)S(1)}, u32[]{:S(2)}, u32[]{:S(2)}) collective-permute-start(bf16[2,6,32,128]{3,2,1,0:T(8,128)(2,1)S(1)} %get-tuple-element.51), channel_id=1, source_target_pairs={{0,16},{16,32},{32,48},{48,64},{64,80},{80,96},{96,112},{112,0},{1... | collective-permute-start | bytes 294920 | tf_op jit(solution)/shard_map/ppermute | solution.py:22
  45.6 4.1 %bottom_kernel.1 = (bf16[2,2,32,256]{3,2,1,0:T(8,128)(2,1)}, bf16[24,32,128]{2,1,0:T(8,128)(2,1)S(1)}, bf16[4,4,64,128]{3,2,1,0:T(8,128)(2,1)S(1)}, bf16[4,2,64,...) custom-call(bf16[2,2,32,128]{3,2,1,0:T(8,128)(2,1)S(1)} %get-tuple-element.50.own, ...), custom_call_target="tpu_custom_call" | custom-call | flops 45298484 | bytes 181862 | tf_op jit(solution)/shard_map/bottom_kernel/pallas_call | solution.py:371
  49.8 5.1 %collective-permute-start.11 = (bf16[4,2,64,128]{3,2,1,0:T(8,128)(2,1)S(1)}, bf16[4,2,64,128]{3,2,1,0:T(8,128)(2,1)S(1)}, u32[]{:S(2)}, u32[]{:S(2)}) collective-permute-start(bf16[4,2,64,128]{3,2,1,0:T(8,128)(2,1)S(1)} %get-tuple-element.59), channel_id=1, source_target_pairs={{0,15},{1,0},{2,1},{3,2},{4,3},{5,4},{6,5},{7,6},{8,7},{9,8},{10,9... | collective-permute-start | bytes 393224 | tf_op jit(solution)/shard_map/ppermute | solution.py:22
  55.3 3.2 %collective-permute-done.10.before = bf16[4,2,64,128]{3,2,1,0:T(8,128)(2,1)S(1)} collective-permute-done((bf16[4,2,64,128]{3,2,1,0:T(8,128)(2,1)S(1)}, bf16[4,2,64,128]{3,2,1,0:T(8,128)(2,1)S(1)}, u32[]{:S(2)}, u32[]{:S(2)}) %collective-permute-start.10) | collective-permute-done | bytes 131104 | tf_op jit(solution)/shard_map/ppermute | solution.py:22
  59.3 2.9 %collective-permute-start.12 = (bf16[24,32,128]{2,1,0:T(8,128)(2,1)S(1)}, bf16[24,32,128]{2,1,0:T(8,128)(2,1)S(1)}, u32[]{:S(2)}, u32[]{:S(2)}) collective-permute-start(bf16[24,32,128]{2,1,0:T(8,128)(2,1)S(1)} %get-tuple-element.62.own), channel_id=1, source_target_pairs={{0,16},{16,0},{1,17},{17,1},{2,18},{18,2},{3,19},{19,3},{4,20},{20... | collective-permute-start | bytes 589832 | tf_op jit(solution)/shard_map/ppermute | solution.py:26
  65.4 5.0 %first_errors_kernel.1 = (bf16[6,6,64,128]{3,2,1,0:T(8,128)(2,1)}, bf16[4,4,64,128]{3,2,1,0:T(8,128)(2,1)S(1)}, bf16[4,4,64,128]{3,2,1,0:T(8,128)(2,1)S(1)}) custom-call(s32[1]{0:T(128)} %bitcast.2.core, bf16[4,4,64,128]{3,2,1,0:T(8,128)(2,1)S(1)} %get-tuple-element.57.own, bf16[4,2,64,128]{3,2,1,0:T(8,128)(2,1)S(1)} %collective-permute-done.10.before, ...), custom_call_target="tpu_custom_call" | custom-call | flops 90596968 | bytes 126157 | tf_op jit(solution)/shard_map/first_errors_kernel/pallas_call | solution.py:371
  71.4 2.1 %own_grads_kernel.1.own_total = f32[1152,384]{1,0:T(8,128)S(1)} custom-call(bf16[6,6,64,128]{3,2,1,0:T(8,128)(2,1)S(1)} %copy-done.3, bf16[4,4,64,128]{3,2,1,0:T(8,128)(2,1)S(1)} %get-tuple-element.69.errors), custom_call_target="tpu_custom_call" | custom-call | flops 45298484 | bytes 42598 | tf_op jit(solution)/shard_map/own_grads_kernel/pallas_call | solution.py:371
  73.5 3.5 %pair_grads_kernel.1 = bf16[64,112,128]{2,1,0:T(8,128)(2,1)} custom-call(bf16[6,6,64,128]{3,2,1,0:T(8,128)(2,1)S(1)} %collective-permute-done.9.fields, bf16[4,4,64,128]{3,2,1,0:T(8,128)(2,1)S(1)} %collective-permute-done.15.errors, f32[1152,384]{1,0:T(8,128)S(1)} %own_grads_kernel.1.own_total, bf16[64,56,128]{2,1,0:T(8,128)(2,1)S(1)} %bottom_grads_kernel.1.three), custom_call_target="tpu_custom_call" | custom-call | flops 45298484 | bytes 176947 | tf_op jit(solution)/shard_map/pair_grads_kernel/pallas_call | solution.py:371
  77.0 9.6 %all-to-all-start.1 = ((bf16[64,112,128]{2,1,0:T(8,128)(2,1)}), bf16[64,112,128]{2,1,0:T(8,128)(2,1)S(1)}, u32[]{:S(2)}, u32[]{:S(2)}) async-start(bf16[64,112,128]{2,1,0:T(8,128)(2,1)} %pair_grads_kernel.1), calls=%async_computation.1 | async-start | bytes 3670016 | tf_op jit(solution)/shard_map/all_to_all | solution.py:454
  86.6 2.8 %input_kernel.1 = bf16[4,4,64,128]{3,2,1,0:T(8,128)(2,1)} custom-call(bf16[6,6,64,128]{3,2,1,0:T(8,128)(2,1)S(1)} %copy-done.4, bf16[27,128,128]{2,1,0:T(8,128)(2,1)S(1)} %bitcast.40), custom_call_target="tpu_custom_call" | custom-call | flops 45298484 | bytes 73728 | tf_op jit(solution)/shard_map/input_kernel/pallas_call | solution.py:371
  89.4 22.1 %all-to-all-done.1.pieces = bf16[64,112,128]{2,1,0:T(8,128)(2,1)S(1)} async-done(((bf16[64,112,128]{2,1,0:T(8,128)(2,1)}), bf16[64,112,128]{2,1,0:T(8,128)(2,1)S(1)}, u32[]{:S(2)}, u32[]{:S(2)}) %all-to-all-start.1) | async-done | bytes 1835040 | tf_op jit(solution)/shard_map/all_to_all | solution.py:454
  112.7 6.1 %all-to-all-start.2 = ((bf16[64,56,128]{2,1,0:T(8,128)(2,1)}), bf16[64,56,128]{2,1,0:T(8,128)(2,1)S(1)}, u32[]{:S(2)}, u32[]{:S(2)}) async-start(bf16[64,56,128]{2,1,0:T(8,128)(2,1)} %get-tuple-element.74), calls=%async_computation.2 | async-start | bytes 1835008 | tf_op jit(solution)/shard_map/all_to_all | solution.py:461
  122.9 2.6 %collective-permute-start.18 = (bf16[2,56,128]{2,1,0:T(8,128)(2,1)S(1)}, bf16[2,56,128]{2,1,0:T(8,128)(2,1)S(1)}, u32[]{:S(2)}, u32[]{:S(2)}) collective-permute-start(bf16[2,56,128]{2,1,0:T(8,128)(2,1)S(1)} %maximum_select_fusion.1.pair_0), channel_id=1, source_target_pairs={{0,64},{32,96},{64,0},{96,32},{1,65},{33,97},{65,1},{97,33},{2,66}... | collective-permute-start | bytes 86024 | tf_op jit(solution)/shard_map/ppermute | solution.py:30
  126.5 4.8 %collective-permute-done.17.pair_1 = bf16[2,56,128]{2,1,0:T(8,128)(2,1)S(1)} collective-permute-done((bf16[2,56,128]{2,1,0:T(8,128)(2,1)S(1)}, bf16[2,56,128]{2,1,0:T(8,128)(2,1)S(1)}, u32[]{:S(2)}, u32[]{:S(2)}) %collective-permute-start.17) | collective-permute-done | bytes 28704 | tf_op jit(solution)/shard_map/ppermute | solution.py:30
  133.7 3.9 %collective-permute-start.20 = (bf16[3584,128]{1,0:T(8,128)(2,1)S(1)}, bf16[3584,128]{1,0:T(8,128)(2,1)S(1)}, u32[]{:S(2)}, u32[]{:S(2)}) collective-permute-start(bf16[3584,128]{1,0:T(8,128)(2,1)S(1)} %bitcast.37), channel_id=1, source_target_pairs={{0,16},{16,0},{1,17},{17,1},{2,18},{18,2},{3,19},{19,3},{4,20},{20... | collective-permute-start | bytes 2752520 | tf_op jit(solution)/shard_map/ppermute | solution.py:26
  137.5 2.1 %collective-permute-done.20.other = bf16[3584,128]{1,0:T(8,128)(2,1)S(1)} collective-permute-done((bf16[3584,128]{1,0:T(8,128)(2,1)S(1)}, bf16[3584,128]{1,0:T(8,128)(2,1)S(1)}, u32[]{:S(2)}, u32[]{:S(2)}) %collective-permute-start.20) | collective-permute-done | bytes 917536 | tf_op jit(solution)/shard_map/ppermute | solution.py:26
  (63 shorter events, 26.6 us)
Async XLA Ops:
  2.5 13.4 %collective-permute-start = (bf16[5,2,64,128]{3,2,1,0:T(8,128)(2,1)S(1)}, bf16[5,2,64,128]{3,2,1,0:T(8,128)(2,1)S(1)}, u32[]{:S(2)}, u32[]{:S(2)}) collective-permute-start(bf16[5,2,64,128]{3,2,1,0:T(8,128)(2,1)S(1)} %pad_maximum_fusion.1), channel_id=1, source_target_pairs={{0,1},{1,2},{2,3},{3,4},{4,5},{5,6},{6,7},{7,8},{8,9},{9,10},{10,1... | collective-permute-start | bytes 491528 | tf_op jit(solution)/shard_map/ppermute | solution.py:22
  4.7 11.2 %collective-permute-start.1 = (bf16[5,2,64,128]{3,2,1,0:T(8,128)(2,1)S(1)}, bf16[5,2,64,128]{3,2,1,0:T(8,128)(2,1)S(1)}, u32[]{:S(2)}, u32[]{:S(2)}) collective-permute-start(bf16[5,2,64,128]{3,2,1,0:T(8,128)(2,1)S(1)} %pad_maximum_fusion), channel_id=1, source_target_pairs={{0,15},{1,0},{2,1},{3,2},{4,3},{5,4},{6,5},{7,6},{8,7},{9,8},{10,9... | collective-permute-start | bytes 491528 | tf_op jit(solution)/shard_map/ppermute | solution.py:22
  11.6 21.1 %all-to-all-start = ((bf16[16,27,8,128]{3,2,1,0:T(8,128)(2,1)}), bf16[16,27,8,128]{3,2,1,0:T(8,128)(2,1)}, u32[]{:S(2)}, u32[]{:S(2)}) async-start(bf16[16,27,8,128]{3,2,1,0:T(8,128)(2,1)} %broadcast_in_dim.3), calls=%async_computation | async-start | bytes 1769472 | tf_op jit(solution)/shard_map/all_to_all | solution.py:401
  16.0 6.1 %collective-permute-start.2 = (bf16[20,64,128]{2,1,0:T(8,128)(2,1)S(1)}, bf16[20,64,128]{2,1,0:T(8,128)(2,1)S(1)}, u32[]{:S(2)}, u32[]{:S(2)}) collective-permute-start(bf16[20,64,128]{2,1,0:T(8,128)(2,1)S(1)} %get-tuple-element.47), channel_id=1, source_target_pairs={{0,16},{16,32},{32,48},{48,64},{64,80},{80,96},{96,112},{112,0},{1... | collective-permute-start | bytes 983048 | tf_op jit(solution)/shard_map/ppermute | solution.py:22
  18.1 6.9 %collective-permute-start.3 = (bf16[20,64,128]{2,1,0:T(8,128)(2,1)S(1)}, bf16[20,64,128]{2,1,0:T(8,128)(2,1)S(1)}, u32[]{:S(2)}, u32[]{:S(2)}) collective-permute-start(bf16[20,64,128]{2,1,0:T(8,128)(2,1)S(1)} %get-tuple-element.48), channel_id=1, source_target_pairs={{0,112},{16,0},{32,16},{48,32},{64,48},{80,64},{96,80},{112,96},{1... | collective-permute-start | bytes 983048 | tf_op jit(solution)/shard_map/ppermute | solution.py:22
  32.6 8.9 %collective-permute-start.8 = (bf16[16,27,8,128]{3,2,1,0:T(8,128)(2,1)}, bf16[16,27,8,128]{3,2,1,0:T(8,128)(2,1)S(1)}, u32[]{:S(2)}, u32[]{:S(2)}) collective-permute-start(bf16[16,27,8,128]{3,2,1,0:T(8,128)(2,1)} %all-to-all-done), channel_id=1, source_target_pairs={{0,16},{16,0},{1,17},{17,1},{2,18},{18,2},{3,19},{19,3},{4,20},{20... | collective-permute-start | bytes 2654216 | tf_op jit(solution)/shard_map/ppermute | solution.py:26
  32.6 6.2 %collective-permute-start.4 = (bf16[2,2,32,128]{3,2,1,0:T(8,128)(2,1)S(1)}, bf16[2,2,32,128]{3,2,1,0:T(8,128)(2,1)S(1)}, u32[]{:S(2)}, u32[]{:S(2)}) collective-permute-start(bf16[2,2,32,128]{3,2,1,0:T(8,128)(2,1)S(1)} %get-tuple-element.50.own), channel_id=1, source_target_pairs={{0,1},{1,2},{2,3},{3,4},{4,5},{5,6},{6,7},{7,8},{8,9},{9,10},{10,1... | collective-permute-start | bytes 98312 | tf_op jit(solution)/shard_map/ppermute | solution.py:22
  34.2 4.7 %collective-permute-start.5 = (bf16[2,2,32,128]{3,2,1,0:T(8,128)(2,1)S(1)}, bf16[2,2,32,128]{3,2,1,0:T(8,128)(2,1)S(1)}, u32[]{:S(2)}, u32[]{:S(2)}) collective-permute-start(bf16[2,2,32,128]{3,2,1,0:T(8,128)(2,1)S(1)} %get-tuple-element.50.own), channel_id=1, source_target_pairs={{0,15},{1,0},{2,1},{3,2},{4,3},{5,4},{6,5},{7,6},{8,7},{9,8},{10,9... | collective-permute-start | bytes 98312 | tf_op jit(solution)/shard_map/ppermute | solution.py:22
  38.9 4.9 %collective-permute-start.6 = (bf16[2,6,32,128]{3,2,1,0:T(8,128)(2,1)S(1)}, bf16[2,6,32,128]{3,2,1,0:T(8,128)(2,1)S(1)}, u32[]{:S(2)}, u32[]{:S(2)}) collective-permute-start(bf16[2,6,32,128]{3,2,1,0:T(8,128)(2,1)S(1)} %get-tuple-element.51), channel_id=1, source_target_pairs={{0,16},{16,32},{32,48},{48,64},{64,80},{80,96},{96,112},{112,0},{1... | collective-permute-start | bytes 294920 | tf_op jit(solution)/shard_map/ppermute | solution.py:22
  41.5 4.0 %collective-permute-start.7 = (bf16[2,6,32,128]{3,2,1,0:T(8,128)(2,1)S(1)}, bf16[2,6,32,128]{3,2,1,0:T(8,128)(2,1)S(1)}, u32[]{:S(2)}, u32[]{:S(2)}) collective-permute-start(bf16[2,6,32,128]{3,2,1,0:T(8,128)(2,1)S(1)} %get-tuple-element.52), channel_id=1, source_target_pairs={{0,112},{16,0},{32,16},{48,32},{64,48},{80,64},{96,80},{112,96},{1... | collective-permute-start | bytes 294920 | tf_op jit(solution)/shard_map/ppermute | solution.py:22
  49.7 8.9 %collective-permute-start.10 = (bf16[4,2,64,128]{3,2,1,0:T(8,128)(2,1)S(1)}, bf16[4,2,64,128]{3,2,1,0:T(8,128)(2,1)S(1)}, u32[]{:S(2)}, u32[]{:S(2)}) collective-permute-start(bf16[4,2,64,128]{3,2,1,0:T(8,128)(2,1)S(1)} %get-tuple-element.58), channel_id=1, source_target_pairs={{0,1},{1,2},{2,3},{3,4},{4,5},{5,6},{6,7},{7,8},{8,9},{9,10},{10,1... | collective-permute-start | bytes 393224 | tf_op jit(solution)/shard_map/ppermute | solution.py:22
  49.8 8.8 %collective-permute-start.11 = (bf16[4,2,64,128]{3,2,1,0:T(8,128)(2,1)S(1)}, bf16[4,2,64,128]{3,2,1,0:T(8,128)(2,1)S(1)}, u32[]{:S(2)}, u32[]{:S(2)}) collective-permute-start(bf16[4,2,64,128]{3,2,1,0:T(8,128)(2,1)S(1)} %get-tuple-element.59), channel_id=1, source_target_pairs={{0,15},{1,0},{2,1},{3,2},{4,3},{5,4},{6,5},{7,6},{8,7},{9,8},{10,9... | collective-permute-start | bytes 393224 | tf_op jit(solution)/shard_map/ppermute | solution.py:22
  54.9 18.6 %collective-permute-start.9 = (bf16[6,6,64,128]{3,2,1,0:T(8,128)(2,1)S(1)}, bf16[6,6,64,128]{3,2,1,0:T(8,128)(2,1)S(1)}, u32[]{:S(2)}, u32[]{:S(2)}) collective-permute-start(bf16[6,6,64,128]{3,2,1,0:T(8,128)(2,1)S(1)} %copy-done.7), channel_id=1, source_target_pairs={{0,16},{16,0},{1,17},{17,1},{2,18},{18,2},{3,19},{19,3},{4,20},{20... | collective-permute-start | bytes 1769480 | tf_op jit(solution)/shard_map/ppermute | solution.py:26
  58.6 6.8 %collective-permute-start.13 = (bf16[2,8,64,128]{3,2,1,0:T(8,128)(2,1)S(1)}, bf16[2,8,64,128]{3,2,1,0:T(8,128)(2,1)S(1)}, u32[]{:S(2)}, u32[]{:S(2)}) collective-permute-start(bf16[2,8,64,128]{3,2,1,0:T(8,128)(2,1)S(1)} %get-tuple-element.61), channel_id=1, source_target_pairs={{0,16},{16,32},{32,48},{48,64},{64,80},{80,96},{96,112},{112,0},{1... | collective-permute-start | bytes 786440 | tf_op jit(solution)/shard_map/ppermute | solution.py:22
  58.9 6.5 %collective-permute-start.14 = (bf16[2,8,64,128]{3,2,1,0:T(8,128)(2,1)S(1)}, bf16[2,8,64,128]{3,2,1,0:T(8,128)(2,1)S(1)}, u32[]{:S(2)}, u32[]{:S(2)}) collective-permute-start(bf16[2,8,64,128]{3,2,1,0:T(8,128)(2,1)S(1)} %get-tuple-element.63), channel_id=1, source_target_pairs={{0,112},{16,0},{32,16},{48,32},{64,48},{80,64},{96,80},{112,96},{1... | collective-permute-start | bytes 786440 | tf_op jit(solution)/shard_map/ppermute | solution.py:22
  59.3 4.0 %collective-permute-start.12 = (bf16[24,32,128]{2,1,0:T(8,128)(2,1)S(1)}, bf16[24,32,128]{2,1,0:T(8,128)(2,1)S(1)}, u32[]{:S(2)}, u32[]{:S(2)}) collective-permute-start(bf16[24,32,128]{2,1,0:T(8,128)(2,1)S(1)} %get-tuple-element.62.own), channel_id=1, source_target_pairs={{0,16},{16,0},{1,17},{17,1},{2,18},{18,2},{3,19},{19,3},{4,20},{20... | collective-permute-start | bytes 589832 | tf_op jit(solution)/shard_map/ppermute | solution.py:26
  70.4 3.0 %collective-permute-start.15 = (bf16[4,4,64,128]{3,2,1,0:T(8,128)(2,1)S(1)}, bf16[4,4,64,128]{3,2,1,0:T(8,128)(2,1)S(1)}, u32[]{:S(2)}, u32[]{:S(2)}) collective-permute-start(bf16[4,4,64,128]{3,2,1,0:T(8,128)(2,1)S(1)} %get-tuple-element.67), channel_id=1, source_target_pairs={{0,16},{16,0},{1,17},{17,1},{2,18},{18,2},{3,19},{19,3},{4,20},{20... | collective-permute-start | bytes 786440 | tf_op jit(solution)/shard_map/ppermute | solution.py:26
  77.0 34.5 %all-to-all-start.1 = ((bf16[64,112,128]{2,1,0:T(8,128)(2,1)}), bf16[64,112,128]{2,1,0:T(8,128)(2,1)S(1)}, u32[]{:S(2)}, u32[]{:S(2)}) async-start(bf16[64,112,128]{2,1,0:T(8,128)(2,1)} %pair_grads_kernel.1), calls=%async_computation.1 | async-start | bytes 3670016 | tf_op jit(solution)/shard_map/all_to_all | solution.py:454
  112.7 21.0 %all-to-all-start.2 = ((bf16[64,56,128]{2,1,0:T(8,128)(2,1)}), bf16[64,56,128]{2,1,0:T(8,128)(2,1)S(1)}, u32[]{:S(2)}, u32[]{:S(2)}) async-start(bf16[64,56,128]{2,1,0:T(8,128)(2,1)} %get-tuple-element.74), calls=%async_computation.2 | async-start | bytes 1835008 | tf_op jit(solution)/shard_map/all_to_all | solution.py:461
  118.8 2.7 %collective-permute-start.16 = (bf16[56,128]{1,0:T(8,128)(2,1)S(1)}, bf16[56,128]{1,0:T(8,128)(2,1)S(1)}, u32[]{:S(2)}, u32[]{:S(2)}) collective-permute-start(bf16[56,128]{1,0:T(8,128)(2,1)S(1)} %get-tuple-element.76), channel_id=1, source_target_pairs={{0,16},{16,0},{1,17},{17,1},{2,18},{18,2},{3,19},{19,3},{4,20},{20... | collective-permute-start | bytes 43016 | tf_op jit(solution)/shard_map/ppermute | solution.py:26
  121.5 9.8 %collective-permute-start.17 = (bf16[2,56,128]{2,1,0:T(8,128)(2,1)S(1)}, bf16[2,56,128]{2,1,0:T(8,128)(2,1)S(1)}, u32[]{:S(2)}, u32[]{:S(2)}) collective-permute-start(bf16[2,56,128]{2,1,0:T(8,128)(2,1)S(1)} %maximum_select_fusion.1.pair_0), channel_id=1, source_target_pairs={{0,32},{32,64},{64,96},{96,0},{1,33},{33,65},{65,97},{97,1},{2,34}... | collective-permute-start | bytes 86024 | tf_op jit(solution)/shard_map/ppermute | solution.py:30
  122.9 8.4 %collective-permute-start.18 = (bf16[2,56,128]{2,1,0:T(8,128)(2,1)S(1)}, bf16[2,56,128]{2,1,0:T(8,128)(2,1)S(1)}, u32[]{:S(2)}, u32[]{:S(2)}) collective-permute-start(bf16[2,56,128]{2,1,0:T(8,128)(2,1)S(1)} %maximum_select_fusion.1.pair_0), channel_id=1, source_target_pairs={{0,64},{32,96},{64,0},{96,32},{1,65},{33,97},{65,1},{97,33},{2,66}... | collective-permute-start | bytes 86024 | tf_op jit(solution)/shard_map/ppermute | solution.py:30
  125.5 5.8 %collective-permute-start.19 = (bf16[2,56,128]{2,1,0:T(8,128)(2,1)S(1)}, bf16[2,56,128]{2,1,0:T(8,128)(2,1)S(1)}, u32[]{:S(2)}, u32[]{:S(2)}) collective-permute-start(bf16[2,56,128]{2,1,0:T(8,128)(2,1)S(1)} %maximum_select_fusion.1.pair_0), channel_id=1, source_target_pairs={{0,96},{32,0},{64,32},{96,64},{1,97},{33,1},{65,33},{97,65},{2,98}... | collective-permute-start | bytes 86024 | tf_op jit(solution)/shard_map/ppermute | solution.py:30
  133.7 6.0 %collective-permute-start.20 = (bf16[3584,128]{1,0:T(8,128)(2,1)S(1)}, bf16[3584,128]{1,0:T(8,128)(2,1)S(1)}, u32[]{:S(2)}, u32[]{:S(2)}) collective-permute-start(bf16[3584,128]{1,0:T(8,128)(2,1)S(1)} %bitcast.37), channel_id=1, source_target_pairs={{0,16},{16,0},{1,17},{17,1},{2,18},{18,2},{3,19},{19,3},{4,20},{20... | collective-permute-start | bytes 2752520 | tf_op jit(solution)/shard_map/ppermute | solution.py:26
  (8 other events, 91.8 us)

commit v9 on v8

--- a/solution.py
+++ b/solution.py
@@ -64,7 +64,7 @@
     size_x, size_y, size_z, chans = own.shape
     slab = (width, size_y + 2 * width, size_z, chans)
     low, high = call(slab_kernel, [(slab, BF16)] * 2, [], 0, own, before, after)
-    return (own, before, after, *exchange_x(low, high)), high
+    return own, before, after, *exchange_x(low, high)
 
 
 def fill_padded(padded, own, before, after, left, right):
@@ -184,7 +184,7 @@
 
 
 def bottom_kernel(own, before, after, left, right, g_own, f_before, f_after, f_left, f_right,
-                  taps_three, slope_two, skip, bottleneck, bundle, err_two, err_first, err_last,
+                  taps_three, slope_two, skip, bottleneck, bundle, err_two, err_near, err_first, err_last,
                   padded, grads, packed, errors, wide):
     fill_padded(padded, own, before, after, left, right)
     for half in range(2):
@@ -231,6 +231,7 @@
                     err = skip[at].astype(F32) + wide[...]
                     err = (err * slope_two[at].astype(F32)).astype(BF16)
                     err_two[at] = err
+                    err_near[at] = err
                     edge = err_first if at_y == 0 else err_last
                     edge[2 * row + dx, dy] = err
 
@@ -248,22 +249,16 @@
     add_tap_grads(total, fields, errors)
 
 
-def pair_grads_kernel(fields, errors, own_total, three, out, total):
+def pair_grads_kernel(fields, errors, own_total, out, total):
     total[...] = own_total[...]
     add_tap_grads(total, fields, errors)
     for at in range(9):
         for kz in range(3):
-            start = (at * 3 + kz) * 128
-            done = 0
-            while done < 128:
-                piece, row = divmod(start + done, PIECE)
-                size = min(PIECE - row, 128 - done)
-                rows = slice(at * 128 + done, at * 128 + done + size)
-                out[piece, row : row + size] = total[rows, kz * 128 : kz * 128 + 128].astype(BF16)
-                done += size
-    out[61, 40:PIECE] = jnp.zeros((PIECE - 40, 128), BF16)
-    out[62:64, 0:PIECE] = jnp.zeros((2, PIECE, 128), BF16)
-    out[:, PIECE : 2 * PIECE] = three[...]
+            rows = (at * 3 + kz) * 128
+            out[rows : rows + 128] = total[
+                at * 128 : at * 128 + 128, kz * 128 : kz * 128 + 128
+            ].astype(BF16)
+    out[3456:3584] = jnp.zeros((128, 128), BF16)
 
 
 def bottom_grads_kernel(core, own, other, out, total):
@@ -326,14 +321,13 @@
     lax.fori_loop(0, 4, step, 0)
 
 
-def sum_kernel(pieces, out, three):
+def sum_kernel(pieces, out):
     total = pieces[0].astype(F32)
     for at in range(1, 64):
         total = total + pieces[at].astype(F32)
     total = total.astype(BF16)
-    three[...] = total[PIECE : 2 * PIECE]
-    for at in range(64):
-        out[at] = total[0:PIECE]
+    for at in range(out.shape[0]):
+        out[at] = total
 
 
 def place_kernel(chip, pair_0, pair_1, pair_2, pair_3, out, *, scale):
@@ -422,37 +416,42 @@
     theirs = swap_cores(mine)
     both = jnp.where(first_core, jnp.stack([mine, theirs]), jnp.stack([theirs, mine]))
     taps_three = jnp.transpose(both, (2, 1, 0, 3, 4)).reshape(27, 256, 128)
-    p_pieces, _ = halo_pieces(pooled, 2, pooled, pooled)
-    bottleneck, bundle, err_two, err_first, err_last = call(
+    p_pieces = halo_pieces(pooled, 2, pooled, pooled)
+    bottleneck, bundle, err_two, err_near, err_first, err_last = call(
         bottom_kernel,
-        [((2, 2, 32, 256), BF16, True), ((24, 32, 128), BF16), (block, BF16), (edge, BF16), (edge, BF16)],
+        [((2, 2, 32, 256), BF16, True), ((24, 32, 128), BF16), (block, BF16, True), (block, BF16), (edge, BF16), (edge, BF16)],
         [((6, 6, 32, 128), BF16), ((4, 4, 32, 256), BF16), ((768, 1152), BF16),
          ((4, 4, 32, 256), BF16), ((64, 128), F32)],
         conv_flops, *p_pieces, bottom_grad, f_before, f_after, f_left, f_right,
         taps_three, in_hbm(slope_two), in_hbm(skip_grad),
     )
-    e_pieces, e_high = halo_pieces(err_two, 2, err_first, err_last)
-    bundle, e_high = lax.optimization_barrier((bundle, e_high))
     (three,) = call(
-        bottom_grads_kernel, [((64, PIECE, 128), BF16)], [((768, 1152), F32)],
+        bottom_grads_kernel, [((64, PIECE, 128), BF16, True)], [((768, 1152), F32)],
         conv_flops // 2, core_ref, bundle, swap_cores(bundle),
     )
-    three, *e_ends = lax.optimization_barrier((three, *e_pieces[3:]))
+    e_before, e_after = shifted(err_last, GY, 1), shifted(err_first, GY, -1)
+    three, e_before, e_after = lax.optimization_barrier((three, e_before, e_after))
+    low, high = call(slab_kernel, [((2, 8, 64, 128), BF16)] * 2, [], 0, err_near, e_before, e_after)
+    three_pieces = lax.all_to_all(three, FLAT, 0, 0)
     err_one, err_keep, err_send = call(
         first_errors_kernel, [(field, BF16, True), (block, BF16), (block, BF16)],
         [((8, 8, 64, 128), BF16), ((384, 1152), BF16)],
-        2 * conv_flops, core_ref, *e_pieces[:3], *e_ends, taps_two, slope_one,
+        10**11, core_ref, in_hbm(err_two), e_before, e_after, *exchange_x(low, high),
+        taps_two, in_hbm(slope_one),
     )
     err_other = swap_cores(err_send)
     (total,) = call(own_grads_kernel, [((1152, 384), F32)], [], conv_flops, field_keep, err_keep)
     (kept,) = call(
-        pair_grads_kernel, [((64, 2 * PIECE, 128), BF16, True)], [((1152, 384), F32)],
-        conv_flops, field_other, err_other, total, three,
-    )
-    part, three_part = call(
-        sum_kernel, [((64, PIECE, 128), BF16, True), ((PIECE, 128), BF16)], [], 0,
-        lax.all_to_all(kept, FLAT, 0, 0),
-    )
+        pair_grads_kernel, [((3584, 128), BF16, True)], [((1152, 384), F32)],
+        conv_flops, field_other, err_other, total,
+    )
+    kept, three_pieces = lax.optimization_barrier((kept, three_pieces))
+    kept = kept.reshape(64, PIECE, 128)
+    (part,) = call(
+        sum_kernel, [((64, PIECE, 128), BF16, True)], [], 0, lax.all_to_all(kept, FLAT, 0, 0)
+    )
+    (three_part,) = call(sum_kernel, [((1, PIECE, 128), BF16)], [], 0, three_pieces)
+    three_part = three_part[0]
     (input_grad,) = call(
         input_kernel, [(block, BF16, True)], [((384, 1152), BF16)],
         conv_flops, err_one, taps_one,

time: 142 us -> 140 us (0.986)
  waiting for transfers between devices: 45.6 us -> 35.2 us
  starting transfers between devices: 57.9 us -> 62.3 us
  Pallas kernels: 31.3 us -> 34.6 us
    all_to_all x0 -> x1, starting transfers between devices: none -> 9.79 us  [on_device(): three_pieces = lax.all_to_all(three, FLAT, 0, 0)]
    all_to_all x1, waiting for transfers between devices: 22.1 us -> 12.8 us  [on_device(): lax.all_to_all(kept, FLAT, 0, 0)]
    pallas_call x11 -> x12, Pallas kernels: 28.5 us -> 31.8 us  [call(): pl.pallas_call(kernel, out_shape=shapes, in_specs=[pl.BlockSpec(memory_sp...]
    ppermute x6, starting transfers between devices: 10 us -> 6.96 us  [swap_cores(): return lax.ppermute(array, 'c', [(0, 1), (1, 0)])]
    all_to_all x0 -> x1, waiting for transfers between devices: none -> 2.77 us  [on_device(): three_pieces = lax.all_to_all(three, FLAT, 0, 0)]
    ppermute x12, waiting for transfers between devices: 13.2 us -> 10.5 us  [shifted(): lax.ppermute(array, axes, [(i, (i + step) % count) for i in range(count)])]
    all_to_all x1, starting transfers between devices: 9.55 us -> 7.42 us  [on_device(): lax.all_to_all(kept, FLAT, 0, 0)]
  transfers between devices with their start and end apart: 24 -> 25, of which waited for: 11 -> 11; matrix products, arithmetic and copies ran while one was open for 3% -> 3% of each run, Pallas kernels for 14% -> 19%
where the time goes in v9:
time: 140 us; the launch traced here: 139 us
  starting transfers between devices  62.3 us (44%)
  waiting for transfers between devices  35.2 us (25%)
  Pallas kernels  34.6 us (25%)
  local copies, waits for them, and re-layouts  3.31 us (2%)
  other arithmetic  2.68 us (2%)
    pallas_call x12, Pallas kernels, call(): pl.pallas_call(kernel, out_shape=shapes, in_specs=[pl.BlockSpec(memory_sp...  31.8 us
    ppermute x12, starting transfers between devices, shifted(): lax.ppermute(array, axes, [(i, (i + step) % count) for i in range(count)])  23.5 us
    all_to_all x1, waiting for transfers between devices, on_device(): lax.all_to_all(kept, FLAT, 0, 0)  12.8 us
    ppermute x12, waiting for transfers between devices, shifted(): lax.ppermute(array, axes, [(i, (i + step) % count) for i in range(count)])  10.5 us
    all_to_all x1, starting transfers between devices, on_device(): three_pieces = lax.all_to_all(three, FLAT, 0, 0)  9.79 us
    all_to_all x1, starting transfers between devices, on_device(): lax.all_to_all(kept, FLAT, 0, 0)  7.42 us
    ppermute x6, starting transfers between devices, swap_cores(): return lax.ppermute(array, 'c', [(0, 1), (1, 0)])  6.96 us
    all_to_all x1, starting transfers between devices, on_device(): whole = lax.all_to_all(part, FLAT, 0, 0).reshape(64 * PIECE, 128)  5.24 us
  transfers between devices with their start and end apart: 25, of which 11 were waited for; matrix products, arithmetic and copies ran while one was open for 3% of the time, Pallas kernels for 19%

profile of v9, /device:TPU:1, one launch (start us, length us, event | category | flops | bytes accessed | tf_op | source)
XLA Modules:
  0.0 139.0 jit_solution(7917627858977868166)
XLA Ops:
  2.5 2.2 %collective-permute-start = (bf16[5,2,64,128]{3,2,1,0:T(8,128)(2,1)S(1)}, bf16[5,2,64,128]{3,2,1,0:T(8,128)(2,1)S(1)}, u32[]{:S(2)}, u32[]{:S(2)}) collective-permute-start(bf16[5,2,64,128]{3,2,1,0:T(8,128)(2,1)S(1)} %pad_maximum_fusion.1), channel_id=1, source_target_pairs={{0,1},{1,2},{2,3},{3,4},{4,5},{5,6},{6,7},{7,8},{8,9},{9,10},{10,1... | collective-permute-start | bytes 491528 | tf_op jit(solution)/shard_map/ppermute | solution.py:22
  4.7 5.0 %collective-permute-start.1 = (bf16[5,2,64,128]{3,2,1,0:T(8,128)(2,1)S(1)}, bf16[5,2,64,128]{3,2,1,0:T(8,128)(2,1)S(1)}, u32[]{:S(2)}, u32[]{:S(2)}) collective-permute-start(bf16[5,2,64,128]{3,2,1,0:T(8,128)(2,1)S(1)} %pad_maximum_fusion), channel_id=1, source_target_pairs={{0,15},{1,0},{2,1},{3,2},{4,3},{5,4},{6,5},{7,6},{8,7},{9,8},{10,9... | collective-permute-start | bytes 491528 | tf_op jit(solution)/shard_map/ppermute | solution.py:22
  11.6 4.3 %all-to-all-start = ((bf16[16,27,8,128]{3,2,1,0:T(8,128)(2,1)}), bf16[16,27,8,128]{3,2,1,0:T(8,128)(2,1)}, u32[]{:S(2)}, u32[]{:S(2)}) async-start(bf16[16,27,8,128]{3,2,1,0:T(8,128)(2,1)} %broadcast_in_dim.3), calls=%async_computation | async-start | bytes 1769472 | tf_op jit(solution)/shard_map/all_to_all | solution.py:395
  18.1 4.0 %collective-permute-done.2.left.f_left = bf16[20,64,128]{2,1,0:T(8,128)(2,1)S(1)} collective-permute-done((bf16[20,64,128]{2,1,0:T(8,128)(2,1)S(1)}, bf16[20,64,128]{2,1,0:T(8,128)(2,1)S(1)}, u32[]{:S(2)}, u32[]{:S(2)}) %collective-permute-start.2) | collective-permute-done | bytes 327712 | tf_op jit(solution)/shard_map/ppermute | solution.py:22
  22.1 2.9 %collective-permute-done.3.right.f_right = bf16[20,64,128]{2,1,0:T(8,128)(2,1)S(1)} collective-permute-done((bf16[20,64,128]{2,1,0:T(8,128)(2,1)S(1)}, bf16[20,64,128]{2,1,0:T(8,128)(2,1)S(1)}, u32[]{:S(2)}, u32[]{:S(2)}) %collective-permute-start.3) | collective-permute-done | bytes 327712 | tf_op jit(solution)/shard_map/ppermute | solution.py:22
  25.0 7.7 %forward_kernel.1 = (bf16[6,6,64,128]{3,2,1,0:T(8,128)(2,1)}, bf16[6,6,64,128]{3,2,1,0:T(8,128)(2,1)}, bf16[6,6,64,128]{3,2,1,0:T(8,128)(2,1)}, bf16[4,4,64,128]...) custom-call(s32[1]{0:T(128)} %bitcast.2.core, bf16[4,4,64,128]{3,2,1,0:T(8,128)(2,1)S(1)} %copy-done.1, ...), custom_call_target="tpu_custom_call" | custom-call | flops 135895456 | bytes 150733 | tf_op jit(solution)/shard_map/forward_kernel/pallas_call | solution.py:365
  34.2 3.5 %collective-permute-start.5 = (bf16[2,2,32,128]{3,2,1,0:T(8,128)(2,1)S(1)}, bf16[2,2,32,128]{3,2,1,0:T(8,128)(2,1)S(1)}, u32[]{:S(2)}, u32[]{:S(2)}) collective-permute-start(bf16[2,2,32,128]{3,2,1,0:T(8,128)(2,1)S(1)} %get-tuple-element.50.own), channel_id=1, source_target_pairs={{0,15},{1,0},{2,1},{3,2},{4,3},{5,4},{6,5},{7,6},{8,7},{9,8},{10,9... | collective-permute-start | bytes 98312 | tf_op jit(solution)/shard_map/ppermute | solution.py:22
  38.9 2.6 %collective-permute-start.6 = (bf16[2,6,32,128]{3,2,1,0:T(8,128)(2,1)S(1)}, bf16[2,6,32,128]{3,2,1,0:T(8,128)(2,1)S(1)}, u32[]{:S(2)}, u32[]{:S(2)}) collective-permute-start(bf16[2,6,32,128]{3,2,1,0:T(8,128)(2,1)S(1)} %get-tuple-element.51), channel_id=1, source_target_pairs={{0,16},{16,32},{32,48},{48,64},{64,80},{80,96},{96,112},{112,0},{1... | collective-permute-start | bytes 294920 | tf_op jit(solution)/shard_map/ppermute | solution.py:22
  45.6 4.7 %bottom_kernel.1 = (bf16[2,2,32,256]{3,2,1,0:T(8,128)(2,1)}, bf16[24,32,128]{2,1,0:T(8,128)(2,1)S(1)}, bf16[4,4,64,128]{3,2,1,0:T(8,128)(2,1)}, bf16[4,4,64,128]...) custom-call(bf16[2,2,32,128]{3,2,1,0:T(8,128)(2,1)S(1)} %get-tuple-element.50.own, ...), custom_call_target="tpu_custom_call" | custom-call | flops 45298484 | bytes 181862 | tf_op jit(solution)/shard_map/bottom_kernel/pallas_call | solution.py:365
  50.4 5.1 %collective-permute-start.12 = (bf16[4,2,64,128]{3,2,1,0:T(8,128)(2,1)S(1)}, bf16[4,2,64,128]{3,2,1,0:T(8,128)(2,1)S(1)}, u32[]{:S(2)}, u32[]{:S(2)}) collective-permute-start(bf16[4,2,64,128]{3,2,1,0:T(8,128)(2,1)S(1)} %get-tuple-element.60), channel_id=1, source_target_pairs={{0,15},{1,0},{2,1},{3,2},{4,3},{5,4},{6,5},{7,6},{8,7},{9,8},{10,9... | collective-permute-start | bytes 393224 | tf_op jit(solution)/shard_map/ppermute | solution.py:22
  55.5 3.0 %bottom_grads_kernel.1 = bf16[64,56,128]{2,1,0:T(8,128)(2,1)} custom-call(s32[1]{0:T(128)} %bitcast.2.core, bf16[24,32,128]{2,1,0:T(8,128)(2,1)S(1)} %get-tuple-element.58.own, bf16[24,32,128]{2,1,0:T(8,128)(2,1)S(1)} %collective-permute-done.10.other), custom_call_target="tpu_custom_call" | custom-call | flops 22649240 | bytes 19661 | tf_op jit(solution)/shard_map/bottom_grads_kernel/pallas_call | solution.py:365
  61.5 9.8 %all-to-all-start.1 = ((bf16[64,56,128]{2,1,0:T(8,128)(2,1)}), bf16[64,56,128]{2,1,0:T(8,128)(2,1)S(1)}, u32[]{:S(2)}, u32[]{:S(2)}) async-start(bf16[64,56,128]{2,1,0:T(8,128)(2,1)} %bottom_grads_kernel.1), calls=%async_computation.1 | async-start | bytes 1835008 | tf_op jit(solution)/shard_map/all_to_all | solution.py:435
  72.3 6.2 %first_errors_kernel.1 = (bf16[6,6,64,128]{3,2,1,0:T(8,128)(2,1)}, bf16[4,4,64,128]{3,2,1,0:T(8,128)(2,1)S(1)}, bf16[4,4,64,128]{3,2,1,0:T(8,128)(2,1)S(1)}) custom-call(s32[1]{0:T(128)} %bitcast.2.core, bf16[4,4,64,128]{3,2,1,0:T(8,128)(2,1)} %get-tuple-element.57.own, bf16[4,2,64,128]{3,2,1,0:T(8,128)(2,1)S(1)} %collective-permute-done.11.before, ...), custom_call_target="tpu_custom_call" | custom-call | flops 5000000000 | bytes 126157 | tf_op jit(solution)/shard_map/first_errors_kernel/pallas_call | solution.py:365
  78.6 2.1 %own_grads_kernel.1.own_total = f32[1152,384]{1,0:T(8,128)S(1)} custom-call(bf16[6,6,64,128]{3,2,1,0:T(8,128)(2,1)S(1)} %copy-done.3, bf16[4,4,64,128]{3,2,1,0:T(8,128)(2,1)S(1)} %get-tuple-element.69.errors), custom_call_target="tpu_custom_call" | custom-call | flops 45298484 | bytes 42598 | tf_op jit(solution)/shard_map/own_grads_kernel/pallas_call | solution.py:365
  80.7 3.1 %pair_grads_kernel.1 = bf16[3584,128]{1,0:T(8,128)(2,1)} custom-call(bf16[6,6,64,128]{3,2,1,0:T(8,128)(2,1)S(1)} %collective-permute-done.9.fields, bf16[4,4,64,128]{3,2,1,0:T(8,128)(2,1)S(1)} %collective-permute-done.15.errors, f32[1152,384]{1,0:T(8,128)S(1)} %own_grads_kernel.1.own_total), custom_call_target="tpu_custom_call" | custom-call | flops 45298484 | bytes 131072 | tf_op jit(solution)/shard_map/pair_grads_kernel/pallas_call | solution.py:365
  83.8 2.8 %all-to-all-done.1.pieces = bf16[64,56,128]{2,1,0:T(8,128)(2,1)S(1)} async-done(((bf16[64,56,128]{2,1,0:T(8,128)(2,1)}), bf16[64,56,128]{2,1,0:T(8,128)(2,1)S(1)}, u32[]{:S(2)}, u32[]{:S(2)}) %all-to-all-start.1) | async-done | bytes 917536 | tf_op jit(solution)/shard_map/all_to_all | solution.py:435
  86.6 7.4 %all-to-all-start.2 = ((bf16[64,56,128]{2,1,0:T(8,128)(2,1)}), bf16[64,56,128]{2,1,0:T(8,128)(2,1)S(1)}, u32[]{:S(2)}, u32[]{:S(2)}) async-start(bf16[64,56,128]{2,1,0:T(8,128)(2,1)} %bitcast.45), calls=%async_computation.2 | async-start | bytes 1835008 | tf_op jit(solution)/shard_map/all_to_all | solution.py:451
  94.0 2.8 %input_kernel.1 = bf16[4,4,64,128]{3,2,1,0:T(8,128)(2,1)} custom-call(bf16[6,6,64,128]{3,2,1,0:T(8,128)(2,1)S(1)} %copy-done.4, bf16[27,128,128]{2,1,0:T(8,128)(2,1)S(1)} %bitcast.41), custom_call_target="tpu_custom_call" | custom-call | flops 45298484 | bytes 73728 | tf_op jit(solution)/shard_map/input_kernel/pallas_call | solution.py:365
  96.9 12.8 %all-to-all-done.2.pieces = bf16[64,56,128]{2,1,0:T(8,128)(2,1)S(1)} async-done(((bf16[64,56,128]{2,1,0:T(8,128)(2,1)}), bf16[64,56,128]{2,1,0:T(8,128)(2,1)S(1)}, u32[]{:S(2)}, u32[]{:S(2)}) %all-to-all-start.2) | async-done | bytes 917536 | tf_op jit(solution)/shard_map/all_to_all | solution.py:451
  110.8 5.2 %all-to-all-start.3 = ((bf16[64,56,128]{2,1,0:T(8,128)(2,1)}), bf16[64,56,128]{2,1,0:T(8,128)(2,1)S(1)}, u32[]{:S(2)}, u32[]{:S(2)}) async-start(bf16[64,56,128]{2,1,0:T(8,128)(2,1)} %sum_kernel.2), calls=%async_computation.3 | async-start | bytes 1835008 | tf_op jit(solution)/shard_map/all_to_all | solution.py:460
  120.6 2.6 %collective-permute-start.18 = (bf16[2,56,128]{2,1,0:T(8,128)(2,1)S(1)}, bf16[2,56,128]{2,1,0:T(8,128)(2,1)S(1)}, u32[]{:S(2)}, u32[]{:S(2)}) collective-permute-start(bf16[2,56,128]{2,1,0:T(8,128)(2,1)S(1)} %maximum_select_fusion.1.pair_0), channel_id=1, source_target_pairs={{0,64},{32,96},{64,0},{96,32},{1,65},{33,97},{65,1},{97,33},{2,66}... | collective-permute-start | bytes 86024 | tf_op jit(solution)/shard_map/ppermute | solution.py:30
  124.2 4.3 %collective-permute-done.17.pair_1 = bf16[2,56,128]{2,1,0:T(8,128)(2,1)S(1)} collective-permute-done((bf16[2,56,128]{2,1,0:T(8,128)(2,1)S(1)}, bf16[2,56,128]{2,1,0:T(8,128)(2,1)S(1)}, u32[]{:S(2)}, u32[]{:S(2)}) %collective-permute-start.17) | collective-permute-done | bytes 28704 | tf_op jit(solution)/shard_map/ppermute | solution.py:30
  131.2 3.7 %collective-permute-start.20 = (bf16[3584,128]{1,0:T(8,128)(2,1)S(1)}, bf16[3584,128]{1,0:T(8,128)(2,1)S(1)}, u32[]{:S(2)}, u32[]{:S(2)}) collective-permute-start(bf16[3584,128]{1,0:T(8,128)(2,1)S(1)} %bitcast.38), channel_id=1, source_target_pairs={{0,16},{16,0},{1,17},{17,1},{2,18},{18,2},{3,19},{19,3},{4,20},{20... | collective-permute-start | bytes 2752520 | tf_op jit(solution)/shard_map/ppermute | solution.py:26
  134.9 2.1 %collective-permute-done.20.other = bf16[3584,128]{1,0:T(8,128)(2,1)S(1)} collective-permute-done((bf16[3584,128]{1,0:T(8,128)(2,1)S(1)}, bf16[3584,128]{1,0:T(8,128)(2,1)S(1)}, u32[]{:S(2)}, u32[]{:S(2)}) %collective-permute-start.20) | collective-permute-done | bytes 917536 | tf_op jit(solution)/shard_map/ppermute | solution.py:26
  (62 shorter events, 28.2 us)
Async XLA Ops:
  2.5 13.4 %collective-permute-start = (bf16[5,2,64,128]{3,2,1,0:T(8,128)(2,1)S(1)}, bf16[5,2,64,128]{3,2,1,0:T(8,128)(2,1)S(1)}, u32[]{:S(2)}, u32[]{:S(2)}) collective-permute-start(bf16[5,2,64,128]{3,2,1,0:T(8,128)(2,1)S(1)} %pad_maximum_fusion.1), channel_id=1, source_target_pairs={{0,1},{1,2},{2,3},{3,4},{4,5},{5,6},{6,7},{7,8},{8,9},{9,10},{10,1... | collective-permute-start | bytes 491528 | tf_op jit(solution)/shard_map/ppermute | solution.py:22
  4.7 11.2 %collective-permute-start.1 = (bf16[5,2,64,128]{3,2,1,0:T(8,128)(2,1)S(1)}, bf16[5,2,64,128]{3,2,1,0:T(8,128)(2,1)S(1)}, u32[]{:S(2)}, u32[]{:S(2)}) collective-permute-start(bf16[5,2,64,128]{3,2,1,0:T(8,128)(2,1)S(1)} %pad_maximum_fusion), channel_id=1, source_target_pairs={{0,15},{1,0},{2,1},{3,2},{4,3},{5,4},{6,5},{7,6},{8,7},{9,8},{10,9... | collective-permute-start | bytes 491528 | tf_op jit(solution)/shard_map/ppermute | solution.py:22
  11.6 21.1 %all-to-all-start = ((bf16[16,27,8,128]{3,2,1,0:T(8,128)(2,1)}), bf16[16,27,8,128]{3,2,1,0:T(8,128)(2,1)}, u32[]{:S(2)}, u32[]{:S(2)}) async-start(bf16[16,27,8,128]{3,2,1,0:T(8,128)(2,1)} %broadcast_in_dim.3), calls=%async_computation | async-start | bytes 1769472 | tf_op jit(solution)/shard_map/all_to_all | solution.py:395
  16.0 6.1 %collective-permute-start.2 = (bf16[20,64,128]{2,1,0:T(8,128)(2,1)S(1)}, bf16[20,64,128]{2,1,0:T(8,128)(2,1)S(1)}, u32[]{:S(2)}, u32[]{:S(2)}) collective-permute-start(bf16[20,64,128]{2,1,0:T(8,128)(2,1)S(1)} %get-tuple-element.47), channel_id=1, source_target_pairs={{0,16},{16,32},{32,48},{48,64},{64,80},{80,96},{96,112},{112,0},{1... | collective-permute-start | bytes 983048 | tf_op jit(solution)/shard_map/ppermute | solution.py:22
  18.1 6.9 %collective-permute-start.3 = (bf16[20,64,128]{2,1,0:T(8,128)(2,1)S(1)}, bf16[20,64,128]{2,1,0:T(8,128)(2,1)S(1)}, u32[]{:S(2)}, u32[]{:S(2)}) collective-permute-start(bf16[20,64,128]{2,1,0:T(8,128)(2,1)S(1)} %get-tuple-element.48), channel_id=1, source_target_pairs={{0,112},{16,0},{32,16},{48,32},{64,48},{80,64},{96,80},{112,96},{1... | collective-permute-start | bytes 983048 | tf_op jit(solution)/shard_map/ppermute | solution.py:22
  32.7 8.9 %collective-permute-start.8 = (bf16[16,27,8,128]{3,2,1,0:T(8,128)(2,1)}, bf16[16,27,8,128]{3,2,1,0:T(8,128)(2,1)S(1)}, u32[]{:S(2)}, u32[]{:S(2)}) collective-permute-start(bf16[16,27,8,128]{3,2,1,0:T(8,128)(2,1)} %all-to-all-done), channel_id=1, source_target_pairs={{0,16},{16,0},{1,17},{17,1},{2,18},{18,2},{3,19},{19,3},{4,20},{20... | collective-permute-start | bytes 2654216 | tf_op jit(solution)/shard_map/ppermute | solution.py:26
  32.7 6.2 %collective-permute-start.4 = (bf16[2,2,32,128]{3,2,1,0:T(8,128)(2,1)S(1)}, bf16[2,2,32,128]{3,2,1,0:T(8,128)(2,1)S(1)}, u32[]{:S(2)}, u32[]{:S(2)}) collective-permute-start(bf16[2,2,32,128]{3,2,1,0:T(8,128)(2,1)S(1)} %get-tuple-element.50.own), channel_id=1, source_target_pairs={{0,1},{1,2},{2,3},{3,4},{4,5},{5,6},{6,7},{7,8},{8,9},{9,10},{10,1... | collective-permute-start | bytes 98312 | tf_op jit(solution)/shard_map/ppermute | solution.py:22
  34.2 4.7 %collective-permute-start.5 = (bf16[2,2,32,128]{3,2,1,0:T(8,128)(2,1)S(1)}, bf16[2,2,32,128]{3,2,1,0:T(8,128)(2,1)S(1)}, u32[]{:S(2)}, u32[]{:S(2)}) collective-permute-start(bf16[2,2,32,128]{3,2,1,0:T(8,128)(2,1)S(1)} %get-tuple-element.50.own), channel_id=1, source_target_pairs={{0,15},{1,0},{2,1},{3,2},{4,3},{5,4},{6,5},{7,6},{8,7},{9,8},{10,9... | collective-permute-start | bytes 98312 | tf_op jit(solution)/shard_map/ppermute | solution.py:22
  38.9 4.9 %collective-permute-start.6 = (bf16[2,6,32,128]{3,2,1,0:T(8,128)(2,1)S(1)}, bf16[2,6,32,128]{3,2,1,0:T(8,128)(2,1)S(1)}, u32[]{:S(2)}, u32[]{:S(2)}) collective-permute-start(bf16[2,6,32,128]{3,2,1,0:T(8,128)(2,1)S(1)} %get-tuple-element.51), channel_id=1, source_target_pairs={{0,16},{16,32},{32,48},{48,64},{64,80},{80,96},{96,112},{112,0},{1... | collective-permute-start | bytes 294920 | tf_op jit(solution)/shard_map/ppermute | solution.py:22
  41.5 4.0 %collective-permute-start.7 = (bf16[2,6,32,128]{3,2,1,0:T(8,128)(2,1)S(1)}, bf16[2,6,32,128]{3,2,1,0:T(8,128)(2,1)S(1)}, u32[]{:S(2)}, u32[]{:S(2)}) collective-permute-start(bf16[2,6,32,128]{3,2,1,0:T(8,128)(2,1)S(1)} %get-tuple-element.52), channel_id=1, source_target_pairs={{0,112},{16,0},{32,16},{48,32},{64,48},{80,64},{96,80},{112,96},{1... | collective-permute-start | bytes 294920 | tf_op jit(solution)/shard_map/ppermute | solution.py:22
  50.3 5.2 %collective-permute-start.10 = (bf16[24,32,128]{2,1,0:T(8,128)(2,1)S(1)}, bf16[24,32,128]{2,1,0:T(8,128)(2,1)S(1)}, u32[]{:S(2)}, u32[]{:S(2)}) collective-permute-start(bf16[24,32,128]{2,1,0:T(8,128)(2,1)S(1)} %get-tuple-element.58.own), channel_id=1, source_target_pairs={{0,16},{16,0},{1,17},{17,1},{2,18},{18,2},{3,19},{19,3},{4,20},{20... | collective-permute-start | bytes 589832 | tf_op jit(solution)/shard_map/ppermute | solution.py:26
  50.4 8.6 %collective-permute-start.11 = (bf16[4,2,64,128]{3,2,1,0:T(8,128)(2,1)S(1)}, bf16[4,2,64,128]{3,2,1,0:T(8,128)(2,1)S(1)}, u32[]{:S(2)}, u32[]{:S(2)}) collective-permute-start(bf16[4,2,64,128]{3,2,1,0:T(8,128)(2,1)S(1)} %get-tuple-element.59), channel_id=1, source_target_pairs={{0,1},{1,2},{2,3},{3,4},{4,5},{5,6},{6,7},{7,8},{8,9},{9,10},{10,1... | collective-permute-start | bytes 393224 | tf_op jit(solution)/shard_map/ppermute | solution.py:22
  50.4 8.6 %collective-permute-start.12 = (bf16[4,2,64,128]{3,2,1,0:T(8,128)(2,1)S(1)}, bf16[4,2,64,128]{3,2,1,0:T(8,128)(2,1)S(1)}, u32[]{:S(2)}, u32[]{:S(2)}) collective-permute-start(bf16[4,2,64,128]{3,2,1,0:T(8,128)(2,1)S(1)} %get-tuple-element.60), channel_id=1, source_target_pairs={{0,15},{1,0},{2,1},{3,2},{4,3},{5,4},{6,5},{7,6},{8,7},{9,8},{10,9... | collective-permute-start | bytes 393224 | tf_op jit(solution)/shard_map/ppermute | solution.py:22
  59.9 12.4 %collective-permute-start.13 = (bf16[2,8,64,128]{3,2,1,0:T(8,128)(2,1)}, bf16[2,8,64,128]{3,2,1,0:T(8,128)(2,1)S(1)}, u32[]{:S(2)}, u32[]{:S(2)}) collective-permute-start(bf16[2,8,64,128]{3,2,1,0:T(8,128)(2,1)} %get-tuple-element.64), channel_id=1, source_target_pairs={{0,16},{16,32},{32,48},{48,64},{64,80},{80,96},{96,112},{112,0},{1... | collective-permute-start | bytes 786440 | tf_op jit(solution)/shard_map/ppermute | solution.py:22
  61.5 10.8 %collective-permute-start.14 = (bf16[2,8,64,128]{3,2,1,0:T(8,128)(2,1)}, bf16[2,8,64,128]{3,2,1,0:T(8,128)(2,1)S(1)}, u32[]{:S(2)}, u32[]{:S(2)}) collective-permute-start(bf16[2,8,64,128]{3,2,1,0:T(8,128)(2,1)} %get-tuple-element.65), channel_id=1, source_target_pairs={{0,112},{16,0},{32,16},{48,32},{64,48},{80,64},{96,80},{112,96},{1... | collective-permute-start | bytes 786440 | tf_op jit(solution)/shard_map/ppermute | solution.py:22
  61.5 25.2 %all-to-all-start.1 = ((bf16[64,56,128]{2,1,0:T(8,128)(2,1)}), bf16[64,56,128]{2,1,0:T(8,128)(2,1)S(1)}, u32[]{:S(2)}, u32[]{:S(2)}) async-start(bf16[64,56,128]{2,1,0:T(8,128)(2,1)} %bottom_grads_kernel.1), calls=%async_computation.1 | async-start | bytes 1835008 | tf_op jit(solution)/shard_map/all_to_all | solution.py:435
  71.3 9.4 %collective-permute-start.9 = (bf16[6,6,64,128]{3,2,1,0:T(8,128)(2,1)}, bf16[6,6,64,128]{3,2,1,0:T(8,128)(2,1)S(1)}, u32[]{:S(2)}, u32[]{:S(2)}) collective-permute-start(bf16[6,6,64,128]{3,2,1,0:T(8,128)(2,1)} %get-tuple-element.56), channel_id=1, source_target_pairs={{0,16},{16,0},{1,17},{17,1},{2,18},{18,2},{3,19},{19,3},{4,20},{20... | collective-permute-start | bytes 1769480 | tf_op jit(solution)/shard_map/ppermute | solution.py:26
  86.6 23.1 %all-to-all-start.2 = ((bf16[64,56,128]{2,1,0:T(8,128)(2,1)}), bf16[64,56,128]{2,1,0:T(8,128)(2,1)S(1)}, u32[]{:S(2)}, u32[]{:S(2)}) async-start(bf16[64,56,128]{2,1,0:T(8,128)(2,1)} %bitcast.45), calls=%async_computation.2 | async-start | bytes 1835008 | tf_op jit(solution)/shard_map/all_to_all | solution.py:451
  110.8 20.3 %all-to-all-start.3 = ((bf16[64,56,128]{2,1,0:T(8,128)(2,1)}), bf16[64,56,128]{2,1,0:T(8,128)(2,1)S(1)}, u32[]{:S(2)}, u32[]{:S(2)}) async-start(bf16[64,56,128]{2,1,0:T(8,128)(2,1)} %sum_kernel.2), calls=%async_computation.3 | async-start | bytes 1835008 | tf_op jit(solution)/shard_map/all_to_all | solution.py:460
  116.3 2.9 %collective-permute-start.16 = (bf16[56,128]{1,0:T(8,128)(2,1)S(1)}, bf16[56,128]{1,0:T(8,128)(2,1)S(1)}, u32[]{:S(2)}, u32[]{:S(2)}) collective-permute-start(bf16[56,128]{1,0:T(8,128)(2,1)S(1)} %bitcast.44), channel_id=1, source_target_pairs={{0,16},{16,0},{1,17},{17,1},{2,18},{18,2},{3,19},{19,3},{4,20},{20... | collective-permute-start | bytes 43016 | tf_op jit(solution)/shard_map/ppermute | solution.py:26
  119.2 9.4 %collective-permute-start.17 = (bf16[2,56,128]{2,1,0:T(8,128)(2,1)S(1)}, bf16[2,56,128]{2,1,0:T(8,128)(2,1)S(1)}, u32[]{:S(2)}, u32[]{:S(2)}) collective-permute-start(bf16[2,56,128]{2,1,0:T(8,128)(2,1)S(1)} %maximum_select_fusion.1.pair_0), channel_id=1, source_target_pairs={{0,32},{32,64},{64,96},{96,0},{1,33},{33,65},{65,97},{97,1},{2,34}... | collective-permute-start | bytes 86024 | tf_op jit(solution)/shard_map/ppermute | solution.py:30
  120.6 8.0 %collective-permute-start.18 = (bf16[2,56,128]{2,1,0:T(8,128)(2,1)S(1)}, bf16[2,56,128]{2,1,0:T(8,128)(2,1)S(1)}, u32[]{:S(2)}, u32[]{:S(2)}) collective-permute-start(bf16[2,56,128]{2,1,0:T(8,128)(2,1)S(1)} %maximum_select_fusion.1.pair_0), channel_id=1, source_target_pairs={{0,64},{32,96},{64,0},{96,32},{1,65},{33,97},{65,1},{97,33},{2,66}... | collective-permute-start | bytes 86024 | tf_op jit(solution)/shard_map/ppermute | solution.py:30
  123.2 5.4 %collective-permute-start.19 = (bf16[2,56,128]{2,1,0:T(8,128)(2,1)S(1)}, bf16[2,56,128]{2,1,0:T(8,128)(2,1)S(1)}, u32[]{:S(2)}, u32[]{:S(2)}) collective-permute-start(bf16[2,56,128]{2,1,0:T(8,128)(2,1)S(1)} %maximum_select_fusion.1.pair_0), channel_id=1, source_target_pairs={{0,96},{32,0},{64,32},{96,64},{1,97},{33,1},{65,33},{97,65},{2,98}... | collective-permute-start | bytes 86024 | tf_op jit(solution)/shard_map/ppermute | solution.py:30
  131.2 5.8 %collective-permute-start.20 = (bf16[3584,128]{1,0:T(8,128)(2,1)S(1)}, bf16[3584,128]{1,0:T(8,128)(2,1)S(1)}, u32[]{:S(2)}, u32[]{:S(2)}) collective-permute-start(bf16[3584,128]{1,0:T(8,128)(2,1)S(1)} %bitcast.38), channel_id=1, source_target_pairs={{0,16},{16,0},{1,17},{17,1},{2,18},{18,2},{3,19},{19,3},{4,20},{20... | collective-permute-start | bytes 2752520 | tf_op jit(solution)/shard_map/ppermute | solution.py:26
  (7 other events, 63.9 us)

commit v10 on v9

--- a/solution.py
+++ b/solution.py
@@ -39,6 +39,13 @@
         for part in (before, own, after):
             slab[:, columns : columns + part.shape[1]] = part[rows]
             columns += part.shape[1]
+
+
+def first_edge_kernel(own, grads, first, last):
+    for edge, start in ((first, 0), (last, 1)):
+        edge[0:4] = own[:, 2 * start : 2 * start + 2]
+        for half in range(2):
+            edge[4, :, half * 32 : half * 32 + 32] = grads[:, start, :, half * 128 : half * 128 + 128]
 
 
 def first_slab_kernel(own, before, after, grads, low, high):
@@ -159,7 +166,11 @@
         act_one[row] = act
         field_keep[row] = jnp.where(first_core, field, act)
         field_send[row] = jnp.where(first_core, act, field)
-        slope_one[row] = slope.astype(BF16)
+
+        @pl.when((row >= 1) & (row <= 4))
+        def _():
+            slope_one[row - 1] = slope[1:5].astype(BF16)
+
         return 0
 
     lax.fori_loop(0, 6, first, 0)
@@ -232,8 +243,9 @@
                     err = (err * slope_two[at].astype(F32)).astype(BF16)
                     err_two[at] = err
                     err_near[at] = err
-                    edge = err_first if at_y == 0 else err_last
-                    edge[2 * row + dx, dy] = err
+                    if dy == at_y:
+                        edge = err_first if at_y == 0 else err_last
+                        edge[2 * row + dx, 0] = err
 
 
 def add_tap_grads(total, fields, errors):
@@ -292,29 +304,31 @@
 
 
 def first_errors_kernel(core, own, before, after, left, right, taps_two, slope_one,
-                        err_one, err_keep, err_send, padded, packed):
+                        err_one, err_first, err_last, err_keep, err_send, padded, packed):
     fill_padded(padded, own, before, after, left, right)
     fill_backward(packed, taps_two)
+    first_core = core[0] == 0
 
     def step(row, _):
-        product = dot_nt(window_rows(padded, row, 6), packed[...])
-        back = join_taps(product, 6, 64, 128)
-        err_one[row] = (back * slope_one[row].astype(F32)).astype(BF16)
-        return 0
-
-    lax.fori_loop(0, 6, step, 0)
-    first_core = core[0] == 0
-    for row in range(4):
-        first, second = err_one[row + 1, 1:5], own[row]
+        product = dot_nt(window_rows(padded, row, 4), packed[...])
+        back = join_taps(product, 4, 64, 128)
+        first, second = (back * slope_one[row].astype(F32)).astype(BF16), own[row]
+        err_one[row] = first
+        err_first[row] = first[0:1]
+        err_last[row] = first[3:4]
         err_keep[row] = jnp.where(first_core, first, second)
         err_send[row] = jnp.where(first_core, second, first)
-
-
-def input_kernel(err_one, taps_one, out, packed):
+        return 0
+
+    lax.fori_loop(0, 4, step, 0)
+
+
+def input_kernel(own, before, after, left, right, taps_one, out, padded, packed):
+    fill_padded(padded, own, before, after, left, right)
     fill_backward(packed, taps_one)
 
     def step(row, _):
-        product = dot_nt(window_rows(err_one, row, 4), packed[...])
+        product = dot_nt(window_rows(padded, row, 4), packed[...])
         out[row] = join_taps(product, 4, 64, 128).astype(BF16)
         return 0
 
@@ -378,10 +392,9 @@
 
 def on_device(features, skip_grad, bottom_grad, conv_one, conv_two, conv_three):
     core = lax.axis_index("c")
-    first = jnp.concatenate([bottom_grad[:, :1, :, :128], bottom_grad[:, :1, :, 128:]], axis=2)
-    last = jnp.concatenate([bottom_grad[:, 1:, :, :128], bottom_grad[:, 1:, :, 128:]], axis=2)
-    first = jnp.concatenate([features[:, :2], first.reshape(1, 2, 64, 128)], axis=0)
-    last = jnp.concatenate([features[:, -2:], last.reshape(1, 2, 64, 128)], axis=0)
+    first, last = call(
+        first_edge_kernel, [((5, 2, 64, 128), BF16)] * 2, [], 0, in_hbm(features), in_hbm(bottom_grad)
+    )
     first, last, first_core, core_ref, chip = lax.optimization_barrier(
         (first, last, core == 0, core.reshape(1), lax.axis_index("x").reshape(1))
     )
@@ -404,10 +417,10 @@
     conv_flops = 2 * 1152 * 128 * 1024 * 3
     field = (6, 6, 64, 128)
     block = (4, 4, 64, 128)
-    edge = (4, 2, 64, 128)
+    edge = (4, 1, 64, 128)
     field_keep, field_send, slope_one, slope_two, pooled = call(
         forward_kernel,
-        [(field, BF16, True), (field, BF16, True), (field, BF16, True), (block, BF16, True), ((2, 2, 32, 128), BF16)],
+        [(field, BF16, True), (field, BF16, True), (block, BF16, True), (block, BF16, True), ((2, 2, 32, 128), BF16)],
         [((8, 8, 64, 128), BF16), ((1152, 384), BF16), (field, BF16), ((4, 2, 64, 128), F32)],
         3 * conv_flops, core_ref, features, f_before, f_after, f_left, f_right, taps_one, taps_two,
     )
@@ -431,12 +444,13 @@
     )
     e_before, e_after = shifted(err_last, GY, 1), shifted(err_first, GY, -1)
     three, e_before, e_after = lax.optimization_barrier((three, e_before, e_after))
-    low, high = call(slab_kernel, [((2, 8, 64, 128), BF16)] * 2, [], 0, err_near, e_before, e_after)
+    low, high = call(slab_kernel, [((1, 6, 64, 128), BF16)] * 2, [], 0, err_near, e_before, e_after)
     three_pieces = lax.all_to_all(three, FLAT, 0, 0)
-    err_one, err_keep, err_send = call(
-        first_errors_kernel, [(field, BF16, True), (block, BF16), (block, BF16)],
-        [((8, 8, 64, 128), BF16), ((384, 1152), BF16)],
-        10**11, core_ref, in_hbm(err_two), e_before, e_after, *exchange_x(low, high),
+    err_one, one_first, one_last, err_keep, err_send = call(
+        first_errors_kernel,
+        [(block, BF16, True), (edge, BF16, True), (edge, BF16, True), (block, BF16), (block, BF16)],
+        [(field, BF16), ((384, 1152), BF16)],
+        2 * 10**11, core_ref, in_hbm(err_two), e_before, e_after, *exchange_x(low, high),
         taps_two, in_hbm(slope_one),
     )
     err_other = swap_cores(err_send)
@@ -445,7 +459,9 @@
         pair_grads_kernel, [((3584, 128), BF16, True)], [((1152, 384), F32)],
         conv_flops, field_other, err_other, total,
     )
-    kept, three_pieces = lax.optimization_barrier((kept, three_pieces))
+    kept, three_pieces, one_first, one_last = lax.optimization_barrier(
+        (kept, three_pieces, one_first, one_last)
+    )
     kept = kept.reshape(64, PIECE, 128)
     (part,) = call(
         sum_kernel, [((64, PIECE, 128), BF16, True)], [], 0, lax.all_to_all(kept, FLAT, 0, 0)
@@ -453,8 +469,8 @@
     (three_part,) = call(sum_kernel, [((1, PIECE, 128), BF16)], [], 0, three_pieces)
     three_part = three_part[0]
     (input_grad,) = call(
-        input_kernel, [(block, BF16, True)], [((384, 1152), BF16)],
-        conv_flops, err_one, taps_one,
+        input_kernel, [(block, BF16, True)], [(field, BF16), ((384, 1152), BF16)],
+        conv_flops // 4, *halo_pieces(err_one, 1, one_first, one_last), taps_one,
     )
     part, input_grad = lax.optimization_barrier((part, input_grad))
     whole = lax.all_to_all(part, FLAT, 0, 0).reshape(64 * PIECE, 128)

time: 140 us -> 146 us (1.043)
  starting transfers between devices: 62.3 us -> 68.5 us
  waiting for transfers between devices: 35.2 us -> 38.6 us
  local copies, waits for them, and re-layouts: 3.31 us -> 1.54 us
    ppermute x12 -> x16, starting transfers between devices: 23.5 us -> 37.2 us  [shifted(): lax.ppermute(array, axes, [(i, (i + step) % count) for i in range(count)])]
    all_to_all x1, waiting for transfers between devices: 12.8 us -> 0.01 us  [on_device(): lax.all_to_all(kept, FLAT, 0, 0)]
    ppermute x12 -> x16, waiting for transfers between devices: 10.5 us -> 18.4 us  [shifted(): lax.ppermute(array, axes, [(i, (i + step) % count) for i in range(count)])]
    ppermute x6, starting transfers between devices: 6.96 us -> 2.64 us  [swap_cores(): return lax.ppermute(array, 'c', [(0, 1), (1, 0)])]
    all_to_all x1, waiting for transfers between devices: 2.77 us -> 6.61 us  [on_device(): three_pieces = lax.all_to_all(three, FLAT, 0, 0)]
    ppermute x3, waiting for transfers between devices: 4.34 us -> 7.67 us  [ring_pieces(): lax.ppermute(pieces[d], axis, [(i, (i + d) % 4) for i in range(4)])]
    all_to_all x1, starting transfers between devices: 7.42 us -> 4.99 us  [on_device(): lax.all_to_all(kept, FLAT, 0, 0)]
    all_to_all x1, starting transfers between devices: 9.79 us -> 7.8 us  [on_device(): three_pieces = lax.all_to_all(three, FLAT, 0, 0)]
  transfers between devices with their start and end apart: 25 -> 29, of which waited for: 11 -> 13; matrix products, arithmetic and copies ran while one was open for 3% -> 3% of each run, Pallas kernels for 19% -> 16%
where the time goes in v10:
time: 146 us; the launch traced here: 145 us
  starting transfers between devices  68.5 us (47%)
  waiting for transfers between devices  38.6 us (26%)
  Pallas kernels  33.3 us (23%)
  other arithmetic  2.57 us (2%)
  local copies, waits for them, and re-layouts  1.54 us (1%)
    ppermute x16, starting transfers between devices, shifted(): lax.ppermute(array, axes, [(i, (i + step) % count) for i in range(count)])  37.2 us
    pallas_call x14, Pallas kernels, call(): pl.pallas_call(kernel, out_shape=shapes, in_specs=[pl.BlockSpec(memory_sp...  30.5 us
    ppermute x16, waiting for transfers between devices, shifted(): lax.ppermute(array, axes, [(i, (i + step) % count) for i in range(count)])  18.4 us
    all_to_all x1, starting transfers between devices, on_device(): three_pieces = lax.all_to_all(three, FLAT, 0, 0)  7.8 us
    ppermute x3, waiting for transfers between devices, ring_pieces(): lax.ppermute(pieces[d], axis, [(i, (i + d) % 4) for i in range(4)])  7.67 us
    all_to_all x1, starting transfers between devices, on_device(): whole = lax.all_to_all(part, FLAT, 0, 0).reshape(64 * PIECE, 128)  6.8 us
    all_to_all x1, waiting for transfers between devices, on_device(): three_pieces = lax.all_to_all(three, FLAT, 0, 0)  6.61 us
    all_to_all x1, starting transfers between devices, on_device(): lax.all_to_all(kept, FLAT, 0, 0)  4.99 us
  transfers between devices with their start and end apart: 29, of which 13 were waited for; matrix products, arithmetic and copies ran while one was open for 3% of the time, Pallas kernels for 16%

profile of v10, /device:TPU:1, one launch (start us, length us, event | category | flops | bytes accessed | tf_op | source)
XLA Modules:
  0.0 145.5 jit_solution(4039062500667399287)
XLA Ops:
  3.9 5.0 %collective-permute-start.1 = (bf16[5,2,64,128]{3,2,1,0:T(8,128)(2,1)S(1)}, bf16[5,2,64,128]{3,2,1,0:T(8,128)(2,1)S(1)}, u32[]{:S(2)}, u32[]{:S(2)}) collective-permute-start(bf16[5,2,64,128]{3,2,1,0:T(8,128)(2,1)S(1)} %get-tuple-element.56), channel_id=1, source_target_pairs={{0,15},{1,0},{2,1},{3,2},{4,3},{5,4},{6,5},{7,6},{8,7},{9,8},{10,9... | collective-permute-start | bytes 491528 | tf_op jit(solution)/shard_map/ppermute | solution.py:22
  10.8 4.3 %all-to-all-start = ((bf16[16,27,8,128]{3,2,1,0:T(8,128)(2,1)}), bf16[16,27,8,128]{3,2,1,0:T(8,128)(2,1)}, u32[]{:S(2)}, u32[]{:S(2)}) async-start(bf16[16,27,8,128]{3,2,1,0:T(8,128)(2,1)} %broadcast_in_dim.3), calls=%async_computation | async-start | bytes 1769472 | tf_op jit(solution)/shard_map/all_to_all | solution.py:408
  17.3 4.0 %collective-permute-done.2.left.f_left = bf16[20,64,128]{2,1,0:T(8,128)(2,1)S(1)} collective-permute-done((bf16[20,64,128]{2,1,0:T(8,128)(2,1)S(1)}, bf16[20,64,128]{2,1,0:T(8,128)(2,1)S(1)}, u32[]{:S(2)}, u32[]{:S(2)}) %collective-permute-start.2) | collective-permute-done | bytes 327712 | tf_op jit(solution)/shard_map/ppermute | solution.py:22
  21.3 2.9 %collective-permute-done.3.right.f_right = bf16[20,64,128]{2,1,0:T(8,128)(2,1)S(1)} collective-permute-done((bf16[20,64,128]{2,1,0:T(8,128)(2,1)S(1)}, bf16[20,64,128]{2,1,0:T(8,128)(2,1)S(1)}, u32[]{:S(2)}, u32[]{:S(2)}) %collective-permute-start.3) | collective-permute-done | bytes 327712 | tf_op jit(solution)/shard_map/ppermute | solution.py:22
  24.2 7.5 %forward_kernel.1 = (bf16[6,6,64,128]{3,2,1,0:T(8,128)(2,1)}, bf16[6,6,64,128]{3,2,1,0:T(8,128)(2,1)}, bf16[4,4,64,128]{3,2,1,0:T(8,128)(2,1)}, bf16[4,4,64,128]...) custom-call(s32[1]{0:T(128)} %bitcast.core, bf16[4,4,64,128]{3,2,1,0:T(8,128)(2,1)S(1)} %copy-done.1, ...), custom_call_target="tpu_custom_call" | custom-call | flops 135895456 | bytes 150733 | tf_op jit(solution)/shard_map/forward_kernel/pallas_call | solution.py:379
  33.2 3.5 %collective-permute-start.5 = (bf16[2,2,32,128]{3,2,1,0:T(8,128)(2,1)S(1)}, bf16[2,2,32,128]{3,2,1,0:T(8,128)(2,1)S(1)}, u32[]{:S(2)}, u32[]{:S(2)}) collective-permute-start(bf16[2,2,32,128]{3,2,1,0:T(8,128)(2,1)S(1)} %get-tuple-element.60.own), channel_id=1, source_target_pairs={{0,15},{1,0},{2,1},{3,2},{4,3},{5,4},{6,5},{7,6},{8,7},{9,8},{10,9... | collective-permute-start | bytes 98312 | tf_op jit(solution)/shard_map/ppermute | solution.py:22
  38.0 2.6 %collective-permute-start.6 = (bf16[2,6,32,128]{3,2,1,0:T(8,128)(2,1)S(1)}, bf16[2,6,32,128]{3,2,1,0:T(8,128)(2,1)S(1)}, u32[]{:S(2)}, u32[]{:S(2)}) collective-permute-start(bf16[2,6,32,128]{3,2,1,0:T(8,128)(2,1)S(1)} %get-tuple-element.61), channel_id=1, source_target_pairs={{0,16},{16,32},{32,48},{48,64},{64,80},{80,96},{96,112},{112,0},{1... | collective-permute-start | bytes 294920 | tf_op jit(solution)/shard_map/ppermute | solution.py:22
  44.6 4.7 %bottom_kernel.1 = (bf16[2,2,32,256]{3,2,1,0:T(8,128)(2,1)}, bf16[24,32,128]{2,1,0:T(8,128)(2,1)S(1)}, bf16[4,4,64,128]{3,2,1,0:T(8,128)(2,1)}, bf16[4,4,64,128]...) custom-call(bf16[2,2,32,128]{3,2,1,0:T(8,128)(2,1)S(1)} %get-tuple-element.60.own, ...), custom_call_target="tpu_custom_call" | custom-call | flops 45298484 | bytes 181862 | tf_op jit(solution)/shard_map/bottom_kernel/pallas_call | solution.py:379
  49.5 5.1 %collective-permute-start.12 = (bf16[4,1,64,128]{3,2,1,0:T(8,128)(2,1)S(1)}, bf16[4,1,64,128]{3,2,1,0:T(8,128)(2,1)S(1)}, u32[]{:S(2)}, u32[]{:S(2)}) collective-permute-start(bf16[4,1,64,128]{3,2,1,0:T(8,128)(2,1)S(1)} %get-tuple-element.70), channel_id=1, source_target_pairs={{0,15},{1,0},{2,1},{3,2},{4,3},{5,4},{6,5},{7,6},{8,7},{9,8},{10,9... | collective-permute-start | bytes 196616 | tf_op jit(solution)/shard_map/ppermute | solution.py:22
  54.6 3.0 %bottom_grads_kernel.1 = bf16[64,56,128]{2,1,0:T(8,128)(2,1)} custom-call(s32[1]{0:T(128)} %bitcast.core, bf16[24,32,128]{2,1,0:T(8,128)(2,1)S(1)} %get-tuple-element.68.own, bf16[24,32,128]{2,1,0:T(8,128)(2,1)S(1)} %collective-permute-done.10.other), custom_call_target="tpu_custom_call" | custom-call | flops 22649240 | bytes 19661 | tf_op jit(solution)/shard_map/bottom_grads_kernel/pallas_call | solution.py:379
  61.8 7.8 %all-to-all-start.1 = ((bf16[64,56,128]{2,1,0:T(8,128)(2,1)}), bf16[64,56,128]{2,1,0:T(8,128)(2,1)S(1)}, u32[]{:S(2)}, u32[]{:S(2)}) async-start(bf16[64,56,128]{2,1,0:T(8,128)(2,1)} %bottom_grads_kernel.1), calls=%async_computation.1 | async-start | bytes 1835008 | tf_op jit(solution)/shard_map/all_to_all | solution.py:448
  69.7 4.1 %first_errors_kernel.1 = (bf16[4,4,64,128]{3,2,1,0:T(8,128)(2,1)}, bf16[4,1,64,128]{3,2,1,0:T(8,128)(2,1)}, bf16[4,1,64,128]{3,2,1,0:T(8,128)(2,1)}, bf16[4,4,64...) custom-call(s32[1]{0:T(128)} %bitcast.core, bf16[4,4,64,128]{3,2,1,0:T(8,128)(2,1)} %get-tuple-element.67.own, ...), custom_call_target="tpu_custom_call" | custom-call | flops 10000000000 | bytes 86835 | tf_op jit(solution)/shard_map/first_errors_kernel/pallas_call | solution.py:379
  76.2 3.1 %pair_grads_kernel.1 = bf16[3584,128]{1,0:T(8,128)(2,1)} custom-call(bf16[6,6,64,128]{3,2,1,0:T(8,128)(2,1)S(1)} %collective-permute-done.9.fields, bf16[4,4,64,128]{3,2,1,0:T(8,128)(2,1)S(1)} %collective-permute-done.15.errors, f32[1152,384]{1,0:T(8,128)S(1)} %own_grads_kernel.1.own_total), custom_call_target="tpu_custom_call" | custom-call | flops 45298484 | bytes 131072 | tf_op jit(solution)/shard_map/pair_grads_kernel/pallas_call | solution.py:379
  79.3 6.6 %all-to-all-done.1.pieces = bf16[64,56,128]{2,1,0:T(8,128)(2,1)S(1)} async-done(((bf16[64,56,128]{2,1,0:T(8,128)(2,1)}), bf16[64,56,128]{2,1,0:T(8,128)(2,1)S(1)}, u32[]{:S(2)}, u32[]{:S(2)}) %all-to-all-start.1) | async-done | bytes 917536 | tf_op jit(solution)/shard_map/all_to_all | solution.py:448
  86.0 5.0 %all-to-all-start.2 = ((bf16[64,56,128]{2,1,0:T(8,128)(2,1)}), bf16[64,56,128]{2,1,0:T(8,128)(2,1)S(1)}, u32[]{:S(2)}, u32[]{:S(2)}) async-start(bf16[64,56,128]{2,1,0:T(8,128)(2,1)} %bitcast.33), calls=%async_computation.2 | async-start | bytes 1835008 | tf_op jit(solution)/shard_map/all_to_all | solution.py:467
  92.0 3.8 %collective-permute-start.17 = (bf16[4,1,64,128]{3,2,1,0:T(8,128)(2,1)S(1)}, bf16[4,1,64,128]{3,2,1,0:T(8,128)(2,1)S(1)}, u32[]{:S(2)}, u32[]{:S(2)}) collective-permute-start(bf16[4,1,64,128]{3,2,1,0:T(8,128)(2,1)S(1)} %copy-done.6), channel_id=1, source_target_pairs={{0,15},{1,0},{2,1},{3,2},{4,3},{5,4},{6,5},{7,6},{8,7},{9,8},{10,9... | collective-permute-start | bytes 196616 | tf_op jit(solution)/shard_map/ppermute | solution.py:22
  95.8 4.4 %collective-permute-done.16.before = bf16[4,1,64,128]{3,2,1,0:T(8,128)(2,1)S(1)} collective-permute-done((bf16[4,1,64,128]{3,2,1,0:T(8,128)(2,1)S(1)}, bf16[4,1,64,128]{3,2,1,0:T(8,128)(2,1)S(1)}, u32[]{:S(2)}, u32[]{:S(2)}) %collective-permute-start.16) | collective-permute-done | bytes 65568 | tf_op jit(solution)/shard_map/ppermute | solution.py:22
  100.2 9.0 %collective-permute-start.18 = (bf16[1,6,64,128]{3,2,1,0:T(8,128)(2,1)S(1)}, bf16[1,6,64,128]{3,2,1,0:T(8,128)(2,1)S(1)}, u32[]{:S(2)}, u32[]{:S(2)}) collective-permute-start(bf16[1,6,64,128]{3,2,1,0:T(8,128)(2,1)S(1)} %get-tuple-element.87), channel_id=1, source_target_pairs={{0,16},{16,32},{32,48},{48,64},{64,80},{80,96},{96,112},{112,0},{1... | collective-permute-start | bytes 294920 | tf_op jit(solution)/shard_map/ppermute | solution.py:22
  110.8 2.4 %collective-permute-done.19.right = bf16[1,6,64,128]{3,2,1,0:T(8,128)(2,1)S(1)} collective-permute-done((bf16[1,6,64,128]{3,2,1,0:T(8,128)(2,1)S(1)}, bf16[1,6,64,128]{3,2,1,0:T(8,128)(2,1)S(1)}, u32[]{:S(2)}, u32[]{:S(2)}) %collective-permute-start.19) | collective-permute-done | bytes 98336 | tf_op jit(solution)/shard_map/ppermute | solution.py:22
  113.2 2.9 %input_kernel.1 = bf16[4,4,64,128]{3,2,1,0:T(8,128)(2,1)} custom-call(bf16[4,4,64,128]{3,2,1,0:T(8,128)(2,1)S(1)} %copy-done.2, bf16[4,1,64,128]{3,2,1,0:T(8,128)(2,1)S(1)} %collective-permute-done.16.before, bf16[4,1,64,128]{3,2,1,0:T(8,128)(2,1)S(1)} %collective-permute-done.17.after, bf16[1,6,64,128]{3,2,1,0:T(8,128)(2,1)S(1)} %collective-permute-done.18.left, ...), custom_call_target="tpu_custom_call" | custom-call | flops 11324620 | bytes 73728 | tf_op jit(solution)/shard_map/input_kernel/pallas_call | solution.py:379
  117.2 6.8 %all-to-all-start.3 = ((bf16[64,56,128]{2,1,0:T(8,128)(2,1)}), bf16[64,56,128]{2,1,0:T(8,128)(2,1)S(1)}, u32[]{:S(2)}, u32[]{:S(2)}) async-start(bf16[64,56,128]{2,1,0:T(8,128)(2,1)} %sum_kernel.2), calls=%async_computation.3 | async-start | bytes 1835008 | tf_op jit(solution)/shard_map/all_to_all | solution.py:476
  126.6 2.6 %collective-permute-start.22 = (bf16[2,56,128]{2,1,0:T(8,128)(2,1)S(1)}, bf16[2,56,128]{2,1,0:T(8,128)(2,1)S(1)}, u32[]{:S(2)}, u32[]{:S(2)}) collective-permute-start(bf16[2,56,128]{2,1,0:T(8,128)(2,1)S(1)} %maximum_select_fusion.1.pair_0), channel_id=1, source_target_pairs={{0,64},{32,96},{64,0},{96,32},{1,65},{33,97},{65,1},{97,33},{2,66}... | collective-permute-start | bytes 86024 | tf_op jit(solution)/shard_map/ppermute | solution.py:30
  130.2 7.2 %collective-permute-done.21.pair_1 = bf16[2,56,128]{2,1,0:T(8,128)(2,1)S(1)} collective-permute-done((bf16[2,56,128]{2,1,0:T(8,128)(2,1)S(1)}, bf16[2,56,128]{2,1,0:T(8,128)(2,1)S(1)}, u32[]{:S(2)}, u32[]{:S(2)}) %collective-permute-start.21) | collective-permute-done | bytes 28704 | tf_op jit(solution)/shard_map/ppermute | solution.py:30
  140.9 2.5 %collective-permute-done.24.other = bf16[3584,128]{1,0:T(8,128)(2,1)S(1)} collective-permute-done((bf16[3584,128]{1,0:T(8,128)(2,1)S(1)}, bf16[3584,128]{1,0:T(8,128)(2,1)S(1)}, u32[]{:S(2)}, u32[]{:S(2)}) %collective-permute-start.24) | collective-permute-done | bytes 917536 | tf_op jit(solution)/shard_map/ppermute | solution.py:26
  (71 shorter events, 33.9 us)
Async XLA Ops:
  1.7 13.4 %collective-permute-start = (bf16[5,2,64,128]{3,2,1,0:T(8,128)(2,1)S(1)}, bf16[5,2,64,128]{3,2,1,0:T(8,128)(2,1)S(1)}, u32[]{:S(2)}, u32[]{:S(2)}) collective-permute-start(bf16[5,2,64,128]{3,2,1,0:T(8,128)(2,1)S(1)} %get-tuple-element.55), channel_id=1, source_target_pairs={{0,1},{1,2},{2,3},{3,4},{4,5},{5,6},{6,7},{7,8},{8,9},{9,10},{10,1... | collective-permute-start | bytes 491528 | tf_op jit(solution)/shard_map/ppermute | solution.py:22
  3.9 11.2 %collective-permute-start.1 = (bf16[5,2,64,128]{3,2,1,0:T(8,128)(2,1)S(1)}, bf16[5,2,64,128]{3,2,1,0:T(8,128)(2,1)S(1)}, u32[]{:S(2)}, u32[]{:S(2)}) collective-permute-start(bf16[5,2,64,128]{3,2,1,0:T(8,128)(2,1)S(1)} %get-tuple-element.56), channel_id=1, source_target_pairs={{0,15},{1,0},{2,1},{3,2},{4,3},{5,4},{6,5},{7,6},{8,7},{9,8},{10,9... | collective-permute-start | bytes 491528 | tf_op jit(solution)/shard_map/ppermute | solution.py:22
  10.8 21.0 %all-to-all-start = ((bf16[16,27,8,128]{3,2,1,0:T(8,128)(2,1)}), bf16[16,27,8,128]{3,2,1,0:T(8,128)(2,1)}, u32[]{:S(2)}, u32[]{:S(2)}) async-start(bf16[16,27,8,128]{3,2,1,0:T(8,128)(2,1)} %broadcast_in_dim.3), calls=%async_computation | async-start | bytes 1769472 | tf_op jit(solution)/shard_map/all_to_all | solution.py:408
  15.2 6.1 %collective-permute-start.2 = (bf16[20,64,128]{2,1,0:T(8,128)(2,1)S(1)}, bf16[20,64,128]{2,1,0:T(8,128)(2,1)S(1)}, u32[]{:S(2)}, u32[]{:S(2)}) collective-permute-start(bf16[20,64,128]{2,1,0:T(8,128)(2,1)S(1)} %get-tuple-element.57), channel_id=1, source_target_pairs={{0,16},{16,32},{32,48},{48,64},{64,80},{80,96},{96,112},{112,0},{1... | collective-permute-start | bytes 983048 | tf_op jit(solution)/shard_map/ppermute | solution.py:22
  17.3 6.9 %collective-permute-start.3 = (bf16[20,64,128]{2,1,0:T(8,128)(2,1)S(1)}, bf16[20,64,128]{2,1,0:T(8,128)(2,1)S(1)}, u32[]{:S(2)}, u32[]{:S(2)}) collective-permute-start(bf16[20,64,128]{2,1,0:T(8,128)(2,1)S(1)} %get-tuple-element.58), channel_id=1, source_target_pairs={{0,112},{16,0},{32,16},{48,32},{64,48},{80,64},{96,80},{112,96},{1... | collective-permute-start | bytes 983048 | tf_op jit(solution)/shard_map/ppermute | solution.py:22
  31.7 8.9 %collective-permute-start.8 = (bf16[16,27,8,128]{3,2,1,0:T(8,128)(2,1)}, bf16[16,27,8,128]{3,2,1,0:T(8,128)(2,1)S(1)}, u32[]{:S(2)}, u32[]{:S(2)}) collective-permute-start(bf16[16,27,8,128]{3,2,1,0:T(8,128)(2,1)} %all-to-all-done), channel_id=1, source_target_pairs={{0,16},{16,0},{1,17},{17,1},{2,18},{18,2},{3,19},{19,3},{4,20},{20... | collective-permute-start | bytes 2654216 | tf_op jit(solution)/shard_map/ppermute | solution.py:26
  31.7 6.2 %collective-permute-start.4 = (bf16[2,2,32,128]{3,2,1,0:T(8,128)(2,1)S(1)}, bf16[2,2,32,128]{3,2,1,0:T(8,128)(2,1)S(1)}, u32[]{:S(2)}, u32[]{:S(2)}) collective-permute-start(bf16[2,2,32,128]{3,2,1,0:T(8,128)(2,1)S(1)} %get-tuple-element.60.own), channel_id=1, source_target_pairs={{0,1},{1,2},{2,3},{3,4},{4,5},{5,6},{6,7},{7,8},{8,9},{9,10},{10,1... | collective-permute-start | bytes 98312 | tf_op jit(solution)/shard_map/ppermute | solution.py:22
  33.2 4.7 %collective-permute-start.5 = (bf16[2,2,32,128]{3,2,1,0:T(8,128)(2,1)S(1)}, bf16[2,2,32,128]{3,2,1,0:T(8,128)(2,1)S(1)}, u32[]{:S(2)}, u32[]{:S(2)}) collective-permute-start(bf16[2,2,32,128]{3,2,1,0:T(8,128)(2,1)S(1)} %get-tuple-element.60.own), channel_id=1, source_target_pairs={{0,15},{1,0},{2,1},{3,2},{4,3},{5,4},{6,5},{7,6},{8,7},{9,8},{10,9... | collective-permute-start | bytes 98312 | tf_op jit(solution)/shard_map/ppermute | solution.py:22
  38.0 4.8 %collective-permute-start.6 = (bf16[2,6,32,128]{3,2,1,0:T(8,128)(2,1)S(1)}, bf16[2,6,32,128]{3,2,1,0:T(8,128)(2,1)S(1)}, u32[]{:S(2)}, u32[]{:S(2)}) collective-permute-start(bf16[2,6,32,128]{3,2,1,0:T(8,128)(2,1)S(1)} %get-tuple-element.61), channel_id=1, source_target_pairs={{0,16},{16,32},{32,48},{48,64},{64,80},{80,96},{96,112},{112,0},{1... | collective-permute-start | bytes 294920 | tf_op jit(solution)/shard_map/ppermute | solution.py:22
  49.4 5.2 %collective-permute-start.10 = (bf16[24,32,128]{2,1,0:T(8,128)(2,1)S(1)}, bf16[24,32,128]{2,1,0:T(8,128)(2,1)S(1)}, u32[]{:S(2)}, u32[]{:S(2)}) collective-permute-start(bf16[24,32,128]{2,1,0:T(8,128)(2,1)S(1)} %get-tuple-element.68.own), channel_id=1, source_target_pairs={{0,16},{16,0},{1,17},{17,1},{2,18},{18,2},{3,19},{19,3},{4,20},{20... | collective-permute-start | bytes 589832 | tf_op jit(solution)/shard_map/ppermute | solution.py:26
  49.5 8.0 %collective-permute-start.11 = (bf16[4,1,64,128]{3,2,1,0:T(8,128)(2,1)S(1)}, bf16[4,1,64,128]{3,2,1,0:T(8,128)(2,1)S(1)}, u32[]{:S(2)}, u32[]{:S(2)}) collective-permute-start(bf16[4,1,64,128]{3,2,1,0:T(8,128)(2,1)S(1)} %get-tuple-element.69), channel_id=1, source_target_pairs={{0,1},{1,2},{2,3},{3,4},{4,5},{5,6},{6,7},{7,8},{8,9},{9,10},{10,1... | collective-permute-start | bytes 196616 | tf_op jit(solution)/shard_map/ppermute | solution.py:22
  49.5 8.0 %collective-permute-start.12 = (bf16[4,1,64,128]{3,2,1,0:T(8,128)(2,1)S(1)}, bf16[4,1,64,128]{3,2,1,0:T(8,128)(2,1)S(1)}, u32[]{:S(2)}, u32[]{:S(2)}) collective-permute-start(bf16[4,1,64,128]{3,2,1,0:T(8,128)(2,1)S(1)} %get-tuple-element.70), channel_id=1, source_target_pairs={{0,15},{1,0},{2,1},{3,2},{4,3},{5,4},{6,5},{7,6},{8,7},{9,8},{10,9... | collective-permute-start | bytes 196616 | tf_op jit(solution)/shard_map/ppermute | solution.py:22
  58.2 11.4 %collective-permute-start.13 = (bf16[1,6,64,128]{3,2,1,0:T(8,128)(2,1)}, bf16[1,6,64,128]{3,2,1,0:T(8,128)(2,1)S(1)}, u32[]{:S(2)}, u32[]{:S(2)}) collective-permute-start(bf16[1,6,64,128]{3,2,1,0:T(8,128)(2,1)} %get-tuple-element.74), channel_id=1, source_target_pairs={{0,16},{16,32},{32,48},{48,64},{64,80},{80,96},{96,112},{112,0},{1... | collective-permute-start | bytes 294920 | tf_op jit(solution)/shard_map/ppermute | solution.py:22
  59.7 10.0 %collective-permute-start.14 = (bf16[1,6,64,128]{3,2,1,0:T(8,128)(2,1)}, bf16[1,6,64,128]{3,2,1,0:T(8,128)(2,1)}, u32[]{:S(2)}, u32[]{:S(2)}) collective-permute-start(bf16[1,6,64,128]{3,2,1,0:T(8,128)(2,1)} %get-tuple-element.75), channel_id=1, source_target_pairs={{0,112},{16,0},{32,16},{48,32},{64,48},{80,64},{96,80},{112,96},{1... | collective-permute-start | bytes 294920 | tf_op jit(solution)/shard_map/ppermute | solution.py:22
  59.7 16.5 %collective-permute-start.9 = (bf16[6,6,64,128]{3,2,1,0:T(8,128)(2,1)}, bf16[6,6,64,128]{3,2,1,0:T(8,128)(2,1)S(1)}, u32[]{:S(2)}, u32[]{:S(2)}) collective-permute-start(bf16[6,6,64,128]{3,2,1,0:T(8,128)(2,1)} %get-tuple-element.66), channel_id=1, source_target_pairs={{0,16},{16,0},{1,17},{17,1},{2,18},{18,2},{3,19},{19,3},{4,20},{20... | collective-permute-start | bytes 1769480 | tf_op jit(solution)/shard_map/ppermute | solution.py:26
  61.8 24.1 %all-to-all-start.1 = ((bf16[64,56,128]{2,1,0:T(8,128)(2,1)}), bf16[64,56,128]{2,1,0:T(8,128)(2,1)S(1)}, u32[]{:S(2)}, u32[]{:S(2)}) async-start(bf16[64,56,128]{2,1,0:T(8,128)(2,1)} %bottom_grads_kernel.1), calls=%async_computation.1 | async-start | bytes 1835008 | tf_op jit(solution)/shard_map/all_to_all | solution.py:448
  86.0 30.2 %all-to-all-start.2 = ((bf16[64,56,128]{2,1,0:T(8,128)(2,1)}), bf16[64,56,128]{2,1,0:T(8,128)(2,1)S(1)}, u32[]{:S(2)}, u32[]{:S(2)}) async-start(bf16[64,56,128]{2,1,0:T(8,128)(2,1)} %bitcast.33), calls=%async_computation.2 | async-start | bytes 1835008 | tf_op jit(solution)/shard_map/all_to_all | solution.py:467
  91.0 9.3 %collective-permute-start.16 = (bf16[4,1,64,128]{3,2,1,0:T(8,128)(2,1)S(1)}, bf16[4,1,64,128]{3,2,1,0:T(8,128)(2,1)S(1)}, u32[]{:S(2)}, u32[]{:S(2)}) collective-permute-start(bf16[4,1,64,128]{3,2,1,0:T(8,128)(2,1)S(1)} %copy-done.7), channel_id=1, source_target_pairs={{0,1},{1,2},{2,3},{3,4},{4,5},{5,6},{6,7},{7,8},{8,9},{9,10},{10,1... | collective-permute-start | bytes 196616 | tf_op jit(solution)/shard_map/ppermute | solution.py:22
  92.0 8.2 %collective-permute-start.17 = (bf16[4,1,64,128]{3,2,1,0:T(8,128)(2,1)S(1)}, bf16[4,1,64,128]{3,2,1,0:T(8,128)(2,1)S(1)}, u32[]{:S(2)}, u32[]{:S(2)}) collective-permute-start(bf16[4,1,64,128]{3,2,1,0:T(8,128)(2,1)S(1)} %copy-done.6), channel_id=1, source_target_pairs={{0,15},{1,0},{2,1},{3,2},{4,3},{5,4},{6,5},{7,6},{8,7},{9,8},{10,9... | collective-permute-start | bytes 196616 | tf_op jit(solution)/shard_map/ppermute | solution.py:22
  100.2 10.6 %collective-permute-start.18 = (bf16[1,6,64,128]{3,2,1,0:T(8,128)(2,1)S(1)}, bf16[1,6,64,128]{3,2,1,0:T(8,128)(2,1)S(1)}, u32[]{:S(2)}, u32[]{:S(2)}) collective-permute-start(bf16[1,6,64,128]{3,2,1,0:T(8,128)(2,1)S(1)} %get-tuple-element.87), channel_id=1, source_target_pairs={{0,16},{16,32},{32,48},{48,64},{64,80},{80,96},{96,112},{112,0},{1... | collective-permute-start | bytes 294920 | tf_op jit(solution)/shard_map/ppermute | solution.py:22
  117.2 23.7 %all-to-all-start.3 = ((bf16[64,56,128]{2,1,0:T(8,128)(2,1)}), bf16[64,56,128]{2,1,0:T(8,128)(2,1)S(1)}, u32[]{:S(2)}, u32[]{:S(2)}) async-start(bf16[64,56,128]{2,1,0:T(8,128)(2,1)} %sum_kernel.2), calls=%async_computation.3 | async-start | bytes 1835008 | tf_op jit(solution)/shard_map/all_to_all | solution.py:476
  125.5 11.9 %collective-permute-start.21 = (bf16[2,56,128]{2,1,0:T(8,128)(2,1)S(1)}, bf16[2,56,128]{2,1,0:T(8,128)(2,1)S(1)}, u32[]{:S(2)}, u32[]{:S(2)}) collective-permute-start(bf16[2,56,128]{2,1,0:T(8,128)(2,1)S(1)} %maximum_select_fusion.1.pair_0), channel_id=1, source_target_pairs={{0,32},{32,64},{64,96},{96,0},{1,33},{33,65},{65,97},{97,1},{2,34}... | collective-permute-start | bytes 86024 | tf_op jit(solution)/shard_map/ppermute | solution.py:30
  126.6 11.3 %collective-permute-start.22 = (bf16[2,56,128]{2,1,0:T(8,128)(2,1)S(1)}, bf16[2,56,128]{2,1,0:T(8,128)(2,1)S(1)}, u32[]{:S(2)}, u32[]{:S(2)}) collective-permute-start(bf16[2,56,128]{2,1,0:T(8,128)(2,1)S(1)} %maximum_select_fusion.1.pair_0), channel_id=1, source_target_pairs={{0,64},{32,96},{64,0},{96,32},{1,65},{33,97},{65,1},{97,33},{2,66}... | collective-permute-start | bytes 86024 | tf_op jit(solution)/shard_map/ppermute | solution.py:30
  129.2 8.7 %collective-permute-start.23 = (bf16[2,56,128]{2,1,0:T(8,128)(2,1)S(1)}, bf16[2,56,128]{2,1,0:T(8,128)(2,1)S(1)}, u32[]{:S(2)}, u32[]{:S(2)}) collective-permute-start(bf16[2,56,128]{2,1,0:T(8,128)(2,1)S(1)} %maximum_select_fusion.1.pair_0), channel_id=1, source_target_pairs={{0,96},{32,0},{64,32},{96,64},{1,97},{33,1},{65,33},{97,65},{2,98}... | collective-permute-start | bytes 86024 | tf_op jit(solution)/shard_map/ppermute | solution.py:30
  (13 other events, 111.0 us)

commit v11 on v8

--- a/solution.py
+++ b/solution.py
@@ -39,6 +39,13 @@
         for part in (before, own, after):
             slab[:, columns : columns + part.shape[1]] = part[rows]
             columns += part.shape[1]
+
+
+def first_edge_kernel(own, grads, first, last):
+    for edge, start in ((first, 0), (last, 1)):
+        edge[0:4] = own[:, 2 * start : 2 * start + 2]
+        for half in range(2):
+            edge[4, :, half * 32 : half * 32 + 32] = grads[:, start, :, half * 128 : half * 128 + 128]
 
 
 def first_slab_kernel(own, before, after, grads, low, high):
@@ -64,7 +71,7 @@
     size_x, size_y, size_z, chans = own.shape
     slab = (width, size_y + 2 * width, size_z, chans)
     low, high = call(slab_kernel, [(slab, BF16)] * 2, [], 0, own, before, after)
-    return (own, before, after, *exchange_x(low, high)), high
+    return own, before, after, *exchange_x(low, high)
 
 
 def fill_padded(padded, own, before, after, left, right):
@@ -83,12 +90,12 @@
     return values * sigma, sigma * (1.0 + values * (1.0 - sigma))
 
 
-def window_rows(source, row, count, skip=0):
+def window_rows(source, row, count, skip=0, rows=1):
     pieces = []
     for kx in range(3):
         for ky in range(3):
-            block = source[row + kx + skip, ky + skip : ky + skip + count]
-            pieces.append(block.reshape(block.shape[0] * block.shape[1], block.shape[2]))
+            block = source[pl.ds(row + kx + skip, rows), ky + skip : ky + skip + count]
+            pieces.append(block.reshape(rows * block.shape[1] * block.shape[2], block.shape[3]))
     return jnp.concatenate(pieces, axis=1)
 
 
@@ -151,29 +158,39 @@
     fill_forward(packed, taps_one)
     first_core = core[0] == 0
 
-    def first(row, _):
-        product = dot_nn(window_rows(padded, row, 6), packed[...])
-        act, slope = slope_and_silu(join_taps(product, 6, 64, 128))
+    def first(step, _):
+        product = dot_nn(window_rows(padded, step * 2, 6, rows=2), packed[...])
+        act, slope = slope_and_silu(join_taps(product, 12, 64, 128))
         act = act.astype(BF16)
-        field = padded[row + 1, 1:7]
-        act_one[row] = act
-        field_keep[row] = jnp.where(first_core, field, act)
-        field_send[row] = jnp.where(first_core, act, field)
-        slope_one[row] = slope.astype(BF16)
+        for at in range(2):
+            row = step * 2 + at
+            part = act[6 * at : 6 * at + 6]
+            field = padded[row + 1, 1:7]
+            act_one[row] = part
+            field_keep[row] = jnp.where(first_core, field, part)
+            field_send[row] = jnp.where(first_core, part, field)
+
+            @pl.when((row >= 1) & (row <= 4))
+            def _():
+                slope_one[row - 1] = slope[6 * at + 1 : 6 * at + 5].astype(BF16)
+
         return 0
 
-    lax.fori_loop(0, 6, first, 0)
+    lax.fori_loop(0, 3, first, 0)
     fill_forward(packed, taps_two)
 
-    def second(row, _):
-        product = dot_nn(window_rows(act_one, row, 4), packed[...])
-        act, slope = slope_and_silu(join_taps(product, 4, 64, 128))
-        slope_two[row] = slope.astype(BF16)
+    def second(step, _):
+        product = dot_nn(window_rows(act_one, step * 2, 4, rows=2), packed[...])
+        act, slope = slope_and_silu(join_taps(product, 8, 64, 128))
+        slope = slope.astype(BF16)
         act = act.astype(BF16).astype(F32)
-        halves[row] = act.reshape(2, 2, 64, 128).sum(axis=1)
+        for at in range(2):
+            row = step * 2 + at
+            slope_two[row] = slope[4 * at : 4 * at + 4]
+            halves[row] = act[4 * at : 4 * at + 4].reshape(2, 2, 64, 128).sum(axis=1)
         return 0
 
-    lax.fori_loop(0, 4, second, 0)
+    lax.fori_loop(0, 2, second, 0)
     for at_x in range(2):
         for at_y in range(2):
             total = 0.0
@@ -231,16 +248,18 @@
                     err = skip[at].astype(F32) + wide[...]
                     err = (err * slope_two[at].astype(F32)).astype(BF16)
                     err_two[at] = err
-                    edge = err_first if at_y == 0 else err_last
-                    edge[2 * row + dx, dy] = err
+                    if dy == at_y:
+                        edge = err_first if at_y == 0 else err_last
+                        edge[2 * row + dx, 0] = err
 
 
 def add_tap_grads(total, fields, errors):
-    def step(row, _):
-        total[...] += dot_tn(window_rows(fields, row, 4), spread_errors(errors[row].astype(F32)))
+    def step(at, _):
+        spread = spread_errors(errors[pl.ds(at * 2, 2)].reshape(8, 64, 128).astype(F32))
+        total[...] += dot_tn(window_rows(fields, at * 2, 4, rows=2), spread)
         return 0
 
-    lax.fori_loop(0, 4, step, 0)
+    lax.fori_loop(0, 2, step, 0)
 
 
 def own_grads_kernel(fields, errors, total):
@@ -297,29 +316,34 @@
 
 
 def first_errors_kernel(core, own, before, after, left, right, taps_two, slope_one,
-                        err_one, err_keep, err_send, padded, packed):
+                        err_one, err_first, err_last, err_keep, err_send, padded, packed):
     fill_padded(padded, own, before, after, left, right)
     fill_backward(packed, taps_two)
+    first_core = core[0] == 0
+
+    def step(at, _):
+        product = dot_nt(window_rows(padded, at * 2, 4, rows=2), packed[...])
+        back = join_taps(product, 8, 64, 128)
+        for half in range(2):
+            row = at * 2 + half
+            first = back[4 * half : 4 * half + 4] * slope_one[row].astype(F32)
+            first, second = first.astype(BF16), own[row]
+            err_one[row] = first
+            err_first[row] = first[0:1]
+            err_last[row] = first[3:4]
+            err_keep[row] = jnp.where(first_core, first, second)
+            err_send[row] = jnp.where(first_core, second, first)
+        return 0
+
+    lax.fori_loop(0, 2, step, 0)
+
+
+def input_kernel(own, before, after, left, right, taps_one, out, padded, packed):
+    fill_padded(padded, own, before, after, left, right)
+    fill_backward(packed, taps_one)
 
     def step(row, _):
-        product = dot_nt(window_rows(padded, row, 6), packed[...])
-        back = join_taps(product, 6, 64, 128)
-        err_one[row] = (back * slope_one[row].astype(F32)).astype(BF16)
-        return 0
-
-    lax.fori_loop(0, 6, step, 0)
-    first_core = core[0] == 0
-    for row in range(4):
-        first, second = err_one[row + 1, 1:5], own[row]
-        err_keep[row] = jnp.where(first_core, first, second)
-        err_send[row] = jnp.where(first_core, second, first)
-
-
-def input_kernel(err_one, taps_one, out, packed):
-    fill_backward(packed, taps_one)
-
-    def step(row, _):
-        product = dot_nt(window_rows(err_one, row, 4), packed[...])
+        product = dot_nt(window_rows(padded, row, 4), packed[...])
         out[row] = join_taps(product, 4, 64, 128).astype(BF16)
         return 0
 
@@ -384,10 +408,9 @@
 
 def on_device(features, skip_grad, bottom_grad, conv_one, conv_two, conv_three):
     core = lax.axis_index("c")
-    first = jnp.concatenate([bottom_grad[:, :1, :, :128], bottom_grad[:, :1, :, 128:]], axis=2)
-    last = jnp.concatenate([bottom_grad[:, 1:, :, :128], bottom_grad[:, 1:, :, 128:]], axis=2)
-    first = jnp.concatenate([features[:, :2], first.reshape(1, 2, 64, 128)], axis=0)
-    last = jnp.concatenate([features[:, -2:], last.reshape(1, 2, 64, 128)], axis=0)
+    first, last = call(
+        first_edge_kernel, [((5, 2, 64, 128), BF16)] * 2, [], 0, in_hbm(features), in_hbm(bottom_grad)
+    )
     first, last, first_core, core_ref, chip = lax.optimization_barrier(
         (first, last, core == 0, core.reshape(1), lax.axis_index("x").reshape(1))
     )
@@ -410,10 +433,10 @@
     conv_flops = 2 * 1152 * 128 * 1024 * 3
     field = (6, 6, 64, 128)
     block = (4, 4, 64, 128)
-    edge = (4, 2, 64, 128)
+    edge = (4, 1, 64, 128)
     field_keep, field_send, slope_one, slope_two, pooled = call(
         forward_kernel,
-        [(field, BF16, True), (field, BF16, True), (field, BF16, True), (block, BF16, True), ((2, 2, 32, 128), BF16)],
+        [(field, BF16, True), (field, BF16, True), (block, BF16, True), (block, BF16, True), ((2, 2, 32, 128), BF16)],
         [((8, 8, 64, 128), BF16), ((1152, 384), BF16), (field, BF16), ((4, 2, 64, 128), F32)],
         3 * conv_flops, core_ref, features, f_before, f_after, f_left, f_right, taps_one, taps_two,
     )
@@ -422,7 +445,7 @@
     theirs = swap_cores(mine)
     both = jnp.where(first_core, jnp.stack([mine, theirs]), jnp.stack([theirs, mine]))
     taps_three = jnp.transpose(both, (2, 1, 0, 3, 4)).reshape(27, 256, 128)
-    p_pieces, _ = halo_pieces(pooled, 2, pooled, pooled)
+    p_pieces = halo_pieces(pooled, 2, pooled, pooled)
     bottleneck, bundle, err_two, err_first, err_last = call(
         bottom_kernel,
         [((2, 2, 32, 256), BF16, True), ((24, 32, 128), BF16), (block, BF16), (edge, BF16), (edge, BF16)],
@@ -431,17 +454,20 @@
         conv_flops, *p_pieces, bottom_grad, f_before, f_after, f_left, f_right,
         taps_three, in_hbm(slope_two), in_hbm(skip_grad),
     )
-    e_pieces, e_high = halo_pieces(err_two, 2, err_first, err_last)
-    bundle, e_high = lax.optimization_barrier((bundle, e_high))
+    e_before, e_after = shifted(err_last, GY, 1), shifted(err_first, GY, -1)
+    low, high = call(slab_kernel, [((1, 6, 64, 128), BF16)] * 2, [], 0, err_two, e_before, e_after)
+    bundle, low, high = lax.optimization_barrier((bundle, low, high))
+    e_left, e_right = exchange_x(low, high)
     (three,) = call(
         bottom_grads_kernel, [((64, PIECE, 128), BF16)], [((768, 1152), F32)],
         conv_flops // 2, core_ref, bundle, swap_cores(bundle),
     )
-    three, *e_ends = lax.optimization_barrier((three, *e_pieces[3:]))
-    err_one, err_keep, err_send = call(
-        first_errors_kernel, [(field, BF16, True), (block, BF16), (block, BF16)],
-        [((8, 8, 64, 128), BF16), ((384, 1152), BF16)],
-        2 * conv_flops, core_ref, *e_pieces[:3], *e_ends, taps_two, slope_one,
+    three, e_left, e_right = lax.optimization_barrier((three, e_left, e_right))
+    err_one, one_first, one_last, err_keep, err_send = call(
+        first_errors_kernel,
+        [(block, BF16, True), (edge, BF16, True), (edge, BF16, True), (block, BF16), (block, BF16)],
+        [(field, BF16), ((384, 1152), BF16)],
+        conv_flops, core_ref, err_two, e_before, e_after, e_left, e_right, taps_two, slope_one,
     )
     err_other = swap_cores(err_send)
     (total,) = call(own_grads_kernel, [((1152, 384), F32)], [], conv_flops, field_keep, err_keep)
@@ -449,13 +475,14 @@
         pair_grads_kernel, [((64, 2 * PIECE, 128), BF16, True)], [((1152, 384), F32)],
         conv_flops, field_other, err_other, total, three,
     )
+    kept, one_first, one_last = lax.optimization_barrier((kept, one_first, one_last))
     part, three_part = call(
         sum_kernel, [((64, PIECE, 128), BF16, True), ((PIECE, 128), BF16)], [], 0,
         lax.all_to_all(kept, FLAT, 0, 0),
     )
     (input_grad,) = call(
-        input_kernel, [(block, BF16, True)], [((384, 1152), BF16)],
-        conv_flops, err_one, taps_one,
+        input_kernel, [(block, BF16, True)], [(field, BF16), ((384, 1152), BF16)],
+        conv_flops // 4, *halo_pieces(err_one, 1, one_first, one_last), taps_one,
     )
     part, input_grad = lax.optimization_barrier((part, input_grad))
     whole = lax.all_to_all(part, FLAT, 0, 0).reshape(64 * PIECE, 128)

time: 142 us -> 144 us (1.014)
  waiting for transfers between devices: 45.6 us -> 50.3 us
  Pallas kernels: 31.3 us -> 28.4 us
  local copies, waits for them, and re-layouts: 3.32 us -> 1.55 us
  starting transfers between devices: 57.9 us -> 59.5 us
    ppermute x12 -> x16, waiting for transfers between devices: 13.2 us -> 36.1 us  [shifted(): lax.ppermute(array, axes, [(i, (i + step) % count) for i in range(count)])]
    all_to_all x1, waiting for transfers between devices: 22.1 us -> 0.01 us  [on_device(): lax.all_to_all(kept, FLAT, 0, 0)]
    ppermute x12 -> x16, starting transfers between devices: 22.8 us -> 31.6 us  [shifted(): lax.ppermute(array, axes, [(i, (i + step) % count) for i in range(count)])]
    ppermute x6, starting transfers between devices: 10 us -> 2.96 us  [swap_cores(): return lax.ppermute(array, 'c', [(0, 1), (1, 0)])]
    ppermute x3, waiting for transfers between devices: 4.77 us -> 7.74 us  [ring_pieces(): lax.ppermute(pieces[d], axis, [(i, (i + d) % 4) for i in range(4)])]
    pallas_call x11 -> x13, Pallas kernels: 28.5 us -> 25.6 us  [call(): pl.pallas_call(kernel, out_shape=shapes, in_specs=[pl.BlockSpec(memory_sp...]
  transfers between devices with their start and end apart: 24 -> 28, of which waited for: 11 -> 15; matrix products, arithmetic and copies ran while one was open for 3% -> 3% of each run, Pallas kernels for 14% -> 15%
where the time goes in v11:
time: 144 us; the launch traced here: 143 us
  starting transfers between devices  59.5 us (41%)
  waiting for transfers between devices  50.3 us (35%)
  Pallas kernels  28.4 us (20%)
  other arithmetic  2.57 us (2%)
  local copies, waits for them, and re-layouts  1.55 us (1%)
    ppermute x16, waiting for transfers between devices, shifted(): lax.ppermute(array, axes, [(i, (i + step) % count) for i in range(count)])  36.1 us
    ppermute x16, starting transfers between devices, shifted(): lax.ppermute(array, axes, [(i, (i + step) % count) for i in range(count)])  31.6 us
    pallas_call x13, Pallas kernels, call(): pl.pallas_call(kernel, out_shape=shapes, in_specs=[pl.BlockSpec(memory_sp...  25.6 us
    all_to_all x1, starting transfers between devices, on_device(): lax.all_to_all(kept, FLAT, 0, 0)  9.55 us
    ppermute x3, waiting for transfers between devices, ring_pieces(): lax.ppermute(pieces[d], axis, [(i, (i + d) % 4) for i in range(4)])  7.74 us
    all_to_all x1, starting transfers between devices, on_device(): whole = lax.all_to_all(part, FLAT, 0, 0).reshape(64 * PIECE, 128)  6.39 us
    ppermute x3, starting transfers between devices, ring_pieces(): lax.ppermute(pieces[d], axis, [(i, (i + d) % 4) for i in range(4)])  4.75 us
    all_to_all x1, starting transfers between devices, on_device(): lax.all_to_all(jnp.broadcast_to(half_taps, (16, 27, 8, 128)), GY, 0, 0)  4.3 us
  transfers between devices with their start and end apart: 28, of which 15 were waited for; matrix products, arithmetic and copies ran while one was open for 3% of the time, Pallas kernels for 15%

profile of v11, /device:TPU:1, one launch (start us, length us, event | category | flops | bytes accessed | tf_op | source)
XLA Modules:
  0.0 143.3 jit_solution(16019825017076318640)
XLA Ops:
  1.7 2.2 %collective-permute-start = (bf16[5,2,64,128]{3,2,1,0:T(8,128)(2,1)S(1)}, bf16[5,2,64,128]{3,2,1,0:T(8,128)(2,1)S(1)}, u32[]{:S(2)}, u32[]{:S(2)}) collective-permute-start(bf16[5,2,64,128]{3,2,1,0:T(8,128)(2,1)S(1)} %get-tuple-element.58), channel_id=1, source_target_pairs={{0,1},{1,2},{2,3},{3,4},{4,5},{5,6},{6,7},{7,8},{8,9},{9,10},{10,1... | collective-permute-start | bytes 491528 | tf_op jit(solution)/shard_map/ppermute | solution.py:22
  3.9 5.0 %collective-permute-start.1 = (bf16[5,2,64,128]{3,2,1,0:T(8,128)(2,1)S(1)}, bf16[5,2,64,128]{3,2,1,0:T(8,128)(2,1)S(1)}, u32[]{:S(2)}, u32[]{:S(2)}) collective-permute-start(bf16[5,2,64,128]{3,2,1,0:T(8,128)(2,1)S(1)} %get-tuple-element.59), channel_id=1, source_target_pairs={{0,15},{1,0},{2,1},{3,2},{4,3},{5,4},{6,5},{7,6},{8,7},{9,8},{10,9... | collective-permute-start | bytes 491528 | tf_op jit(solution)/shard_map/ppermute | solution.py:22
  10.8 4.3 %all-to-all-start = ((bf16[16,27,8,128]{3,2,1,0:T(8,128)(2,1)}), bf16[16,27,8,128]{3,2,1,0:T(8,128)(2,1)}, u32[]{:S(2)}, u32[]{:S(2)}) async-start(bf16[16,27,8,128]{3,2,1,0:T(8,128)(2,1)} %broadcast_in_dim.3), calls=%async_computation | async-start | bytes 1769472 | tf_op jit(solution)/shard_map/all_to_all | solution.py:424
  17.3 4.0 %collective-permute-done.2.left.f_left = bf16[20,64,128]{2,1,0:T(8,128)(2,1)S(1)} collective-permute-done((bf16[20,64,128]{2,1,0:T(8,128)(2,1)S(1)}, bf16[20,64,128]{2,1,0:T(8,128)(2,1)S(1)}, u32[]{:S(2)}, u32[]{:S(2)}) %collective-permute-start.2) | collective-permute-done | bytes 327712 | tf_op jit(solution)/shard_map/ppermute | solution.py:22
  21.3 2.9 %collective-permute-done.3.right.f_right = bf16[20,64,128]{2,1,0:T(8,128)(2,1)S(1)} collective-permute-done((bf16[20,64,128]{2,1,0:T(8,128)(2,1)S(1)}, bf16[20,64,128]{2,1,0:T(8,128)(2,1)S(1)}, u32[]{:S(2)}, u32[]{:S(2)}) %collective-permute-start.3) | collective-permute-done | bytes 327712 | tf_op jit(solution)/shard_map/ppermute | solution.py:22
  24.2 6.8 %forward_kernel.1 = (bf16[6,6,64,128]{3,2,1,0:T(8,128)(2,1)}, bf16[6,6,64,128]{3,2,1,0:T(8,128)(2,1)}, bf16[4,4,64,128]{3,2,1,0:T(8,128)(2,1)}, bf16[4,4,64,128]...) custom-call(s32[1]{0:T(128)} %bitcast.core, bf16[4,4,64,128]{3,2,1,0:T(8,128)(2,1)S(1)} %copy-done.2, ...), custom_call_target="tpu_custom_call" | custom-call | flops 135895456 | bytes 150733 | tf_op jit(solution)/shard_map/forward_kernel/pallas_call | solution.py:395
  32.4 4.1 %collective-permute-start.5 = (bf16[2,2,32,128]{3,2,1,0:T(8,128)(2,1)S(1)}, bf16[2,2,32,128]{3,2,1,0:T(8,128)(2,1)S(1)}, u32[]{:S(2)}, u32[]{:S(2)}) collective-permute-start(bf16[2,2,32,128]{3,2,1,0:T(8,128)(2,1)S(1)} %get-tuple-element.63.own), channel_id=1, source_target_pairs={{0,15},{1,0},{2,1},{3,2},{4,3},{5,4},{6,5},{7,6},{8,7},{9,8},{10,9... | collective-permute-start | bytes 98312 | tf_op jit(solution)/shard_map/ppermute | solution.py:22
  37.8 2.3 %collective-permute-start.6 = (bf16[2,6,32,128]{3,2,1,0:T(8,128)(2,1)S(1)}, bf16[2,6,32,128]{3,2,1,0:T(8,128)(2,1)S(1)}, u32[]{:S(2)}, u32[]{:S(2)}) collective-permute-start(bf16[2,6,32,128]{3,2,1,0:T(8,128)(2,1)S(1)} %get-tuple-element.64), channel_id=1, source_target_pairs={{0,16},{16,32},{32,48},{48,64},{64,80},{80,96},{96,112},{112,0},{1... | collective-permute-start | bytes 294920 | tf_op jit(solution)/shard_map/ppermute | solution.py:22
  44.1 4.1 %bottom_kernel.1 = (bf16[2,2,32,256]{3,2,1,0:T(8,128)(2,1)}, bf16[24,32,128]{2,1,0:T(8,128)(2,1)S(1)}, bf16[4,4,64,128]{3,2,1,0:T(8,128)(2,1)S(1)}, bf16[4,1,64,...) custom-call(bf16[2,2,32,128]{3,2,1,0:T(8,128)(2,1)S(1)} %get-tuple-element.63.own, ...), custom_call_target="tpu_custom_call" | custom-call | flops 45298484 | bytes 181862 | tf_op jit(solution)/shard_map/bottom_kernel/pallas_call | solution.py:395
  48.3 5.1 %collective-permute-start.11 = (bf16[4,1,64,128]{3,2,1,0:T(8,128)(2,1)S(1)}, bf16[4,1,64,128]{3,2,1,0:T(8,128)(2,1)S(1)}, u32[]{:S(2)}, u32[]{:S(2)}) collective-permute-start(bf16[4,1,64,128]{3,2,1,0:T(8,128)(2,1)S(1)} %get-tuple-element.72), channel_id=1, source_target_pairs={{0,15},{1,0},{2,1},{3,2},{4,3},{5,4},{6,5},{7,6},{8,7},{9,8},{10,9... | collective-permute-start | bytes 196616 | tf_op jit(solution)/shard_map/ppermute | solution.py:22
  53.5 2.2 %collective-permute-done.10.before = bf16[4,1,64,128]{3,2,1,0:T(8,128)(2,1)S(1)} collective-permute-done((bf16[4,1,64,128]{3,2,1,0:T(8,128)(2,1)S(1)}, bf16[4,1,64,128]{3,2,1,0:T(8,128)(2,1)S(1)}, u32[]{:S(2)}, u32[]{:S(2)}) %collective-permute-start.10) | collective-permute-done | bytes 65568 | tf_op jit(solution)/shard_map/ppermute | solution.py:22
  61.1 2.6 %first_errors_kernel.1 = (bf16[4,4,64,128]{3,2,1,0:T(8,128)(2,1)}, bf16[4,1,64,128]{3,2,1,0:T(8,128)(2,1)}, bf16[4,1,64,128]{3,2,1,0:T(8,128)(2,1)}, bf16[4,4,64...) custom-call(s32[1]{0:T(128)} %bitcast.core, bf16[4,4,64,128]{3,2,1,0:T(8,128)(2,1)S(1)} %get-tuple-element.70.own, ...), custom_call_target="tpu_custom_call" | custom-call | flops 45298484 | bytes 86835 | tf_op jit(solution)/shard_map/first_errors_kernel/pallas_call | solution.py:395
  66.2 3.2 %pair_grads_kernel.1 = bf16[64,112,128]{2,1,0:T(8,128)(2,1)} custom-call(bf16[6,6,64,128]{3,2,1,0:T(8,128)(2,1)S(1)} %collective-permute-done.9.fields, bf16[4,4,64,128]{3,2,1,0:T(8,128)(2,1)S(1)} %collective-permute-done.15.errors, f32[1152,384]{1,0:T(8,128)S(1)} %own_grads_kernel.1.own_total, bf16[64,56,128]{2,1,0:T(8,128)(2,1)S(1)} %bottom_grads_kernel.1.three), custom_call_target="tpu_custom_call" | custom-call | flops 45298484 | bytes 176947 | tf_op jit(solution)/shard_map/pair_grads_kernel/pallas_call | solution.py:395
  69.4 9.6 %all-to-all-start.1 = ((bf16[64,112,128]{2,1,0:T(8,128)(2,1)}), bf16[64,112,128]{2,1,0:T(8,128)(2,1)S(1)}, u32[]{:S(2)}, u32[]{:S(2)}) async-start(bf16[64,112,128]{2,1,0:T(8,128)(2,1)} %pair_grads_kernel.1), calls=%async_computation.1 | async-start | bytes 3670016 | tf_op jit(solution)/shard_map/all_to_all | solution.py:481
  80.1 3.8 %collective-permute-start.17 = (bf16[4,1,64,128]{3,2,1,0:T(8,128)(2,1)S(1)}, bf16[4,1,64,128]{3,2,1,0:T(8,128)(2,1)S(1)}, u32[]{:S(2)}, u32[]{:S(2)}) collective-permute-start(bf16[4,1,64,128]{3,2,1,0:T(8,128)(2,1)S(1)} %copy-done.7), channel_id=1, source_target_pairs={{0,15},{1,0},{2,1},{3,2},{4,3},{5,4},{6,5},{7,6},{8,7},{9,8},{10,9... | collective-permute-start | bytes 196616 | tf_op jit(solution)/shard_map/ppermute | solution.py:22
  83.9 18.9 %collective-permute-done.16.before = bf16[4,1,64,128]{3,2,1,0:T(8,128)(2,1)S(1)} collective-permute-done((bf16[4,1,64,128]{3,2,1,0:T(8,128)(2,1)S(1)}, bf16[4,1,64,128]{3,2,1,0:T(8,128)(2,1)S(1)}, u32[]{:S(2)}, u32[]{:S(2)}) %collective-permute-start.16) | collective-permute-done | bytes 65568 | tf_op jit(solution)/shard_map/ppermute | solution.py:22
  102.8 4.7 %collective-permute-start.18 = (bf16[1,6,64,128]{3,2,1,0:T(8,128)(2,1)S(1)}, bf16[1,6,64,128]{3,2,1,0:T(8,128)(2,1)S(1)}, u32[]{:S(2)}, u32[]{:S(2)}) collective-permute-start(bf16[1,6,64,128]{3,2,1,0:T(8,128)(2,1)S(1)} %get-tuple-element.93), channel_id=1, source_target_pairs={{0,16},{16,32},{32,48},{48,64},{64,80},{80,96},{96,112},{112,0},{1... | collective-permute-start | bytes 294920 | tf_op jit(solution)/shard_map/ppermute | solution.py:22
  109.1 2.4 %collective-permute-done.19.right = bf16[1,6,64,128]{3,2,1,0:T(8,128)(2,1)S(1)} collective-permute-done((bf16[1,6,64,128]{3,2,1,0:T(8,128)(2,1)S(1)}, bf16[1,6,64,128]{3,2,1,0:T(8,128)(2,1)S(1)}, u32[]{:S(2)}, u32[]{:S(2)}) %collective-permute-start.19) | collective-permute-done | bytes 98336 | tf_op jit(solution)/shard_map/ppermute | solution.py:22
  111.5 2.9 %input_kernel.1 = bf16[4,4,64,128]{3,2,1,0:T(8,128)(2,1)} custom-call(bf16[4,4,64,128]{3,2,1,0:T(8,128)(2,1)S(1)} %copy-done.3, bf16[4,1,64,128]{3,2,1,0:T(8,128)(2,1)S(1)} %collective-permute-done.16.before, bf16[4,1,64,128]{3,2,1,0:T(8,128)(2,1)S(1)} %collective-permute-done.17.after, bf16[1,6,64,128]{3,2,1,0:T(8,128)(2,1)S(1)} %collective-permute-done.18.left, ...), custom_call_target="tpu_custom_call" | custom-call | flops 11324620 | bytes 73728 | tf_op jit(solution)/shard_map/input_kernel/pallas_call | solution.py:395
  115.5 6.4 %all-to-all-start.2 = ((bf16[64,56,128]{2,1,0:T(8,128)(2,1)}), bf16[64,56,128]{2,1,0:T(8,128)(2,1)S(1)}, u32[]{:S(2)}, u32[]{:S(2)}) async-start(bf16[64,56,128]{2,1,0:T(8,128)(2,1)} %get-tuple-element.96), calls=%async_computation.2 | async-start | bytes 1835008 | tf_op jit(solution)/shard_map/all_to_all | solution.py:488
  124.3 2.6 %collective-permute-start.22 = (bf16[2,56,128]{2,1,0:T(8,128)(2,1)S(1)}, bf16[2,56,128]{2,1,0:T(8,128)(2,1)S(1)}, u32[]{:S(2)}, u32[]{:S(2)}) collective-permute-start(bf16[2,56,128]{2,1,0:T(8,128)(2,1)S(1)} %maximum_select_fusion.1.pair_0), channel_id=1, source_target_pairs={{0,64},{32,96},{64,0},{96,32},{1,65},{33,97},{65,1},{97,33},{2,66}... | collective-permute-start | bytes 86024 | tf_op jit(solution)/shard_map/ppermute | solution.py:30
  128.0 7.2 %collective-permute-done.21.pair_1 = bf16[2,56,128]{2,1,0:T(8,128)(2,1)S(1)} collective-permute-done((bf16[2,56,128]{2,1,0:T(8,128)(2,1)S(1)}, bf16[2,56,128]{2,1,0:T(8,128)(2,1)S(1)}, u32[]{:S(2)}, u32[]{:S(2)}) %collective-permute-start.21) | collective-permute-done | bytes 28704 | tf_op jit(solution)/shard_map/ppermute | solution.py:30
  136.4 2.3 %all-to-all-done.2 = bf16[64,56,128]{2,1,0:T(8,128)(2,1)S(1)} async-done(((bf16[64,56,128]{2,1,0:T(8,128)(2,1)}), bf16[64,56,128]{2,1,0:T(8,128)(2,1)S(1)}, u32[]{:S(2)}, u32[]{:S(2)}) %all-to-all-start.2) | async-done | bytes 917536 | tf_op jit(solution)/shard_map/all_to_all | solution.py:488
  138.8 2.5 %collective-permute-done.24.other = bf16[3584,128]{1,0:T(8,128)(2,1)S(1)} collective-permute-done((bf16[3584,128]{1,0:T(8,128)(2,1)S(1)}, bf16[3584,128]{1,0:T(8,128)(2,1)S(1)}, u32[]{:S(2)}, u32[]{:S(2)}) %collective-permute-start.24) | collective-permute-done | bytes 917536 | tf_op jit(solution)/shard_map/ppermute | solution.py:26
  (70 shorter events, 30.4 us)
Async XLA Ops:
  1.7 13.4 %collective-permute-start = (bf16[5,2,64,128]{3,2,1,0:T(8,128)(2,1)S(1)}, bf16[5,2,64,128]{3,2,1,0:T(8,128)(2,1)S(1)}, u32[]{:S(2)}, u32[]{:S(2)}) collective-permute-start(bf16[5,2,64,128]{3,2,1,0:T(8,128)(2,1)S(1)} %get-tuple-element.58), channel_id=1, source_target_pairs={{0,1},{1,2},{2,3},{3,4},{4,5},{5,6},{6,7},{7,8},{8,9},{9,10},{10,1... | collective-permute-start | bytes 491528 | tf_op jit(solution)/shard_map/ppermute | solution.py:22
  3.9 11.2 %collective-permute-start.1 = (bf16[5,2,64,128]{3,2,1,0:T(8,128)(2,1)S(1)}, bf16[5,2,64,128]{3,2,1,0:T(8,128)(2,1)S(1)}, u32[]{:S(2)}, u32[]{:S(2)}) collective-permute-start(bf16[5,2,64,128]{3,2,1,0:T(8,128)(2,1)S(1)} %get-tuple-element.59), channel_id=1, source_target_pairs={{0,15},{1,0},{2,1},{3,2},{4,3},{5,4},{6,5},{7,6},{8,7},{9,8},{10,9... | collective-permute-start | bytes 491528 | tf_op jit(solution)/shard_map/ppermute | solution.py:22
  10.8 20.2 %all-to-all-start = ((bf16[16,27,8,128]{3,2,1,0:T(8,128)(2,1)}), bf16[16,27,8,128]{3,2,1,0:T(8,128)(2,1)}, u32[]{:S(2)}, u32[]{:S(2)}) async-start(bf16[16,27,8,128]{3,2,1,0:T(8,128)(2,1)} %broadcast_in_dim.3), calls=%async_computation | async-start | bytes 1769472 | tf_op jit(solution)/shard_map/all_to_all | solution.py:424
  15.2 6.1 %collective-permute-start.2 = (bf16[20,64,128]{2,1,0:T(8,128)(2,1)S(1)}, bf16[20,64,128]{2,1,0:T(8,128)(2,1)S(1)}, u32[]{:S(2)}, u32[]{:S(2)}) collective-permute-start(bf16[20,64,128]{2,1,0:T(8,128)(2,1)S(1)} %get-tuple-element.60), channel_id=1, source_target_pairs={{0,16},{16,32},{32,48},{48,64},{64,80},{80,96},{96,112},{112,0},{1... | collective-permute-start | bytes 983048 | tf_op jit(solution)/shard_map/ppermute | solution.py:22
  17.3 6.9 %collective-permute-start.3 = (bf16[20,64,128]{2,1,0:T(8,128)(2,1)S(1)}, bf16[20,64,128]{2,1,0:T(8,128)(2,1)S(1)}, u32[]{:S(2)}, u32[]{:S(2)}) collective-permute-start(bf16[20,64,128]{2,1,0:T(8,128)(2,1)S(1)} %get-tuple-element.61), channel_id=1, source_target_pairs={{0,112},{16,0},{32,16},{48,32},{64,48},{80,64},{96,80},{112,96},{1... | collective-permute-start | bytes 983048 | tf_op jit(solution)/shard_map/ppermute | solution.py:22
  30.9 9.2 %collective-permute-start.8 = (bf16[16,27,8,128]{3,2,1,0:T(8,128)(2,1)}, bf16[16,27,8,128]{3,2,1,0:T(8,128)(2,1)S(1)}, u32[]{:S(2)}, u32[]{:S(2)}) collective-permute-start(bf16[16,27,8,128]{3,2,1,0:T(8,128)(2,1)} %all-to-all-done), channel_id=1, source_target_pairs={{0,16},{16,0},{1,17},{17,1},{2,18},{18,2},{3,19},{19,3},{4,20},{20... | collective-permute-start | bytes 2654216 | tf_op jit(solution)/shard_map/ppermute | solution.py:26
  31.7 6.1 %collective-permute-start.4 = (bf16[2,2,32,128]{3,2,1,0:T(8,128)(2,1)S(1)}, bf16[2,2,32,128]{3,2,1,0:T(8,128)(2,1)S(1)}, u32[]{:S(2)}, u32[]{:S(2)}) collective-permute-start(bf16[2,2,32,128]{3,2,1,0:T(8,128)(2,1)S(1)} %get-tuple-element.63.own), channel_id=1, source_target_pairs={{0,1},{1,2},{2,3},{3,4},{4,5},{5,6},{6,7},{7,8},{8,9},{9,10},{10,1... | collective-permute-start | bytes 98312 | tf_op jit(solution)/shard_map/ppermute | solution.py:22
  32.4 5.4 %collective-permute-start.5 = (bf16[2,2,32,128]{3,2,1,0:T(8,128)(2,1)S(1)}, bf16[2,2,32,128]{3,2,1,0:T(8,128)(2,1)S(1)}, u32[]{:S(2)}, u32[]{:S(2)}) collective-permute-start(bf16[2,2,32,128]{3,2,1,0:T(8,128)(2,1)S(1)} %get-tuple-element.63.own), channel_id=1, source_target_pairs={{0,15},{1,0},{2,1},{3,2},{4,3},{5,4},{6,5},{7,6},{8,7},{9,8},{10,9... | collective-permute-start | bytes 98312 | tf_op jit(solution)/shard_map/ppermute | solution.py:22
  36.5 29.7 %collective-permute-start.9 = (bf16[6,6,64,128]{3,2,1,0:T(8,128)(2,1)}, bf16[6,6,64,128]{3,2,1,0:T(8,128)(2,1)S(1)}, u32[]{:S(2)}, u32[]{:S(2)}) collective-permute-start(bf16[6,6,64,128]{3,2,1,0:T(8,128)(2,1)} %get-tuple-element.69), channel_id=1, source_target_pairs={{0,16},{16,0},{1,17},{17,1},{2,18},{18,2},{3,19},{19,3},{4,20},{20... | collective-permute-start | bytes 1769480 | tf_op jit(solution)/shard_map/ppermute | solution.py:26
  37.8 4.5 %collective-permute-start.6 = (bf16[2,6,32,128]{3,2,1,0:T(8,128)(2,1)S(1)}, bf16[2,6,32,128]{3,2,1,0:T(8,128)(2,1)S(1)}, u32[]{:S(2)}, u32[]{:S(2)}) collective-permute-start(bf16[2,6,32,128]{3,2,1,0:T(8,128)(2,1)S(1)} %get-tuple-element.64), channel_id=1, source_target_pairs={{0,16},{16,32},{32,48},{48,64},{64,80},{80,96},{96,112},{112,0},{1... | collective-permute-start | bytes 294920 | tf_op jit(solution)/shard_map/ppermute | solution.py:22
  40.1 4.0 %collective-permute-start.7 = (bf16[2,6,32,128]{3,2,1,0:T(8,128)(2,1)S(1)}, bf16[2,6,32,128]{3,2,1,0:T(8,128)(2,1)S(1)}, u32[]{:S(2)}, u32[]{:S(2)}) collective-permute-start(bf16[2,6,32,128]{3,2,1,0:T(8,128)(2,1)S(1)} %get-tuple-element.65), channel_id=1, source_target_pairs={{0,112},{16,0},{32,16},{48,32},{64,48},{80,64},{96,80},{112,96},{1... | collective-permute-start | bytes 294920 | tf_op jit(solution)/shard_map/ppermute | solution.py:22
  48.3 7.5 %collective-permute-start.10 = (bf16[4,1,64,128]{3,2,1,0:T(8,128)(2,1)S(1)}, bf16[4,1,64,128]{3,2,1,0:T(8,128)(2,1)S(1)}, u32[]{:S(2)}, u32[]{:S(2)}) collective-permute-start(bf16[4,1,64,128]{3,2,1,0:T(8,128)(2,1)S(1)} %get-tuple-element.71), channel_id=1, source_target_pairs={{0,1},{1,2},{2,3},{3,4},{4,5},{5,6},{6,7},{7,8},{8,9},{9,10},{10,1... | collective-permute-start | bytes 196616 | tf_op jit(solution)/shard_map/ppermute | solution.py:22
  48.3 7.4 %collective-permute-start.11 = (bf16[4,1,64,128]{3,2,1,0:T(8,128)(2,1)S(1)}, bf16[4,1,64,128]{3,2,1,0:T(8,128)(2,1)S(1)}, u32[]{:S(2)}, u32[]{:S(2)}) collective-permute-start(bf16[4,1,64,128]{3,2,1,0:T(8,128)(2,1)S(1)} %get-tuple-element.72), channel_id=1, source_target_pairs={{0,15},{1,0},{2,1},{3,2},{4,3},{5,4},{6,5},{7,6},{8,7},{9,8},{10,9... | collective-permute-start | bytes 196616 | tf_op jit(solution)/shard_map/ppermute | solution.py:22
  56.5 3.1 %collective-permute-start.13 = (bf16[1,6,64,128]{3,2,1,0:T(8,128)(2,1)S(1)}, bf16[1,6,64,128]{3,2,1,0:T(8,128)(2,1)S(1)}, u32[]{:S(2)}, u32[]{:S(2)}) collective-permute-start(bf16[1,6,64,128]{3,2,1,0:T(8,128)(2,1)S(1)} %get-tuple-element.77), channel_id=1, source_target_pairs={{0,16},{16,32},{32,48},{48,64},{64,80},{80,96},{96,112},{112,0},{1... | collective-permute-start | bytes 294920 | tf_op jit(solution)/shard_map/ppermute | solution.py:22
  56.8 4.3 %collective-permute-start.14 = (bf16[1,6,64,128]{3,2,1,0:T(8,128)(2,1)S(1)}, bf16[1,6,64,128]{3,2,1,0:T(8,128)(2,1)S(1)}, u32[]{:S(2)}, u32[]{:S(2)}) collective-permute-start(bf16[1,6,64,128]{3,2,1,0:T(8,128)(2,1)S(1)} %get-tuple-element.78), channel_id=1, source_target_pairs={{0,112},{16,0},{32,16},{48,32},{64,48},{80,64},{96,80},{112,96},{1... | collective-permute-start | bytes 294920 | tf_op jit(solution)/shard_map/ppermute | solution.py:22
  69.4 45.0 %all-to-all-start.1 = ((bf16[64,112,128]{2,1,0:T(8,128)(2,1)}), bf16[64,112,128]{2,1,0:T(8,128)(2,1)S(1)}, u32[]{:S(2)}, u32[]{:S(2)}) async-start(bf16[64,112,128]{2,1,0:T(8,128)(2,1)} %pair_grads_kernel.1), calls=%async_computation.1 | async-start | bytes 3670016 | tf_op jit(solution)/shard_map/all_to_all | solution.py:481
  79.0 23.8 %collective-permute-start.16 = (bf16[4,1,64,128]{3,2,1,0:T(8,128)(2,1)S(1)}, bf16[4,1,64,128]{3,2,1,0:T(8,128)(2,1)S(1)}, u32[]{:S(2)}, u32[]{:S(2)}) collective-permute-start(bf16[4,1,64,128]{3,2,1,0:T(8,128)(2,1)S(1)} %copy-done.8), channel_id=1, source_target_pairs={{0,1},{1,2},{2,3},{3,4},{4,5},{5,6},{6,7},{7,8},{8,9},{9,10},{10,1... | collective-permute-start | bytes 196616 | tf_op jit(solution)/shard_map/ppermute | solution.py:22
  80.1 22.7 %collective-permute-start.17 = (bf16[4,1,64,128]{3,2,1,0:T(8,128)(2,1)S(1)}, bf16[4,1,64,128]{3,2,1,0:T(8,128)(2,1)S(1)}, u32[]{:S(2)}, u32[]{:S(2)}) collective-permute-start(bf16[4,1,64,128]{3,2,1,0:T(8,128)(2,1)S(1)} %copy-done.7), channel_id=1, source_target_pairs={{0,15},{1,0},{2,1},{3,2},{4,3},{5,4},{6,5},{7,6},{8,7},{9,8},{10,9... | collective-permute-start | bytes 196616 | tf_op jit(solution)/shard_map/ppermute | solution.py:22
  102.8 6.3 %collective-permute-start.18 = (bf16[1,6,64,128]{3,2,1,0:T(8,128)(2,1)S(1)}, bf16[1,6,64,128]{3,2,1,0:T(8,128)(2,1)S(1)}, u32[]{:S(2)}, u32[]{:S(2)}) collective-permute-start(bf16[1,6,64,128]{3,2,1,0:T(8,128)(2,1)S(1)} %get-tuple-element.93), channel_id=1, source_target_pairs={{0,16},{16,32},{32,48},{48,64},{64,80},{80,96},{96,112},{112,0},{1... | collective-permute-start | bytes 294920 | tf_op jit(solution)/shard_map/ppermute | solution.py:22
  107.5 4.0 %collective-permute-start.19 = (bf16[1,6,64,128]{3,2,1,0:T(8,128)(2,1)S(1)}, bf16[1,6,64,128]{3,2,1,0:T(8,128)(2,1)S(1)}, u32[]{:S(2)}, u32[]{:S(2)}) collective-permute-start(bf16[1,6,64,128]{3,2,1,0:T(8,128)(2,1)S(1)} %get-tuple-element.94), channel_id=1, source_target_pairs={{0,112},{16,0},{32,16},{48,32},{64,48},{80,64},{96,80},{112,96},{1... | collective-permute-start | bytes 294920 | tf_op jit(solution)/shard_map/ppermute | solution.py:22
  115.5 23.2 %all-to-all-start.2 = ((bf16[64,56,128]{2,1,0:T(8,128)(2,1)}), bf16[64,56,128]{2,1,0:T(8,128)(2,1)S(1)}, u32[]{:S(2)}, u32[]{:S(2)}) async-start(bf16[64,56,128]{2,1,0:T(8,128)(2,1)} %get-tuple-element.96), calls=%async_computation.2 | async-start | bytes 1835008 | tf_op jit(solution)/shard_map/all_to_all | solution.py:488
  123.2 12.0 %collective-permute-start.21 = (bf16[2,56,128]{2,1,0:T(8,128)(2,1)S(1)}, bf16[2,56,128]{2,1,0:T(8,128)(2,1)S(1)}, u32[]{:S(2)}, u32[]{:S(2)}) collective-permute-start(bf16[2,56,128]{2,1,0:T(8,128)(2,1)S(1)} %maximum_select_fusion.1.pair_0), channel_id=1, source_target_pairs={{0,32},{32,64},{64,96},{96,0},{1,33},{33,65},{65,97},{97,1},{2,34}... | collective-permute-start | bytes 86024 | tf_op jit(solution)/shard_map/ppermute | solution.py:30
  124.3 11.4 %collective-permute-start.22 = (bf16[2,56,128]{2,1,0:T(8,128)(2,1)S(1)}, bf16[2,56,128]{2,1,0:T(8,128)(2,1)S(1)}, u32[]{:S(2)}, u32[]{:S(2)}) collective-permute-start(bf16[2,56,128]{2,1,0:T(8,128)(2,1)S(1)} %maximum_select_fusion.1.pair_0), channel_id=1, source_target_pairs={{0,64},{32,96},{64,0},{96,32},{1,65},{33,97},{65,1},{97,33},{2,66}... | collective-permute-start | bytes 86024 | tf_op jit(solution)/shard_map/ppermute | solution.py:30
  126.9 8.8 %collective-permute-start.23 = (bf16[2,56,128]{2,1,0:T(8,128)(2,1)S(1)}, bf16[2,56,128]{2,1,0:T(8,128)(2,1)S(1)}, u32[]{:S(2)}, u32[]{:S(2)}) collective-permute-start(bf16[2,56,128]{2,1,0:T(8,128)(2,1)S(1)} %maximum_select_fusion.1.pair_0), channel_id=1, source_target_pairs={{0,96},{32,0},{64,32},{96,64},{1,97},{33,1},{65,33},{97,65},{2,98}... | collective-permute-start | bytes 86024 | tf_op jit(solution)/shard_map/ppermute | solution.py:30
  (13 other events, 142.0 us)

commit v12 on v11

--- a/solution.py
+++ b/solution.py
@@ -342,12 +342,12 @@
     fill_padded(padded, own, before, after, left, right)
     fill_backward(packed, taps_one)
 
-    def step(row, _):
-        product = dot_nt(window_rows(padded, row, 4), packed[...])
-        out[row] = join_taps(product, 4, 64, 128).astype(BF16)
+    def step(at, _):
+        product = dot_nt(window_rows(padded, at * 2, 4, rows=2), packed[...])
+        out[pl.ds(at * 2, 2)] = join_taps(product, 8, 64, 128).reshape(2, 4, 64, 128).astype(BF16)
         return 0
 
-    lax.fori_loop(0, 4, step, 0)
+    lax.fori_loop(0, 2, step, 0)
 
 
 def sum_kernel(pieces, out, three):
@@ -476,15 +476,14 @@
         conv_flops, field_other, err_other, total, three,
     )
     kept, one_first, one_last = lax.optimization_barrier((kept, one_first, one_last))
+    one_before, one_after = shifted(one_last, GY, 1), shifted(one_first, GY, -1)
     part, three_part = call(
         sum_kernel, [((64, PIECE, 128), BF16, True), ((PIECE, 128), BF16)], [], 0,
         lax.all_to_all(kept, FLAT, 0, 0),
     )
-    (input_grad,) = call(
-        input_kernel, [(block, BF16, True)], [(field, BF16), ((384, 1152), BF16)],
-        conv_flops // 4, *halo_pieces(err_one, 1, one_first, one_last), taps_one,
-    )
-    part, input_grad = lax.optimization_barrier((part, input_grad))
+    part, one_before, one_after = lax.optimization_barrier((part, one_before, one_after))
+    low, high = call(slab_kernel, [((1, 6, 64, 128), BF16)] * 2, [], 0, err_one, one_before, one_after)
+    one_left, one_right = exchange_x(low, high)
     whole = lax.all_to_all(part, FLAT, 0, 0).reshape(64 * PIECE, 128)
     both = swap_cores(three_part)
     both = jnp.where(first_core, jnp.stack([three_part, both]), jnp.stack([both, three_part]))
@@ -496,7 +495,14 @@
         compiler_params=pltpu.CompilerParams(vmem_limit_bytes=8 << 20),
         name="place_kernel",
     )(chip, *ring_pieces([both] * 4, "x"))
-    whole, grad_three = lax.optimization_barrier((whole, grad_three))
+    whole, grad_three, one_left, one_right = lax.optimization_barrier(
+        (whole, grad_three, one_left, one_right)
+    )
+    (input_grad,) = call(
+        input_kernel, [(block, BF16, True)], [(field, BF16), ((384, 1152), BF16)],
+        conv_flops // 4, in_hbm(err_one), in_hbm(one_before), in_hbm(one_after), one_left, one_right,
+        in_hbm(taps_one),
+    )
     grad_three = jnp.swapaxes(grad_three, 1, 2).reshape(3, 3, 3, 128, 16)
     grad_one, grad_two = pl.pallas_call(
         functools.partial(finish_kernel, scale=fine_scale),

time: 144 us -> 138 us (0.958)
  waiting for transfers between devices: 50.3 us -> 46.6 us
  starting transfers between devices: 59.5 us -> 57.8 us
    all_to_all x1, waiting for transfers between devices: 0.01 us -> 20.1 us  [on_device(): lax.all_to_all(kept, FLAT, 0, 0)]
    ppermute x16, waiting for transfers between devices: 36.1 us -> 18.9 us  [shifted(): lax.ppermute(array, axes, [(i, (i + step) % count) for i in range(count)])]
    ppermute x6, starting transfers between devices: 2.96 us -> 9.42 us  [swap_cores(): return lax.ppermute(array, 'c', [(0, 1), (1, 0)])]
    all_to_all x1, starting transfers between devices: 9.55 us -> 4.98 us  [on_device(): lax.all_to_all(kept, FLAT, 0, 0)]
    ppermute x6, waiting for transfers between devices: 4.2 us -> 0.57 us  [swap_cores(): return lax.ppermute(array, 'c', [(0, 1), (1, 0)])]
    ppermute x16, starting transfers between devices: 31.6 us -> 28 us  [shifted(): lax.ppermute(array, axes, [(i, (i + step) % count) for i in range(count)])]
    all_to_all x1, waiting for transfers between devices: 2.32 us -> 0.01 us  [on_device(): whole = lax.all_to_all(part, FLAT, 0, 0).reshape(64 * PIECE, 128)]
  transfers between devices with their start and end apart: 28 -> 28, of which waited for: 15 -> 11; matrix products, arithmetic and copies ran while one was open for 3% -> 2% of each run, Pallas kernels for 15% -> 17%
where the time goes in v12:
time: 138 us; the launch traced here: 137 us
  starting transfers between devices  57.8 us (42%)
  waiting for transfers between devices  46.6 us (34%)
  Pallas kernels  29.3 us (21%)
  local copies, waits for them, and re-layouts  1.56 us (1%)
    ppermute x16, starting transfers between devices, shifted(): lax.ppermute(array, axes, [(i, (i + step) % count) for i in range(count)])  28 us
    pallas_call x13, Pallas kernels, call(): pl.pallas_call(kernel, out_shape=shapes, in_specs=[pl.BlockSpec(memory_sp...  26.6 us
    all_to_all x1, waiting for transfers between devices, on_device(): lax.all_to_all(kept, FLAT, 0, 0)  20.1 us
    ppermute x16, waiting for transfers between devices, shifted(): lax.ppermute(array, axes, [(i, (i + step) % count) for i in range(count)])  18.9 us
    ppermute x6, starting transfers between devices, swap_cores(): return lax.ppermute(array, 'c', [(0, 1), (1, 0)])  9.42 us
    ppermute x3, waiting for transfers between devices, ring_pieces(): lax.ppermute(pieces[d], axis, [(i, (i + d) % 4) for i in range(4)])  7.03 us
    all_to_all x1, starting transfers between devices, on_device(): whole = lax.all_to_all(part, FLAT, 0, 0).reshape(64 * PIECE, 128)  6.99 us
    all_to_all x1, starting transfers between devices, on_device(): lax.all_to_all(kept, FLAT, 0, 0)  4.98 us
  transfers between devices with their start and end apart: 28, of which 11 were waited for; matrix products, arithmetic and copies ran while one was open for 2% of the time, Pallas kernels for 17%

profile of v12, /device:TPU:1, one launch (start us, length us, event | category | flops | bytes accessed | tf_op | source)
XLA Modules:
  0.0 137.3 jit_solution(11741050966384311778)
XLA Ops:
  1.7 2.2 %collective-permute-start = (bf16[5,2,64,128]{3,2,1,0:T(8,128)(2,1)S(1)}, bf16[5,2,64,128]{3,2,1,0:T(8,128)(2,1)S(1)}, u32[]{:S(2)}, u32[]{:S(2)}) collective-permute-start(bf16[5,2,64,128]{3,2,1,0:T(8,128)(2,1)S(1)} %get-tuple-element.61), channel_id=1, source_target_pairs={{0,1},{1,2},{2,3},{3,4},{4,5},{5,6},{6,7},{7,8},{8,9},{9,10},{10,1... | collective-permute-start | bytes 491528 | tf_op jit(solution)/shard_map/ppermute | solution.py:22
  3.9 5.0 %collective-permute-start.1 = (bf16[5,2,64,128]{3,2,1,0:T(8,128)(2,1)S(1)}, bf16[5,2,64,128]{3,2,1,0:T(8,128)(2,1)S(1)}, u32[]{:S(2)}, u32[]{:S(2)}) collective-permute-start(bf16[5,2,64,128]{3,2,1,0:T(8,128)(2,1)S(1)} %get-tuple-element.62), channel_id=1, source_target_pairs={{0,15},{1,0},{2,1},{3,2},{4,3},{5,4},{6,5},{7,6},{8,7},{9,8},{10,9... | collective-permute-start | bytes 491528 | tf_op jit(solution)/shard_map/ppermute | solution.py:22
  10.8 3.6 %all-to-all-start = ((bf16[16,27,8,128]{3,2,1,0:T(8,128)(2,1)}), bf16[16,27,8,128]{3,2,1,0:T(8,128)(2,1)S(1)}, u32[]{:S(2)}, u32[]{:S(2)}) async-start(bf16[16,27,8,128]{3,2,1,0:T(8,128)(2,1)} %broadcast_in_dim.3), calls=%async_computation | async-start | bytes 1769472 | tf_op jit(solution)/shard_map/all_to_all | solution.py:424
  14.5 2.1 %collective-permute-start.2 = (bf16[20,64,128]{2,1,0:T(8,128)(2,1)S(1)}, bf16[20,64,128]{2,1,0:T(8,128)(2,1)S(1)}, u32[]{:S(2)}, u32[]{:S(2)}) collective-permute-start(bf16[20,64,128]{2,1,0:T(8,128)(2,1)S(1)} %get-tuple-element.63), channel_id=1, source_target_pairs={{0,16},{16,32},{32,48},{48,64},{64,80},{80,96},{96,112},{112,0},{1... | collective-permute-start | bytes 983048 | tf_op jit(solution)/shard_map/ppermute | solution.py:22
  16.6 4.0 %collective-permute-done.2.left.f_left = bf16[20,64,128]{2,1,0:T(8,128)(2,1)S(1)} collective-permute-done((bf16[20,64,128]{2,1,0:T(8,128)(2,1)S(1)}, bf16[20,64,128]{2,1,0:T(8,128)(2,1)S(1)}, u32[]{:S(2)}, u32[]{:S(2)}) %collective-permute-start.2) | collective-permute-done | bytes 327712 | tf_op jit(solution)/shard_map/ppermute | solution.py:22
  20.6 2.8 %collective-permute-done.3.right.f_right = bf16[20,64,128]{2,1,0:T(8,128)(2,1)S(1)} collective-permute-done((bf16[20,64,128]{2,1,0:T(8,128)(2,1)S(1)}, bf16[20,64,128]{2,1,0:T(8,128)(2,1)S(1)}, u32[]{:S(2)}, u32[]{:S(2)}) %collective-permute-start.3) | collective-permute-done | bytes 327712 | tf_op jit(solution)/shard_map/ppermute | solution.py:22
  23.4 6.8 %forward_kernel.1 = (bf16[6,6,64,128]{3,2,1,0:T(8,128)(2,1)}, bf16[6,6,64,128]{3,2,1,0:T(8,128)(2,1)}, bf16[4,4,64,128]{3,2,1,0:T(8,128)(2,1)}, bf16[4,4,64,128]...) custom-call(s32[1]{0:T(128)} %bitcast.core, bf16[4,4,64,128]{3,2,1,0:T(8,128)(2,1)S(1)} %copy-done.2, ...), custom_call_target="tpu_custom_call" | custom-call | flops 135895456 | bytes 150733 | tf_op jit(solution)/shard_map/forward_kernel/pallas_call | solution.py:395
  31.7 4.1 %collective-permute-start.5 = (bf16[2,2,32,128]{3,2,1,0:T(8,128)(2,1)S(1)}, bf16[2,2,32,128]{3,2,1,0:T(8,128)(2,1)S(1)}, u32[]{:S(2)}, u32[]{:S(2)}) collective-permute-start(bf16[2,2,32,128]{3,2,1,0:T(8,128)(2,1)S(1)} %get-tuple-element.66.own), channel_id=1, source_target_pairs={{0,15},{1,0},{2,1},{3,2},{4,3},{5,4},{6,5},{7,6},{8,7},{9,8},{10,9... | collective-permute-start | bytes 98312 | tf_op jit(solution)/shard_map/ppermute | solution.py:22
  37.1 2.3 %collective-permute-start.6 = (bf16[2,6,32,128]{3,2,1,0:T(8,128)(2,1)S(1)}, bf16[2,6,32,128]{3,2,1,0:T(8,128)(2,1)S(1)}, u32[]{:S(2)}, u32[]{:S(2)}) collective-permute-start(bf16[2,6,32,128]{3,2,1,0:T(8,128)(2,1)S(1)} %get-tuple-element.67), channel_id=1, source_target_pairs={{0,16},{16,32},{32,48},{48,64},{64,80},{80,96},{96,112},{112,0},{1... | collective-permute-start | bytes 294920 | tf_op jit(solution)/shard_map/ppermute | solution.py:22
  41.0 2.4 %collective-permute-done.7.right = bf16[2,6,32,128]{3,2,1,0:T(8,128)(2,1)S(1)} collective-permute-done((bf16[2,6,32,128]{3,2,1,0:T(8,128)(2,1)S(1)}, bf16[2,6,32,128]{3,2,1,0:T(8,128)(2,1)S(1)}, u32[]{:S(2)}, u32[]{:S(2)}) %collective-permute-start.7) | collective-permute-done | bytes 98336 | tf_op jit(solution)/shard_map/ppermute | solution.py:22
  43.4 4.1 %bottom_kernel.1 = (bf16[2,2,32,256]{3,2,1,0:T(8,128)(2,1)}, bf16[24,32,128]{2,1,0:T(8,128)(2,1)S(1)}, bf16[4,4,64,128]{3,2,1,0:T(8,128)(2,1)S(1)}, bf16[4,1,64,...) custom-call(bf16[2,2,32,128]{3,2,1,0:T(8,128)(2,1)S(1)} %get-tuple-element.66.own, ...), custom_call_target="tpu_custom_call" | custom-call | flops 45298484 | bytes 181862 | tf_op jit(solution)/shard_map/bottom_kernel/pallas_call | solution.py:395
  47.5 5.1 %collective-permute-start.10 = (bf16[4,1,64,128]{3,2,1,0:T(8,128)(2,1)S(1)}, bf16[4,1,64,128]{3,2,1,0:T(8,128)(2,1)S(1)}, u32[]{:S(2)}, u32[]{:S(2)}) collective-permute-start(bf16[4,1,64,128]{3,2,1,0:T(8,128)(2,1)S(1)} %get-tuple-element.74), channel_id=1, source_target_pairs={{0,15},{1,0},{2,1},{3,2},{4,3},{5,4},{6,5},{7,6},{8,7},{9,8},{10,9... | collective-permute-start | bytes 196616 | tf_op jit(solution)/shard_map/ppermute | solution.py:22
  54.0 5.1 %collective-permute-done.9.before = bf16[4,1,64,128]{3,2,1,0:T(8,128)(2,1)S(1)} collective-permute-done((bf16[4,1,64,128]{3,2,1,0:T(8,128)(2,1)S(1)}, bf16[4,1,64,128]{3,2,1,0:T(8,128)(2,1)S(1)}, u32[]{:S(2)}, u32[]{:S(2)}) %collective-permute-start.9) | collective-permute-done | bytes 65568 | tf_op jit(solution)/shard_map/ppermute | solution.py:22
  65.5 2.6 %first_errors_kernel.1 = (bf16[4,4,64,128]{3,2,1,0:T(8,128)(2,1)}, bf16[4,1,64,128]{3,2,1,0:T(8,128)(2,1)}, bf16[4,1,64,128]{3,2,1,0:T(8,128)(2,1)}, bf16[4,4,64...) custom-call(s32[1]{0:T(128)} %bitcast.core, bf16[4,4,64,128]{3,2,1,0:T(8,128)(2,1)S(1)} %get-tuple-element.72.own, ...), custom_call_target="tpu_custom_call" | custom-call | flops 45298484 | bytes 86835 | tf_op jit(solution)/shard_map/first_errors_kernel/pallas_call | solution.py:395
  70.5 3.2 %pair_grads_kernel.1 = bf16[64,112,128]{2,1,0:T(8,128)(2,1)} custom-call(bf16[6,6,64,128]{3,2,1,0:T(8,128)(2,1)S(1)} %collective-permute-done.14.fields, bf16[4,4,64,128]{3,2,1,0:T(8,128)(2,1)S(1)} %collective-permute-done.15.errors, f32[1152,384]{1,0:T(8,128)S(1)} %own_grads_kernel.1.own_total, bf16[64,56,128]{2,1,0:T(8,128)(2,1)S(1)} %bottom_grads_kernel.1.three), custom_call_target="tpu_custom_call" | custom-call | flops 45298484 | bytes 176947 | tf_op jit(solution)/shard_map/pair_grads_kernel/pallas_call | solution.py:395
  73.7 5.0 %all-to-all-start.1 = ((bf16[64,112,128]{2,1,0:T(8,128)(2,1)}), bf16[64,112,128]{2,1,0:T(8,128)(2,1)S(1)}, u32[]{:S(2)}, u32[]{:S(2)}) async-start(bf16[64,112,128]{2,1,0:T(8,128)(2,1)} %pair_grads_kernel.1), calls=%async_computation.1 | async-start | bytes 3670016 | tf_op jit(solution)/shard_map/all_to_all | solution.py:482
  79.7 3.8 %collective-permute-start.17 = (bf16[4,1,64,128]{3,2,1,0:T(8,128)(2,1)S(1)}, bf16[4,1,64,128]{3,2,1,0:T(8,128)(2,1)S(1)}, u32[]{:S(2)}, u32[]{:S(2)}) collective-permute-start(bf16[4,1,64,128]{3,2,1,0:T(8,128)(2,1)S(1)} %copy-done.9), channel_id=1, source_target_pairs={{0,15},{1,0},{2,1},{3,2},{4,3},{5,4},{6,5},{7,6},{8,7},{9,8},{10,9... | collective-permute-start | bytes 196616 | tf_op jit(solution)/shard_map/ppermute | solution.py:22
  83.5 20.1 %all-to-all-done.1.pieces = bf16[64,112,128]{2,1,0:T(8,128)(2,1)S(1)} async-done(((bf16[64,112,128]{2,1,0:T(8,128)(2,1)}), bf16[64,112,128]{2,1,0:T(8,128)(2,1)S(1)}, u32[]{:S(2)}, u32[]{:S(2)}) %all-to-all-start.1) | async-done | bytes 1835040 | tf_op jit(solution)/shard_map/all_to_all | solution.py:482
  104.8 7.0 %all-to-all-start.2 = ((bf16[64,56,128]{2,1,0:T(8,128)(2,1)}), bf16[64,56,128]{2,1,0:T(8,128)(2,1)S(1)}, u32[]{:S(2)}, u32[]{:S(2)}) async-start(bf16[64,56,128]{2,1,0:T(8,128)(2,1)} %get-tuple-element.98), calls=%async_computation.2 | async-start | bytes 1835008 | tf_op jit(solution)/shard_map/all_to_all | solution.py:487
  116.4 2.2 %collective-permute-start.20 = (bf16[2,56,128]{2,1,0:T(8,128)(2,1)S(1)}, bf16[2,56,128]{2,1,0:T(8,128)(2,1)S(1)}, u32[]{:S(2)}, u32[]{:S(2)}) collective-permute-start(bf16[2,56,128]{2,1,0:T(8,128)(2,1)S(1)} %maximum_select_fusion.1.pair_0), channel_id=1, source_target_pairs={{0,64},{32,96},{64,0},{96,32},{1,65},{33,97},{65,1},{97,33},{2,66}... | collective-permute-start | bytes 86024 | tf_op jit(solution)/shard_map/ppermute | solution.py:30
  119.8 7.0 %collective-permute-done.19.pair_1 = bf16[2,56,128]{2,1,0:T(8,128)(2,1)S(1)} collective-permute-done((bf16[2,56,128]{2,1,0:T(8,128)(2,1)S(1)}, bf16[2,56,128]{2,1,0:T(8,128)(2,1)S(1)}, u32[]{:S(2)}, u32[]{:S(2)}) %collective-permute-start.19) | collective-permute-done | bytes 28704 | tf_op jit(solution)/shard_map/ppermute | solution.py:30
  127.6 3.8 %collective-permute-start.24 = (bf16[3584,128]{1,0:T(8,128)(2,1)S(1)}, bf16[3584,128]{1,0:T(8,128)(2,1)S(1)}, u32[]{:S(2)}, u32[]{:S(2)}) collective-permute-start(bf16[3584,128]{1,0:T(8,128)(2,1)S(1)} %bitcast.25), channel_id=1, source_target_pairs={{0,16},{16,0},{1,17},{17,1},{2,18},{18,2},{3,19},{19,3},{4,20},{20... | collective-permute-start | bytes 2752520 | tf_op jit(solution)/shard_map/ppermute | solution.py:26
  131.4 3.8 %input_kernel.1 = bf16[4,4,64,128]{3,2,1,0:T(8,128)(2,1)} custom-call(bf16[4,4,64,128]{3,2,1,0:T(8,128)(2,1)} %get-tuple-element.84.own, bf16[4,1,64,128]{3,2,1,0:T(8,128)(2,1)} %copy-done.7, bf16[4,1,64,128]{3,2,1,0:T(8,128)(2,1)} %copy-done.8, bf16[1,6,64,128]{3,2,1,0:T(8,128)(2,1)S(1)} %collective-permute-done.22.left, ...), custom_call_target="tpu_custom_call" | custom-call | flops 11324620 | bytes 73728 | tf_op jit(solution)/shard_map/input_kernel/pallas_call | solution.py:395
  135.2 2.1 %finish_kernel.1 = (f32[3456,128]{1,0:T(8,128)}, f32[3456,128]{1,0:T(8,128)}) custom-call(s32[1]{0:T(128)} %bitcast.core, bf16[3584,128]{1,0:T(8,128)(2,1)S(1)} %bitcast.26, bf16[3584,128]{1,0:T(8,128)(2,1)S(1)} %collective-permute-done.24.other), custom_call_target="tpu_custom_call" | custom-call | tf_op jit(solution)/shard_map/finish_kernel/pallas_call | solution.py:507
  (74 shorter events, 26.3 us)
Async XLA Ops:
  1.7 12.7 %collective-permute-start = (bf16[5,2,64,128]{3,2,1,0:T(8,128)(2,1)S(1)}, bf16[5,2,64,128]{3,2,1,0:T(8,128)(2,1)S(1)}, u32[]{:S(2)}, u32[]{:S(2)}) collective-permute-start(bf16[5,2,64,128]{3,2,1,0:T(8,128)(2,1)S(1)} %get-tuple-element.61), channel_id=1, source_target_pairs={{0,1},{1,2},{2,3},{3,4},{4,5},{5,6},{6,7},{7,8},{8,9},{9,10},{10,1... | collective-permute-start | bytes 491528 | tf_op jit(solution)/shard_map/ppermute | solution.py:22
  3.9 10.6 %collective-permute-start.1 = (bf16[5,2,64,128]{3,2,1,0:T(8,128)(2,1)S(1)}, bf16[5,2,64,128]{3,2,1,0:T(8,128)(2,1)S(1)}, u32[]{:S(2)}, u32[]{:S(2)}) collective-permute-start(bf16[5,2,64,128]{3,2,1,0:T(8,128)(2,1)S(1)} %get-tuple-element.62), channel_id=1, source_target_pairs={{0,15},{1,0},{2,1},{3,2},{4,3},{5,4},{6,5},{7,6},{8,7},{9,8},{10,9... | collective-permute-start | bytes 491528 | tf_op jit(solution)/shard_map/ppermute | solution.py:22
  10.8 19.4 %all-to-all-start = ((bf16[16,27,8,128]{3,2,1,0:T(8,128)(2,1)}), bf16[16,27,8,128]{3,2,1,0:T(8,128)(2,1)S(1)}, u32[]{:S(2)}, u32[]{:S(2)}) async-start(bf16[16,27,8,128]{3,2,1,0:T(8,128)(2,1)} %broadcast_in_dim.3), calls=%async_computation | async-start | bytes 1769472 | tf_op jit(solution)/shard_map/all_to_all | solution.py:424
  14.5 6.1 %collective-permute-start.2 = (bf16[20,64,128]{2,1,0:T(8,128)(2,1)S(1)}, bf16[20,64,128]{2,1,0:T(8,128)(2,1)S(1)}, u32[]{:S(2)}, u32[]{:S(2)}) collective-permute-start(bf16[20,64,128]{2,1,0:T(8,128)(2,1)S(1)} %get-tuple-element.63), channel_id=1, source_target_pairs={{0,16},{16,32},{32,48},{48,64},{64,80},{80,96},{96,112},{112,0},{1... | collective-permute-start | bytes 983048 | tf_op jit(solution)/shard_map/ppermute | solution.py:22
  16.6 6.8 %collective-permute-start.3 = (bf16[20,64,128]{2,1,0:T(8,128)(2,1)S(1)}, bf16[20,64,128]{2,1,0:T(8,128)(2,1)S(1)}, u32[]{:S(2)}, u32[]{:S(2)}) collective-permute-start(bf16[20,64,128]{2,1,0:T(8,128)(2,1)S(1)} %get-tuple-element.64), channel_id=1, source_target_pairs={{0,112},{16,0},{32,16},{48,32},{64,48},{80,64},{96,80},{112,96},{1... | collective-permute-start | bytes 983048 | tf_op jit(solution)/shard_map/ppermute | solution.py:22
  30.1 9.2 %collective-permute-start.8 = (bf16[16,27,8,128]{3,2,1,0:T(8,128)(2,1)S(1)}, bf16[16,27,8,128]{3,2,1,0:T(8,128)(2,1)S(1)}, u32[]{:S(2)}, u32[]{:S(2)}) collective-permute-start(bf16[16,27,8,128]{3,2,1,0:T(8,128)(2,1)S(1)} %all-to-all-done), channel_id=1, source_target_pairs={{0,16},{16,0},{1,17},{17,1},{2,18},{18,2},{3,19},{19,3},{4,20},{20... | collective-permute-start | bytes 2654216 | tf_op jit(solution)/shard_map/ppermute | solution.py:26
  31.0 6.1 %collective-permute-start.4 = (bf16[2,2,32,128]{3,2,1,0:T(8,128)(2,1)S(1)}, bf16[2,2,32,128]{3,2,1,0:T(8,128)(2,1)S(1)}, u32[]{:S(2)}, u32[]{:S(2)}) collective-permute-start(bf16[2,2,32,128]{3,2,1,0:T(8,128)(2,1)S(1)} %get-tuple-element.66.own), channel_id=1, source_target_pairs={{0,1},{1,2},{2,3},{3,4},{4,5},{5,6},{6,7},{7,8},{8,9},{9,10},{10,1... | collective-permute-start | bytes 98312 | tf_op jit(solution)/shard_map/ppermute | solution.py:22
  31.7 5.4 %collective-permute-start.5 = (bf16[2,2,32,128]{3,2,1,0:T(8,128)(2,1)S(1)}, bf16[2,2,32,128]{3,2,1,0:T(8,128)(2,1)S(1)}, u32[]{:S(2)}, u32[]{:S(2)}) collective-permute-start(bf16[2,2,32,128]{3,2,1,0:T(8,128)(2,1)S(1)} %get-tuple-element.66.own), channel_id=1, source_target_pairs={{0,15},{1,0},{2,1},{3,2},{4,3},{5,4},{6,5},{7,6},{8,7},{9,8},{10,9... | collective-permute-start | bytes 98312 | tf_op jit(solution)/shard_map/ppermute | solution.py:22
  35.8 34.7 %collective-permute-start.14 = (bf16[6,6,64,128]{3,2,1,0:T(8,128)(2,1)}, bf16[6,6,64,128]{3,2,1,0:T(8,128)(2,1)S(1)}, u32[]{:S(2)}, u32[]{:S(2)}) collective-permute-start(bf16[6,6,64,128]{3,2,1,0:T(8,128)(2,1)} %get-tuple-element.85), channel_id=1, source_target_pairs={{0,16},{16,0},{1,17},{17,1},{2,18},{18,2},{3,19},{19,3},{4,20},{20... | collective-permute-start | bytes 1769480 | tf_op jit(solution)/shard_map/ppermute | solution.py:26
  37.1 3.9 %collective-permute-start.6 = (bf16[2,6,32,128]{3,2,1,0:T(8,128)(2,1)S(1)}, bf16[2,6,32,128]{3,2,1,0:T(8,128)(2,1)S(1)}, u32[]{:S(2)}, u32[]{:S(2)}) collective-permute-start(bf16[2,6,32,128]{3,2,1,0:T(8,128)(2,1)S(1)} %get-tuple-element.67), channel_id=1, source_target_pairs={{0,16},{16,32},{32,48},{48,64},{64,80},{80,96},{96,112},{112,0},{1... | collective-permute-start | bytes 294920 | tf_op jit(solution)/shard_map/ppermute | solution.py:22
  39.4 4.0 %collective-permute-start.7 = (bf16[2,6,32,128]{3,2,1,0:T(8,128)(2,1)S(1)}, bf16[2,6,32,128]{3,2,1,0:T(8,128)(2,1)S(1)}, u32[]{:S(2)}, u32[]{:S(2)}) collective-permute-start(bf16[2,6,32,128]{3,2,1,0:T(8,128)(2,1)S(1)} %get-tuple-element.68), channel_id=1, source_target_pairs={{0,112},{16,0},{32,16},{48,32},{64,48},{80,64},{96,80},{112,96},{1... | collective-permute-start | bytes 294920 | tf_op jit(solution)/shard_map/ppermute | solution.py:22
  47.5 6.5 %collective-permute-start.10 = (bf16[4,1,64,128]{3,2,1,0:T(8,128)(2,1)S(1)}, bf16[4,1,64,128]{3,2,1,0:T(8,128)(2,1)S(1)}, u32[]{:S(2)}, u32[]{:S(2)}) collective-permute-start(bf16[4,1,64,128]{3,2,1,0:T(8,128)(2,1)S(1)} %get-tuple-element.74), channel_id=1, source_target_pairs={{0,15},{1,0},{2,1},{3,2},{4,3},{5,4},{6,5},{7,6},{8,7},{9,8},{10,9... | collective-permute-start | bytes 196616 | tf_op jit(solution)/shard_map/ppermute | solution.py:22
  52.7 6.4 %collective-permute-start.9 = (bf16[4,1,64,128]{3,2,1,0:T(8,128)(2,1)S(1)}, bf16[4,1,64,128]{3,2,1,0:T(8,128)(2,1)S(1)}, u32[]{:S(2)}, u32[]{:S(2)}) collective-permute-start(bf16[4,1,64,128]{3,2,1,0:T(8,128)(2,1)S(1)} %get-tuple-element.73), channel_id=1, source_target_pairs={{0,1},{1,2},{2,3},{3,4},{4,5},{5,6},{6,7},{7,8},{8,9},{9,10},{10,1... | collective-permute-start | bytes 196616 | tf_op jit(solution)/shard_map/ppermute | solution.py:22
  61.2 4.3 %collective-permute-start.13 = (bf16[1,6,64,128]{3,2,1,0:T(8,128)(2,1)S(1)}, bf16[1,6,64,128]{3,2,1,0:T(8,128)(2,1)S(1)}, u32[]{:S(2)}, u32[]{:S(2)}) collective-permute-start(bf16[1,6,64,128]{3,2,1,0:T(8,128)(2,1)S(1)} %get-tuple-element.80), channel_id=1, source_target_pairs={{0,112},{16,0},{32,16},{48,32},{64,48},{80,64},{96,80},{112,96},{1... | collective-permute-start | bytes 294920 | tf_op jit(solution)/shard_map/ppermute | solution.py:22
  73.7 30.0 %all-to-all-start.1 = ((bf16[64,112,128]{2,1,0:T(8,128)(2,1)}), bf16[64,112,128]{2,1,0:T(8,128)(2,1)S(1)}, u32[]{:S(2)}, u32[]{:S(2)}) async-start(bf16[64,112,128]{2,1,0:T(8,128)(2,1)} %pair_grads_kernel.1), calls=%async_computation.1 | async-start | bytes 3670016 | tf_op jit(solution)/shard_map/all_to_all | solution.py:482
  78.7 26.1 %collective-permute-start.16 = (bf16[4,1,64,128]{3,2,1,0:T(8,128)(2,1)S(1)}, bf16[4,1,64,128]{3,2,1,0:T(8,128)(2,1)S(1)}, u32[]{:S(2)}, u32[]{:S(2)}) collective-permute-start(bf16[4,1,64,128]{3,2,1,0:T(8,128)(2,1)S(1)} %copy-done.10), channel_id=1, source_target_pairs={{0,1},{1,2},{2,3},{3,4},{4,5},{5,6},{6,7},{7,8},{8,9},{9,10},{10,1... | collective-permute-start | bytes 196616 | tf_op jit(solution)/shard_map/ppermute | solution.py:22
  79.7 25.0 %collective-permute-start.17 = (bf16[4,1,64,128]{3,2,1,0:T(8,128)(2,1)S(1)}, bf16[4,1,64,128]{3,2,1,0:T(8,128)(2,1)S(1)}, u32[]{:S(2)}, u32[]{:S(2)}) collective-permute-start(bf16[4,1,64,128]{3,2,1,0:T(8,128)(2,1)S(1)} %copy-done.9), channel_id=1, source_target_pairs={{0,15},{1,0},{2,1},{3,2},{4,3},{5,4},{6,5},{7,6},{8,7},{9,8},{10,9... | collective-permute-start | bytes 196616 | tf_op jit(solution)/shard_map/ppermute | solution.py:22
  104.8 22.8 %all-to-all-start.2 = ((bf16[64,56,128]{2,1,0:T(8,128)(2,1)}), bf16[64,56,128]{2,1,0:T(8,128)(2,1)S(1)}, u32[]{:S(2)}, u32[]{:S(2)}) async-start(bf16[64,56,128]{2,1,0:T(8,128)(2,1)} %get-tuple-element.98), calls=%async_computation.2 | async-start | bytes 1835008 | tf_op jit(solution)/shard_map/all_to_all | solution.py:487
  113.8 13.7 %collective-permute-start.22 = (bf16[1,6,64,128]{3,2,1,0:T(8,128)(2,1)S(1)}, bf16[1,6,64,128]{3,2,1,0:T(8,128)(2,1)S(1)}, u32[]{:S(2)}, u32[]{:S(2)}) collective-permute-start(bf16[1,6,64,128]{3,2,1,0:T(8,128)(2,1)S(1)} %get-tuple-element.101), channel_id=1, source_target_pairs={{0,16},{16,32},{32,48},{48,64},{64,80},{80,96},{96,112},{112,0},{1... | collective-permute-start | bytes 294920 | tf_op jit(solution)/shard_map/ppermute | solution.py:22
  115.0 12.5 %collective-permute-start.23 = (bf16[1,6,64,128]{3,2,1,0:T(8,128)(2,1)S(1)}, bf16[1,6,64,128]{3,2,1,0:T(8,128)(2,1)S(1)}, u32[]{:S(2)}, u32[]{:S(2)}) collective-permute-start(bf16[1,6,64,128]{3,2,1,0:T(8,128)(2,1)S(1)} %get-tuple-element.102), channel_id=1, source_target_pairs={{0,112},{16,0},{32,16},{48,32},{64,48},{80,64},{96,80},{112,96},{1... | collective-permute-start | bytes 294920 | tf_op jit(solution)/shard_map/ppermute | solution.py:22
  115.1 11.8 %collective-permute-start.19 = (bf16[2,56,128]{2,1,0:T(8,128)(2,1)S(1)}, bf16[2,56,128]{2,1,0:T(8,128)(2,1)S(1)}, u32[]{:S(2)}, u32[]{:S(2)}) collective-permute-start(bf16[2,56,128]{2,1,0:T(8,128)(2,1)S(1)} %maximum_select_fusion.1.pair_0), channel_id=1, source_target_pairs={{0,32},{32,64},{64,96},{96,0},{1,33},{33,65},{65,97},{97,1},{2,34}... | collective-permute-start | bytes 86024 | tf_op jit(solution)/shard_map/ppermute | solution.py:30
  116.4 10.4 %collective-permute-start.20 = (bf16[2,56,128]{2,1,0:T(8,128)(2,1)S(1)}, bf16[2,56,128]{2,1,0:T(8,128)(2,1)S(1)}, u32[]{:S(2)}, u32[]{:S(2)}) collective-permute-start(bf16[2,56,128]{2,1,0:T(8,128)(2,1)S(1)} %maximum_select_fusion.1.pair_0), channel_id=1, source_target_pairs={{0,64},{32,96},{64,0},{96,32},{1,65},{33,97},{65,1},{97,33},{2,66}... | collective-permute-start | bytes 86024 | tf_op jit(solution)/shard_map/ppermute | solution.py:30
  118.6 8.2 %collective-permute-start.21 = (bf16[2,56,128]{2,1,0:T(8,128)(2,1)S(1)}, bf16[2,56,128]{2,1,0:T(8,128)(2,1)S(1)}, u32[]{:S(2)}, u32[]{:S(2)}) collective-permute-start(bf16[2,56,128]{2,1,0:T(8,128)(2,1)S(1)} %maximum_select_fusion.1.pair_0), channel_id=1, source_target_pairs={{0,96},{32,0},{64,32},{96,64},{1,97},{33,1},{65,33},{97,65},{2,98}... | collective-permute-start | bytes 86024 | tf_op jit(solution)/shard_map/ppermute | solution.py:30
  127.6 7.7 %collective-permute-start.24 = (bf16[3584,128]{1,0:T(8,128)(2,1)S(1)}, bf16[3584,128]{1,0:T(8,128)(2,1)S(1)}, u32[]{:S(2)}, u32[]{:S(2)}) collective-permute-start(bf16[3584,128]{1,0:T(8,128)(2,1)S(1)} %bitcast.25), channel_id=1, source_target_pairs={{0,16},{16,0},{1,17},{17,1},{2,18},{18,2},{3,19},{19,3},{4,20},{20... | collective-permute-start | bytes 2752520 | tf_op jit(solution)/shard_map/ppermute | solution.py:26
  (15 other events, 199.8 us)

commit v13 on v12

--- a/solution.py
+++ b/solution.py
@@ -215,12 +215,13 @@
     for at in range(9):
         for kz in range(3):
             packed[kz * 256 : kz * 256 + 256, at * 128 : at * 128 + 128] = taps_three[at * 3 + kz]
+    product = dot_nt(window_rows(padded, 0, 4, rows=4), packed[...])
+    acts, slopes = slope_and_silu(join_taps(product, 16, 32, 256))
     for row in range(4):
-        product = dot_nt(window_rows(padded, row, 4), packed[...])
-        act, slope = slope_and_silu(join_taps(product, 4, 32, 256))
+        columns = slice(4 * row, 4 * row + 4)
         if row in (1, 2):
-            bottleneck[row - 1] = act[1:3].astype(BF16)
-        errs = (grads[row].astype(F32) * slope).astype(BF16)
+            bottleneck[row - 1] = acts[columns][1:3].astype(BF16)
+        errs = (grads[row].astype(F32) * slopes[columns]).astype(BF16)
         errors[row] = errs
         bundle[row * 4 : row * 4 + 4] = padded[row + 1, 1:5]
         if row in (1, 2):
@@ -228,17 +229,16 @@
                 for half in range(2):
                     at = 16 + ((row - 1) * 2 + at_y) * 2 + half
                     bundle[at] = errs[1 + at_y, :, half * 128 : half * 128 + 128]
+    total = jnp.zeros((128, 384), F32)
+    for kx in range(3):
+        for ky in range(3):
+            block = errors[kx : kx + 2, ky : ky + 2].reshape(128, 256)
+            at = kx * 3 + ky
+            back = jnp.concatenate([taps_three[26 - at * 3 - kz] for kz in range(3)], axis=1)
+            total = total + dot_nn(block, back)
+    upwards = join_taps(total, 4, 32, 128) * 0.125
     for row in range(2):
-        total = jnp.zeros((64, 384), F32)
-        for kx in range(3):
-            for ky in range(3):
-                block = errors[row + kx, ky : ky + 2].reshape(64, 256)
-                at = kx * 3 + ky
-                back = jnp.concatenate(
-                    [taps_three[26 - at * 3 - kz] for kz in range(3)], axis=1
-                )
-                total = total + dot_nn(block, back)
-        upward = join_taps(total, 2, 32, 128) * 0.125
+        upward = upwards[2 * row : 2 * row + 2]
         for at_y in range(2):
             wide[pl.ds(0, 32, stride=2), :] = upward[at_y]
             wide[pl.ds(1, 32, stride=2), :] = upward[at_y]
@@ -253,23 +253,17 @@
                         edge[2 * row + dx, 0] = err
 
 
-def add_tap_grads(total, fields, errors):
-    def step(at, _):
-        spread = spread_errors(errors[pl.ds(at * 2, 2)].reshape(8, 64, 128).astype(F32))
-        total[...] += dot_tn(window_rows(fields, at * 2, 4, rows=2), spread)
-        return 0
-
-    lax.fori_loop(0, 2, step, 0)
+def tap_grads(fields, errors):
+    spread = spread_errors(errors[...].reshape(16, 64, 128).astype(F32))
+    return dot_tn(window_rows(fields, 0, 4, rows=4), spread)
 
 
 def own_grads_kernel(fields, errors, total):
-    total[...] = jnp.zeros_like(total)
-    add_tap_grads(total, fields, errors)
+    total[...] = tap_grads(fields, errors)
 
 
 def pair_grads_kernel(fields, errors, own_total, three, out, total):
-    total[...] = own_total[...]
-    add_tap_grads(total, fields, errors)
+    total[...] = own_total[...] + tap_grads(fields, errors)
     for at in range(9):
         for kz in range(3):
             start = (at * 3 + kz) * 128
@@ -286,24 +280,20 @@
 
 
 def bottom_grads_kernel(core, own, other, out, total):
-    for step, bundle in ((0, own), (1, other)):
+    fields, errors = [], []
+    for bundle in (own, other):
         for row in range(2):
-            fields = []
+            columns = []
             for kx in range(3):
                 for ky in range(3):
                     at = (row + kx) * 4 + ky
-                    fields.append(bundle[at : at + 2].reshape(64, 128))
-            at = 16 + row * 4
-            errors = [
-                jnp.concatenate([bundle[at + 2 * y], bundle[at + 2 * y + 1]], axis=1).reshape(1, 32, 256)
-                for y in range(2)
-            ]
-            errors = jnp.concatenate(errors, axis=0).astype(F32)
-            term = dot_tn(spread_errors(errors), jnp.concatenate(fields, axis=1))
-            if step == 0 and row == 0:
-                total[...] = term
-            else:
-                total[...] += term
+                    columns.append(bundle[at : at + 2].reshape(64, 128))
+            fields.append(jnp.concatenate(columns, axis=1))
+            for at_y in range(2):
+                at = 16 + row * 4 + 2 * at_y
+                errors.append(jnp.concatenate([bundle[at], bundle[at + 1]], axis=1).reshape(1, 32, 256))
+    errors = jnp.concatenate(errors, axis=0).astype(F32)
+    total[...] = dot_tn(spread_errors(errors), jnp.concatenate(fields, axis=0))
     first_core = core[0] == 0
     out[48:64, 48:56] = jnp.zeros((16, 8, 128), BF16)
     for unit in range(27):

time: 138 us -> 137 us (level)
  Pallas kernels: 29.3 us -> 27 us
  waiting for transfers between devices: 46.6 us -> 48 us
    pallas_call x13, Pallas kernels: 26.6 us -> 24.2 us  [call(): pl.pallas_call(kernel, out_shape=shapes, in_specs=[pl.BlockSpec(memory_sp...]
  transfers between devices with their start and end apart: 28 -> 28, of which waited for: 11 -> 12; matrix products, arithmetic and copies ran while one was open for 2% -> 2% of each run, Pallas kernels for 17% -> 16%
where the time goes in v13:
time: 137 us; the launch traced here: 136 us
  starting transfers between devices  57.7 us (42%)
  waiting for transfers between devices  48 us (35%)
  Pallas kernels  27 us (20%)
  local copies, waits for them, and re-layouts  1.55 us (1%)
    ppermute x16, starting transfers between devices, shifted(): lax.ppermute(array, axes, [(i, (i + step) % count) for i in range(count)])  28 us
    pallas_call x13, Pallas kernels, call(): pl.pallas_call(kernel, out_shape=shapes, in_specs=[pl.BlockSpec(memory_sp...  24.2 us
    ppermute x16, waiting for transfers between devices, shifted(): lax.ppermute(array, axes, [(i, (i + step) % count) for i in range(count)])  20.2 us
    all_to_all x1, waiting for transfers between devices, on_device(): lax.all_to_all(kept, FLAT, 0, 0)  20.2 us
    ppermute x6, starting transfers between devices, swap_cores(): return lax.ppermute(array, 'c', [(0, 1), (1, 0)])  9.42 us
    ppermute x3, waiting for transfers between devices, ring_pieces(): lax.ppermute(pieces[d], axis, [(i, (i + d) % 4) for i in range(4)])  7.03 us
    all_to_all x1, starting transfers between devices, on_device(): whole = lax.all_to_all(part, FLAT, 0, 0).reshape(64 * PIECE, 128)  6.9 us
    all_to_all x1, starting transfers between devices, on_device(): lax.all_to_all(kept, FLAT, 0, 0)  5.07 us
  transfers between devices with their start and end apart: 28, of which 12 were waited for; matrix products, arithmetic and copies ran while one was open for 2% of the time, Pallas kernels for 16%

profile of v13, /device:TPU:1, one launch (start us, length us, event | category | flops | bytes accessed | tf_op | source)
XLA Modules:
  0.0 136.3 jit_solution(8742293708187602544)
XLA Ops:
  1.7 2.2 %collective-permute-start = (bf16[5,2,64,128]{3,2,1,0:T(8,128)(2,1)S(1)}, bf16[5,2,64,128]{3,2,1,0:T(8,128)(2,1)S(1)}, u32[]{:S(2)}, u32[]{:S(2)}) collective-permute-start(bf16[5,2,64,128]{3,2,1,0:T(8,128)(2,1)S(1)} %get-tuple-element.61), channel_id=1, source_target_pairs={{0,1},{1,2},{2,3},{3,4},{4,5},{5,6},{6,7},{7,8},{8,9},{9,10},{10,1... | collective-permute-start | bytes 491528 | tf_op jit(solution)/shard_map/ppermute | solution.py:22
  3.9 5.0 %collective-permute-start.1 = (bf16[5,2,64,128]{3,2,1,0:T(8,128)(2,1)S(1)}, bf16[5,2,64,128]{3,2,1,0:T(8,128)(2,1)S(1)}, u32[]{:S(2)}, u32[]{:S(2)}) collective-permute-start(bf16[5,2,64,128]{3,2,1,0:T(8,128)(2,1)S(1)} %get-tuple-element.62), channel_id=1, source_target_pairs={{0,15},{1,0},{2,1},{3,2},{4,3},{5,4},{6,5},{7,6},{8,7},{9,8},{10,9... | collective-permute-start | bytes 491528 | tf_op jit(solution)/shard_map/ppermute | solution.py:22
  10.8 3.6 %all-to-all-start = ((bf16[16,27,8,128]{3,2,1,0:T(8,128)(2,1)}), bf16[16,27,8,128]{3,2,1,0:T(8,128)(2,1)S(1)}, u32[]{:S(2)}, u32[]{:S(2)}) async-start(bf16[16,27,8,128]{3,2,1,0:T(8,128)(2,1)} %broadcast_in_dim.3), calls=%async_computation | async-start | bytes 1769472 | tf_op jit(solution)/shard_map/all_to_all | solution.py:414
  14.5 2.1 %collective-permute-start.2 = (bf16[20,64,128]{2,1,0:T(8,128)(2,1)S(1)}, bf16[20,64,128]{2,1,0:T(8,128)(2,1)S(1)}, u32[]{:S(2)}, u32[]{:S(2)}) collective-permute-start(bf16[20,64,128]{2,1,0:T(8,128)(2,1)S(1)} %get-tuple-element.63), channel_id=1, source_target_pairs={{0,16},{16,32},{32,48},{48,64},{64,80},{80,96},{96,112},{112,0},{1... | collective-permute-start | bytes 983048 | tf_op jit(solution)/shard_map/ppermute | solution.py:22
  16.6 4.0 %collective-permute-done.2.left.f_left = bf16[20,64,128]{2,1,0:T(8,128)(2,1)S(1)} collective-permute-done((bf16[20,64,128]{2,1,0:T(8,128)(2,1)S(1)}, bf16[20,64,128]{2,1,0:T(8,128)(2,1)S(1)}, u32[]{:S(2)}, u32[]{:S(2)}) %collective-permute-start.2) | collective-permute-done | bytes 327712 | tf_op jit(solution)/shard_map/ppermute | solution.py:22
  20.6 2.8 %collective-permute-done.3.right.f_right = bf16[20,64,128]{2,1,0:T(8,128)(2,1)S(1)} collective-permute-done((bf16[20,64,128]{2,1,0:T(8,128)(2,1)S(1)}, bf16[20,64,128]{2,1,0:T(8,128)(2,1)S(1)}, u32[]{:S(2)}, u32[]{:S(2)}) %collective-permute-start.3) | collective-permute-done | bytes 327712 | tf_op jit(solution)/shard_map/ppermute | solution.py:22
  23.4 6.8 %forward_kernel.1 = (bf16[6,6,64,128]{3,2,1,0:T(8,128)(2,1)}, bf16[6,6,64,128]{3,2,1,0:T(8,128)(2,1)}, bf16[4,4,64,128]{3,2,1,0:T(8,128)(2,1)}, bf16[4,4,64,128]...) custom-call(s32[1]{0:T(128)} %bitcast.core, bf16[4,4,64,128]{3,2,1,0:T(8,128)(2,1)S(1)} %copy-done.2, ...), custom_call_target="tpu_custom_call" | custom-call | flops 135895456 | bytes 150733 | tf_op jit(solution)/shard_map/forward_kernel/pallas_call | solution.py:385
  31.7 4.1 %collective-permute-start.5 = (bf16[2,2,32,128]{3,2,1,0:T(8,128)(2,1)S(1)}, bf16[2,2,32,128]{3,2,1,0:T(8,128)(2,1)S(1)}, u32[]{:S(2)}, u32[]{:S(2)}) collective-permute-start(bf16[2,2,32,128]{3,2,1,0:T(8,128)(2,1)S(1)} %get-tuple-element.66.own), channel_id=1, source_target_pairs={{0,15},{1,0},{2,1},{3,2},{4,3},{5,4},{6,5},{7,6},{8,7},{9,8},{10,9... | collective-permute-start | bytes 98312 | tf_op jit(solution)/shard_map/ppermute | solution.py:22
  37.1 2.3 %collective-permute-start.6 = (bf16[2,6,32,128]{3,2,1,0:T(8,128)(2,1)S(1)}, bf16[2,6,32,128]{3,2,1,0:T(8,128)(2,1)S(1)}, u32[]{:S(2)}, u32[]{:S(2)}) collective-permute-start(bf16[2,6,32,128]{3,2,1,0:T(8,128)(2,1)S(1)} %get-tuple-element.67), channel_id=1, source_target_pairs={{0,16},{16,32},{32,48},{48,64},{64,80},{80,96},{96,112},{112,0},{1... | collective-permute-start | bytes 294920 | tf_op jit(solution)/shard_map/ppermute | solution.py:22
  41.0 2.4 %collective-permute-done.7.right = bf16[2,6,32,128]{3,2,1,0:T(8,128)(2,1)S(1)} collective-permute-done((bf16[2,6,32,128]{3,2,1,0:T(8,128)(2,1)S(1)}, bf16[2,6,32,128]{3,2,1,0:T(8,128)(2,1)S(1)}, u32[]{:S(2)}, u32[]{:S(2)}) %collective-permute-start.7) | collective-permute-done | bytes 98336 | tf_op jit(solution)/shard_map/ppermute | solution.py:22
  43.4 3.9 %bottom_kernel.1 = (bf16[2,2,32,256]{3,2,1,0:T(8,128)(2,1)}, bf16[24,32,128]{2,1,0:T(8,128)(2,1)S(1)}, bf16[4,4,64,128]{3,2,1,0:T(8,128)(2,1)S(1)}, bf16[4,1,64,...) custom-call(bf16[2,2,32,128]{3,2,1,0:T(8,128)(2,1)S(1)} %get-tuple-element.66.own, ...), custom_call_target="tpu_custom_call" | custom-call | flops 45298484 | bytes 181862 | tf_op jit(solution)/shard_map/bottom_kernel/pallas_call | solution.py:385
  47.3 5.1 %collective-permute-start.10 = (bf16[4,1,64,128]{3,2,1,0:T(8,128)(2,1)S(1)}, bf16[4,1,64,128]{3,2,1,0:T(8,128)(2,1)S(1)}, u32[]{:S(2)}, u32[]{:S(2)}) collective-permute-start(bf16[4,1,64,128]{3,2,1,0:T(8,128)(2,1)S(1)} %get-tuple-element.74), channel_id=1, source_target_pairs={{0,15},{1,0},{2,1},{3,2},{4,3},{5,4},{6,5},{7,6},{8,7},{9,8},{10,9... | collective-permute-start | bytes 196616 | tf_op jit(solution)/shard_map/ppermute | solution.py:22
  53.7 5.1 %collective-permute-done.9.before = bf16[4,1,64,128]{3,2,1,0:T(8,128)(2,1)S(1)} collective-permute-done((bf16[4,1,64,128]{3,2,1,0:T(8,128)(2,1)S(1)}, bf16[4,1,64,128]{3,2,1,0:T(8,128)(2,1)S(1)}, u32[]{:S(2)}, u32[]{:S(2)}) %collective-permute-start.9) | collective-permute-done | bytes 65568 | tf_op jit(solution)/shard_map/ppermute | solution.py:22
  62.5 2.7 %collective-permute-done.13.right = bf16[1,6,64,128]{3,2,1,0:T(8,128)(2,1)S(1)} collective-permute-done((bf16[1,6,64,128]{3,2,1,0:T(8,128)(2,1)S(1)}, bf16[1,6,64,128]{3,2,1,0:T(8,128)(2,1)S(1)}, u32[]{:S(2)}, u32[]{:S(2)}) %collective-permute-start.13) | collective-permute-done | bytes 98336 | tf_op jit(solution)/shard_map/ppermute | solution.py:22
  65.2 2.6 %first_errors_kernel.1 = (bf16[4,4,64,128]{3,2,1,0:T(8,128)(2,1)}, bf16[4,1,64,128]{3,2,1,0:T(8,128)(2,1)}, bf16[4,1,64,128]{3,2,1,0:T(8,128)(2,1)}, bf16[4,4,64...) custom-call(s32[1]{0:T(128)} %bitcast.core, bf16[4,4,64,128]{3,2,1,0:T(8,128)(2,1)S(1)} %get-tuple-element.72.own, ...), custom_call_target="tpu_custom_call" | custom-call | flops 45298484 | bytes 86835 | tf_op jit(solution)/shard_map/first_errors_kernel/pallas_call | solution.py:385
  69.8 2.7 %pair_grads_kernel.1 = bf16[64,112,128]{2,1,0:T(8,128)(2,1)} custom-call(bf16[6,6,64,128]{3,2,1,0:T(8,128)(2,1)S(1)} %collective-permute-done.14.fields, bf16[4,4,64,128]{3,2,1,0:T(8,128)(2,1)S(1)} %collective-permute-done.15.errors, f32[1152,384]{1,0:T(8,128)S(1)} %own_grads_kernel.1.own_total, bf16[64,56,128]{2,1,0:T(8,128)(2,1)S(1)} %bottom_grads_kernel.1.three), custom_call_target="tpu_custom_call" | custom-call | flops 45298484 | bytes 176947 | tf_op jit(solution)/shard_map/pair_grads_kernel/pallas_call | solution.py:385
  72.6 5.1 %all-to-all-start.1 = ((bf16[64,112,128]{2,1,0:T(8,128)(2,1)}), bf16[64,112,128]{2,1,0:T(8,128)(2,1)S(1)}, u32[]{:S(2)}, u32[]{:S(2)}) async-start(bf16[64,112,128]{2,1,0:T(8,128)(2,1)} %pair_grads_kernel.1), calls=%async_computation.1 | async-start | bytes 3670016 | tf_op jit(solution)/shard_map/all_to_all | solution.py:472
  78.7 3.8 %collective-permute-start.17 = (bf16[4,1,64,128]{3,2,1,0:T(8,128)(2,1)S(1)}, bf16[4,1,64,128]{3,2,1,0:T(8,128)(2,1)S(1)}, u32[]{:S(2)}, u32[]{:S(2)}) collective-permute-start(bf16[4,1,64,128]{3,2,1,0:T(8,128)(2,1)S(1)} %copy-done.9), channel_id=1, source_target_pairs={{0,15},{1,0},{2,1},{3,2},{4,3},{5,4},{6,5},{7,6},{8,7},{9,8},{10,9... | collective-permute-start | bytes 196616 | tf_op jit(solution)/shard_map/ppermute | solution.py:22
  82.5 20.2 %all-to-all-done.1.pieces = bf16[64,112,128]{2,1,0:T(8,128)(2,1)S(1)} async-done(((bf16[64,112,128]{2,1,0:T(8,128)(2,1)}), bf16[64,112,128]{2,1,0:T(8,128)(2,1)S(1)}, u32[]{:S(2)}, u32[]{:S(2)}) %all-to-all-start.1) | async-done | bytes 1835040 | tf_op jit(solution)/shard_map/all_to_all | solution.py:472
  103.9 6.9 %all-to-all-start.2 = ((bf16[64,56,128]{2,1,0:T(8,128)(2,1)}), bf16[64,56,128]{2,1,0:T(8,128)(2,1)S(1)}, u32[]{:S(2)}, u32[]{:S(2)}) async-start(bf16[64,56,128]{2,1,0:T(8,128)(2,1)} %get-tuple-element.98), calls=%async_computation.2 | async-start | bytes 1835008 | tf_op jit(solution)/shard_map/all_to_all | solution.py:477
  115.4 2.2 %collective-permute-start.20 = (bf16[2,56,128]{2,1,0:T(8,128)(2,1)S(1)}, bf16[2,56,128]{2,1,0:T(8,128)(2,1)S(1)}, u32[]{:S(2)}, u32[]{:S(2)}) collective-permute-start(bf16[2,56,128]{2,1,0:T(8,128)(2,1)S(1)} %maximum_select_fusion.1.pair_0), channel_id=1, source_target_pairs={{0,64},{32,96},{64,0},{96,32},{1,65},{33,97},{65,1},{97,33},{2,66}... | collective-permute-start | bytes 86024 | tf_op jit(solution)/shard_map/ppermute | solution.py:30
  118.8 7.0 %collective-permute-done.19.pair_1 = bf16[2,56,128]{2,1,0:T(8,128)(2,1)S(1)} collective-permute-done((bf16[2,56,128]{2,1,0:T(8,128)(2,1)S(1)}, bf16[2,56,128]{2,1,0:T(8,128)(2,1)S(1)}, u32[]{:S(2)}, u32[]{:S(2)}) %collective-permute-start.19) | collective-permute-done | bytes 28704 | tf_op jit(solution)/shard_map/ppermute | solution.py:30
  126.6 3.8 %collective-permute-start.24 = (bf16[3584,128]{1,0:T(8,128)(2,1)S(1)}, bf16[3584,128]{1,0:T(8,128)(2,1)S(1)}, u32[]{:S(2)}, u32[]{:S(2)}) collective-permute-start(bf16[3584,128]{1,0:T(8,128)(2,1)S(1)} %bitcast.25), channel_id=1, source_target_pairs={{0,16},{16,0},{1,17},{17,1},{2,18},{18,2},{3,19},{19,3},{4,20},{20... | collective-permute-start | bytes 2752520 | tf_op jit(solution)/shard_map/ppermute | solution.py:26
  130.4 3.8 %input_kernel.1 = bf16[4,4,64,128]{3,2,1,0:T(8,128)(2,1)} custom-call(bf16[4,4,64,128]{3,2,1,0:T(8,128)(2,1)} %get-tuple-element.84.own, bf16[4,1,64,128]{3,2,1,0:T(8,128)(2,1)} %copy-done.7, bf16[4,1,64,128]{3,2,1,0:T(8,128)(2,1)} %copy-done.8, bf16[1,6,64,128]{3,2,1,0:T(8,128)(2,1)S(1)} %collective-permute-done.22.left, ...), custom_call_target="tpu_custom_call" | custom-call | flops 11324620 | bytes 73728 | tf_op jit(solution)/shard_map/input_kernel/pallas_call | solution.py:385
  (74 shorter events, 25.3 us)
Async XLA Ops:
  1.7 12.7 %collective-permute-start = (bf16[5,2,64,128]{3,2,1,0:T(8,128)(2,1)S(1)}, bf16[5,2,64,128]{3,2,1,0:T(8,128)(2,1)S(1)}, u32[]{:S(2)}, u32[]{:S(2)}) collective-permute-start(bf16[5,2,64,128]{3,2,1,0:T(8,128)(2,1)S(1)} %get-tuple-element.61), channel_id=1, source_target_pairs={{0,1},{1,2},{2,3},{3,4},{4,5},{5,6},{6,7},{7,8},{8,9},{9,10},{10,1... | collective-permute-start | bytes 491528 | tf_op jit(solution)/shard_map/ppermute | solution.py:22
  3.9 10.6 %collective-permute-start.1 = (bf16[5,2,64,128]{3,2,1,0:T(8,128)(2,1)S(1)}, bf16[5,2,64,128]{3,2,1,0:T(8,128)(2,1)S(1)}, u32[]{:S(2)}, u32[]{:S(2)}) collective-permute-start(bf16[5,2,64,128]{3,2,1,0:T(8,128)(2,1)S(1)} %get-tuple-element.62), channel_id=1, source_target_pairs={{0,15},{1,0},{2,1},{3,2},{4,3},{5,4},{6,5},{7,6},{8,7},{9,8},{10,9... | collective-permute-start | bytes 491528 | tf_op jit(solution)/shard_map/ppermute | solution.py:22
  10.8 19.4 %all-to-all-start = ((bf16[16,27,8,128]{3,2,1,0:T(8,128)(2,1)}), bf16[16,27,8,128]{3,2,1,0:T(8,128)(2,1)S(1)}, u32[]{:S(2)}, u32[]{:S(2)}) async-start(bf16[16,27,8,128]{3,2,1,0:T(8,128)(2,1)} %broadcast_in_dim.3), calls=%async_computation | async-start | bytes 1769472 | tf_op jit(solution)/shard_map/all_to_all | solution.py:414
  14.5 6.1 %collective-permute-start.2 = (bf16[20,64,128]{2,1,0:T(8,128)(2,1)S(1)}, bf16[20,64,128]{2,1,0:T(8,128)(2,1)S(1)}, u32[]{:S(2)}, u32[]{:S(2)}) collective-permute-start(bf16[20,64,128]{2,1,0:T(8,128)(2,1)S(1)} %get-tuple-element.63), channel_id=1, source_target_pairs={{0,16},{16,32},{32,48},{48,64},{64,80},{80,96},{96,112},{112,0},{1... | collective-permute-start | bytes 983048 | tf_op jit(solution)/shard_map/ppermute | solution.py:22
  16.6 6.8 %collective-permute-start.3 = (bf16[20,64,128]{2,1,0:T(8,128)(2,1)S(1)}, bf16[20,64,128]{2,1,0:T(8,128)(2,1)S(1)}, u32[]{:S(2)}, u32[]{:S(2)}) collective-permute-start(bf16[20,64,128]{2,1,0:T(8,128)(2,1)S(1)} %get-tuple-element.64), channel_id=1, source_target_pairs={{0,112},{16,0},{32,16},{48,32},{64,48},{80,64},{96,80},{112,96},{1... | collective-permute-start | bytes 983048 | tf_op jit(solution)/shard_map/ppermute | solution.py:22
  30.1 9.2 %collective-permute-start.8 = (bf16[16,27,8,128]{3,2,1,0:T(8,128)(2,1)S(1)}, bf16[16,27,8,128]{3,2,1,0:T(8,128)(2,1)S(1)}, u32[]{:S(2)}, u32[]{:S(2)}) collective-permute-start(bf16[16,27,8,128]{3,2,1,0:T(8,128)(2,1)S(1)} %all-to-all-done), channel_id=1, source_target_pairs={{0,16},{16,0},{1,17},{17,1},{2,18},{18,2},{3,19},{19,3},{4,20},{20... | collective-permute-start | bytes 2654216 | tf_op jit(solution)/shard_map/ppermute | solution.py:26
  31.0 6.1 %collective-permute-start.4 = (bf16[2,2,32,128]{3,2,1,0:T(8,128)(2,1)S(1)}, bf16[2,2,32,128]{3,2,1,0:T(8,128)(2,1)S(1)}, u32[]{:S(2)}, u32[]{:S(2)}) collective-permute-start(bf16[2,2,32,128]{3,2,1,0:T(8,128)(2,1)S(1)} %get-tuple-element.66.own), channel_id=1, source_target_pairs={{0,1},{1,2},{2,3},{3,4},{4,5},{5,6},{6,7},{7,8},{8,9},{9,10},{10,1... | collective-permute-start | bytes 98312 | tf_op jit(solution)/shard_map/ppermute | solution.py:22
  31.7 5.4 %collective-permute-start.5 = (bf16[2,2,32,128]{3,2,1,0:T(8,128)(2,1)S(1)}, bf16[2,2,32,128]{3,2,1,0:T(8,128)(2,1)S(1)}, u32[]{:S(2)}, u32[]{:S(2)}) collective-permute-start(bf16[2,2,32,128]{3,2,1,0:T(8,128)(2,1)S(1)} %get-tuple-element.66.own), channel_id=1, source_target_pairs={{0,15},{1,0},{2,1},{3,2},{4,3},{5,4},{6,5},{7,6},{8,7},{9,8},{10,9... | collective-permute-start | bytes 98312 | tf_op jit(solution)/shard_map/ppermute | solution.py:22
  35.8 34.1 %collective-permute-start.14 = (bf16[6,6,64,128]{3,2,1,0:T(8,128)(2,1)}, bf16[6,6,64,128]{3,2,1,0:T(8,128)(2,1)S(1)}, u32[]{:S(2)}, u32[]{:S(2)}) collective-permute-start(bf16[6,6,64,128]{3,2,1,0:T(8,128)(2,1)} %get-tuple-element.85), channel_id=1, source_target_pairs={{0,16},{16,0},{1,17},{17,1},{2,18},{18,2},{3,19},{19,3},{4,20},{20... | collective-permute-start | bytes 1769480 | tf_op jit(solution)/shard_map/ppermute | solution.py:26
  37.1 3.9 %collective-permute-start.6 = (bf16[2,6,32,128]{3,2,1,0:T(8,128)(2,1)S(1)}, bf16[2,6,32,128]{3,2,1,0:T(8,128)(2,1)S(1)}, u32[]{:S(2)}, u32[]{:S(2)}) collective-permute-start(bf16[2,6,32,128]{3,2,1,0:T(8,128)(2,1)S(1)} %get-tuple-element.67), channel_id=1, source_target_pairs={{0,16},{16,32},{32,48},{48,64},{64,80},{80,96},{96,112},{112,0},{1... | collective-permute-start | bytes 294920 | tf_op jit(solution)/shard_map/ppermute | solution.py:22
  39.4 4.0 %collective-permute-start.7 = (bf16[2,6,32,128]{3,2,1,0:T(8,128)(2,1)S(1)}, bf16[2,6,32,128]{3,2,1,0:T(8,128)(2,1)S(1)}, u32[]{:S(2)}, u32[]{:S(2)}) collective-permute-start(bf16[2,6,32,128]{3,2,1,0:T(8,128)(2,1)S(1)} %get-tuple-element.68), channel_id=1, source_target_pairs={{0,112},{16,0},{32,16},{48,32},{64,48},{80,64},{96,80},{112,96},{1... | collective-permute-start | bytes 294920 | tf_op jit(solution)/shard_map/ppermute | solution.py:22
  47.3 6.4 %collective-permute-start.10 = (bf16[4,1,64,128]{3,2,1,0:T(8,128)(2,1)S(1)}, bf16[4,1,64,128]{3,2,1,0:T(8,128)(2,1)S(1)}, u32[]{:S(2)}, u32[]{:S(2)}) collective-permute-start(bf16[4,1,64,128]{3,2,1,0:T(8,128)(2,1)S(1)} %get-tuple-element.74), channel_id=1, source_target_pairs={{0,15},{1,0},{2,1},{3,2},{4,3},{5,4},{6,5},{7,6},{8,7},{9,8},{10,9... | collective-permute-start | bytes 196616 | tf_op jit(solution)/shard_map/ppermute | solution.py:22
  52.4 6.4 %collective-permute-start.9 = (bf16[4,1,64,128]{3,2,1,0:T(8,128)(2,1)S(1)}, bf16[4,1,64,128]{3,2,1,0:T(8,128)(2,1)S(1)}, u32[]{:S(2)}, u32[]{:S(2)}) collective-permute-start(bf16[4,1,64,128]{3,2,1,0:T(8,128)(2,1)S(1)} %get-tuple-element.73), channel_id=1, source_target_pairs={{0,1},{1,2},{2,3},{3,4},{4,5},{5,6},{6,7},{7,8},{8,9},{9,10},{10,1... | collective-permute-start | bytes 196616 | tf_op jit(solution)/shard_map/ppermute | solution.py:22
  60.9 4.3 %collective-permute-start.13 = (bf16[1,6,64,128]{3,2,1,0:T(8,128)(2,1)S(1)}, bf16[1,6,64,128]{3,2,1,0:T(8,128)(2,1)S(1)}, u32[]{:S(2)}, u32[]{:S(2)}) collective-permute-start(bf16[1,6,64,128]{3,2,1,0:T(8,128)(2,1)S(1)} %get-tuple-element.80), channel_id=1, source_target_pairs={{0,112},{16,0},{32,16},{48,32},{64,48},{80,64},{96,80},{112,96},{1... | collective-permute-start | bytes 294920 | tf_op jit(solution)/shard_map/ppermute | solution.py:22
  72.6 30.1 %all-to-all-start.1 = ((bf16[64,112,128]{2,1,0:T(8,128)(2,1)}), bf16[64,112,128]{2,1,0:T(8,128)(2,1)S(1)}, u32[]{:S(2)}, u32[]{:S(2)}) async-start(bf16[64,112,128]{2,1,0:T(8,128)(2,1)} %pair_grads_kernel.1), calls=%async_computation.1 | async-start | bytes 3670016 | tf_op jit(solution)/shard_map/all_to_all | solution.py:472
  77.7 26.2 %collective-permute-start.16 = (bf16[4,1,64,128]{3,2,1,0:T(8,128)(2,1)S(1)}, bf16[4,1,64,128]{3,2,1,0:T(8,128)(2,1)S(1)}, u32[]{:S(2)}, u32[]{:S(2)}) collective-permute-start(bf16[4,1,64,128]{3,2,1,0:T(8,128)(2,1)S(1)} %copy-done.10), channel_id=1, source_target_pairs={{0,1},{1,2},{2,3},{3,4},{4,5},{5,6},{6,7},{7,8},{8,9},{9,10},{10,1... | collective-permute-start | bytes 196616 | tf_op jit(solution)/shard_map/ppermute | solution.py:22
  78.7 25.1 %collective-permute-start.17 = (bf16[4,1,64,128]{3,2,1,0:T(8,128)(2,1)S(1)}, bf16[4,1,64,128]{3,2,1,0:T(8,128)(2,1)S(1)}, u32[]{:S(2)}, u32[]{:S(2)}) collective-permute-start(bf16[4,1,64,128]{3,2,1,0:T(8,128)(2,1)S(1)} %copy-done.9), channel_id=1, source_target_pairs={{0,15},{1,0},{2,1},{3,2},{4,3},{5,4},{6,5},{7,6},{8,7},{9,8},{10,9... | collective-permute-start | bytes 196616 | tf_op jit(solution)/shard_map/ppermute | solution.py:22
  103.9 22.7 %all-to-all-start.2 = ((bf16[64,56,128]{2,1,0:T(8,128)(2,1)}), bf16[64,56,128]{2,1,0:T(8,128)(2,1)S(1)}, u32[]{:S(2)}, u32[]{:S(2)}) async-start(bf16[64,56,128]{2,1,0:T(8,128)(2,1)} %get-tuple-element.98), calls=%async_computation.2 | async-start | bytes 1835008 | tf_op jit(solution)/shard_map/all_to_all | solution.py:477
  112.8 13.7 %collective-permute-start.22 = (bf16[1,6,64,128]{3,2,1,0:T(8,128)(2,1)S(1)}, bf16[1,6,64,128]{3,2,1,0:T(8,128)(2,1)S(1)}, u32[]{:S(2)}, u32[]{:S(2)}) collective-permute-start(bf16[1,6,64,128]{3,2,1,0:T(8,128)(2,1)S(1)} %get-tuple-element.101), channel_id=1, source_target_pairs={{0,16},{16,32},{32,48},{48,64},{64,80},{80,96},{96,112},{112,0},{1... | collective-permute-start | bytes 294920 | tf_op jit(solution)/shard_map/ppermute | solution.py:22
  114.0 12.5 %collective-permute-start.23 = (bf16[1,6,64,128]{3,2,1,0:T(8,128)(2,1)S(1)}, bf16[1,6,64,128]{3,2,1,0:T(8,128)(2,1)S(1)}, u32[]{:S(2)}, u32[]{:S(2)}) collective-permute-start(bf16[1,6,64,128]{3,2,1,0:T(8,128)(2,1)S(1)} %get-tuple-element.102), channel_id=1, source_target_pairs={{0,112},{16,0},{32,16},{48,32},{64,48},{80,64},{96,80},{112,96},{1... | collective-permute-start | bytes 294920 | tf_op jit(solution)/shard_map/ppermute | solution.py:22
  114.1 11.8 %collective-permute-start.19 = (bf16[2,56,128]{2,1,0:T(8,128)(2,1)S(1)}, bf16[2,56,128]{2,1,0:T(8,128)(2,1)S(1)}, u32[]{:S(2)}, u32[]{:S(2)}) collective-permute-start(bf16[2,56,128]{2,1,0:T(8,128)(2,1)S(1)} %maximum_select_fusion.1.pair_0), channel_id=1, source_target_pairs={{0,32},{32,64},{64,96},{96,0},{1,33},{33,65},{65,97},{97,1},{2,34}... | collective-permute-start | bytes 86024 | tf_op jit(solution)/shard_map/ppermute | solution.py:30
  115.4 10.4 %collective-permute-start.20 = (bf16[2,56,128]{2,1,0:T(8,128)(2,1)S(1)}, bf16[2,56,128]{2,1,0:T(8,128)(2,1)S(1)}, u32[]{:S(2)}, u32[]{:S(2)}) collective-permute-start(bf16[2,56,128]{2,1,0:T(8,128)(2,1)S(1)} %maximum_select_fusion.1.pair_0), channel_id=1, source_target_pairs={{0,64},{32,96},{64,0},{96,32},{1,65},{33,97},{65,1},{97,33},{2,66}... | collective-permute-start | bytes 86024 | tf_op jit(solution)/shard_map/ppermute | solution.py:30
  117.6 8.2 %collective-permute-start.21 = (bf16[2,56,128]{2,1,0:T(8,128)(2,1)S(1)}, bf16[2,56,128]{2,1,0:T(8,128)(2,1)S(1)}, u32[]{:S(2)}, u32[]{:S(2)}) collective-permute-start(bf16[2,56,128]{2,1,0:T(8,128)(2,1)S(1)} %maximum_select_fusion.1.pair_0), channel_id=1, source_target_pairs={{0,96},{32,0},{64,32},{96,64},{1,97},{33,1},{65,33},{97,65},{2,98}... | collective-permute-start | bytes 86024 | tf_op jit(solution)/shard_map/ppermute | solution.py:30
  126.6 7.7 %collective-permute-start.24 = (bf16[3584,128]{1,0:T(8,128)(2,1)S(1)}, bf16[3584,128]{1,0:T(8,128)(2,1)S(1)}, u32[]{:S(2)}, u32[]{:S(2)}) collective-permute-start(bf16[3584,128]{1,0:T(8,128)(2,1)S(1)} %bitcast.25), channel_id=1, source_target_pairs={{0,16},{16,0},{1,17},{17,1},{2,18},{18,2},{3,19},{19,3},{4,20},{20... | collective-permute-start | bytes 2752520 | tf_op jit(solution)/shard_map/ppermute | solution.py:26
  (15 other events, 198.0 us)

commit v14 on v13

--- a/solution.py
+++ b/solution.py
@@ -328,16 +328,24 @@
     lax.fori_loop(0, 2, step, 0)
 
 
-def input_kernel(own, before, after, left, right, taps_one, out, padded, packed):
+def inner_input_kernel(own, before, after, taps_one, out, padded, packed):
+    padded[:, 0:1] = before[...]
+    padded[:, 1:5] = own[...]
+    padded[:, 5:6] = after[...]
+    fill_backward(packed, taps_one)
+    product = dot_nt(window_rows(padded, 0, 4, rows=2), packed[...])
+    out[...] = join_taps(product, 8, 64, 128).reshape(2, 4, 64, 128).astype(BF16)
+
+
+def outer_input_kernel(own, before, after, left, right, taps_one, inner, out, padded, packed):
     fill_padded(padded, own, before, after, left, right)
     fill_backward(packed, taps_one)
-
-    def step(at, _):
-        product = dot_nt(window_rows(padded, at * 2, 4, rows=2), packed[...])
-        out[pl.ds(at * 2, 2)] = join_taps(product, 8, 64, 128).reshape(2, 4, 64, 128).astype(BF16)
-        return 0
-
-    lax.fori_loop(0, 2, step, 0)
+    out[1:3] = inner[...]
+    windows = [window_rows(padded, 0, 4), window_rows(padded, 3, 4)]
+    product = dot_nt(jnp.concatenate(windows, axis=0), packed[...])
+    rows = join_taps(product, 8, 64, 128).astype(BF16)
+    out[0] = rows[0:4]
+    out[3] = rows[4:8]
 
 
 def sum_kernel(pieces, out, three):
@@ -485,13 +493,17 @@
         compiler_params=pltpu.CompilerParams(vmem_limit_bytes=8 << 20),
         name="place_kernel",
     )(chip, *ring_pieces([both] * 4, "x"))
-    whole, grad_three, one_left, one_right = lax.optimization_barrier(
-        (whole, grad_three, one_left, one_right)
+    (inner,) = call(
+        inner_input_kernel, [((2, 4, 64, 128), BF16, True)], [((4, 6, 64, 128), BF16), ((384, 1152), BF16)],
+        conv_flops // 4, err_one, one_before, one_after, taps_one,
+    )
+    whole, grad_three, one_left, one_right, inner = lax.optimization_barrier(
+        (whole, grad_three, one_left, one_right, inner)
     )
     (input_grad,) = call(
-        input_kernel, [(block, BF16, True)], [(field, BF16), ((384, 1152), BF16)],
+        outer_input_kernel, [(block, BF16, True)], [(field, BF16), ((384, 1152), BF16)],
         conv_flops // 4, in_hbm(err_one), in_hbm(one_before), in_hbm(one_after), one_left, one_right,
-        in_hbm(taps_one),
+        in_hbm(taps_one), in_hbm(inner),
     )
     grad_three = jnp.swapaxes(grad_three, 1, 2).reshape(3, 3, 3, 128, 16)
     grad_one, grad_two = pl.pallas_call(

time: 137 us -> 137 us (level)
  waiting for transfers between devices: 48 us -> 45.1 us
  other arithmetic: 1.16 us -> 2.57 us
    ppermute x3, waiting for transfers between devices: 7.03 us -> 5.49 us  [ring_pieces(): lax.ppermute(pieces[d], axis, [(i, (i + d) % 4) for i in range(4)])]
    transpose x1, other arithmetic: 0.29 us -> 1.7 us  [on_device(): taps_three = jnp.transpose(both, (2, 1, 0, 3, 4)).reshape(27, 256, 128)]
    pallas_call x13 -> x14, Pallas kernels: 24.2 us -> 24.8 us  [call(): pl.pallas_call(kernel, out_shape=shapes, in_specs=[pl.BlockSpec(memory_sp...]
  transfers between devices with their start and end apart: 28 -> 28, of which waited for: 12 -> 11; matrix products, arithmetic and copies ran while one was open for 2% -> 3% of each run, Pallas kernels for 16% -> 16%
where the time goes in v14:
time: 137 us; the launch traced here: 136 us
  starting transfers between devices  58.3 us (43%)
  waiting for transfers between devices  45.1 us (33%)
  Pallas kernels  27.6 us (20%)
  other arithmetic  2.57 us (2%)
  local copies, waits for them, and re-layouts  1.55 us (1%)
    ppermute x16, starting transfers between devices, shifted(): lax.ppermute(array, axes, [(i, (i + step) % count) for i in range(count)])  28 us
    pallas_call x14, Pallas kernels, call(): pl.pallas_call(kernel, out_shape=shapes, in_specs=[pl.BlockSpec(memory_sp...  24.8 us
    all_to_all x1, waiting for transfers between devices, on_device(): lax.all_to_all(kept, FLAT, 0, 0)  20.2 us
    ppermute x16, waiting for transfers between devices, shifted(): lax.ppermute(array, axes, [(i, (i + step) % count) for i in range(count)])  18.9 us
    ppermute x6, starting transfers between devices, swap_cores(): return lax.ppermute(array, 'c', [(0, 1), (1, 0)])  9.37 us
    all_to_all x1, starting transfers between devices, on_device(): whole = lax.all_to_all(part, FLAT, 0, 0).reshape(64 * PIECE, 128)  6.9 us
    ppermute x3, waiting for transfers between devices, ring_pieces(): lax.ppermute(pieces[d], axis, [(i, (i + d) % 4) for i in range(4)])  5.49 us
    all_to_all x1, starting transfers between devices, on_device(): lax.all_to_all(kept, FLAT, 0, 0)  5.07 us
  transfers between devices with their start and end apart: 28, of which 11 were waited for; matrix products, arithmetic and copies ran while one was open for 3% of the time, Pallas kernels for 16%

profile of v14, /device:TPU:1, one launch (start us, length us, event | category | flops | bytes accessed | tf_op | source)
XLA Modules:
  0.0 136.0 jit_solution(6176434480265422110)
XLA Ops:
  1.7 2.2 %collective-permute-start = (bf16[5,2,64,128]{3,2,1,0:T(8,128)(2,1)S(1)}, bf16[5,2,64,128]{3,2,1,0:T(8,128)(2,1)S(1)}, u32[]{:S(2)}, u32[]{:S(2)}) collective-permute-start(bf16[5,2,64,128]{3,2,1,0:T(8,128)(2,1)S(1)} %get-tuple-element.62), channel_id=1, source_target_pairs={{0,1},{1,2},{2,3},{3,4},{4,5},{5,6},{6,7},{7,8},{8,9},{9,10},{10,1... | collective-permute-start | bytes 491528 | tf_op jit(solution)/shard_map/ppermute | solution.py:22
  3.9 5.0 %collective-permute-start.1 = (bf16[5,2,64,128]{3,2,1,0:T(8,128)(2,1)S(1)}, bf16[5,2,64,128]{3,2,1,0:T(8,128)(2,1)S(1)}, u32[]{:S(2)}, u32[]{:S(2)}) collective-permute-start(bf16[5,2,64,128]{3,2,1,0:T(8,128)(2,1)S(1)} %get-tuple-element.63), channel_id=1, source_target_pairs={{0,15},{1,0},{2,1},{3,2},{4,3},{5,4},{6,5},{7,6},{8,7},{9,8},{10,9... | collective-permute-start | bytes 491528 | tf_op jit(solution)/shard_map/ppermute | solution.py:22
  10.8 4.3 %all-to-all-start = ((bf16[16,27,8,128]{3,2,1,0:T(8,128)(2,1)}), bf16[16,27,8,128]{3,2,1,0:T(8,128)(2,1)}, u32[]{:S(2)}, u32[]{:S(2)}) async-start(bf16[16,27,8,128]{3,2,1,0:T(8,128)(2,1)} %broadcast_in_dim.3), calls=%async_computation | async-start | bytes 1769472 | tf_op jit(solution)/shard_map/all_to_all | solution.py:422
  15.2 2.1 %collective-permute-start.2 = (bf16[20,64,128]{2,1,0:T(8,128)(2,1)S(1)}, bf16[20,64,128]{2,1,0:T(8,128)(2,1)S(1)}, u32[]{:S(2)}, u32[]{:S(2)}) collective-permute-start(bf16[20,64,128]{2,1,0:T(8,128)(2,1)S(1)} %get-tuple-element.64), channel_id=1, source_target_pairs={{0,16},{16,32},{32,48},{48,64},{64,80},{80,96},{96,112},{112,0},{1... | collective-permute-start | bytes 983048 | tf_op jit(solution)/shard_map/ppermute | solution.py:22
  17.3 4.0 %collective-permute-done.2.left.f_left = bf16[20,64,128]{2,1,0:T(8,128)(2,1)S(1)} collective-permute-done((bf16[20,64,128]{2,1,0:T(8,128)(2,1)S(1)}, bf16[20,64,128]{2,1,0:T(8,128)(2,1)S(1)}, u32[]{:S(2)}, u32[]{:S(2)}) %collective-permute-start.2) | collective-permute-done | bytes 327712 | tf_op jit(solution)/shard_map/ppermute | solution.py:22
  21.3 2.9 %collective-permute-done.3.right.f_right = bf16[20,64,128]{2,1,0:T(8,128)(2,1)S(1)} collective-permute-done((bf16[20,64,128]{2,1,0:T(8,128)(2,1)S(1)}, bf16[20,64,128]{2,1,0:T(8,128)(2,1)S(1)}, u32[]{:S(2)}, u32[]{:S(2)}) %collective-permute-start.3) | collective-permute-done | bytes 327712 | tf_op jit(solution)/shard_map/ppermute | solution.py:22
  24.2 6.8 %forward_kernel.1 = (bf16[6,6,64,128]{3,2,1,0:T(8,128)(2,1)}, bf16[6,6,64,128]{3,2,1,0:T(8,128)(2,1)}, bf16[4,4,64,128]{3,2,1,0:T(8,128)(2,1)}, bf16[4,4,64,128]...) custom-call(s32[1]{0:T(128)} %bitcast.core, bf16[4,4,64,128]{3,2,1,0:T(8,128)(2,1)S(1)} %copy-done.3, ...), custom_call_target="tpu_custom_call" | custom-call | flops 135895456 | bytes 150733 | tf_op jit(solution)/shard_map/forward_kernel/pallas_call | solution.py:393
  32.4 4.1 %collective-permute-start.5 = (bf16[2,2,32,128]{3,2,1,0:T(8,128)(2,1)S(1)}, bf16[2,2,32,128]{3,2,1,0:T(8,128)(2,1)S(1)}, u32[]{:S(2)}, u32[]{:S(2)}) collective-permute-start(bf16[2,2,32,128]{3,2,1,0:T(8,128)(2,1)S(1)} %get-tuple-element.67.own), channel_id=1, source_target_pairs={{0,15},{1,0},{2,1},{3,2},{4,3},{5,4},{6,5},{7,6},{8,7},{9,8},{10,9... | collective-permute-start | bytes 98312 | tf_op jit(solution)/shard_map/ppermute | solution.py:22
  37.8 2.3 %collective-permute-start.6 = (bf16[2,6,32,128]{3,2,1,0:T(8,128)(2,1)S(1)}, bf16[2,6,32,128]{3,2,1,0:T(8,128)(2,1)S(1)}, u32[]{:S(2)}, u32[]{:S(2)}) collective-permute-start(bf16[2,6,32,128]{3,2,1,0:T(8,128)(2,1)S(1)} %get-tuple-element.68), channel_id=1, source_target_pairs={{0,16},{16,32},{32,48},{48,64},{64,80},{80,96},{96,112},{112,0},{1... | collective-permute-start | bytes 294920 | tf_op jit(solution)/shard_map/ppermute | solution.py:22
  44.1 3.9 %bottom_kernel.1 = (bf16[2,2,32,256]{3,2,1,0:T(8,128)(2,1)}, bf16[24,32,128]{2,1,0:T(8,128)(2,1)S(1)}, bf16[4,4,64,128]{3,2,1,0:T(8,128)(2,1)S(1)}, bf16[4,1,64,...) custom-call(bf16[2,2,32,128]{3,2,1,0:T(8,128)(2,1)S(1)} %get-tuple-element.67.own, ...), custom_call_target="tpu_custom_call" | custom-call | flops 45298484 | bytes 181862 | tf_op jit(solution)/shard_map/bottom_kernel/pallas_call | solution.py:393
  48.0 5.1 %collective-permute-start.10 = (bf16[4,1,64,128]{3,2,1,0:T(8,128)(2,1)S(1)}, bf16[4,1,64,128]{3,2,1,0:T(8,128)(2,1)S(1)}, u32[]{:S(2)}, u32[]{:S(2)}) collective-permute-start(bf16[4,1,64,128]{3,2,1,0:T(8,128)(2,1)S(1)} %get-tuple-element.75), channel_id=1, source_target_pairs={{0,15},{1,0},{2,1},{3,2},{4,3},{5,4},{6,5},{7,6},{8,7},{9,8},{10,9... | collective-permute-start | bytes 196616 | tf_op jit(solution)/shard_map/ppermute | solution.py:22
  54.4 5.1 %collective-permute-done.9.before = bf16[4,1,64,128]{3,2,1,0:T(8,128)(2,1)S(1)} collective-permute-done((bf16[4,1,64,128]{3,2,1,0:T(8,128)(2,1)S(1)}, bf16[4,1,64,128]{3,2,1,0:T(8,128)(2,1)S(1)}, u32[]{:S(2)}, u32[]{:S(2)}) %collective-permute-start.9) | collective-permute-done | bytes 65568 | tf_op jit(solution)/shard_map/ppermute | solution.py:22
  63.2 2.7 %collective-permute-done.13.right = bf16[1,6,64,128]{3,2,1,0:T(8,128)(2,1)S(1)} collective-permute-done((bf16[1,6,64,128]{3,2,1,0:T(8,128)(2,1)S(1)}, bf16[1,6,64,128]{3,2,1,0:T(8,128)(2,1)S(1)}, u32[]{:S(2)}, u32[]{:S(2)}) %collective-permute-start.13) | collective-permute-done | bytes 98336 | tf_op jit(solution)/shard_map/ppermute | solution.py:22
  65.9 2.6 %first_errors_kernel.1 = (bf16[4,4,64,128]{3,2,1,0:T(8,128)(2,1)}, bf16[4,1,64,128]{3,2,1,0:T(8,128)(2,1)}, bf16[4,1,64,128]{3,2,1,0:T(8,128)(2,1)}, bf16[4,4,64...) custom-call(s32[1]{0:T(128)} %bitcast.core, bf16[4,4,64,128]{3,2,1,0:T(8,128)(2,1)S(1)} %get-tuple-element.73.own, ...), custom_call_target="tpu_custom_call" | custom-call | flops 45298484 | bytes 86835 | tf_op jit(solution)/shard_map/first_errors_kernel/pallas_call | solution.py:393
  70.6 2.7 %pair_grads_kernel.1 = bf16[64,112,128]{2,1,0:T(8,128)(2,1)} custom-call(bf16[6,6,64,128]{3,2,1,0:T(8,128)(2,1)S(1)} %collective-permute-done.14.fields, bf16[4,4,64,128]{3,2,1,0:T(8,128)(2,1)S(1)} %collective-permute-done.15.errors, f32[1152,384]{1,0:T(8,128)S(1)} %own_grads_kernel.1.own_total, bf16[64,56,128]{2,1,0:T(8,128)(2,1)S(1)} %bottom_grads_kernel.1.three), custom_call_target="tpu_custom_call" | custom-call | flops 45298484 | bytes 176947 | tf_op jit(solution)/shard_map/pair_grads_kernel/pallas_call | solution.py:393
  73.3 5.1 %all-to-all-start.1 = ((bf16[64,112,128]{2,1,0:T(8,128)(2,1)}), bf16[64,112,128]{2,1,0:T(8,128)(2,1)S(1)}, u32[]{:S(2)}, u32[]{:S(2)}) async-start(bf16[64,112,128]{2,1,0:T(8,128)(2,1)} %pair_grads_kernel.1), calls=%async_computation.1 | async-start | bytes 3670016 | tf_op jit(solution)/shard_map/all_to_all | solution.py:480
  79.4 3.8 %collective-permute-start.17 = (bf16[4,1,64,128]{3,2,1,0:T(8,128)(2,1)S(1)}, bf16[4,1,64,128]{3,2,1,0:T(8,128)(2,1)S(1)}, u32[]{:S(2)}, u32[]{:S(2)}) collective-permute-start(bf16[4,1,64,128]{3,2,1,0:T(8,128)(2,1)S(1)} %copy-done.9), channel_id=1, source_target_pairs={{0,15},{1,0},{2,1},{3,2},{4,3},{5,4},{6,5},{7,6},{8,7},{9,8},{10,9... | collective-permute-start | bytes 196616 | tf_op jit(solution)/shard_map/ppermute | solution.py:22
  83.2 20.2 %all-to-all-done.1.pieces = bf16[64,112,128]{2,1,0:T(8,128)(2,1)S(1)} async-done(((bf16[64,112,128]{2,1,0:T(8,128)(2,1)}), bf16[64,112,128]{2,1,0:T(8,128)(2,1)S(1)}, u32[]{:S(2)}, u32[]{:S(2)}) %all-to-all-start.1) | async-done | bytes 1835040 | tf_op jit(solution)/shard_map/all_to_all | solution.py:480
  104.6 6.9 %all-to-all-start.2 = ((bf16[64,56,128]{2,1,0:T(8,128)(2,1)}), bf16[64,56,128]{2,1,0:T(8,128)(2,1)S(1)}, u32[]{:S(2)}, u32[]{:S(2)}) async-start(bf16[64,56,128]{2,1,0:T(8,128)(2,1)} %get-tuple-element.99), calls=%async_computation.2 | async-start | bytes 1835008 | tf_op jit(solution)/shard_map/all_to_all | solution.py:485
  116.1 2.2 %collective-permute-start.20 = (bf16[2,56,128]{2,1,0:T(8,128)(2,1)S(1)}, bf16[2,56,128]{2,1,0:T(8,128)(2,1)S(1)}, u32[]{:S(2)}, u32[]{:S(2)}) collective-permute-start(bf16[2,56,128]{2,1,0:T(8,128)(2,1)S(1)} %maximum_select_fusion.1.pair_0), channel_id=1, source_target_pairs={{0,64},{32,96},{64,0},{96,32},{1,65},{33,97},{65,1},{97,33},{2,66}... | collective-permute-start | bytes 86024 | tf_op jit(solution)/shard_map/ppermute | solution.py:30
  121.0 5.5 %collective-permute-done.19.pair_1 = bf16[2,56,128]{2,1,0:T(8,128)(2,1)S(1)} collective-permute-done((bf16[2,56,128]{2,1,0:T(8,128)(2,1)S(1)}, bf16[2,56,128]{2,1,0:T(8,128)(2,1)S(1)}, u32[]{:S(2)}, u32[]{:S(2)}) %collective-permute-start.19) | collective-permute-done | bytes 28704 | tf_op jit(solution)/shard_map/ppermute | solution.py:30
  127.3 3.8 %collective-permute-start.24 = (bf16[3584,128]{1,0:T(8,128)(2,1)S(1)}, bf16[3584,128]{1,0:T(8,128)(2,1)S(1)}, u32[]{:S(2)}, u32[]{:S(2)}) collective-permute-start(bf16[3584,128]{1,0:T(8,128)(2,1)S(1)} %bitcast.28), channel_id=1, source_target_pairs={{0,16},{16,0},{1,17},{17,1},{2,18},{18,2},{3,19},{19,3},{4,20},{20... | collective-permute-start | bytes 2752520 | tf_op jit(solution)/shard_map/ppermute | solution.py:26
  131.1 2.9 %outer_input_kernel.1 = bf16[4,4,64,128]{3,2,1,0:T(8,128)(2,1)} custom-call(bf16[4,4,64,128]{3,2,1,0:T(8,128)(2,1)} %get-tuple-element.85.own, bf16[4,1,64,128]{3,2,1,0:T(8,128)(2,1)} %copy-done.5, bf16[4,1,64,128]{3,2,1,0:T(8,128)(2,1)} %copy-done.6, bf16[1,6,64,128]{3,2,1,0:T(8,128)(2,1)S(1)} %collective-permute-done.22.left, ...), custom_call_target="tpu_custom_call" | custom-call | flops 11324620 | bytes 80281 | tf_op jit(solution)/shard_map/outer_input_kernel/pallas_call | solution.py:393
  134.0 2.1 %finish_kernel.1 = (f32[3456,128]{1,0:T(8,128)}, f32[3456,128]{1,0:T(8,128)}) custom-call(s32[1]{0:T(128)} %bitcast.core, bf16[3584,128]{1,0:T(8,128)(2,1)S(1)} %bitcast.29, bf16[3584,128]{1,0:T(8,128)(2,1)S(1)} %collective-permute-done.24.other), custom_call_target="tpu_custom_call" | custom-call | tf_op jit(solution)/shard_map/finish_kernel/pallas_call | solution.py:509
  (75 shorter events, 27.1 us)
Async XLA Ops:
  1.7 13.4 %collective-permute-start = (bf16[5,2,64,128]{3,2,1,0:T(8,128)(2,1)S(1)}, bf16[5,2,64,128]{3,2,1,0:T(8,128)(2,1)S(1)}, u32[]{:S(2)}, u32[]{:S(2)}) collective-permute-start(bf16[5,2,64,128]{3,2,1,0:T(8,128)(2,1)S(1)} %get-tuple-element.62), channel_id=1, source_target_pairs={{0,1},{1,2},{2,3},{3,4},{4,5},{5,6},{6,7},{7,8},{8,9},{9,10},{10,1... | collective-permute-start | bytes 491528 | tf_op jit(solution)/shard_map/ppermute | solution.py:22
  3.9 11.2 %collective-permute-start.1 = (bf16[5,2,64,128]{3,2,1,0:T(8,128)(2,1)S(1)}, bf16[5,2,64,128]{3,2,1,0:T(8,128)(2,1)S(1)}, u32[]{:S(2)}, u32[]{:S(2)}) collective-permute-start(bf16[5,2,64,128]{3,2,1,0:T(8,128)(2,1)S(1)} %get-tuple-element.63), channel_id=1, source_target_pairs={{0,15},{1,0},{2,1},{3,2},{4,3},{5,4},{6,5},{7,6},{8,7},{9,8},{10,9... | collective-permute-start | bytes 491528 | tf_op jit(solution)/shard_map/ppermute | solution.py:22
  10.8 20.2 %all-to-all-start = ((bf16[16,27,8,128]{3,2,1,0:T(8,128)(2,1)}), bf16[16,27,8,128]{3,2,1,0:T(8,128)(2,1)}, u32[]{:S(2)}, u32[]{:S(2)}) async-start(bf16[16,27,8,128]{3,2,1,0:T(8,128)(2,1)} %broadcast_in_dim.3), calls=%async_computation | async-start | bytes 1769472 | tf_op jit(solution)/shard_map/all_to_all | solution.py:422
  15.2 6.1 %collective-permute-start.2 = (bf16[20,64,128]{2,1,0:T(8,128)(2,1)S(1)}, bf16[20,64,128]{2,1,0:T(8,128)(2,1)S(1)}, u32[]{:S(2)}, u32[]{:S(2)}) collective-permute-start(bf16[20,64,128]{2,1,0:T(8,128)(2,1)S(1)} %get-tuple-element.64), channel_id=1, source_target_pairs={{0,16},{16,32},{32,48},{48,64},{64,80},{80,96},{96,112},{112,0},{1... | collective-permute-start | bytes 983048 | tf_op jit(solution)/shard_map/ppermute | solution.py:22
  17.3 6.9 %collective-permute-start.3 = (bf16[20,64,128]{2,1,0:T(8,128)(2,1)S(1)}, bf16[20,64,128]{2,1,0:T(8,128)(2,1)S(1)}, u32[]{:S(2)}, u32[]{:S(2)}) collective-permute-start(bf16[20,64,128]{2,1,0:T(8,128)(2,1)S(1)} %get-tuple-element.65), channel_id=1, source_target_pairs={{0,112},{16,0},{32,16},{48,32},{64,48},{80,64},{96,80},{112,96},{1... | collective-permute-start | bytes 983048 | tf_op jit(solution)/shard_map/ppermute | solution.py:22
  30.9 9.2 %collective-permute-start.8 = (bf16[16,27,8,128]{3,2,1,0:T(8,128)(2,1)}, bf16[16,27,8,128]{3,2,1,0:T(8,128)(2,1)S(1)}, u32[]{:S(2)}, u32[]{:S(2)}) collective-permute-start(bf16[16,27,8,128]{3,2,1,0:T(8,128)(2,1)} %all-to-all-done), channel_id=1, source_target_pairs={{0,16},{16,0},{1,17},{17,1},{2,18},{18,2},{3,19},{19,3},{4,20},{20... | collective-permute-start | bytes 2654216 | tf_op jit(solution)/shard_map/ppermute | solution.py:26
  31.7 6.1 %collective-permute-start.4 = (bf16[2,2,32,128]{3,2,1,0:T(8,128)(2,1)S(1)}, bf16[2,2,32,128]{3,2,1,0:T(8,128)(2,1)S(1)}, u32[]{:S(2)}, u32[]{:S(2)}) collective-permute-start(bf16[2,2,32,128]{3,2,1,0:T(8,128)(2,1)S(1)} %get-tuple-element.67.own), channel_id=1, source_target_pairs={{0,1},{1,2},{2,3},{3,4},{4,5},{5,6},{6,7},{7,8},{8,9},{9,10},{10,1... | collective-permute-start | bytes 98312 | tf_op jit(solution)/shard_map/ppermute | solution.py:22
  32.4 5.4 %collective-permute-start.5 = (bf16[2,2,32,128]{3,2,1,0:T(8,128)(2,1)S(1)}, bf16[2,2,32,128]{3,2,1,0:T(8,128)(2,1)S(1)}, u32[]{:S(2)}, u32[]{:S(2)}) collective-permute-start(bf16[2,2,32,128]{3,2,1,0:T(8,128)(2,1)S(1)} %get-tuple-element.67.own), channel_id=1, source_target_pairs={{0,15},{1,0},{2,1},{3,2},{4,3},{5,4},{6,5},{7,6},{8,7},{9,8},{10,9... | collective-permute-start | bytes 98312 | tf_op jit(solution)/shard_map/ppermute | solution.py:22
  36.5 34.0 %collective-permute-start.14 = (bf16[6,6,64,128]{3,2,1,0:T(8,128)(2,1)}, bf16[6,6,64,128]{3,2,1,0:T(8,128)(2,1)S(1)}, u32[]{:S(2)}, u32[]{:S(2)}) collective-permute-start(bf16[6,6,64,128]{3,2,1,0:T(8,128)(2,1)} %get-tuple-element.86), channel_id=1, source_target_pairs={{0,16},{16,0},{1,17},{17,1},{2,18},{18,2},{3,19},{19,3},{4,20},{20... | collective-permute-start | bytes 1769480 | tf_op jit(solution)/shard_map/ppermute | solution.py:26
  37.8 4.5 %collective-permute-start.6 = (bf16[2,6,32,128]{3,2,1,0:T(8,128)(2,1)S(1)}, bf16[2,6,32,128]{3,2,1,0:T(8,128)(2,1)S(1)}, u32[]{:S(2)}, u32[]{:S(2)}) collective-permute-start(bf16[2,6,32,128]{3,2,1,0:T(8,128)(2,1)S(1)} %get-tuple-element.68), channel_id=1, source_target_pairs={{0,16},{16,32},{32,48},{48,64},{64,80},{80,96},{96,112},{112,0},{1... | collective-permute-start | bytes 294920 | tf_op jit(solution)/shard_map/ppermute | solution.py:22
  40.1 4.0 %collective-permute-start.7 = (bf16[2,6,32,128]{3,2,1,0:T(8,128)(2,1)S(1)}, bf16[2,6,32,128]{3,2,1,0:T(8,128)(2,1)S(1)}, u32[]{:S(2)}, u32[]{:S(2)}) collective-permute-start(bf16[2,6,32,128]{3,2,1,0:T(8,128)(2,1)S(1)} %get-tuple-element.69), channel_id=1, source_target_pairs={{0,112},{16,0},{32,16},{48,32},{64,48},{80,64},{96,80},{112,96},{1... | collective-permute-start | bytes 294920 | tf_op jit(solution)/shard_map/ppermute | solution.py:22
  48.0 6.4 %collective-permute-start.10 = (bf16[4,1,64,128]{3,2,1,0:T(8,128)(2,1)S(1)}, bf16[4,1,64,128]{3,2,1,0:T(8,128)(2,1)S(1)}, u32[]{:S(2)}, u32[]{:S(2)}) collective-permute-start(bf16[4,1,64,128]{3,2,1,0:T(8,128)(2,1)S(1)} %get-tuple-element.75), channel_id=1, source_target_pairs={{0,15},{1,0},{2,1},{3,2},{4,3},{5,4},{6,5},{7,6},{8,7},{9,8},{10,9... | collective-permute-start | bytes 196616 | tf_op jit(solution)/shard_map/ppermute | solution.py:22
  53.1 6.4 %collective-permute-start.9 = (bf16[4,1,64,128]{3,2,1,0:T(8,128)(2,1)S(1)}, bf16[4,1,64,128]{3,2,1,0:T(8,128)(2,1)S(1)}, u32[]{:S(2)}, u32[]{:S(2)}) collective-permute-start(bf16[4,1,64,128]{3,2,1,0:T(8,128)(2,1)S(1)} %get-tuple-element.74), channel_id=1, source_target_pairs={{0,1},{1,2},{2,3},{3,4},{4,5},{5,6},{6,7},{7,8},{8,9},{9,10},{10,1... | collective-permute-start | bytes 196616 | tf_op jit(solution)/shard_map/ppermute | solution.py:22
  61.6 4.3 %collective-permute-start.13 = (bf16[1,6,64,128]{3,2,1,0:T(8,128)(2,1)S(1)}, bf16[1,6,64,128]{3,2,1,0:T(8,128)(2,1)S(1)}, u32[]{:S(2)}, u32[]{:S(2)}) collective-permute-start(bf16[1,6,64,128]{3,2,1,0:T(8,128)(2,1)S(1)} %get-tuple-element.81), channel_id=1, source_target_pairs={{0,112},{16,0},{32,16},{48,32},{64,48},{80,64},{96,80},{112,96},{1... | collective-permute-start | bytes 294920 | tf_op jit(solution)/shard_map/ppermute | solution.py:22
  73.3 30.1 %all-to-all-start.1 = ((bf16[64,112,128]{2,1,0:T(8,128)(2,1)}), bf16[64,112,128]{2,1,0:T(8,128)(2,1)S(1)}, u32[]{:S(2)}, u32[]{:S(2)}) async-start(bf16[64,112,128]{2,1,0:T(8,128)(2,1)} %pair_grads_kernel.1), calls=%async_computation.1 | async-start | bytes 3670016 | tf_op jit(solution)/shard_map/all_to_all | solution.py:480
  78.4 26.2 %collective-permute-start.16 = (bf16[4,1,64,128]{3,2,1,0:T(8,128)(2,1)S(1)}, bf16[4,1,64,128]{3,2,1,0:T(8,128)(2,1)S(1)}, u32[]{:S(2)}, u32[]{:S(2)}) collective-permute-start(bf16[4,1,64,128]{3,2,1,0:T(8,128)(2,1)S(1)} %copy-done.10), channel_id=1, source_target_pairs={{0,1},{1,2},{2,3},{3,4},{4,5},{5,6},{6,7},{7,8},{8,9},{9,10},{10,1... | collective-permute-start | bytes 196616 | tf_op jit(solution)/shard_map/ppermute | solution.py:22
  79.4 25.1 %collective-permute-start.17 = (bf16[4,1,64,128]{3,2,1,0:T(8,128)(2,1)S(1)}, bf16[4,1,64,128]{3,2,1,0:T(8,128)(2,1)S(1)}, u32[]{:S(2)}, u32[]{:S(2)}) collective-permute-start(bf16[4,1,64,128]{3,2,1,0:T(8,128)(2,1)S(1)} %copy-done.9), channel_id=1, source_target_pairs={{0,15},{1,0},{2,1},{3,2},{4,3},{5,4},{6,5},{7,6},{8,7},{9,8},{10,9... | collective-permute-start | bytes 196616 | tf_op jit(solution)/shard_map/ppermute | solution.py:22
  104.6 22.7 %all-to-all-start.2 = ((bf16[64,56,128]{2,1,0:T(8,128)(2,1)}), bf16[64,56,128]{2,1,0:T(8,128)(2,1)S(1)}, u32[]{:S(2)}, u32[]{:S(2)}) async-start(bf16[64,56,128]{2,1,0:T(8,128)(2,1)} %get-tuple-element.99), calls=%async_computation.2 | async-start | bytes 1835008 | tf_op jit(solution)/shard_map/all_to_all | solution.py:485
  113.5 13.7 %collective-permute-start.22 = (bf16[1,6,64,128]{3,2,1,0:T(8,128)(2,1)S(1)}, bf16[1,6,64,128]{3,2,1,0:T(8,128)(2,1)S(1)}, u32[]{:S(2)}, u32[]{:S(2)}) collective-permute-start(bf16[1,6,64,128]{3,2,1,0:T(8,128)(2,1)S(1)} %get-tuple-element.102), channel_id=1, source_target_pairs={{0,16},{16,32},{32,48},{48,64},{64,80},{80,96},{96,112},{112,0},{1... | collective-permute-start | bytes 294920 | tf_op jit(solution)/shard_map/ppermute | solution.py:22
  114.7 12.5 %collective-permute-start.23 = (bf16[1,6,64,128]{3,2,1,0:T(8,128)(2,1)S(1)}, bf16[1,6,64,128]{3,2,1,0:T(8,128)(2,1)S(1)}, u32[]{:S(2)}, u32[]{:S(2)}) collective-permute-start(bf16[1,6,64,128]{3,2,1,0:T(8,128)(2,1)S(1)} %get-tuple-element.103), channel_id=1, source_target_pairs={{0,112},{16,0},{32,16},{48,32},{64,48},{80,64},{96,80},{112,96},{1... | collective-permute-start | bytes 294920 | tf_op jit(solution)/shard_map/ppermute | solution.py:22
  114.8 11.8 %collective-permute-start.19 = (bf16[2,56,128]{2,1,0:T(8,128)(2,1)S(1)}, bf16[2,56,128]{2,1,0:T(8,128)(2,1)S(1)}, u32[]{:S(2)}, u32[]{:S(2)}) collective-permute-start(bf16[2,56,128]{2,1,0:T(8,128)(2,1)S(1)} %maximum_select_fusion.1.pair_0), channel_id=1, source_target_pairs={{0,32},{32,64},{64,96},{96,0},{1,33},{33,65},{65,97},{97,1},{2,34}... | collective-permute-start | bytes 86024 | tf_op jit(solution)/shard_map/ppermute | solution.py:30
  116.1 10.4 %collective-permute-start.20 = (bf16[2,56,128]{2,1,0:T(8,128)(2,1)S(1)}, bf16[2,56,128]{2,1,0:T(8,128)(2,1)S(1)}, u32[]{:S(2)}, u32[]{:S(2)}) collective-permute-start(bf16[2,56,128]{2,1,0:T(8,128)(2,1)S(1)} %maximum_select_fusion.1.pair_0), channel_id=1, source_target_pairs={{0,64},{32,96},{64,0},{96,32},{1,65},{33,97},{65,1},{97,33},{2,66}... | collective-permute-start | bytes 86024 | tf_op jit(solution)/shard_map/ppermute | solution.py:30
  118.3 8.2 %collective-permute-start.21 = (bf16[2,56,128]{2,1,0:T(8,128)(2,1)S(1)}, bf16[2,56,128]{2,1,0:T(8,128)(2,1)S(1)}, u32[]{:S(2)}, u32[]{:S(2)}) collective-permute-start(bf16[2,56,128]{2,1,0:T(8,128)(2,1)S(1)} %maximum_select_fusion.1.pair_0), channel_id=1, source_target_pairs={{0,96},{32,0},{64,32},{96,64},{1,97},{33,1},{65,33},{97,65},{2,98}... | collective-permute-start | bytes 86024 | tf_op jit(solution)/shard_map/ppermute | solution.py:30
  127.3 6.7 %collective-permute-start.24 = (bf16[3584,128]{1,0:T(8,128)(2,1)S(1)}, bf16[3584,128]{1,0:T(8,128)(2,1)S(1)}, u32[]{:S(2)}, u32[]{:S(2)}) collective-permute-start(bf16[3584,128]{1,0:T(8,128)(2,1)S(1)} %bitcast.28), channel_id=1, source_target_pairs={{0,16},{16,0},{1,17},{17,1},{2,18},{18,2},{3,19},{19,3},{4,20},{20... | collective-permute-start | bytes 2752520 | tf_op jit(solution)/shard_map/ppermute | solution.py:26
  (15 other events, 179.4 us)

commit v15 on v14

--- a/solution.py
+++ b/solution.py
@@ -66,14 +66,6 @@
     return shifted(high, GX, 1), shifted(low, GX, -1)
 
 
-def halo_pieces(own, width, first, last):
-    before, after = shifted(last, GY, 1), shifted(first, GY, -1)
-    size_x, size_y, size_z, chans = own.shape
-    slab = (width, size_y + 2 * width, size_z, chans)
-    low, high = call(slab_kernel, [(slab, BF16)] * 2, [], 0, own, before, after)
-    return own, before, after, *exchange_x(low, high)
-
-
 def fill_padded(padded, own, before, after, left, right):
     size_x, size_y = own.shape[0], own.shape[1]
     width = left.shape[0]
@@ -198,6 +190,19 @@
                 for start in range(2):
                     total = total + halves[2 * at_x + part, at_y, pl.ds(start, 32, stride=2), :]
             pooled[at_x, at_y] = (total * 0.125).astype(BF16)
+
+
+def interleave_kernel(core, mine, theirs, out):
+    first_core = core[0] == 0
+
+    def step(tap, _):
+        own, other = mine[:, tap].astype(F32), theirs[:, tap].astype(F32)
+        parts = [jnp.where(first_core, own, other), jnp.where(first_core, other, own)]
+        parts = [p.reshape(16, 1, 8, 128) for p in parts]
+        out[tap] = jnp.concatenate(parts, axis=1).reshape(256, 128).astype(BF16)
+        return 0
+
+    lax.fori_loop(0, 27, step, 0)
 
 
 def bottom_kernel(own, before, after, left, right, g_own, f_before, f_after, f_left, f_right,
@@ -434,16 +439,17 @@
     edge = (4, 1, 64, 128)
     field_keep, field_send, slope_one, slope_two, pooled = call(
         forward_kernel,
-        [(field, BF16, True), (field, BF16, True), (block, BF16, True), (block, BF16, True), ((2, 2, 32, 128), BF16)],
+        [(field, BF16, True), (field, BF16, True), (block, BF16, True), (block, BF16, True), ((2, 2, 32, 128), BF16, True)],
         [((8, 8, 64, 128), BF16), ((1152, 384), BF16), (field, BF16), ((4, 2, 64, 128), F32)],
         3 * conv_flops, core_ref, features, f_before, f_after, f_left, f_right, taps_one, taps_two,
     )
     field_other = swap_cores(field_send)
     mine, pooled = lax.optimization_barrier((mine, pooled))
     theirs = swap_cores(mine)
-    both = jnp.where(first_core, jnp.stack([mine, theirs]), jnp.stack([theirs, mine]))
-    taps_three = jnp.transpose(both, (2, 1, 0, 3, 4)).reshape(27, 256, 128)
-    p_pieces = halo_pieces(pooled, 2, pooled, pooled)
+    (taps_three,) = call(interleave_kernel, [((27, 256, 128), BF16)], [], 0, core_ref, mine, theirs)
+    p_before, p_after = shifted(pooled, GY, 1), shifted(pooled, GY, -1)
+    low, high = call(slab_kernel, [((2, 6, 32, 128), BF16)] * 2, [], 0, in_hbm(pooled), p_before, p_after)
+    p_pieces = pooled, p_before, p_after, *exchange_x(low, high)
     bottleneck, bundle, err_two, err_first, err_last = call(
         bottom_kernel,
         [((2, 2, 32, 256), BF16, True), ((24, 32, 128), BF16), (block, BF16), (edge, BF16), (edge, BF16)],

time: 137 us -> 139 us (1.015)
  Pallas kernels: 27.6 us -> 29.4 us
  other arithmetic: 2.57 us -> 0.87 us
    pallas_call x14 -> x15, Pallas kernels: 24.8 us -> 26.6 us  [call(): pl.pallas_call(kernel, out_shape=shapes, in_specs=[pl.BlockSpec(memory_sp...]
    transpose x1 -> x0, other arithmetic: 1.7 us -> none  [on_device(): taps_three = jnp.transpose(both, (2, 1, 0, 3, 4)).reshape(27, 256, 128)]
    unnamed x22 -> x32, local copies, waits for them, and re-layouts: 0.05 us -> 1.58 us
  transfers between devices with their start and end apart: 28 -> 28, of which waited for: 11 -> 11; matrix products, arithmetic and copies ran while one was open for 3% -> 1% of each run, Pallas kernels for 16% -> 17%
where the time goes in v15:
time: 139 us; the launch traced here: 138 us
  starting transfers between devices  58.6 us (42%)
  waiting for transfers between devices  45.7 us (33%)
  Pallas kernels  29.4 us (21%)
  local copies, waits for them, and re-layouts  2.6 us (2%)
    ppermute x16, starting transfers between devices, shifted(): lax.ppermute(array, axes, [(i, (i + step) % count) for i in range(count)])  28.5 us
    pallas_call x15, Pallas kernels, call(): pl.pallas_call(kernel, out_shape=shapes, in_specs=[pl.BlockSpec(memory_sp...  26.6 us
    all_to_all x1, waiting for transfers between devices, on_device(): lax.all_to_all(kept, FLAT, 0, 0)  20.2 us
    ppermute x16, waiting for transfers between devices, shifted(): lax.ppermute(array, axes, [(i, (i + step) % count) for i in range(count)])  19.6 us
    ppermute x6, starting transfers between devices, swap_cores(): return lax.ppermute(array, 'c', [(0, 1), (1, 0)])  9.74 us
    all_to_all x1, starting transfers between devices, on_device(): whole = lax.all_to_all(part, FLAT, 0, 0).reshape(64 * PIECE, 128)  6.9 us
    ppermute x3, waiting for transfers between devices, ring_pieces(): lax.ppermute(pieces[d], axis, [(i, (i + d) % 4) for i in range(4)])  5.5 us
    all_to_all x1, starting transfers between devices, on_device(): lax.all_to_all(kept, FLAT, 0, 0)  5.06 us
  transfers between devices with their start and end apart: 28, of which 11 were waited for; matrix products, arithmetic and copies ran while one was open for 1% of the time, Pallas kernels for 17%

profile of v15, /device:TPU:1, one launch (start us, length us, event | category | flops | bytes accessed | tf_op | source)
XLA Modules:
  0.0 138.0 jit_solution(187939507728995147)
XLA Ops:
  2.3 2.1 %collective-permute-start = (bf16[5,2,64,128]{3,2,1,0:T(8,128)(2,1)}, bf16[5,2,64,128]{3,2,1,0:T(8,128)(2,1)S(1)}, u32[]{:S(2)}, u32[]{:S(2)}) collective-permute-start(bf16[5,2,64,128]{3,2,1,0:T(8,128)(2,1)} %get-tuple-element.62), channel_id=1, source_target_pairs={{0,1},{1,2},{2,3},{3,4},{4,5},{5,6},{6,7},{7,8},{8,9},{9,10},{10,1... | collective-permute-start | bytes 491528 | tf_op jit(solution)/shard_map/ppermute | solution.py:22
  4.5 4.9 %collective-permute-start.1 = (bf16[5,2,64,128]{3,2,1,0:T(8,128)(2,1)S(1)}, bf16[5,2,64,128]{3,2,1,0:T(8,128)(2,1)S(1)}, u32[]{:S(2)}, u32[]{:S(2)}) collective-permute-start(bf16[5,2,64,128]{3,2,1,0:T(8,128)(2,1)S(1)} %get-tuple-element.63), channel_id=1, source_target_pairs={{0,15},{1,0},{2,1},{3,2},{4,3},{5,4},{6,5},{7,6},{8,7},{9,8},{10,9... | collective-permute-start | bytes 491528 | tf_op jit(solution)/shard_map/ppermute | solution.py:22
  11.3 3.6 %all-to-all-start = ((bf16[16,27,8,128]{3,2,1,0:T(8,128)(2,1)}), bf16[16,27,8,128]{3,2,1,0:T(8,128)(2,1)S(1)}, u32[]{:S(2)}, u32[]{:S(2)}) async-start(bf16[16,27,8,128]{3,2,1,0:T(8,128)(2,1)} %broadcast_in_dim.3), calls=%async_computation | async-start | bytes 1769472 | tf_op jit(solution)/shard_map/all_to_all | solution.py:427
  15.7 2.1 %collective-permute-start.2 = (bf16[20,64,128]{2,1,0:T(8,128)(2,1)S(1)}, bf16[20,64,128]{2,1,0:T(8,128)(2,1)S(1)}, u32[]{:S(2)}, u32[]{:S(2)}) collective-permute-start(bf16[20,64,128]{2,1,0:T(8,128)(2,1)S(1)} %get-tuple-element.64), channel_id=1, source_target_pairs={{0,16},{16,32},{32,48},{48,64},{64,80},{80,96},{96,112},{112,0},{1... | collective-permute-start | bytes 983048 | tf_op jit(solution)/shard_map/ppermute | solution.py:22
  17.7 4.0 %collective-permute-done.2.left.f_left = bf16[20,64,128]{2,1,0:T(8,128)(2,1)S(1)} collective-permute-done((bf16[20,64,128]{2,1,0:T(8,128)(2,1)S(1)}, bf16[20,64,128]{2,1,0:T(8,128)(2,1)S(1)}, u32[]{:S(2)}, u32[]{:S(2)}) %collective-permute-start.2) | collective-permute-done | bytes 327712 | tf_op jit(solution)/shard_map/ppermute | solution.py:22
  21.7 2.8 %collective-permute-done.3.right.f_right = bf16[20,64,128]{2,1,0:T(8,128)(2,1)S(1)} collective-permute-done((bf16[20,64,128]{2,1,0:T(8,128)(2,1)S(1)}, bf16[20,64,128]{2,1,0:T(8,128)(2,1)S(1)}, u32[]{:S(2)}, u32[]{:S(2)}) %collective-permute-start.3) | collective-permute-done | bytes 327712 | tf_op jit(solution)/shard_map/ppermute | solution.py:22
  25.4 6.8 %forward_kernel.1 = (bf16[6,6,64,128]{3,2,1,0:T(8,128)(2,1)}, bf16[6,6,64,128]{3,2,1,0:T(8,128)(2,1)}, bf16[4,4,64,128]{3,2,1,0:T(8,128)(2,1)}, bf16[4,4,64,128]{3,2,1,0:T(8,128)(2,1)}, bf16[2,2,32,128]{3,2,1,0:T(8,128)(2,1)}) custom-call(s32[1]{0:T(128)} %bitcast.core, bf16[4,4,64,128]{3,2,1,0:T(8,128)(2,1)S(1)} %copy-done.4, ...), custom_call_target="tpu_custom_call" | custom-call | flops 135895456 | bytes 150733 | tf_op jit(solution)/shard_map/forward_kernel/pallas_call | solution.py:398
  33.8 3.4 %collective-permute-start.5 = (bf16[2,2,32,128]{3,2,1,0:T(8,128)(2,1)}, bf16[2,2,32,128]{3,2,1,0:T(8,128)(2,1)S(1)}, u32[]{:S(2)}, u32[]{:S(2)}) collective-permute-start(bf16[2,2,32,128]{3,2,1,0:T(8,128)(2,1)} %get-tuple-element.67.own), channel_id=1, source_target_pairs={{0,15},{1,0},{2,1},{3,2},{4,3},{5,4},{6,5},{7,6},{8,7},{9,8},{10,9... | collective-permute-start | bytes 98312 | tf_op jit(solution)/shard_map/ppermute | solution.py:22
  39.4 2.6 %collective-permute-start.6 = (bf16[2,6,32,128]{3,2,1,0:T(8,128)(2,1)S(1)}, bf16[2,6,32,128]{3,2,1,0:T(8,128)(2,1)S(1)}, u32[]{:S(2)}, u32[]{:S(2)}) collective-permute-start(bf16[2,6,32,128]{3,2,1,0:T(8,128)(2,1)S(1)} %get-tuple-element.68), channel_id=1, source_target_pairs={{0,16},{16,32},{32,48},{48,64},{64,80},{80,96},{96,112},{112,0},{1... | collective-permute-start | bytes 294920 | tf_op jit(solution)/shard_map/ppermute | solution.py:22
  46.1 3.9 %bottom_kernel.1 = (bf16[2,2,32,256]{3,2,1,0:T(8,128)(2,1)}, bf16[24,32,128]{2,1,0:T(8,128)(2,1)S(1)}, bf16[4,4,64,128]{3,2,1,0:T(8,128)(2,1)S(1)}, bf16[4,1,64,...) custom-call(bf16[2,2,32,128]{3,2,1,0:T(8,128)(2,1)S(1)} %copy-done.13, ...), custom_call_target="tpu_custom_call" | custom-call | flops 45298484 | bytes 181862 | tf_op jit(solution)/shard_map/bottom_kernel/pallas_call | solution.py:398
  50.0 5.1 %collective-permute-start.10 = (bf16[4,1,64,128]{3,2,1,0:T(8,128)(2,1)S(1)}, bf16[4,1,64,128]{3,2,1,0:T(8,128)(2,1)S(1)}, u32[]{:S(2)}, u32[]{:S(2)}) collective-permute-start(bf16[4,1,64,128]{3,2,1,0:T(8,128)(2,1)S(1)} %get-tuple-element.75), channel_id=1, source_target_pairs={{0,15},{1,0},{2,1},{3,2},{4,3},{5,4},{6,5},{7,6},{8,7},{9,8},{10,9... | collective-permute-start | bytes 196616 | tf_op jit(solution)/shard_map/ppermute | solution.py:22
  56.4 5.1 %collective-permute-done.9.before = bf16[4,1,64,128]{3,2,1,0:T(8,128)(2,1)S(1)} collective-permute-done((bf16[4,1,64,128]{3,2,1,0:T(8,128)(2,1)S(1)}, bf16[4,1,64,128]{3,2,1,0:T(8,128)(2,1)S(1)}, u32[]{:S(2)}, u32[]{:S(2)}) %collective-permute-start.9) | collective-permute-done | bytes 65568 | tf_op jit(solution)/shard_map/ppermute | solution.py:22
  65.4 2.6 %collective-permute-done.13.right = bf16[1,6,64,128]{3,2,1,0:T(8,128)(2,1)S(1)} collective-permute-done((bf16[1,6,64,128]{3,2,1,0:T(8,128)(2,1)S(1)}, bf16[1,6,64,128]{3,2,1,0:T(8,128)(2,1)S(1)}, u32[]{:S(2)}, u32[]{:S(2)}) %collective-permute-start.13) | collective-permute-done | bytes 98336 | tf_op jit(solution)/shard_map/ppermute | solution.py:22
  68.0 2.6 %first_errors_kernel.1 = (bf16[4,4,64,128]{3,2,1,0:T(8,128)(2,1)}, bf16[4,1,64,128]{3,2,1,0:T(8,128)(2,1)}, bf16[4,1,64,128]{3,2,1,0:T(8,128)(2,1)}, bf16[4,4,64...) custom-call(s32[1]{0:T(128)} %bitcast.core, bf16[4,4,64,128]{3,2,1,0:T(8,128)(2,1)S(1)} %get-tuple-element.73.own, ...), custom_call_target="tpu_custom_call" | custom-call | flops 45298484 | bytes 86835 | tf_op jit(solution)/shard_map/first_errors_kernel/pallas_call | solution.py:398
  72.5 2.7 %pair_grads_kernel.1 = bf16[64,112,128]{2,1,0:T(8,128)(2,1)} custom-call(bf16[6,6,64,128]{3,2,1,0:T(8,128)(2,1)S(1)} %collective-permute-done.14.fields, bf16[4,4,64,128]{3,2,1,0:T(8,128)(2,1)S(1)} %collective-permute-done.15.errors, f32[1152,384]{1,0:T(8,128)S(1)} %own_grads_kernel.1.own_total, bf16[64,56,128]{2,1,0:T(8,128)(2,1)S(1)} %bottom_grads_kernel.1.three), custom_call_target="tpu_custom_call" | custom-call | flops 45298484 | bytes 176947 | tf_op jit(solution)/shard_map/pair_grads_kernel/pallas_call | solution.py:398
  75.3 5.1 %all-to-all-start.1 = ((bf16[64,112,128]{2,1,0:T(8,128)(2,1)}), bf16[64,112,128]{2,1,0:T(8,128)(2,1)S(1)}, u32[]{:S(2)}, u32[]{:S(2)}) async-start(bf16[64,112,128]{2,1,0:T(8,128)(2,1)} %pair_grads_kernel.1), calls=%async_computation.1 | async-start | bytes 3670016 | tf_op jit(solution)/shard_map/all_to_all | solution.py:486
  81.4 3.8 %collective-permute-start.17 = (bf16[4,1,64,128]{3,2,1,0:T(8,128)(2,1)S(1)}, bf16[4,1,64,128]{3,2,1,0:T(8,128)(2,1)S(1)}, u32[]{:S(2)}, u32[]{:S(2)}) collective-permute-start(bf16[4,1,64,128]{3,2,1,0:T(8,128)(2,1)S(1)} %copy-done.14), channel_id=1, source_target_pairs={{0,15},{1,0},{2,1},{3,2},{4,3},{5,4},{6,5},{7,6},{8,7},{9,8},{10,9... | collective-permute-start | bytes 196616 | tf_op jit(solution)/shard_map/ppermute | solution.py:22
  85.2 20.2 %all-to-all-done.1.pieces = bf16[64,112,128]{2,1,0:T(8,128)(2,1)S(1)} async-done(((bf16[64,112,128]{2,1,0:T(8,128)(2,1)}), bf16[64,112,128]{2,1,0:T(8,128)(2,1)S(1)}, u32[]{:S(2)}, u32[]{:S(2)}) %all-to-all-start.1) | async-done | bytes 1835040 | tf_op jit(solution)/shard_map/all_to_all | solution.py:486
  106.5 6.9 %all-to-all-start.2 = ((bf16[64,56,128]{2,1,0:T(8,128)(2,1)}), bf16[64,56,128]{2,1,0:T(8,128)(2,1)S(1)}, u32[]{:S(2)}, u32[]{:S(2)}) async-start(bf16[64,56,128]{2,1,0:T(8,128)(2,1)} %get-tuple-element.99), calls=%async_computation.2 | async-start | bytes 1835008 | tf_op jit(solution)/shard_map/all_to_all | solution.py:491
  118.1 2.2 %collective-permute-start.20 = (bf16[2,56,128]{2,1,0:T(8,128)(2,1)S(1)}, bf16[2,56,128]{2,1,0:T(8,128)(2,1)S(1)}, u32[]{:S(2)}, u32[]{:S(2)}) collective-permute-start(bf16[2,56,128]{2,1,0:T(8,128)(2,1)S(1)} %maximum_select_fusion.pair_0), channel_id=1, source_target_pairs={{0,64},{32,96},{64,0},{96,32},{1,65},{33,97},{65,1},{97,33},{2,66}... | collective-permute-start | bytes 86024 | tf_op jit(solution)/shard_map/ppermute | solution.py:30
  123.0 5.5 %collective-permute-done.19.pair_1 = bf16[2,56,128]{2,1,0:T(8,128)(2,1)S(1)} collective-permute-done((bf16[2,56,128]{2,1,0:T(8,128)(2,1)S(1)}, bf16[2,56,128]{2,1,0:T(8,128)(2,1)S(1)}, u32[]{:S(2)}, u32[]{:S(2)}) %collective-permute-start.19) | collective-permute-done | bytes 28704 | tf_op jit(solution)/shard_map/ppermute | solution.py:30
  129.3 3.8 %collective-permute-start.24 = (bf16[3584,128]{1,0:T(8,128)(2,1)S(1)}, bf16[3584,128]{1,0:T(8,128)(2,1)S(1)}, u32[]{:S(2)}, u32[]{:S(2)}) collective-permute-start(bf16[3584,128]{1,0:T(8,128)(2,1)S(1)} %bitcast.22), channel_id=1, source_target_pairs={{0,16},{16,0},{1,17},{17,1},{2,18},{18,2},{3,19},{19,3},{4,20},{20... | collective-permute-start | bytes 2752520 | tf_op jit(solution)/shard_map/ppermute | solution.py:26
  133.1 2.9 %outer_input_kernel.1 = bf16[4,4,64,128]{3,2,1,0:T(8,128)(2,1)} custom-call(bf16[4,4,64,128]{3,2,1,0:T(8,128)(2,1)} %get-tuple-element.85.own, bf16[4,1,64,128]{3,2,1,0:T(8,128)(2,1)} %copy-done.9, bf16[4,1,64,128]{3,2,1,0:T(8,128)(2,1)} %copy-done.10, bf16[1,6,64,128]{3,2,1,0:T(8,128)(2,1)S(1)} %collective-permute-done.22.left, ...), custom_call_target="tpu_custom_call" | custom-call | flops 11324620 | bytes 80281 | tf_op jit(solution)/shard_map/outer_input_kernel/pallas_call | solution.py:398
  136.0 2.1 %finish_kernel.1 = (f32[3456,128]{1,0:T(8,128)}, f32[3456,128]{1,0:T(8,128)}) custom-call(s32[1]{0:T(128)} %bitcast.core, bf16[3584,128]{1,0:T(8,128)(2,1)S(1)} %bitcast.23, bf16[3584,128]{1,0:T(8,128)(2,1)S(1)} %collective-permute-done.24.other), custom_call_target="tpu_custom_call" | custom-call | tf_op jit(solution)/shard_map/finish_kernel/pallas_call | solution.py:515
  (84 shorter events, 30.4 us)
Async XLA Ops:
  2.3 12.6 %collective-permute-start = (bf16[5,2,64,128]{3,2,1,0:T(8,128)(2,1)}, bf16[5,2,64,128]{3,2,1,0:T(8,128)(2,1)S(1)}, u32[]{:S(2)}, u32[]{:S(2)}) collective-permute-start(bf16[5,2,64,128]{3,2,1,0:T(8,128)(2,1)} %get-tuple-element.62), channel_id=1, source_target_pairs={{0,1},{1,2},{2,3},{3,4},{4,5},{5,6},{6,7},{7,8},{8,9},{9,10},{10,1... | collective-permute-start | bytes 491528 | tf_op jit(solution)/shard_map/ppermute | solution.py:22
  4.5 10.5 %collective-permute-start.1 = (bf16[5,2,64,128]{3,2,1,0:T(8,128)(2,1)S(1)}, bf16[5,2,64,128]{3,2,1,0:T(8,128)(2,1)S(1)}, u32[]{:S(2)}, u32[]{:S(2)}) collective-permute-start(bf16[5,2,64,128]{3,2,1,0:T(8,128)(2,1)S(1)} %get-tuple-element.63), channel_id=1, source_target_pairs={{0,15},{1,0},{2,1},{3,2},{4,3},{5,4},{6,5},{7,6},{8,7},{9,8},{10,9... | collective-permute-start | bytes 491528 | tf_op jit(solution)/shard_map/ppermute | solution.py:22
  11.3 20.9 %all-to-all-start = ((bf16[16,27,8,128]{3,2,1,0:T(8,128)(2,1)}), bf16[16,27,8,128]{3,2,1,0:T(8,128)(2,1)S(1)}, u32[]{:S(2)}, u32[]{:S(2)}) async-start(bf16[16,27,8,128]{3,2,1,0:T(8,128)(2,1)} %broadcast_in_dim.3), calls=%async_computation | async-start | bytes 1769472 | tf_op jit(solution)/shard_map/all_to_all | solution.py:427
  15.7 6.1 %collective-permute-start.2 = (bf16[20,64,128]{2,1,0:T(8,128)(2,1)S(1)}, bf16[20,64,128]{2,1,0:T(8,128)(2,1)S(1)}, u32[]{:S(2)}, u32[]{:S(2)}) collective-permute-start(bf16[20,64,128]{2,1,0:T(8,128)(2,1)S(1)} %get-tuple-element.64), channel_id=1, source_target_pairs={{0,16},{16,32},{32,48},{48,64},{64,80},{80,96},{96,112},{112,0},{1... | collective-permute-start | bytes 983048 | tf_op jit(solution)/shard_map/ppermute | solution.py:22
  17.7 6.8 %collective-permute-start.3 = (bf16[20,64,128]{2,1,0:T(8,128)(2,1)S(1)}, bf16[20,64,128]{2,1,0:T(8,128)(2,1)S(1)}, u32[]{:S(2)}, u32[]{:S(2)}) collective-permute-start(bf16[20,64,128]{2,1,0:T(8,128)(2,1)S(1)} %get-tuple-element.65), channel_id=1, source_target_pairs={{0,112},{16,0},{32,16},{48,32},{64,48},{80,64},{96,80},{112,96},{1... | collective-permute-start | bytes 983048 | tf_op jit(solution)/shard_map/ppermute | solution.py:22
  32.2 11.7 %collective-permute-start.8 = (bf16[16,27,8,128]{3,2,1,0:T(8,128)(2,1)S(1)}, bf16[16,27,8,128]{3,2,1,0:T(8,128)(2,1)S(1)}, u32[]{:S(2)}, u32[]{:S(2)}) collective-permute-start(bf16[16,27,8,128]{3,2,1,0:T(8,128)(2,1)S(1)} %all-to-all-done.mine), channel_id=1, source_target_pairs={{0,16},{16,0},{1,17},{17,1},{2,18},{18,2},{3,19},{19,3},{4,20},{20... | collective-permute-start | bytes 2654216 | tf_op jit(solution)/shard_map/ppermute | solution.py:26
  32.2 6.5 %collective-permute-start.4 = (bf16[2,2,32,128]{3,2,1,0:T(8,128)(2,1)}, bf16[2,2,32,128]{3,2,1,0:T(8,128)(2,1)S(1)}, u32[]{:S(2)}, u32[]{:S(2)}) collective-permute-start(bf16[2,2,32,128]{3,2,1,0:T(8,128)(2,1)} %get-tuple-element.67.own), channel_id=1, source_target_pairs={{0,1},{1,2},{2,3},{3,4},{4,5},{5,6},{6,7},{7,8},{8,9},{9,10},{10,1... | collective-permute-start | bytes 98312 | tf_op jit(solution)/shard_map/ppermute | solution.py:22
  33.8 4.9 %collective-permute-start.5 = (bf16[2,2,32,128]{3,2,1,0:T(8,128)(2,1)}, bf16[2,2,32,128]{3,2,1,0:T(8,128)(2,1)S(1)}, u32[]{:S(2)}, u32[]{:S(2)}) collective-permute-start(bf16[2,2,32,128]{3,2,1,0:T(8,128)(2,1)} %get-tuple-element.67.own), channel_id=1, source_target_pairs={{0,15},{1,0},{2,1},{3,2},{4,3},{5,4},{6,5},{7,6},{8,7},{9,8},{10,9... | collective-permute-start | bytes 98312 | tf_op jit(solution)/shard_map/ppermute | solution.py:22
  39.4 4.9 %collective-permute-start.6 = (bf16[2,6,32,128]{3,2,1,0:T(8,128)(2,1)S(1)}, bf16[2,6,32,128]{3,2,1,0:T(8,128)(2,1)S(1)}, u32[]{:S(2)}, u32[]{:S(2)}) collective-permute-start(bf16[2,6,32,128]{3,2,1,0:T(8,128)(2,1)S(1)} %get-tuple-element.68), channel_id=1, source_target_pairs={{0,16},{16,32},{32,48},{48,64},{64,80},{80,96},{96,112},{112,0},{1... | collective-permute-start | bytes 294920 | tf_op jit(solution)/shard_map/ppermute | solution.py:22
  42.1 4.0 %collective-permute-start.7 = (bf16[2,6,32,128]{3,2,1,0:T(8,128)(2,1)S(1)}, bf16[2,6,32,128]{3,2,1,0:T(8,128)(2,1)S(1)}, u32[]{:S(2)}, u32[]{:S(2)}) collective-permute-start(bf16[2,6,32,128]{3,2,1,0:T(8,128)(2,1)S(1)} %get-tuple-element.69), channel_id=1, source_target_pairs={{0,112},{16,0},{32,16},{48,32},{64,48},{80,64},{96,80},{112,96},{1... | collective-permute-start | bytes 294920 | tf_op jit(solution)/shard_map/ppermute | solution.py:22
  42.1 30.4 %collective-permute-start.14 = (bf16[6,6,64,128]{3,2,1,0:T(8,128)(2,1)}, bf16[6,6,64,128]{3,2,1,0:T(8,128)(2,1)S(1)}, u32[]{:S(2)}, u32[]{:S(2)}) collective-permute-start(bf16[6,6,64,128]{3,2,1,0:T(8,128)(2,1)} %get-tuple-element.86), channel_id=1, source_target_pairs={{0,16},{16,0},{1,17},{17,1},{2,18},{18,2},{3,19},{19,3},{4,20},{20... | collective-permute-start | bytes 1769480 | tf_op jit(solution)/shard_map/ppermute | solution.py:26
  50.0 6.4 %collective-permute-start.10 = (bf16[4,1,64,128]{3,2,1,0:T(8,128)(2,1)S(1)}, bf16[4,1,64,128]{3,2,1,0:T(8,128)(2,1)S(1)}, u32[]{:S(2)}, u32[]{:S(2)}) collective-permute-start(bf16[4,1,64,128]{3,2,1,0:T(8,128)(2,1)S(1)} %get-tuple-element.75), channel_id=1, source_target_pairs={{0,15},{1,0},{2,1},{3,2},{4,3},{5,4},{6,5},{7,6},{8,7},{9,8},{10,9... | collective-permute-start | bytes 196616 | tf_op jit(solution)/shard_map/ppermute | solution.py:22
  55.0 6.4 %collective-permute-start.9 = (bf16[4,1,64,128]{3,2,1,0:T(8,128)(2,1)S(1)}, bf16[4,1,64,128]{3,2,1,0:T(8,128)(2,1)S(1)}, u32[]{:S(2)}, u32[]{:S(2)}) collective-permute-start(bf16[4,1,64,128]{3,2,1,0:T(8,128)(2,1)S(1)} %get-tuple-element.74), channel_id=1, source_target_pairs={{0,1},{1,2},{2,3},{3,4},{4,5},{5,6},{6,7},{7,8},{8,9},{9,10},{10,1... | collective-permute-start | bytes 196616 | tf_op jit(solution)/shard_map/ppermute | solution.py:22
  63.8 4.2 %collective-permute-start.13 = (bf16[1,6,64,128]{3,2,1,0:T(8,128)(2,1)S(1)}, bf16[1,6,64,128]{3,2,1,0:T(8,128)(2,1)S(1)}, u32[]{:S(2)}, u32[]{:S(2)}) collective-permute-start(bf16[1,6,64,128]{3,2,1,0:T(8,128)(2,1)S(1)} %get-tuple-element.81), channel_id=1, source_target_pairs={{0,112},{16,0},{32,16},{48,32},{64,48},{80,64},{96,80},{112,96},{1... | collective-permute-start | bytes 294920 | tf_op jit(solution)/shard_map/ppermute | solution.py:22
  75.3 30.1 %all-to-all-start.1 = ((bf16[64,112,128]{2,1,0:T(8,128)(2,1)}), bf16[64,112,128]{2,1,0:T(8,128)(2,1)S(1)}, u32[]{:S(2)}, u32[]{:S(2)}) async-start(bf16[64,112,128]{2,1,0:T(8,128)(2,1)} %pair_grads_kernel.1), calls=%async_computation.1 | async-start | bytes 3670016 | tf_op jit(solution)/shard_map/all_to_all | solution.py:486
  80.4 26.2 %collective-permute-start.16 = (bf16[4,1,64,128]{3,2,1,0:T(8,128)(2,1)S(1)}, bf16[4,1,64,128]{3,2,1,0:T(8,128)(2,1)S(1)}, u32[]{:S(2)}, u32[]{:S(2)}) collective-permute-start(bf16[4,1,64,128]{3,2,1,0:T(8,128)(2,1)S(1)} %copy-done.15), channel_id=1, source_target_pairs={{0,1},{1,2},{2,3},{3,4},{4,5},{5,6},{6,7},{7,8},{8,9},{9,10},{10,1... | collective-permute-start | bytes 196616 | tf_op jit(solution)/shard_map/ppermute | solution.py:22
  81.4 25.1 %collective-permute-start.17 = (bf16[4,1,64,128]{3,2,1,0:T(8,128)(2,1)S(1)}, bf16[4,1,64,128]{3,2,1,0:T(8,128)(2,1)S(1)}, u32[]{:S(2)}, u32[]{:S(2)}) collective-permute-start(bf16[4,1,64,128]{3,2,1,0:T(8,128)(2,1)S(1)} %copy-done.14), channel_id=1, source_target_pairs={{0,15},{1,0},{2,1},{3,2},{4,3},{5,4},{6,5},{7,6},{8,7},{9,8},{10,9... | collective-permute-start | bytes 196616 | tf_op jit(solution)/shard_map/ppermute | solution.py:22
  106.5 22.7 %all-to-all-start.2 = ((bf16[64,56,128]{2,1,0:T(8,128)(2,1)}), bf16[64,56,128]{2,1,0:T(8,128)(2,1)S(1)}, u32[]{:S(2)}, u32[]{:S(2)}) async-start(bf16[64,56,128]{2,1,0:T(8,128)(2,1)} %get-tuple-element.99), calls=%async_computation.2 | async-start | bytes 1835008 | tf_op jit(solution)/shard_map/all_to_all | solution.py:491
  115.5 13.7 %collective-permute-start.22 = (bf16[1,6,64,128]{3,2,1,0:T(8,128)(2,1)S(1)}, bf16[1,6,64,128]{3,2,1,0:T(8,128)(2,1)S(1)}, u32[]{:S(2)}, u32[]{:S(2)}) collective-permute-start(bf16[1,6,64,128]{3,2,1,0:T(8,128)(2,1)S(1)} %get-tuple-element.102), channel_id=1, source_target_pairs={{0,16},{16,32},{32,48},{48,64},{64,80},{80,96},{96,112},{112,0},{1... | collective-permute-start | bytes 294920 | tf_op jit(solution)/shard_map/ppermute | solution.py:22
  116.7 12.5 %collective-permute-start.23 = (bf16[1,6,64,128]{3,2,1,0:T(8,128)(2,1)S(1)}, bf16[1,6,64,128]{3,2,1,0:T(8,128)(2,1)S(1)}, u32[]{:S(2)}, u32[]{:S(2)}) collective-permute-start(bf16[1,6,64,128]{3,2,1,0:T(8,128)(2,1)S(1)} %get-tuple-element.103), channel_id=1, source_target_pairs={{0,112},{16,0},{32,16},{48,32},{64,48},{80,64},{96,80},{112,96},{1... | collective-permute-start | bytes 294920 | tf_op jit(solution)/shard_map/ppermute | solution.py:22
  116.7 11.8 %collective-permute-start.19 = (bf16[2,56,128]{2,1,0:T(8,128)(2,1)S(1)}, bf16[2,56,128]{2,1,0:T(8,128)(2,1)S(1)}, u32[]{:S(2)}, u32[]{:S(2)}) collective-permute-start(bf16[2,56,128]{2,1,0:T(8,128)(2,1)S(1)} %maximum_select_fusion.pair_0), channel_id=1, source_target_pairs={{0,32},{32,64},{64,96},{96,0},{1,33},{33,65},{65,97},{97,1},{2,34}... | collective-permute-start | bytes 86024 | tf_op jit(solution)/shard_map/ppermute | solution.py:30
  118.1 10.4 %collective-permute-start.20 = (bf16[2,56,128]{2,1,0:T(8,128)(2,1)S(1)}, bf16[2,56,128]{2,1,0:T(8,128)(2,1)S(1)}, u32[]{:S(2)}, u32[]{:S(2)}) collective-permute-start(bf16[2,56,128]{2,1,0:T(8,128)(2,1)S(1)} %maximum_select_fusion.pair_0), channel_id=1, source_target_pairs={{0,64},{32,96},{64,0},{96,32},{1,65},{33,97},{65,1},{97,33},{2,66}... | collective-permute-start | bytes 86024 | tf_op jit(solution)/shard_map/ppermute | solution.py:30
  120.3 8.2 %collective-permute-start.21 = (bf16[2,56,128]{2,1,0:T(8,128)(2,1)S(1)}, bf16[2,56,128]{2,1,0:T(8,128)(2,1)S(1)}, u32[]{:S(2)}, u32[]{:S(2)}) collective-permute-start(bf16[2,56,128]{2,1,0:T(8,128)(2,1)S(1)} %maximum_select_fusion.pair_0), channel_id=1, source_target_pairs={{0,96},{32,0},{64,32},{96,64},{1,97},{33,1},{65,33},{97,65},{2,98}... | collective-permute-start | bytes 86024 | tf_op jit(solution)/shard_map/ppermute | solution.py:30
  129.3 6.7 %collective-permute-start.24 = (bf16[3584,128]{1,0:T(8,128)(2,1)S(1)}, bf16[3584,128]{1,0:T(8,128)(2,1)S(1)}, u32[]{:S(2)}, u32[]{:S(2)}) collective-permute-start(bf16[3584,128]{1,0:T(8,128)(2,1)S(1)} %bitcast.22), channel_id=1, source_target_pairs={{0,16},{16,0},{1,17},{17,1},{2,18},{18,2},{3,19},{19,3},{4,20},{20... | collective-permute-start | bytes 2752520 | tf_op jit(solution)/shard_map/ppermute | solution.py:26
  (20 other events, 199.6 us)

commit v16 on v15

--- a/solution.py
+++ b/solution.py
@@ -64,6 +64,14 @@
 
 def exchange_x(low, high):
     return shifted(high, GX, 1), shifted(low, GX, -1)
+
+
+def halo_pieces(own, width, first, last):
+    before, after = shifted(last, GY, 1), shifted(first, GY, -1)
+    size_x, size_y, size_z, chans = own.shape
+    slab = (width, size_y + 2 * width, size_z, chans)
+    low, high = call(slab_kernel, [(slab, BF16)] * 2, [], 0, own, before, after)
+    return own, before, after, *exchange_x(low, high)
 
 
 def fill_padded(padded, own, before, after, left, right):
@@ -439,7 +447,7 @@
     edge = (4, 1, 64, 128)
     field_keep, field_send, slope_one, slope_two, pooled = call(
         forward_kernel,
-        [(field, BF16, True), (field, BF16, True), (block, BF16, True), (block, BF16, True), ((2, 2, 32, 128), BF16, True)],
+        [(field, BF16, True), (field, BF16, True), (block, BF16, True), (block, BF16, True), ((2, 2, 32, 128), BF16)],
         [((8, 8, 64, 128), BF16), ((1152, 384), BF16), (field, BF16), ((4, 2, 64, 128), F32)],
         3 * conv_flops, core_ref, features, f_before, f_after, f_left, f_right, taps_one, taps_two,
     )
@@ -447,9 +455,7 @@
     mine, pooled = lax.optimization_barrier((mine, pooled))
     theirs = swap_cores(mine)
     (taps_three,) = call(interleave_kernel, [((27, 256, 128), BF16)], [], 0, core_ref, mine, theirs)
-    p_before, p_after = shifted(pooled, GY, 1), shifted(pooled, GY, -1)
-    low, high = call(slab_kernel, [((2, 6, 32, 128), BF16)] * 2, [], 0, in_hbm(pooled), p_before, p_after)
-    p_pieces = pooled, p_before, p_after, *exchange_x(low, high)
+    p_pieces = halo_pieces(pooled, 2, pooled, pooled)
     bottleneck, bundle, err_two, err_first, err_last = call(
         bottom_kernel,
         [((2, 2, 32, 256), BF16, True), ((24, 32, 128), BF16), (block, BF16), (edge, BF16), (edge, BF16)],

time: 139 us -> 139 us (level)
    unnamed x32 -> x36, local copies, waits for them, and re-layouts: 1.58 us -> 2.95 us
  transfers between devices with their start and end apart: 28 -> 28, of which waited for: 11 -> 11; matrix products, arithmetic and copies ran while one was open for 1% -> 1% of each run, Pallas kernels for 17% -> 16%
where the time goes in v16:
time: 139 us
  starting transfers between devices  58.6 us (42%)
  waiting for transfers between devices  45.7 us (33%)
  Pallas kernels  28.6 us (21%)
  local copies, waits for them, and re-layouts  3.98 us (3%)
    ppermute x16, starting transfers between devices, shifted(): lax.ppermute(array, axes, [(i, (i + step) % count) for i in range(count)])  28.5 us
    pallas_call x15, Pallas kernels, call(): pl.pallas_call(kernel, out_shape=shapes, in_specs=[pl.BlockSpec(memory_sp...  25.9 us
    all_to_all x1, waiting for transfers between devices, on_device(): lax.all_to_all(kept, FLAT, 0, 0)  20.2 us
    ppermute x16, waiting for transfers between devices, shifted(): lax.ppermute(array, axes, [(i, (i + step) % count) for i in range(count)])  19.6 us
    ppermute x6, starting transfers between devices, swap_cores(): return lax.ppermute(array, 'c', [(0, 1), (1, 0)])  9.74 us
    all_to_all x1, starting transfers between devices, on_device(): whole = lax.all_to_all(part, FLAT, 0, 0).reshape(64 * PIECE, 128)  6.9 us
    ppermute x3, waiting for transfers between devices, ring_pieces(): lax.ppermute(pieces[d], axis, [(i, (i + d) % 4) for i in range(4)])  5.49 us
    all_to_all x1, starting transfers between devices, on_device(): lax.all_to_all(kept, FLAT, 0, 0)  5.06 us
  transfers between devices with their start and end apart: 28, of which 11 were waited for; matrix products, arithmetic and copies ran while one was open for 1% of the time, Pallas kernels for 16%

profile of v16, /device:TPU:1, one launch (start us, length us, event | category | flops | bytes accessed | tf_op | source)
XLA Modules:
  0.0 138.6 jit_solution(1371612543278379004)
XLA Ops:
  2.3 2.1 %collective-permute-start = (bf16[5,2,64,128]{3,2,1,0:T(8,128)(2,1)}, bf16[5,2,64,128]{3,2,1,0:T(8,128)(2,1)S(1)}, u32[]{:S(2)}, u32[]{:S(2)}) collective-permute-start(bf16[5,2,64,128]{3,2,1,0:T(8,128)(2,1)} %get-tuple-element.62), channel_id=1, source_target_pairs={{0,1},{1,2},{2,3},{3,4},{4,5},{5,6},{6,7},{7,8},{8,9},{9,10},{10,1... | collective-permute-start | bytes 491528 | tf_op jit(solution)/shard_map/ppermute | solution.py:22
  4.5 4.9 %collective-permute-start.1 = (bf16[5,2,64,128]{3,2,1,0:T(8,128)(2,1)S(1)}, bf16[5,2,64,128]{3,2,1,0:T(8,128)(2,1)S(1)}, u32[]{:S(2)}, u32[]{:S(2)}) collective-permute-start(bf16[5,2,64,128]{3,2,1,0:T(8,128)(2,1)S(1)} %get-tuple-element.63), channel_id=1, source_target_pairs={{0,15},{1,0},{2,1},{3,2},{4,3},{5,4},{6,5},{7,6},{8,7},{9,8},{10,9... | collective-permute-start | bytes 491528 | tf_op jit(solution)/shard_map/ppermute | solution.py:22
  11.3 3.6 %all-to-all-start = ((bf16[16,27,8,128]{3,2,1,0:T(8,128)(2,1)}), bf16[16,27,8,128]{3,2,1,0:T(8,128)(2,1)S(1)}, u32[]{:S(2)}, u32[]{:S(2)}) async-start(bf16[16,27,8,128]{3,2,1,0:T(8,128)(2,1)} %broadcast_in_dim.3), calls=%async_computation | async-start | bytes 1769472 | tf_op jit(solution)/shard_map/all_to_all | solution.py:435
  15.7 2.1 %collective-permute-start.2 = (bf16[20,64,128]{2,1,0:T(8,128)(2,1)S(1)}, bf16[20,64,128]{2,1,0:T(8,128)(2,1)S(1)}, u32[]{:S(2)}, u32[]{:S(2)}) collective-permute-start(bf16[20,64,128]{2,1,0:T(8,128)(2,1)S(1)} %get-tuple-element.64), channel_id=1, source_target_pairs={{0,16},{16,32},{32,48},{48,64},{64,80},{80,96},{96,112},{112,0},{1... | collective-permute-start | bytes 983048 | tf_op jit(solution)/shard_map/ppermute | solution.py:22
  17.7 4.0 %collective-permute-done.2.left.f_left = bf16[20,64,128]{2,1,0:T(8,128)(2,1)S(1)} collective-permute-done((bf16[20,64,128]{2,1,0:T(8,128)(2,1)S(1)}, bf16[20,64,128]{2,1,0:T(8,128)(2,1)S(1)}, u32[]{:S(2)}, u32[]{:S(2)}) %collective-permute-start.2) | collective-permute-done | bytes 327712 | tf_op jit(solution)/shard_map/ppermute | solution.py:22
  21.7 2.8 %collective-permute-done.3.right.f_right = bf16[20,64,128]{2,1,0:T(8,128)(2,1)S(1)} collective-permute-done((bf16[20,64,128]{2,1,0:T(8,128)(2,1)S(1)}, bf16[20,64,128]{2,1,0:T(8,128)(2,1)S(1)}, u32[]{:S(2)}, u32[]{:S(2)}) %collective-permute-start.3) | collective-permute-done | bytes 327712 | tf_op jit(solution)/shard_map/ppermute | solution.py:22
  25.4 6.8 %forward_kernel.1 = (bf16[6,6,64,128]{3,2,1,0:T(8,128)(2,1)}, bf16[6,6,64,128]{3,2,1,0:T(8,128)(2,1)}, bf16[4,4,64,128]{3,2,1,0:T(8,128)(2,1)}, bf16[4,4,64,128]...) custom-call(s32[1]{0:T(128)} %bitcast.core, bf16[4,4,64,128]{3,2,1,0:T(8,128)(2,1)S(1)} %copy-done.4, ...), custom_call_target="tpu_custom_call" | custom-call | flops 135895456 | bytes 150733 | tf_op jit(solution)/shard_map/forward_kernel/pallas_call | solution.py:406
  34.4 3.4 %collective-permute-start.5 = (bf16[2,2,32,128]{3,2,1,0:T(8,128)(2,1)}, bf16[2,2,32,128]{3,2,1,0:T(8,128)(2,1)S(1)}, u32[]{:S(2)}, u32[]{:S(2)}) collective-permute-start(bf16[2,2,32,128]{3,2,1,0:T(8,128)(2,1)} %copy-done.13), channel_id=1, source_target_pairs={{0,15},{1,0},{2,1},{3,2},{4,3},{5,4},{6,5},{7,6},{8,7},{9,8},{10,9... | collective-permute-start | bytes 98312 | tf_op jit(solution)/shard_map/ppermute | solution.py:22
  40.1 2.6 %collective-permute-start.6 = (bf16[2,6,32,128]{3,2,1,0:T(8,128)(2,1)S(1)}, bf16[2,6,32,128]{3,2,1,0:T(8,128)(2,1)S(1)}, u32[]{:S(2)}, u32[]{:S(2)}) collective-permute-start(bf16[2,6,32,128]{3,2,1,0:T(8,128)(2,1)S(1)} %get-tuple-element.68), channel_id=1, source_target_pairs={{0,16},{16,32},{32,48},{48,64},{64,80},{80,96},{96,112},{112,0},{1... | collective-permute-start | bytes 294920 | tf_op jit(solution)/shard_map/ppermute | solution.py:22
  46.7 3.9 %bottom_kernel.1 = (bf16[2,2,32,256]{3,2,1,0:T(8,128)(2,1)}, bf16[24,32,128]{2,1,0:T(8,128)(2,1)S(1)}, bf16[4,4,64,128]{3,2,1,0:T(8,128)(2,1)S(1)}, bf16[4,1,64,...) custom-call(bf16[2,2,32,128]{3,2,1,0:T(8,128)(2,1)S(1)} %copy-done.15, ...), custom_call_target="tpu_custom_call" | custom-call | flops 45298484 | bytes 181862 | tf_op jit(solution)/shard_map/bottom_kernel/pallas_call | solution.py:406
  50.6 5.1 %collective-permute-start.10 = (bf16[4,1,64,128]{3,2,1,0:T(8,128)(2,1)S(1)}, bf16[4,1,64,128]{3,2,1,0:T(8,128)(2,1)S(1)}, u32[]{:S(2)}, u32[]{:S(2)}) collective-permute-start(bf16[4,1,64,128]{3,2,1,0:T(8,128)(2,1)S(1)} %get-tuple-element.75), channel_id=1, source_target_pairs={{0,15},{1,0},{2,1},{3,2},{4,3},{5,4},{6,5},{7,6},{8,7},{9,8},{10,9... | collective-permute-start | bytes 196616 | tf_op jit(solution)/shard_map/ppermute | solution.py:22
  57.0 5.1 %collective-permute-done.9.before = bf16[4,1,64,128]{3,2,1,0:T(8,128)(2,1)S(1)} collective-permute-done((bf16[4,1,64,128]{3,2,1,0:T(8,128)(2,1)S(1)}, bf16[4,1,64,128]{3,2,1,0:T(8,128)(2,1)S(1)}, u32[]{:S(2)}, u32[]{:S(2)}) %collective-permute-start.9) | collective-permute-done | bytes 65568 | tf_op jit(solution)/shard_map/ppermute | solution.py:22
  66.1 2.6 %collective-permute-done.13.right = bf16[1,6,64,128]{3,2,1,0:T(8,128)(2,1)S(1)} collective-permute-done((bf16[1,6,64,128]{3,2,1,0:T(8,128)(2,1)S(1)}, bf16[1,6,64,128]{3,2,1,0:T(8,128)(2,1)S(1)}, u32[]{:S(2)}, u32[]{:S(2)}) %collective-permute-start.13) | collective-permute-done | bytes 98336 | tf_op jit(solution)/shard_map/ppermute | solution.py:22
  68.7 2.6 %first_errors_kernel.1 = (bf16[4,4,64,128]{3,2,1,0:T(8,128)(2,1)}, bf16[4,1,64,128]{3,2,1,0:T(8,128)(2,1)}, bf16[4,1,64,128]{3,2,1,0:T(8,128)(2,1)}, bf16[4,4,64...) custom-call(s32[1]{0:T(128)} %bitcast.core, bf16[4,4,64,128]{3,2,1,0:T(8,128)(2,1)S(1)} %get-tuple-element.73.own, ...), custom_call_target="tpu_custom_call" | custom-call | flops 45298484 | bytes 86835 | tf_op jit(solution)/shard_map/first_errors_kernel/pallas_call | solution.py:406
  73.1 2.7 %pair_grads_kernel.1 = bf16[64,112,128]{2,1,0:T(8,128)(2,1)} custom-call(bf16[6,6,64,128]{3,2,1,0:T(8,128)(2,1)S(1)} %collective-permute-done.14.fields, bf16[4,4,64,128]{3,2,1,0:T(8,128)(2,1)S(1)} %collective-permute-done.15.errors, f32[1152,384]{1,0:T(8,128)S(1)} %own_grads_kernel.1.own_total, bf16[64,56,128]{2,1,0:T(8,128)(2,1)S(1)} %bottom_grads_kernel.1.three), custom_call_target="tpu_custom_call" | custom-call | flops 45298484 | bytes 176947 | tf_op jit(solution)/shard_map/pair_grads_kernel/pallas_call | solution.py:406
  75.9 5.1 %all-to-all-start.1 = ((bf16[64,112,128]{2,1,0:T(8,128)(2,1)}), bf16[64,112,128]{2,1,0:T(8,128)(2,1)S(1)}, u32[]{:S(2)}, u32[]{:S(2)}) async-start(bf16[64,112,128]{2,1,0:T(8,128)(2,1)} %pair_grads_kernel.1), calls=%async_computation.1 | async-start | bytes 3670016 | tf_op jit(solution)/shard_map/all_to_all | solution.py:492
  82.1 3.8 %collective-permute-start.17 = (bf16[4,1,64,128]{3,2,1,0:T(8,128)(2,1)S(1)}, bf16[4,1,64,128]{3,2,1,0:T(8,128)(2,1)S(1)}, u32[]{:S(2)}, u32[]{:S(2)}) collective-permute-start(bf16[4,1,64,128]{3,2,1,0:T(8,128)(2,1)S(1)} %copy-done.16), channel_id=1, source_target_pairs={{0,15},{1,0},{2,1},{3,2},{4,3},{5,4},{6,5},{7,6},{8,7},{9,8},{10,9... | collective-permute-start | bytes 196616 | tf_op jit(solution)/shard_map/ppermute | solution.py:22
  85.8 20.2 %all-to-all-done.1.pieces = bf16[64,112,128]{2,1,0:T(8,128)(2,1)S(1)} async-done(((bf16[64,112,128]{2,1,0:T(8,128)(2,1)}), bf16[64,112,128]{2,1,0:T(8,128)(2,1)S(1)}, u32[]{:S(2)}, u32[]{:S(2)}) %all-to-all-start.1) | async-done | bytes 1835040 | tf_op jit(solution)/shard_map/all_to_all | solution.py:492
  107.2 6.9 %all-to-all-start.2 = ((bf16[64,56,128]{2,1,0:T(8,128)(2,1)}), bf16[64,56,128]{2,1,0:T(8,128)(2,1)S(1)}, u32[]{:S(2)}, u32[]{:S(2)}) async-start(bf16[64,56,128]{2,1,0:T(8,128)(2,1)} %get-tuple-element.99), calls=%async_computation.2 | async-start | bytes 1835008 | tf_op jit(solution)/shard_map/all_to_all | solution.py:497
  118.7 2.2 %collective-permute-start.20 = (bf16[2,56,128]{2,1,0:T(8,128)(2,1)S(1)}, bf16[2,56,128]{2,1,0:T(8,128)(2,1)S(1)}, u32[]{:S(2)}, u32[]{:S(2)}) collective-permute-start(bf16[2,56,128]{2,1,0:T(8,128)(2,1)S(1)} %maximum_select_fusion.pair_0), channel_id=1, source_target_pairs={{0,64},{32,96},{64,0},{96,32},{1,65},{33,97},{65,1},{97,33},{2,66}... | collective-permute-start | bytes 86024 | tf_op jit(solution)/shard_map/ppermute | solution.py:30
  123.7 5.5 %collective-permute-done.19.pair_1 = bf16[2,56,128]{2,1,0:T(8,128)(2,1)S(1)} collective-permute-done((bf16[2,56,128]{2,1,0:T(8,128)(2,1)S(1)}, bf16[2,56,128]{2,1,0:T(8,128)(2,1)S(1)}, u32[]{:S(2)}, u32[]{:S(2)}) %collective-permute-start.19) | collective-permute-done | bytes 28704 | tf_op jit(solution)/shard_map/ppermute | solution.py:30
  129.9 3.8 %collective-permute-start.24 = (bf16[3584,128]{1,0:T(8,128)(2,1)S(1)}, bf16[3584,128]{1,0:T(8,128)(2,1)S(1)}, u32[]{:S(2)}, u32[]{:S(2)}) collective-permute-start(bf16[3584,128]{1,0:T(8,128)(2,1)S(1)} %bitcast.22), channel_id=1, source_target_pairs={{0,16},{16,0},{1,17},{17,1},{2,18},{18,2},{3,19},{19,3},{4,20},{20... | collective-permute-start | bytes 2752520 | tf_op jit(solution)/shard_map/ppermute | solution.py:26
  133.7 2.9 %outer_input_kernel.1 = bf16[4,4,64,128]{3,2,1,0:T(8,128)(2,1)} custom-call(bf16[4,4,64,128]{3,2,1,0:T(8,128)(2,1)} %get-tuple-element.85.own, bf16[4,1,64,128]{3,2,1,0:T(8,128)(2,1)} %copy-done.9, bf16[4,1,64,128]{3,2,1,0:T(8,128)(2,1)} %copy-done.10, bf16[1,6,64,128]{3,2,1,0:T(8,128)(2,1)S(1)} %collective-permute-done.22.left, ...), custom_call_target="tpu_custom_call" | custom-call | flops 11324620 | bytes 80281 | tf_op jit(solution)/shard_map/outer_input_kernel/pallas_call | solution.py:406
  136.6 2.1 %finish_kernel.1 = (f32[3456,128]{1,0:T(8,128)}, f32[3456,128]{1,0:T(8,128)}) custom-call(s32[1]{0:T(128)} %bitcast.core, bf16[3584,128]{1,0:T(8,128)(2,1)S(1)} %bitcast.23, bf16[3584,128]{1,0:T(8,128)(2,1)S(1)} %collective-permute-done.24.other), custom_call_target="tpu_custom_call" | custom-call | tf_op jit(solution)/shard_map/finish_kernel/pallas_call | solution.py:521
  (88 shorter events, 31.1 us)
Async XLA Ops:
  2.3 12.6 %collective-permute-start = (bf16[5,2,64,128]{3,2,1,0:T(8,128)(2,1)}, bf16[5,2,64,128]{3,2,1,0:T(8,128)(2,1)S(1)}, u32[]{:S(2)}, u32[]{:S(2)}) collective-permute-start(bf16[5,2,64,128]{3,2,1,0:T(8,128)(2,1)} %get-tuple-element.62), channel_id=1, source_target_pairs={{0,1},{1,2},{2,3},{3,4},{4,5},{5,6},{6,7},{7,8},{8,9},{9,10},{10,1... | collective-permute-start | bytes 491528 | tf_op jit(solution)/shard_map/ppermute | solution.py:22
  4.5 10.5 %collective-permute-start.1 = (bf16[5,2,64,128]{3,2,1,0:T(8,128)(2,1)S(1)}, bf16[5,2,64,128]{3,2,1,0:T(8,128)(2,1)S(1)}, u32[]{:S(2)}, u32[]{:S(2)}) collective-permute-start(bf16[5,2,64,128]{3,2,1,0:T(8,128)(2,1)S(1)} %get-tuple-element.63), channel_id=1, source_target_pairs={{0,15},{1,0},{2,1},{3,2},{4,3},{5,4},{6,5},{7,6},{8,7},{9,8},{10,9... | collective-permute-start | bytes 491528 | tf_op jit(solution)/shard_map/ppermute | solution.py:22
  11.3 21.5 %all-to-all-start = ((bf16[16,27,8,128]{3,2,1,0:T(8,128)(2,1)}), bf16[16,27,8,128]{3,2,1,0:T(8,128)(2,1)S(1)}, u32[]{:S(2)}, u32[]{:S(2)}) async-start(bf16[16,27,8,128]{3,2,1,0:T(8,128)(2,1)} %broadcast_in_dim.3), calls=%async_computation | async-start | bytes 1769472 | tf_op jit(solution)/shard_map/all_to_all | solution.py:435
  15.7 6.1 %collective-permute-start.2 = (bf16[20,64,128]{2,1,0:T(8,128)(2,1)S(1)}, bf16[20,64,128]{2,1,0:T(8,128)(2,1)S(1)}, u32[]{:S(2)}, u32[]{:S(2)}) collective-permute-start(bf16[20,64,128]{2,1,0:T(8,128)(2,1)S(1)} %get-tuple-element.64), channel_id=1, source_target_pairs={{0,16},{16,32},{32,48},{48,64},{64,80},{80,96},{96,112},{112,0},{1... | collective-permute-start | bytes 983048 | tf_op jit(solution)/shard_map/ppermute | solution.py:22
  17.7 6.8 %collective-permute-start.3 = (bf16[20,64,128]{2,1,0:T(8,128)(2,1)S(1)}, bf16[20,64,128]{2,1,0:T(8,128)(2,1)S(1)}, u32[]{:S(2)}, u32[]{:S(2)}) collective-permute-start(bf16[20,64,128]{2,1,0:T(8,128)(2,1)S(1)} %get-tuple-element.65), channel_id=1, source_target_pairs={{0,112},{16,0},{32,16},{48,32},{64,48},{80,64},{96,80},{112,96},{1... | collective-permute-start | bytes 983048 | tf_op jit(solution)/shard_map/ppermute | solution.py:22
  32.8 11.7 %collective-permute-start.8 = (bf16[16,27,8,128]{3,2,1,0:T(8,128)(2,1)S(1)}, bf16[16,27,8,128]{3,2,1,0:T(8,128)(2,1)S(1)}, u32[]{:S(2)}, u32[]{:S(2)}) collective-permute-start(bf16[16,27,8,128]{3,2,1,0:T(8,128)(2,1)S(1)} %all-to-all-done.mine), channel_id=1, source_target_pairs={{0,16},{16,0},{1,17},{17,1},{2,18},{18,2},{3,19},{19,3},{4,20},{20... | collective-permute-start | bytes 2654216 | tf_op jit(solution)/shard_map/ppermute | solution.py:26
  32.8 6.5 %collective-permute-start.4 = (bf16[2,2,32,128]{3,2,1,0:T(8,128)(2,1)}, bf16[2,2,32,128]{3,2,1,0:T(8,128)(2,1)S(1)}, u32[]{:S(2)}, u32[]{:S(2)}) collective-permute-start(bf16[2,2,32,128]{3,2,1,0:T(8,128)(2,1)} %copy-done.13), channel_id=1, source_target_pairs={{0,1},{1,2},{2,3},{3,4},{4,5},{5,6},{6,7},{7,8},{8,9},{9,10},{10,1... | collective-permute-start | bytes 98312 | tf_op jit(solution)/shard_map/ppermute | solution.py:22
  34.4 4.9 %collective-permute-start.5 = (bf16[2,2,32,128]{3,2,1,0:T(8,128)(2,1)}, bf16[2,2,32,128]{3,2,1,0:T(8,128)(2,1)S(1)}, u32[]{:S(2)}, u32[]{:S(2)}) collective-permute-start(bf16[2,2,32,128]{3,2,1,0:T(8,128)(2,1)} %copy-done.13), channel_id=1, source_target_pairs={{0,15},{1,0},{2,1},{3,2},{4,3},{5,4},{6,5},{7,6},{8,7},{9,8},{10,9... | collective-permute-start | bytes 98312 | tf_op jit(solution)/shard_map/ppermute | solution.py:22
  40.1 4.9 %collective-permute-start.6 = (bf16[2,6,32,128]{3,2,1,0:T(8,128)(2,1)S(1)}, bf16[2,6,32,128]{3,2,1,0:T(8,128)(2,1)S(1)}, u32[]{:S(2)}, u32[]{:S(2)}) collective-permute-start(bf16[2,6,32,128]{3,2,1,0:T(8,128)(2,1)S(1)} %get-tuple-element.68), channel_id=1, source_target_pairs={{0,16},{16,32},{32,48},{48,64},{64,80},{80,96},{96,112},{112,0},{1... | collective-permute-start | bytes 294920 | tf_op jit(solution)/shard_map/ppermute | solution.py:22
  42.7 4.0 %collective-permute-start.7 = (bf16[2,6,32,128]{3,2,1,0:T(8,128)(2,1)S(1)}, bf16[2,6,32,128]{3,2,1,0:T(8,128)(2,1)S(1)}, u32[]{:S(2)}, u32[]{:S(2)}) collective-permute-start(bf16[2,6,32,128]{3,2,1,0:T(8,128)(2,1)S(1)} %get-tuple-element.69), channel_id=1, source_target_pairs={{0,112},{16,0},{32,16},{48,32},{64,48},{80,64},{96,80},{112,96},{1... | collective-permute-start | bytes 294920 | tf_op jit(solution)/shard_map/ppermute | solution.py:22
  42.7 30.4 %collective-permute-start.14 = (bf16[6,6,64,128]{3,2,1,0:T(8,128)(2,1)}, bf16[6,6,64,128]{3,2,1,0:T(8,128)(2,1)S(1)}, u32[]{:S(2)}, u32[]{:S(2)}) collective-permute-start(bf16[6,6,64,128]{3,2,1,0:T(8,128)(2,1)} %get-tuple-element.86), channel_id=1, source_target_pairs={{0,16},{16,0},{1,17},{17,1},{2,18},{18,2},{3,19},{19,3},{4,20},{20... | collective-permute-start | bytes 1769480 | tf_op jit(solution)/shard_map/ppermute | solution.py:26
  50.6 6.4 %collective-permute-start.10 = (bf16[4,1,64,128]{3,2,1,0:T(8,128)(2,1)S(1)}, bf16[4,1,64,128]{3,2,1,0:T(8,128)(2,1)S(1)}, u32[]{:S(2)}, u32[]{:S(2)}) collective-permute-start(bf16[4,1,64,128]{3,2,1,0:T(8,128)(2,1)S(1)} %get-tuple-element.75), channel_id=1, source_target_pairs={{0,15},{1,0},{2,1},{3,2},{4,3},{5,4},{6,5},{7,6},{8,7},{9,8},{10,9... | collective-permute-start | bytes 196616 | tf_op jit(solution)/shard_map/ppermute | solution.py:22
  55.7 6.4 %collective-permute-start.9 = (bf16[4,1,64,128]{3,2,1,0:T(8,128)(2,1)S(1)}, bf16[4,1,64,128]{3,2,1,0:T(8,128)(2,1)S(1)}, u32[]{:S(2)}, u32[]{:S(2)}) collective-permute-start(bf16[4,1,64,128]{3,2,1,0:T(8,128)(2,1)S(1)} %get-tuple-element.74), channel_id=1, source_target_pairs={{0,1},{1,2},{2,3},{3,4},{4,5},{5,6},{6,7},{7,8},{8,9},{9,10},{10,1... | collective-permute-start | bytes 196616 | tf_op jit(solution)/shard_map/ppermute | solution.py:22
  64.4 4.2 %collective-permute-start.13 = (bf16[1,6,64,128]{3,2,1,0:T(8,128)(2,1)S(1)}, bf16[1,6,64,128]{3,2,1,0:T(8,128)(2,1)S(1)}, u32[]{:S(2)}, u32[]{:S(2)}) collective-permute-start(bf16[1,6,64,128]{3,2,1,0:T(8,128)(2,1)S(1)} %get-tuple-element.81), channel_id=1, source_target_pairs={{0,112},{16,0},{32,16},{48,32},{64,48},{80,64},{96,80},{112,96},{1... | collective-permute-start | bytes 294920 | tf_op jit(solution)/shard_map/ppermute | solution.py:22
  75.9 30.1 %all-to-all-start.1 = ((bf16[64,112,128]{2,1,0:T(8,128)(2,1)}), bf16[64,112,128]{2,1,0:T(8,128)(2,1)S(1)}, u32[]{:S(2)}, u32[]{:S(2)}) async-start(bf16[64,112,128]{2,1,0:T(8,128)(2,1)} %pair_grads_kernel.1), calls=%async_computation.1 | async-start | bytes 3670016 | tf_op jit(solution)/shard_map/all_to_all | solution.py:492
  81.0 26.2 %collective-permute-start.16 = (bf16[4,1,64,128]{3,2,1,0:T(8,128)(2,1)S(1)}, bf16[4,1,64,128]{3,2,1,0:T(8,128)(2,1)S(1)}, u32[]{:S(2)}, u32[]{:S(2)}) collective-permute-start(bf16[4,1,64,128]{3,2,1,0:T(8,128)(2,1)S(1)} %copy-done.17), channel_id=1, source_target_pairs={{0,1},{1,2},{2,3},{3,4},{4,5},{5,6},{6,7},{7,8},{8,9},{9,10},{10,1... | collective-permute-start | bytes 196616 | tf_op jit(solution)/shard_map/ppermute | solution.py:22
  82.1 25.1 %collective-permute-start.17 = (bf16[4,1,64,128]{3,2,1,0:T(8,128)(2,1)S(1)}, bf16[4,1,64,128]{3,2,1,0:T(8,128)(2,1)S(1)}, u32[]{:S(2)}, u32[]{:S(2)}) collective-permute-start(bf16[4,1,64,128]{3,2,1,0:T(8,128)(2,1)S(1)} %copy-done.16), channel_id=1, source_target_pairs={{0,15},{1,0},{2,1},{3,2},{4,3},{5,4},{6,5},{7,6},{8,7},{9,8},{10,9... | collective-permute-start | bytes 196616 | tf_op jit(solution)/shard_map/ppermute | solution.py:22
  107.2 22.7 %all-to-all-start.2 = ((bf16[64,56,128]{2,1,0:T(8,128)(2,1)}), bf16[64,56,128]{2,1,0:T(8,128)(2,1)S(1)}, u32[]{:S(2)}, u32[]{:S(2)}) async-start(bf16[64,56,128]{2,1,0:T(8,128)(2,1)} %get-tuple-element.99), calls=%async_computation.2 | async-start | bytes 1835008 | tf_op jit(solution)/shard_map/all_to_all | solution.py:497
  116.1 13.7 %collective-permute-start.22 = (bf16[1,6,64,128]{3,2,1,0:T(8,128)(2,1)S(1)}, bf16[1,6,64,128]{3,2,1,0:T(8,128)(2,1)S(1)}, u32[]{:S(2)}, u32[]{:S(2)}) collective-permute-start(bf16[1,6,64,128]{3,2,1,0:T(8,128)(2,1)S(1)} %get-tuple-element.102), channel_id=1, source_target_pairs={{0,16},{16,32},{32,48},{48,64},{64,80},{80,96},{96,112},{112,0},{1... | collective-permute-start | bytes 294920 | tf_op jit(solution)/shard_map/ppermute | solution.py:22
  117.4 12.5 %collective-permute-start.23 = (bf16[1,6,64,128]{3,2,1,0:T(8,128)(2,1)S(1)}, bf16[1,6,64,128]{3,2,1,0:T(8,128)(2,1)S(1)}, u32[]{:S(2)}, u32[]{:S(2)}) collective-permute-start(bf16[1,6,64,128]{3,2,1,0:T(8,128)(2,1)S(1)} %get-tuple-element.103), channel_id=1, source_target_pairs={{0,112},{16,0},{32,16},{48,32},{64,48},{80,64},{96,80},{112,96},{1... | collective-permute-start | bytes 294920 | tf_op jit(solution)/shard_map/ppermute | solution.py:22
  117.4 11.8 %collective-permute-start.19 = (bf16[2,56,128]{2,1,0:T(8,128)(2,1)S(1)}, bf16[2,56,128]{2,1,0:T(8,128)(2,1)S(1)}, u32[]{:S(2)}, u32[]{:S(2)}) collective-permute-start(bf16[2,56,128]{2,1,0:T(8,128)(2,1)S(1)} %maximum_select_fusion.pair_0), channel_id=1, source_target_pairs={{0,32},{32,64},{64,96},{96,0},{1,33},{33,65},{65,97},{97,1},{2,34}... | collective-permute-start | bytes 86024 | tf_op jit(solution)/shard_map/ppermute | solution.py:30
  118.7 10.4 %collective-permute-start.20 = (bf16[2,56,128]{2,1,0:T(8,128)(2,1)S(1)}, bf16[2,56,128]{2,1,0:T(8,128)(2,1)S(1)}, u32[]{:S(2)}, u32[]{:S(2)}) collective-permute-start(bf16[2,56,128]{2,1,0:T(8,128)(2,1)S(1)} %maximum_select_fusion.pair_0), channel_id=1, source_target_pairs={{0,64},{32,96},{64,0},{96,32},{1,65},{33,97},{65,1},{97,33},{2,66}... | collective-permute-start | bytes 86024 | tf_op jit(solution)/shard_map/ppermute | solution.py:30
  120.9 8.2 %collective-permute-start.21 = (bf16[2,56,128]{2,1,0:T(8,128)(2,1)S(1)}, bf16[2,56,128]{2,1,0:T(8,128)(2,1)S(1)}, u32[]{:S(2)}, u32[]{:S(2)}) collective-permute-start(bf16[2,56,128]{2,1,0:T(8,128)(2,1)S(1)} %maximum_select_fusion.pair_0), channel_id=1, source_target_pairs={{0,96},{32,0},{64,32},{96,64},{1,97},{33,1},{65,33},{97,65},{2,98}... | collective-permute-start | bytes 86024 | tf_op jit(solution)/shard_map/ppermute | solution.py:30
  129.9 6.7 %collective-permute-start.24 = (bf16[3584,128]{1,0:T(8,128)(2,1)S(1)}, bf16[3584,128]{1,0:T(8,128)(2,1)S(1)}, u32[]{:S(2)}, u32[]{:S(2)}) collective-permute-start(bf16[3584,128]{1,0:T(8,128)(2,1)S(1)} %bitcast.22), channel_id=1, source_target_pairs={{0,16},{16,0},{1,17},{17,1},{2,18},{18,2},{3,19},{19,3},{4,20},{20... | collective-permute-start | bytes 2752520 | tf_op jit(solution)/shard_map/ppermute | solution.py:26
  (22 other events, 201.0 us)
